TPU v7x, 32 devices: a whole 2x2x4 slice. The times are simulated.
32 devices in a mesh: batch: 8 (over z, x), rep: 4 (over y, core).
Axes of the slice: x: 2, y: 2, z: 4, core: 2. Of those that a mesh axis runs over, the one named last changes fastest.
Arguments:
- latents: bfloat16 [4, 16, 512, 1024], P('rep', 'batch'), may hold values from -6 to 6
- query_key_value_weight: bfloat16 [1024, 3072], P('batch'), may hold values from -0.1875 to 0.1875
- output_weight: bfloat16 [1024, 1024], P('batch'), may hold values from -1.5 to 1.5
- up_weight: bfloat16 [1024, 1024], P('batch'), may hold values from -0.1875 to 0.1875
- down_weight: bfloat16 [1024, 1024], P('batch'), may hold values from -0.1875 to 0.1875
- norm_gains: bfloat16 [2, 1024], P(None, 'batch'), may hold values from 0.099609375 to 1.8984375
- biases: bfloat16 [6, 1024], P(None, 'batch'), may hold values from -1.5 to 1.5
- feed_forward_bias: bfloat16 [1024], P('batch'), may hold values from -1.5 to 1.5
- cotangent: bfloat16 [4, 16, 512, 1024], P('rep', 'batch'), may hold values from -6 to 6
Outputs:
- out_latents: bfloat16 [4, 16, 512, 1024], P('rep', 'batch')
- grad_latents: bfloat16 [4, 16, 512, 1024], P('rep', 'batch')
- grad_w_qkv: float32 [1024, 3072], P('batch')
- grad_w_out: float32 [1024, 1024], P('batch')
- grad_w_up: float32 [1024, 1024], P('batch')
- grad_w_down: float32 [1024, 1024], P('batch')
- grad_gains: float32 [2, 1024], P(None, 'batch')
- grad_biases: float32 [6, 1024], P(None, 'batch')
- grad_mlp_bias: float32 [1024], P('batch')
All inputs are finite; a program needn't handle non-finite values.
Results may differ from a plain program's by a relative error of at most 0.014.
The roundings to bfloat16 on the way count: a program that leaves them out, or rounds other values in their place, can miss the bound.
Values may be sent and summed in bfloat16 or wider, within the bound.
No kernel may reach another device: no remote copies, remote signals or barrier semaphores. Data moves between devices by JAX's collectives and lax.ppermute only.
A program may use at most 192 MiB of HBM per device.

v0:
```python
import jax
import jax.numpy as jnp
from jax import lax
from jax.sharding import PartitionSpec as P

HEADS = 8
MICRO = 2


EPS = 1e-05


def layer_norm(values, gain, shift):
    mean = jnp.mean(values, axis=-1, keepdims=True)
    centred = values - mean
    spread = jnp.mean(centred * centred, axis=-1, keepdims=True)
    return centred * lax.rsqrt(spread + EPS) * gain + shift


def split_heads(sequence):
    length = sequence.shape[0]
    width = sequence.shape[1] // 3
    size = width // HEADS
    query = sequence[:, :width].reshape(length, HEADS, size)
    keys = sequence[:, width : 2 * width].reshape(length, HEADS, size)
    values = sequence[:, 2 * width :].reshape(length, HEADS, size)
    return (query, keys, values, size ** (-0.5))


def attend_one(sequence):
    query, keys, values, scale = split_heads(sequence)
    scores = jnp.einsum("qhd,khd->hqk", query, keys, preferred_element_type=jnp.float32) * scale
    top = jnp.max(scores, axis=-1, keepdims=True)
    raised = jnp.exp(scores - top)
    total = jnp.sum(raised, axis=-1, keepdims=True)
    probs = (raised / total).astype(jnp.bfloat16)
    joined = jnp.einsum("hqk,khd->qhd", probs, values, preferred_element_type=jnp.float32)
    mixed_heads = joined.reshape(sequence.shape[0], -1).astype(jnp.bfloat16)
    return (mixed_heads, (top + jnp.log(total))[..., 0])


def attend_back(inputs):
    sequence, log_total, grad_mixed = inputs
    query, keys, values, scale = split_heads(sequence)
    length = sequence.shape[0]
    scores = jnp.einsum("qhd,khd->hqk", query, keys, preferred_element_type=jnp.float32) * scale
    probs = jnp.exp(scores - log_total[..., None])
    grad_heads = grad_mixed.reshape(length, HEADS, -1)
    grad_values = jnp.einsum(
        "hqk,qhd->khd", probs.astype(jnp.bfloat16), grad_heads, preferred_element_type=jnp.float32
    )
    grad_probs = jnp.einsum("qhd,khd->hqk", grad_heads, values, preferred_element_type=jnp.float32)
    inner = jnp.sum(grad_probs * probs, axis=-1, keepdims=True)
    grad_scores = (probs * (grad_probs - inner)).astype(jnp.bfloat16)
    grad_query = (
        jnp.einsum("hqk,khd->qhd", grad_scores, keys, preferred_element_type=jnp.float32) * scale
    )
    grad_keys = (
        jnp.einsum("hqk,qhd->khd", grad_scores, query, preferred_element_type=jnp.float32) * scale
    )
    joined = jnp.concatenate(
        [
            grad_query.reshape(length, -1),
            grad_keys.reshape(length, -1),
            grad_values.reshape(length, -1),
        ],
        axis=1,
    )
    return joined.astype(jnp.bfloat16)


def forward_local(block, params):
    (
        query_key_value_weight,
        output_weight,
        up_weight,
        down_weight,
        norm_gains,
        biases,
        feed_forward_bias,
    ) = params
    gain_vals = norm_gains.astype(jnp.float32)
    shift_vals = biases.astype(jnp.float32)
    inputs = block.astype(jnp.float32)
    first_layer = layer_norm(inputs, gain_vals[0], shift_vals[0]).astype(jnp.bfloat16)
    column_offset = jnp.concatenate([shift_vals[1], jnp.zeros_like(shift_vals[1]), shift_vals[2]])
    packed_rows = (
        jnp.einsum(
            "gxy,yw->gxw", first_layer, query_key_value_weight, preferred_element_type=jnp.float32
        )
        + column_offset
    ).astype(jnp.bfloat16)
    mixed_heads, log_total = lax.map(attend_one, packed_rows)
    middle_state = (
        inputs
        + jnp.einsum("gxy,yw->gxw", mixed_heads, output_weight, preferred_element_type=jnp.float32)
        + shift_vals[3]
    )
    second_layer = layer_norm(middle_state, gain_vals[1], shift_vals[4]).astype(jnp.bfloat16)
    hidden_units = jnp.einsum(
        "uob,bw->uow", second_layer, up_weight, preferred_element_type=jnp.float32
    ) + feed_forward_bias.astype(jnp.float32)
    active_state = jax.nn.gelu(hidden_units).astype(jnp.bfloat16)
    result = (
        middle_state
        + jnp.einsum("rnx,xk->rnk", active_state, down_weight, preferred_element_type=jnp.float32)
        + shift_vals[5]
    )
    return (
        result.astype(jnp.bfloat16),
        (packed_rows, log_total, mixed_heads, middle_state, hidden_units),
    )


def backward_local(block, block_cotangent, memo, params):
    (
        query_key_value_weight,
        output_weight,
        up_weight,
        down_weight,
        norm_gains,
        biases,
        feed_forward_bias,
    ) = params
    packed_rows, log_total, mixed_heads, middle_state, hidden_units = memo
    gain_vals = norm_gains.astype(jnp.float32)
    shift_vals = biases.astype(jnp.float32)
    width = block.shape[-1]
    active_state, gelu_pull = jax.vjp(jax.nn.gelu, hidden_units)
    active_lowered = active_state.astype(jnp.bfloat16)
    grad_down_weight = jnp.einsum(
        "gao,gak->ok", active_lowered, block_cotangent, preferred_element_type=jnp.float32
    )
    bias_down = jnp.sum(block_cotangent, axis=(0, 1), dtype=jnp.float32)
    grad_active_state = jnp.einsum(
        "qbg,hg->qbh", block_cotangent, down_weight, preferred_element_type=jnp.float32
    )
    grad_hidden_units = gelu_pull(grad_active_state)[0].astype(jnp.bfloat16)
    normed_two, second_pull = jax.vjp(layer_norm, middle_state, gain_vals[1], shift_vals[4])
    second_layer = normed_two.astype(jnp.bfloat16)
    grad_up_weight = jnp.einsum(
        "oip,oiy->py", second_layer, grad_hidden_units, preferred_element_type=jnp.float32
    )
    bias_mlp = jnp.sum(grad_hidden_units, axis=(0, 1), dtype=jnp.float32)
    grad_second_layer = jnp.einsum(
        "vxw,aw->vxa", grad_hidden_units, up_weight, preferred_element_type=jnp.float32
    )
    grad_mid, gain_two, shift_two = second_pull(grad_second_layer)
    grad_middle = block_cotangent.astype(jnp.float32) + grad_mid
    grad_attention = grad_middle.astype(jnp.bfloat16)
    grad_output = jnp.einsum(
        "xuz,xuq->zq", mixed_heads, grad_attention, preferred_element_type=jnp.float32
    )
    bias_out = jnp.sum(grad_attention, axis=(0, 1), dtype=jnp.float32)
    grad_mixed = jnp.einsum(
        "gma,ia->gmi", grad_attention, output_weight, preferred_element_type=jnp.float32
    ).astype(jnp.bfloat16)
    grad_packed_rows = lax.map(attend_back, (packed_rows, log_total, grad_mixed))
    normed_one, first_pull = jax.vjp(
        layer_norm, block.astype(jnp.float32), gain_vals[0], shift_vals[0]
    )
    first_layer = normed_one.astype(jnp.bfloat16)
    grad_query_key_value = jnp.einsum(
        "xuz,xuq->zq", first_layer, grad_packed_rows, preferred_element_type=jnp.float32
    )
    packed_sum = jnp.sum(grad_packed_rows, axis=(0, 1), dtype=jnp.float32)
    grad_first_layer = jnp.einsum(
        "gma,ia->gmi", grad_packed_rows, query_key_value_weight, preferred_element_type=jnp.float32
    )
    grad_inputs, gain_one, shift_one = first_pull(grad_first_layer)
    grad_block = (grad_middle + grad_inputs).astype(jnp.bfloat16)
    grad_gains = jnp.stack([gain_one, gain_two])
    grad_biases = jnp.stack(
        [shift_one, packed_sum[:width], packed_sum[2 * width :], bias_out, shift_two, bias_down]
    )
    return (
        grad_block,
        (
            grad_query_key_value,
            grad_output,
            grad_up_weight,
            grad_down_weight,
            grad_gains,
            grad_biases,
            bias_mlp,
        ),
    )


def per_device(
    latents,
    query_key_value_weight,
    output_weight,
    up_weight,
    down_weight,
    norm_gains,
    biases,
    feed_forward_bias,
    cotangent,
):
    rep_count, img_count, length, width = latents.shape
    per_micro = img_count // MICRO
    memos = []
    results = []
    for part in range(MICRO):
        params = (
            lax.all_gather(query_key_value_weight, "batch", axis=0, tiled=True),
            lax.all_gather(output_weight, "batch", axis=0, tiled=True),
            lax.all_gather(up_weight, "batch", axis=0, tiled=True),
            lax.all_gather(down_weight, "batch", axis=0, tiled=True),
            lax.all_gather(norm_gains, "batch", axis=1, tiled=True),
            lax.all_gather(biases, "batch", axis=1, tiled=True),
            lax.all_gather(feed_forward_bias, "batch", axis=0, tiled=True),
        )
        block = latents[:, part * per_micro : (part + 1) * per_micro].reshape(-1, length, width)
        result, memo = forward_local(block, params)
        results.append(result.reshape(rep_count, per_micro, length, width))
        memos.append(memo)
    out_latents = jnp.concatenate(results, axis=1)
    backs = []
    shares = None
    for part in range(MICRO):
        params = (
            lax.all_gather(query_key_value_weight, "batch", axis=0, tiled=True),
            lax.all_gather(output_weight, "batch", axis=0, tiled=True),
            lax.all_gather(up_weight, "batch", axis=0, tiled=True),
            lax.all_gather(down_weight, "batch", axis=0, tiled=True),
            lax.all_gather(norm_gains, "batch", axis=1, tiled=True),
            lax.all_gather(biases, "batch", axis=1, tiled=True),
            lax.all_gather(feed_forward_bias, "batch", axis=0, tiled=True),
        )
        block = latents[:, part * per_micro : (part + 1) * per_micro].reshape(-1, length, width)
        block_cotangent = cotangent[:, part * per_micro : (part + 1) * per_micro].reshape(
            -1, length, width
        )
        grad_block, grads = backward_local(block, block_cotangent, memos[part], params)
        backs.append(grad_block.reshape(rep_count, per_micro, length, width))
        piece = (
            lax.psum_scatter(grads[0], "batch", scatter_dimension=0, tiled=True),
            lax.psum_scatter(grads[1], "batch", scatter_dimension=0, tiled=True),
            lax.psum_scatter(grads[2], "batch", scatter_dimension=0, tiled=True),
            lax.psum_scatter(grads[3], "batch", scatter_dimension=0, tiled=True),
            lax.psum_scatter(grads[4], "batch", scatter_dimension=1, tiled=True),
            lax.psum_scatter(grads[5], "batch", scatter_dimension=1, tiled=True),
            lax.psum_scatter(grads[6], "batch", scatter_dimension=0, tiled=True),
        )
        shares = piece if shares is None else tuple((a + b for a, b in zip(shares, piece)))
    summed = (
        lax.psum(shares[0].astype(jnp.bfloat16), "rep").astype(jnp.float32),
        lax.psum(shares[1].astype(jnp.bfloat16), "rep").astype(jnp.float32),
        lax.psum(shares[2].astype(jnp.bfloat16), "rep").astype(jnp.float32),
        lax.psum(shares[3].astype(jnp.bfloat16), "rep").astype(jnp.float32),
        lax.psum(shares[4].astype(jnp.bfloat16), "rep").astype(jnp.float32),
        lax.psum(shares[5].astype(jnp.bfloat16), "rep").astype(jnp.float32),
        lax.psum(shares[6].astype(jnp.bfloat16), "rep").astype(jnp.float32),
    )
    grad_latents = jnp.concatenate(backs, axis=1)
    return (
        out_latents,
        grad_latents,
        summed[0],
        summed[1],
        summed[2],
        summed[3],
        summed[4],
        summed[5],
        summed[6],
    )


def solution(mesh):
    return jax.shard_map(
        per_device,
        mesh=mesh,
        in_specs=(
            P("rep", "batch", None, None),
            P("batch", None),
            P("batch", None),
            P("batch", None),
            P("batch", None),
            P(None, "batch"),
            P(None, "batch"),
            P("batch"),
            P("rep", "batch", None, None),
        ),
        out_specs=(
            P("rep", "batch", None, None),
            P("rep", "batch", None, None),
            P("batch", None),
            P("batch", None),
            P("batch", None),
            P("batch", None),
            P(None, "batch"),
            P(None, "batch"),
            P("batch"),
        ),
        check_vma=False,
    )
```

profile of v0, /device:TPU:0, one launch (start us, length us, event | category | flops | bytes accessed | tf_op | source)
XLA Modules:
  0.0 926.3 jit_solution(6273656224226095913)
XLA Ops:
  10.0 22.4 %all_gather.14 = bf16[2,1024]{1,0:T(2,128)(2,1)S(1)} all-gather(bf16[2,128]{1,0:T(2,128)(2,1)} %param.14), channel_id=1, replica_groups=mesh['batch'=8,'rep'=4] {'batch'}, dimensions={1}, use_global_device_ids=true | all-gather | bytes 4608 | tf_op jit(solution)/shard_map/all_gather | solution.py:211
  32.4 16.7 %all-gather = bf16[8,1,128]{2,1,0:T(2,128)(2,1)S(1)} all-gather(bf16[1,1,128]{2,1,0:T(2,128)(2,1)} %bitcast.338), channel_id=1, replica_groups=mesh['batch'=8,'rep'=4] {'batch'}, dimensions={0}, use_global_device_ids=true | all-gather | bytes 2304 | tf_op jit(solution)/shard_map/all_gather | solution.py:213
  52.4 26.6 %all_gather.15 = bf16[6,1024]{1,0:T(8,128)(2,1)S(1)} all-gather(bf16[6,128]{1,0:T(8,128)(2,1)S(1)} %copy-done.60), channel_id=1, replica_groups=mesh['batch'=8,'rep'=4] {'batch'}, dimensions={1}, use_global_device_ids=true | all-gather | bytes 13824 | tf_op jit(solution)/shard_map/all_gather | solution.py:212
  79.6 32.7 %all-gather.6.cloned.1.call-done = bf16[1024,3072]{1,0:T(8,128)(2,1)} async-done(((bf16[128,3072]{1,0:T(8,128)(2,1)}), bf16[1024,3072]{1,0:T(8,128)(2,1)}) %all-gather.6.cloned.1.call-update) | async-done | bytes 6291472 | tf_op jit(solution)/shard_map/all_gather | solution.py:207
  112.2 6.7 add_convert_fusion
  122.2 2.6 copy.78
  124.9 6.7 add_convert_fusion.1
  133.3 2.3 copy.77
  135.6 2.3 copy.76
  137.9 3.0 multiply_reduce_fusion.3
  144.1 2.9 fusion.59
  153.8 8.1 all-gather.8.cloned.1.call-done
  161.8 3.3 fusion.130
  170.5 41.2 %all-gather.10.cloned.1.call-done = bf16[1024,1024]{1,0:T(8,128)(2,1)} async-done(((bf16[128,1024]{1,0:T(8,128)(2,1)}), bf16[1024,1024]{1,0:T(8,128)(2,1)}) %all-gather.10.cloned.1.call-update) | async-done | bytes 2097168 | tf_op jit(solution)/shard_map/all_gather | solution.py:209
  211.8 3.7 fusion.119
  221.7 3.7 convolution_add_fusion.1
  225.7 35.9 %all-gather.12.cloned.1.call-done = bf16[1024,1024]{1,0:T(8,128)(2,1)} async-done(((bf16[128,1024]{1,0:T(8,128)(2,1)}), bf16[1024,1024]{1,0:T(8,128)(2,1)}) %all-gather.12.cloned.1.call-update) | async-done | bytes 2097168 | tf_op jit(solution)/shard_map/all_gather | solution.py:210
  261.6 5.2 convert_reduce_fusion.5
  270.6 2.5 convert_reduce_fusion.4
  274.1 3.5 convolution_add_fusion.2
  278.2 3.4 fusion.131
  289.4 3.3 convolution_add_fusion.3
  293.9 4.0 convolution_convert_fusion
  297.9 2.3 convolution_convert_fusion.1
  301.7 2.3 copy.81
  304.0 7.8 multiply_reduce_fusion.1
  313.4 5.0 multiply_convert_fusion.1
  318.4 2.5 multiply_convert_fusion.4
  322.6 4.3 multiply_reduce_fusion
  326.9 4.8 multiply_convert_fusion
  331.7 2.4 multiply_convert_fusion.2
  335.9 2.7 fusion.63
  340.4 3.8 fusion.71
  344.3 10.1 %convolution_add_fusion = f32[1024,3072]{1,0:T(8,128)} fusion(f32[1024,3072]{1,0:T(8,128)S(1)} %fusion.71, bf16[512,1024]{0,1:T(8,128)(2,1)S(1)} %bitcast.265, bf16[512,1024]{0,1:T(8,128)(2,1)} %bitcast.268, bf16[512,1024]{0,1:T(8,128)(2,1)} %bitcast.271, f32[512]{0:T(512)S(1)} %copy-done.54, f32[512]{0:T(512)S(1)} %copy-done.52, f32[1024]{0:T(1024)S(1)} %bitcast.300, ...), kind=kOutput, calls=%fused_computation.18 | convolution fusion | flops 3236954112 | bytes 29372416 | tf_op jit(solution)/shard_map/xuz,xuq->zq/dot_general | solution.py:163
  358.5 6.4 fusion.70
  364.9 7.8 fusion.36
  376.1 2.5 convert_reduce_fusion.1
  380.9 4.8 fusion.66
  389.0 19.7 %all-reduce = bf16[1024]{0:T(1024)(128)(2,1)S(1)} all-reduce(f32[1024]{0:T(1024)S(1)} %add.369), channel_id=15, replica_groups=mesh['batch'=8,'rep'=4] {'batch'}, use_global_device_ids=true, to_apply=%region_55.56.clone | all-reduce | flops 1024 | bytes 6144
  410.5 33.1 %reduce-scatter.13.cloned.1.call-done = f32[128,1024]{1,0:T(8,128)} async-done(((f32[1024,1024]{1,0:T(8,128)}), f32[128,1024]{1,0:T(8,128)}) %reduce-scatter.13.cloned.1.call-update) | async-done | bytes 524304 | tf_op jit(solution)/shard_map/reduce_scatter | solution.py:241
  445.4 89.5 %reduce-scatter.11.cloned.1.call-done = f32[128,1024]{1,0:T(8,128)} async-done(((f32[1024,1024]{1,0:T(8,128)}), f32[128,1024]{1,0:T(8,128)}) %reduce-scatter.11.cloned.1.call-update) | async-done | bytes 524304 | tf_op jit(solution)/shard_map/reduce_scatter | solution.py:240
  536.7 209.4 %reduce-scatter.9.cloned.1.call-done = f32[128,3072]{1,0:T(8,128)} async-done(((f32[1024,3072]{1,0:T(8,128)}), f32[128,3072]{1,0:T(8,128)}) %reduce-scatter.9.cloned.1.call-update) | async-done | bytes 1572880 | tf_op jit(solution)/shard_map/reduce_scatter | solution.py:239
  746.1 2.4 convert_element_type.385
  748.5 5.1 fusion.73
  755.1 56.4 %reduce-scatter.19.cloned.1.call-done = f32[128,2]{1,0:T(8,128)} async-done(((f32[1024,2]{1,0:T(8,128)}), f32[128,2]{1,0:T(8,128)}) %reduce-scatter.19.cloned.1.call-update) | async-done | bytes 1040
  812.4 54.6 %reduce-scatter.17.cloned.1.call-done = f32[6,128]{1,0:T(8,128)} async-done(((f32[6,1024]{1,0:T(8,128)}), f32[6,128]{1,0:T(8,128)}) %reduce-scatter.17.cloned.1.call-update) | async-done | bytes 3088 | tf_op jit(solution)/shard_map/reduce_scatter | solution.py:244
  867.6 5.6 all-reduce.1
  875.0 37.6 %all-reduce.5.cloned.1.call-done = (bf16[128,3072]{1,0:T(8,128)(2,1)}, bf16[128,1024]{1,0:T(8,128)(2,1)}, bf16[128,1024]{1,0:T(8,128)(2,1)}, bf16[128,1024]{1,0:T(8,128)(2,1)}) async-done(((bf16[128,3072]{1,0:T(8,128)(2,1)}, bf16[128,1024]{1,0:T(8,128)(2,1)}, bf16[128,1024]{1,0:T(8,128)(2,1)}, bf16[128,1024]{1,0:T(8,128)(2,1)}), (bf16[128,3072]{1,0:T(8,128)(2,1)}, bf16[128,1024]{1,0:T(8,128)(2,1)}, ...) | async-done | bytes 1572880 | tf_op jit(solution)/shard_map/psum | solution.py:249
  (244 shorter events, 85.2 us)
Async XLA Ops:
  7.2 43.9 %copy-start.2 = (bf16[1,2,512,1024]{3,2,1,0:T(8,128)(2,1)S(1)}, bf16[1,2,512,1024]{3,2,1,0:T(8,128)(2,1)}, u32[]{:S(2)}) copy-start(bf16[1,2,512,1024]{3,2,1,0:T(8,128)(2,1)} %param.9) | copy-start | bytes 6291460
  7.2 105.1 %all-gather.6.cloned.1.call-start = ((), (), s32[]{:S(2)}) async-start(), calls=%async_computation.6 | async-start | bytes 7077888 | tf_op jit(solution)/shard_map/all_gather | solution.py:207
  7.9 153.9 %all-gather.8.cloned.1.call-start = ((), (), s32[]{:S(2)}) async-start(), calls=%async_computation.7 | async-start | bytes 2359296 | tf_op jit(solution)/shard_map/all_gather | solution.py:208
  8.7 203.1 %all-gather.10.cloned.1.call-start = ((), (), s32[]{:S(2)}) async-start(), calls=%async_computation.8 | async-start | bytes 2359296 | tf_op jit(solution)/shard_map/all_gather | solution.py:209
  9.4 252.2 %all-gather.12.cloned.1.call-start = ((), (), s32[]{:S(2)}) async-start(), calls=%async_computation.9 | async-start | bytes 2359296 | tf_op jit(solution)/shard_map/all_gather | solution.py:210
  10.0 398.7 %reduce-scatter.15.cloned.1.call-start = ((), (), s32[]{:S(2)}) async-start(), calls=%async_computation.13 | async-start | bytes 4718592 | tf_op jit(solution)/shard_map/reduce_scatter | solution.py:242
  49.1 3.2 copy-start.60
  51.0 67.9 %copy-start.51 = (f32[512]{0:T(512)}, f32[512]{0:T(512)S(1)}, u32[]{:S(2)}) copy-start(f32[512]{0:T(512)S(1)} %get-tuple-element.145) | copy-start | bytes 6148
  52.3 66.6 %copy-start.53 = (f32[512]{0:T(512)}, f32[512]{0:T(512)S(1)}, u32[]{:S(2)}) copy-start(f32[512]{0:T(512)S(1)} %fusion.102) | copy-start | bytes 6148
  122.2 24.7 %copy-start.17 = (bf16[512,1024]{0,1:T(8,128)(2,1)}, bf16[512,1024]{0,1:T(8,128)(2,1)S(1)}, u32[]{:S(2)}) copy-start(bf16[512,1024]{0,1:T(8,128)(2,1)S(1)} %copy.79) | copy-start | bytes 3145732
  140.8 3.2 copy-start
  148.2 3.2 copy-start.1
  148.3 3.2 copy-start.36
  211.8 5.0 copy-start.8
  225.4 218.2 %reduce-scatter.13.cloned.1.call-start = ((), (), s32[]{:S(2)}) async-start(), calls=%async_computation.12 | async-start | bytes 4718592 | tf_op jit(solution)/shard_map/reduce_scatter | solution.py:241
  261.6 6.2 copy-start.12
  270.6 3.5 copy-start.5
  277.7 257.2 %reduce-scatter.11.cloned.1.call-start = ((), (), s32[]{:S(2)}) async-start(), calls=%async_computation.11 | async-start | bytes 4718592 | tf_op jit(solution)/shard_map/reduce_scatter | solution.py:240
  278.2 3.4 copy-start.6
  278.2 3.4 copy-start.13
  278.2 3.9 copy-start.64
  278.2 4.1 copy-start.67
  292.7 453.5 %reduce-scatter.9.cloned.1.call-start = ((), (), s32[]{:S(2)}) async-start(), calls=%async_computation.10 | async-start | bytes 14155776 | tf_op jit(solution)/shard_map/reduce_scatter | solution.py:239
  293.9 4.0 copy-start.29
  293.9 4.0 copy-start.47
  304.0 7.8 slice-start
  304.0 9.4 %slice-start.1 = ((s8[8388608]{0:T(1024)(128)(4,1)}), s8[4194304]{0:T(1024)(128)(4,1)S(1)}, s32[]{:S(2)}) async-start(s8[8388608]{0:T(1024)(128)(4,1)} %bitcast.249), calls=%async_computation.18 | async-start | bytes 8388608
  304.0 18.6 %slice-start.2 = ((s8[8388608]{0:T(1024)(128)(4,1)}), s8[4194304]{0:T(1024)(128)(4,1)S(1)}, s32[]{:S(2)}) async-start(s8[8388608]{0:T(1024)(128)(4,1)} %bitcast.251), calls=%async_computation.19 | async-start | bytes 8388608
  313.4 5.0 copy-start.22
  313.4 9.2 slice-start.3
  326.9 4.8 copy-start.20
  340.4 3.9 copy-start.34
  340.4 3.9 copy-start.23
  340.4 3.9 copy-start.52
  340.4 3.9 copy-start.54
  354.4 457.0 %reduce-scatter.19.cloned.1.call-start = ((), (), s32[]{:S(2)}) async-start(), calls=%async_computation.15 | async-start | bytes 589824
  358.5 6.4 copy-start.35
  358.5 6.4 copy-start.40
  358.5 6.4 copy-start.42
  364.9 7.9 copy-start.30
  364.9 7.9 copy-start.58
  364.9 7.9 copy-start.56
  379.7 487.2 %reduce-scatter.17.cloned.1.call-start = ((), (), s32[]{:S(2)}) async-start(), calls=%async_computation.14 | async-start | bytes 36864 | tf_op jit(solution)/shard_map/reduce_scatter | solution.py:244
  380.5 532.0 %all-reduce.5.cloned.1.call-start = ((), (), s32[]{:S(2)}) async-start(), calls=%async_computation.16 | async-start | bytes 3145728 | tf_op jit(solution)/shard_map/psum | solution.py:249
  380.9 4.8 copy-start.7
  380.9 4.8 copy-start.45
  380.9 5.0 copy-start.62
  912.5 5.5 copy-start.50
  (36 other events, 64.9 us)
Sparse Core Ops, SparseCore 0:
  10.2 101.9 all-gather.5
  114.4 47.4 all-gather.7
  164.0 47.7 all-gather.9
  213.8 47.7 all-gather.11
  265.0 86.3 reduce-scatter.14
  355.4 88.2 reduce-scatter.12
  447.2 87.6 reduce-scatter.10
  538.9 207.1 reduce-scatter.8
  750.4 61.0 reduce-scatter.18
  814.4 52.4 reduce-scatter.16
  870.1 42.4 all-reduce.4
where the time goes:
time: 936 us; the launch traced here: 926 us
  waiting for transfers between devices  601 us (64%)
  matrix products  126 us (13%)
  blocking collectives  91 us (10%)
  other arithmetic  51.4 us (5%)
  local copies, waits for them, and re-layouts  38.8 us (4%)
  between operations  16 us (2%)
    reduce_scatter x1, waiting for transfers between devices, per_device(): lax.psum_scatter(grads[0], 'batch', scatter_dimension=0, tiled=True)  209 us
    reduce_scatter x1, waiting for transfers between devices, per_device(): lax.psum_scatter(grads[1], 'batch', scatter_dimension=0, tiled=True)  89.5 us
    unnamed x12, waiting for transfers between devices  59.1 us
    reduce_scatter x1, waiting for transfers between devices, per_device(): lax.psum_scatter(grads[5], 'batch', scatter_dimension=1, tiled=True)  54.6 us
    all_gather x1, waiting for transfers between devices, per_device(): lax.all_gather(up_weight, 'batch', axis=0, tiled=True)  41.2 us
    psum x1, waiting for transfers between devices, per_device(): lax.psum(shares[0].astype(jnp.bfloat16), 'rep').astype(jnp.float32)  37.6 us
    all_gather x1, waiting for transfers between devices, per_device(): lax.all_gather(down_weight, 'batch', axis=0, tiled=True)  35.9 us
    reduce_scatter x1, waiting for transfers between devices, per_device(): lax.psum_scatter(grads[2], 'batch', scatter_dimension=0, tiled=True)  33.1 us
  transfers between devices with their start and end apart: 11, of which 10 were waited for; matrix products, arithmetic and copies ran while one was open for 21% of the time, Pallas kernels for 0%

commit v1 on v0

v1 whole, which is shorter than its diff:
```python
import jax
import jax.numpy as jnp
from jax import lax
from jax.sharding import PartitionSpec as P

HEADS = 8
EPS = 1e-05
AXES = ("batch", "rep")
BF = jnp.bfloat16
F32 = jnp.float32


def layer_norm(values, gain, shift):
    mean = jnp.mean(values, axis=-1, keepdims=True)
    centred = values - mean
    spread = jnp.mean(centred * centred, axis=-1, keepdims=True)
    return centred * lax.rsqrt(spread + EPS) * gain + shift


def permutation(move, nb, nr):
    pairs = []
    for b in range(nb):
        for r in range(nr):
            tb, tr = move(b, r)
            pairs.append((b * nr + r, tb * nr + tr))
    return pairs


class Links:
    def __init__(self, nb, nr):
        def swap(kb, kr):
            return permutation(lambda b, r: (b ^ kb, r ^ kr), nb, nr)

        self.core = swap(0, 1)
        self.rep = [swap(0, 1), swap(0, 2), swap(0, 3)]
        self.z = [swap(2, 0), swap(4, 0), swap(6, 0)]
        self.y_or_x = permutation(lambda b, r: (b, r ^ 2) if r % 2 == 0 else (b ^ 1, r), nb, nr)
        self.x_or_y = permutation(lambda b, r: (b ^ 1, r) if r % 2 == 0 else (b, r ^ 2), nb, nr)
        batch, rep = lax.axis_index("batch"), lax.axis_index("rep")
        self.xi, self.zi = batch % 2, batch // 2
        self.ci, self.yi = rep % 2, rep // 2


def move(value, pairs):
    return lax.ppermute(value, AXES, pairs)


def flip_if(bit, value, axis):
    return jnp.where(bit == 1, jnp.flip(value, axis), value)


def gather_rows(local, links):
    rows, n = local.shape
    quarter = lax.dynamic_index_in_dim(
        local.reshape(4, rows // 4, n), links.ci * 2 + links.yi, 0, keepdims=False
    )
    own = jnp.stack([quarter] + [move(quarter, p) for p in links.z])
    first = move(own, links.y_or_x)
    second = move(own, links.x_or_y)
    third = move(first, links.x_or_y)
    halves = []
    here = [own, first, second, third]
    there = [move(part, links.core) for part in here]
    for parts, core in ((here, links.ci), (there, 1 - links.ci)):
        a, f, s, t = parts
        dx = jnp.where(core == 1, f, s)
        dy = jnp.where(core == 1, s, f)
        halves.append(jnp.stack([jnp.stack([a, dy]), jnp.stack([dx, t])]))
    whole = jnp.stack(halves)
    whole = flip_if(links.ci, whole, 0)
    whole = flip_if(links.xi, whole, 1)
    whole = flip_if(links.yi, whole, 2)
    whole = flip_if(links.zi % 2, whole.reshape(2, 2, 2, 2, 2, rows // 4, n), 4)
    whole = flip_if(links.zi // 2, whole, 3)
    whole = whole.transpose(3, 4, 1, 0, 2, 5, 6)
    return whole.reshape(8 * rows, n)


def reduce_rows(partial, links):
    total, n = partial.shape
    rows, q = total // 8, n // 4
    view = partial.reshape(4, 2, rows, 2, 2, q)
    view = view.transpose(3, 1, 4, 0, 2, 5)
    keep = lax.dynamic_index_in_dim(view, links.ci, 0, keepdims=False)
    send = lax.dynamic_index_in_dim(view, 1 - links.ci, 0, keepdims=False).astype(BF)
    held = keep + move(send, links.core).astype(F32)
    held = jnp.where(links.ci == 0, held, held.transpose(1, 0, 2, 3, 4))
    mine = jnp.where(links.ci == 0, links.xi, links.yi)
    keep = lax.dynamic_index_in_dim(held, mine, 0, keepdims=False)
    send = lax.dynamic_index_in_dim(held, 1 - mine, 0, keepdims=False).astype(BF)
    held = keep + move(send, links.x_or_y).astype(F32)
    mine = jnp.where(links.ci == 0, links.yi, links.xi)
    keep = lax.dynamic_index_in_dim(held, mine, 0, keepdims=False)
    send = lax.dynamic_index_in_dim(held, 1 - mine, 0, keepdims=False).astype(BF)
    held = keep + move(send, links.y_or_x).astype(F32)
    out = lax.dynamic_index_in_dim(held, links.zi, 0, keepdims=False)
    for k, pairs in enumerate(links.z):
        send = lax.dynamic_index_in_dim(held, links.zi ^ (k + 1), 0, keepdims=False).astype(BF)
        out = out + move(send, pairs).astype(F32)
    out = out.astype(BF)
    by_core, by_y, by_both = [move(out, p) for p in links.rep]
    grid = jnp.stack([jnp.stack([out, by_y]), jnp.stack([by_core, by_both])])
    grid = flip_if(links.yi, flip_if(links.ci, grid, 0), 1)
    return grid.transpose(2, 0, 1, 3).reshape(rows, n).astype(F32)


def heads_of(packed):
    images, length, width = packed.shape
    size = width // 3 // HEADS
    view = packed.reshape(images, length, 3, HEADS, size)
    return view[:, :, 0], view[:, :, 1], view[:, :, 2], size ** (-0.5)


def per_device(latents, w_qkv, w_out, w_up, w_down, gains, biases, ff_bias, cotangent, *, nb, nr):
    reps, images, length, width = latents.shape
    x = latents.reshape(-1, width).astype(F32)
    cot = cotangent.reshape(-1, width)
    count = reps * images
    small = jnp.concatenate([gains, biases, ff_bias[None]], axis=0)
    native = nb != 8 or nr != 4
    if native:
        small = lax.all_gather(small, "batch", axis=1, tiled=True)
        w_qkv, w_out, w_up, w_down = (
            lax.all_gather(w, "batch", axis=0, tiled=True) for w in (w_qkv, w_out, w_up, w_down)
        )
    else:
        links = Links(nb, nr)
        small = lax.all_gather(small, "batch", axis=1, tiled=True)
        w_qkv = gather_rows(w_qkv, links)
        rest = gather_rows(jnp.concatenate([w_out, w_up, w_down], axis=1), links)
        w_out, w_up, w_down = rest[:, :width], rest[:, width : -width], rest[:, -width:]
    small = small.astype(F32)
    g1, g2 = small[0], small[1]
    b1, bq, bv, bo, b2, bd, bu = (small[i] for i in range(2, 9))

    def dot(a, b, dims):
        return lax.dot_general(a, b, (dims, ((), ())), preferred_element_type=F32)

    NN, NT, TN = ((1,), (0,)), ((1,), (1,)), ((0,), (0,))
    first, pull_one = jax.vjp(layer_norm, x, g1, b1)
    first = first.astype(BF)
    packed = dot(first, w_qkv, NN) + jnp.concatenate([bq, jnp.zeros_like(bq), bv])
    packed = packed.astype(BF).reshape(count, length, 3 * width)
    q, k, v, scale = heads_of(packed)
    scores = jnp.einsum("iqhd,ikhd->ihqk", q, k, preferred_element_type=F32) * scale
    top = jnp.max(scores, axis=-1, keepdims=True)
    raised = jnp.exp(scores - top)
    p = raised / jnp.sum(raised, axis=-1, keepdims=True)
    probs = p.astype(BF)
    mixed = jnp.einsum("ihqk,ikhd->iqhd", probs, v, preferred_element_type=F32)
    mixed = mixed.astype(BF).reshape(-1, width)
    middle = x + dot(mixed, w_out, NN) + bo
    second, pull_two = jax.vjp(layer_norm, middle, g2, b2)
    second = second.astype(BF)
    hidden = dot(second, w_up, NN) + bu
    active, pull_gelu = jax.vjp(jax.nn.gelu, hidden)
    active = active.astype(BF)
    out = (middle + dot(active, w_down, NN) + bd).astype(BF)
    gw_down = dot(active, cot, TN)
    gb_down = jnp.sum(cot.astype(F32), axis=0)
    g_hidden = pull_gelu(dot(cot, w_down, NT))[0].astype(BF)
    gw_up = dot(second, g_hidden, TN)
    gb_up = jnp.sum(g_hidden.astype(F32), axis=0)
    g_mid, gg2, gb2 = pull_two(dot(g_hidden, w_up, NT))
    g_middle = cot.astype(F32) + g_mid
    g_attn = g_middle.astype(BF)
    gw_out = dot(mixed, g_attn, TN)
    gb_out = jnp.sum(g_attn.astype(F32), axis=0)
    g_mixed = dot(g_attn, w_out, NT).astype(BF).reshape(count, length, HEADS, -1)
    g_v = jnp.einsum("ihqk,iqhd->ikhd", probs, g_mixed, preferred_element_type=F32)
    g_p = jnp.einsum("iqhd,ikhd->ihqk", g_mixed, v, preferred_element_type=F32)
    g_s = (p * (g_p - jnp.sum(g_p * p, axis=-1, keepdims=True))).astype(BF)
    g_q = jnp.einsum("ihqk,ikhd->iqhd", g_s, k, preferred_element_type=F32) * scale
    g_k = jnp.einsum("ihqk,iqhd->ikhd", g_s, q, preferred_element_type=F32) * scale
    g_packed = jnp.stack([g_q, g_k, g_v], axis=2).astype(BF).reshape(-1, 3 * width)
    gw_qkv = dot(first, g_packed, TN)
    gb_packed = jnp.sum(g_packed.astype(F32), axis=0)
    g_in, gg1, gb1 = pull_one(dot(g_packed, w_qkv, NT))
    g_lat = (g_middle + g_in).astype(BF)
    zero = jnp.zeros_like(gb_up)
    smalls = jnp.stack(
        [gg1, gg2, gb1, gb_packed[:width], gb_packed[2 * width :], gb_out, gb2, gb_down, gb_up]
        + [zero] * 7
    )
    smalls = lax.psum(smalls, AXES)
    smalls = lax.dynamic_slice_in_dim(smalls, lax.axis_index("batch") * (width // nb), width // nb, 1)
    if native:

        def reduced(g):
            g = lax.psum_scatter(g, "batch", scatter_dimension=0, tiled=True)
            return lax.psum(g.astype(BF), "rep").astype(F32)

        gw_qkv, gw_out, gw_up, gw_down = (reduced(g) for g in (gw_qkv, gw_out, gw_up, gw_down))
    else:
        rest = reduce_rows(jnp.concatenate([gw_out, gw_up, gw_down], axis=1), links)
        gw_qkv = reduce_rows(gw_qkv, links)
        gw_out, gw_up, gw_down = rest[:, :width], rest[:, width : -width], rest[:, -width:]
    return (
        out.reshape(latents.shape),
        g_lat.reshape(latents.shape),
        gw_qkv,
        gw_out,
        gw_up,
        gw_down,
        smalls[:2],
        smalls[2:8],
        smalls[8],
    )


def solution(mesh):
    nb, nr = mesh.shape["batch"], mesh.shape["rep"]

    def body(*args):
        return per_device(*args, nb=nb, nr=nr)

    rows = P("batch", None)
    cols = P(None, "batch")
    data = P("rep", "batch", None, None)
    return jax.shard_map(
        body,
        mesh=mesh,
        in_specs=(data, rows, rows, rows, rows, cols, cols, P("batch"), data),
        out_specs=(data, data, rows, rows, rows, rows, cols, cols, P("batch")),
        check_vma=False,
    )
```

time: 936 us -> 659 us (0.70)
  waiting for transfers between devices: 601 us -> 143 us
  local copies, waits for them, and re-layouts: 38.8 us -> 144 us
  other arithmetic: 51.4 us -> 143 us
  blocking collectives: 91 us -> 45.8 us
  starting transfers between devices: 1.87 us -> 40.6 us
    reduce_scatter x5 -> x0, waiting for transfers between devices: 387 us -> none  [the longest x1 209 us: per_device(): lax.psum_scatter(grads[0], 'batch', scatter_dimension=0, tiled=True)]
    all_gather x4 -> x0, waiting for transfers between devices: 118 us -> none  [the longest x1 41.2 us: per_device(): lax.all_gather(up_weight, 'batch', axis=0, tiled=True)]
    ppermute x0 -> x38, waiting for transfers between devices: none -> 83.7 us  [move(): return lax.ppermute(value, AXES, pairs)]
    unnamed x12 -> x1, waiting for transfers between devices: 59.1 us -> 0.02 us
    select_n x0 -> x14, other arithmetic: none -> 53 us  [the longest x12 49 us: flip_if(): return jnp.where(bit == 1, jnp.flip(value, axis), value)]
    ppermute x0 -> x38, starting transfers between devices: none -> 40.5 us  [move(): return lax.ppermute(value, AXES, pairs)]
    convert_element_type x0 -> x12, local copies, waits for them, and re-layouts: none -> 32.9 us  [the longest x2 19.5 us: per_device(): jnp.stack([g_q, g_k, g_v], axis=2).astype(BF).reshape(-1, 3 * width)]
    unnamed x152 -> x105, local copies, waits for them, and re-layouts: 25.5 us -> 49.5 us
  transfers between devices with their start and end apart: 11 -> 39, of which waited for: 10 -> 13; matrix products, arithmetic and copies ran while one was open for 21% -> 23% of each run, Pallas kernels for 0% -> 0%
where the time goes in v1:
time: 659 us; the launch traced here: 650 us
  local copies, waits for them, and re-layouts  144 us (22%)
  other arithmetic  143 us (22%)
  waiting for transfers between devices  143 us (22%)
  matrix products  119 us (18%)
  blocking collectives  45.8 us (7%)
  starting transfers between devices  40.6 us (6%)
  between operations  15.4 us (2%)
    ppermute x38, waiting for transfers between devices, move(): return lax.ppermute(value, AXES, pairs)  83.7 us
    dot_general x12, matrix products, dot(): return lax.dot_general(a, b, (dims, ((), ())), preferred_element_type=F32)  71.4 us
    psum x1, waiting for transfers between devices, per_device(): smalls = lax.psum(smalls, AXES)  58.8 us
    unnamed x105, local copies, waits for them, and re-layouts  49.5 us
    select_n x12, other arithmetic, flip_if(): return jnp.where(bit == 1, jnp.flip(value, axis), value)  49 us
    all_gather x1, blocking collectives, per_device(): small = lax.all_gather(small, 'batch', axis=1, tiled=True)  45.8 us
    ppermute x38, starting transfers between devices, move(): return lax.ppermute(value, AXES, pairs)  40.5 us
    convert_element_type x2, local copies, waits for them, and re-layouts, per_device(): jnp.stack([g_q, g_k, g_v], axis=2).astype(BF).reshape(-1, 3 * width)  19.5 us
  transfers between devices with their start and end apart: 39, of which 13 were waited for; matrix products, arithmetic and copies ran while one was open for 23% of the time, Pallas kernels for 0%

profile of v1, /device:TPU:0, one launch (start us, length us, event | category | flops | bytes accessed | tf_op | source)
XLA Modules:
  0.0 650.0 jit_solution(16085910962180508302)
XLA Ops:
  8.3 5.1 collective-permute-start.2
  20.9 45.8 %all_gather.3 = bf16[9,1024]{1,0:T(8,128)(2,1)S(1)} all-gather(bf16[9,128]{1,0:T(8,128)(2,1)S(1)} %pad_maximum_fusion.9), channel_id=1, replica_groups=mesh['batch'=8,'rep'=4] {'batch'}, dimensions={1}, use_global_device_ids=true | all-gather | bytes 20736 | tf_op jit(solution)/shard_map/all_gather | solution.py:128
  77.2 7.4 %collective-permute-done.4 = bf16[4,32,3072]{2,1,0:T(8,128)(2,1)} collective-permute-done((bf16[4,32,3072]{2,1,0:T(8,128)(2,1)}, bf16[4,32,3072]{2,1,0:T(8,128)(2,1)}, u32[]{:S(2)}, u32[]{:S(2)}) %collective-permute-start.4) | collective-permute-done | bytes 786464 | tf_op jit(solution)/shard_map/ppermute | solution.py:45
  89.4 12.0 %collective-permute-done.14 = bf16[4,32,3072]{2,1,0:T(8,128)(2,1)S(1)} collective-permute-done((bf16[4,32,3072]{2,1,0:T(8,128)(2,1)S(1)}, bf16[4,32,3072]{2,1,0:T(8,128)(2,1)S(1)}, u32[]{:S(2)}, u32[]{:S(2)}) %collective-permute-start.14) | collective-permute-done | bytes 786464 | tf_op jit(solution)/shard_map/ppermute | solution.py:45
  107.8 8.4 %collective-permute-done.15 = bf16[4,32,3072]{2,1,0:T(8,128)(2,1)} collective-permute-done((bf16[4,32,3072]{2,1,0:T(8,128)(2,1)S(1)}, bf16[4,32,3072]{2,1,0:T(8,128)(2,1)}, u32[]{:S(2)}, u32[]{:S(2)}) %collective-permute-start.15) | collective-permute-done | bytes 786464 | tf_op jit(solution)/shard_map/ppermute | solution.py:45
  130.7 7.5 %reverse_select_fusion.4 = bf16[2,2,2,4,32,3072]{5,4,3,2,1,0:T(8,128)(2,1)S(1)} fusion(bf16[2,2,2,4,32,3072]{5,4,3,2,1,0:T(8,128)(2,1)} %pad_maximum_fusion.2, pred[]{:T(512)S(6)} %eq.23), kind=kLoop, calls=%fused_computation.14 | loop fusion | flops 3145728 | bytes 12582913 | tf_op jit(solution)/shard_map/jit(_where)/select_n | solution.py:49
  138.2 4.4 reverse_select_fusion.8
  142.6 4.4 reverse_select_fusion.3
  147.0 7.6 %reverse_select_fusion.7 = bf16[2,2,2,4,32,3072]{5,4,2,0,1,3:T(8,128)(2,1)S(1)} fusion(bf16[2,2,2,4,32,3072]{5,4,2,0,1,3:T(8,128)(2,1)} %reverse_select_fusion.8, pred[]{:T(512)S(6)} %eq.21), kind=kLoop, calls=%fused_computation.17 | loop fusion | flops 3145728 | bytes 12582913 | tf_op jit(solution)/shard_map/jit(_where)/select_n | solution.py:49
  154.7 4.4 reverse_select_fusion.2
  162.4 4.8 reverse_select_fusion.6
  169.0 7.5 %reverse_select_fusion.5 = bf16[2,2,2,2,2,32,3072]{6,5,2,0,1,4,3:T(8,128)(2,1)S(1)} fusion(bf16[2,2,2,2,2,32,3072]{6,5,2,0,1,4,3:T(8,128)(2,1)} %reverse_select_fusion.6, pred[]{:T(512)S(6)} %eq.19), kind=kLoop, calls=%fused_computation.15 | loop fusion | flops 3145728 | bytes 12582913 | tf_op jit(solution)/shard_map/jit(_where)/select_n | solution.py:49
  176.5 4.4 reverse_select_fusion
  181.3 8.6 %fusion.5 = bf16[128,8,24,128]{3,1,2,0:T(8,128)(2,1)} fusion(f32[3072]{0:T(1024)S(1)} %pad_maximum_fusion.8, bf16[1024,1024]{1,0:T(8,128)(2,1)S(1)} %bitcast.349, bf16[1024,3072]{1,0:T(8,128)(2,1)S(1)} %bitcast.343), kind=kOutput, calls=%fused_computation.22 | convolution fusion | flops 6448742400 | bytes 14692352 | tf_op jit(solution)/shard_map/dot_general | solution.py:137
  189.9 4.7 copy.92
  197.7 4.6 copy.84
  202.3 10.4 %fusion.52 = f32[2,8,512,512]{2,3,1,0:T(8,128)} fusion(bf16[2,512,1,8,128]{4,3,2,1,0:T(8,128)(2,1)} %get-tuple-element.33, bf16[2,512,1,8,128]{4,3,2,1,0:T(8,128)(2,1)} %get-tuple-element.31), kind=kOutput, calls=%fused_computation.106 | convolution fusion | flops 1073741824 | bytes 20971520 | tf_op jit(solution)/shard_map/iqhd,ikhd->ihqk/dot_general | solution.py:145
  212.6 18.9 %fusion.100 = (f32[2,8,512]{2,1,0:T(8,128)S(1)}, f32[2,8,512,512]{2,3,1,0:T(8,128)}) fusion(f32[2,8,512,512]{2,3,1,0:T(8,128)} %fusion.52), kind=kOutput, calls=%fused_computation.208 | output fusion | flops 16777728 | bytes 33587200 | tf_op jit(solution)/shard_map/sub | solution.py:147
  231.6 8.4 %convert_bitcast_fusion.2 = bf16[2,512,8,128]{1,3,2,0:T(8,128)(2,1)} fusion(bf16[2,512,1,8,128]{1,4,3,0,2:T(8,128)(2,1)S(1)} %copy-done.22, f32[2,8,512,512]{2,3,1,0:T(8,128)} %get-tuple-element.74, f32[2,8,512]{2,1,0:T(8,128)S(1)} %get-tuple-element.73), kind=kOutput, calls=%fused_computation.105 | convolution fusion | flops 1083179008 | bytes 21004288 | tf_op jit(solution)/shard_map/ihqk,ikhd->iqhd/dot_general | solution.py:150
  244.3 4.9 fusion.101
  252.3 5.9 convert_reduce_fusion.2
  258.2 4.6 fusion.91
  262.9 4.7 fusion.92
  277.1 4.4 fusion.41
  287.8 10.7 %fusion.38 = bf16[2,512,1,8,128]{1,4,3,0,2:T(8,128)(2,1)} fusion(bf16[2,512,8,128]{1,3,2,0:T(8,128)(2,1)} %copy.53, f32[2,8,512,512]{2,3,1,0:T(8,128)} %get-tuple-element.74, f32[2,8,512]{2,1,0:T(8,128)S(1)} %get-tuple-element.73), kind=kOutput, calls=%fused_computation.94 | convolution fusion | flops 1082130432 | bytes 21004288 | tf_op jit(solution)/shard_map/ihqk,iqhd->ikhd/dot_general | solution.py:170
  298.5 10.9 %multiply_reduce_fusion = (f32[2,8,512]{2,1,0:T(8,128)S(1)}, f32[2,8,512,512]{2,3,1,0:T(8,128)}) fusion(f32[2,8,512,512]{2,3,1,0:T(8,128)} %get-tuple-element.74, f32[2,8,512]{2,1,0:T(8,128)S(1)} %get-tuple-element.73, bf16[2,512,8,128]{1,3,2,0:T(8,128)(2,1)S(1)} %copy-done.25, bf16[2,512,1,8,128]{1,4,3,0,2:T(8,128)(2,1)S(1)} %copy-done.23), kind=kOutput, calls=%fused_computation.2 | convolution fusion | flops 1086316544 | bytes 37814272 | tf_op jit(solution)/shard_map/iqhd,ikhd->ihqk/dot_general | solution.py:171
  309.4 11.9 %multiply_convert_fusion = bf16[2,8,512,512]{2,3,1,0:T(8,128)(2,1)S(1)} fusion(f32[2,8,512,512]{2,3,1,0:T(8,128)} %get-tuple-element.79, f32[2,8,512]{2,1,0:T(8,128)S(1)} %get-tuple-element.78, f32[2,8,512,512]{2,3,1,0:T(8,128)} %get-tuple-element.74, f32[2,8,512]{2,1,0:T(8,128)S(1)} %get-tuple-element.73), kind=kLoop, calls=%fused_computation.1 | loop fusion | flops 16777216 | bytes 42008576 | tf_op jit(solution)/shard_map/convert_element_type | solution.py:172
  330.9 5.7 pad_maximum_fusion
  336.7 16.9 %reshape.232 = f32[4,2,128,2,2,768]{2,1,0,5,4,3:T(2,128)} reshape(f32[1024,3072]{0,1:T(8,128)} %pad_maximum_fusion) | data formatting | bytes 25165824 | tf_op jit(solution)/shard_map/reshape | solution.py:82
  353.6 6.6 %constant_dynamic-slice_fusion.1 = bf16[4,2,128,1,2,768]{2,1,0,5,4,3:T(2,128)(2,1)} fusion(f32[4,2,128,2,2,768]{2,1,0,5,4,3:T(2,128)} %reshape.232, s32[]{:T(128)S(6)} %select_n.250), kind=kLoop, calls=%fused_computation.178 | loop fusion | bytes 6291460 | tf_op jit(solution)/shard_map/jit(dynamic_index_in_dim)/dynamic_slice | solution.py:85
  360.1 8.7 %copy.89 = bf16[4,2,128,1,2,768]{5,2,0,1,4,3:T(8,128)(2,1)} copy(bf16[4,2,128,1,2,768]{2,1,0,5,4,3:T(2,128)(2,1)} %constant_dynamic-slice_fusion.1) | data formatting | bytes 6291456
  369.2 6.1 convert_reduce_fusion
  375.3 9.2 %copy.55 = bf16[2,512,3,8,128]{4,3,2,1,0:T(8,128)(2,1)} copy(bf16[2,512,3,8,128]{1,4,3,0,2:T(8,128)(2,1)} %get-tuple-element.28) | data formatting | bytes 12582912 | tf_op jit(solution)/shard_map/convert_element_type | solution.py:175
  384.5 10.3 %convert_element_type.247 = bf16[1024,3072]{1,0:T(8,128)(2,1)} reshape(bf16[2,512,3,8,128]{4,3,2,1,0:T(8,128)(2,1)} %copy.55) | data formatting | bytes 12582912 | tf_op jit(solution)/shard_map/convert_element_type | solution.py:175
  394.8 12.4 %fusion.93 = (f32[1024]{0:T(1024)S(1)}, f32[1024]{0:T(1024)S(1)}, f32[1024,1024]{1,0:T(8,128)}) fusion(f32[1024]{0:T(1024)S(1)} %bitcast.371, f32[1024]{0:T(1024)S(1)} %bitcast.376, bf16[1,2,512,1024]{3,2,1,0:T(8,128)(2,1)S(1)} %copy-done.2, bf16[1024,3072]{1,0:T(8,128)(2,1)} %convert_element_type.247, bf16[1024,3072]{1,0:T(8,128)(2,1)} %bitcast.344), kind=kOutput, calls=%fused_computation.202 | convolution fusion | flops 6448740352 | bytes 18890752 | tf_op jit(solution)/shard_map/dot_general | solution.py:137
  407.2 8.9 %copy.56 = bf16[3072,1024]{1,0:T(8,128)(2,1)} copy(bf16[3072,1024]{0,1:T(8,128)(2,1)} %bitcast.325) | data formatting | bytes 12582912 | tf_op jit(solution)/shard_map/dot_general | solution.py:137
  416.1 5.1 fusion.25
  425.2 9.5 %fusion.102 = f32[4,2,128,2,2,768]{5,2,4,3,1,0:T(8,128)S(1)} fusion(bf16[4,2,128,1024,1,1]{3,2,5,4,1,0:T(8,128)(2,1)} %bitcast.352, bf16[2,2,768,1024,1,1]{3,2,1,0,5,4:T(8,128)(2,1)} %bitcast.345), kind=kOutput, calls=%fused_computation.210 | convolution fusion | flops 6442450944 | bytes 20971520 | tf_op jit(solution)/shard_map/dot_general | solution.py:137
  434.7 4.5 copy-done.15
  443.4 7.6 %constant_dynamic-slice_fusion.2 = f32[4,2,128,1,2,768]{2,1,0,5,4,3:T(2,128)} fusion(f32[4,2,128,2,2,768]{2,1,0,5,4,3:T(2,128)} %reshape.232, s32[]{:T(128)S(6)} %select_n.249), kind=kLoop, calls=%fused_computation.179 | loop fusion | bytes 12582916 | tf_op jit(solution)/shard_map/dynamic-slice.2
  451.0 10.5 %copy.88 = f32[4,2,128,1,2,768]{5,2,0,1,4,3:T(8,128)} copy(f32[4,2,128,1,2,768]{2,1,0,5,4,3:T(2,128)} %constant_dynamic-slice_fusion.2) | data formatting | bytes 12582912
  462.9 4.4 bitcast_add_fusion.1
  469.4 4.5 bitcast_add_fusion
  480.5 8.5 %add_convert_fusion.2 = bf16[1024,1024]{1,0:T(8,128)(2,1)} fusion(f32[1024,1024]{1,0:T(8,128)} %copy-done.10, f32[1024]{0:T(1024)S(1)} %bitcast.394, bf16[1024,3072]{1,0:T(8,128)(2,1)} %bitcast.336, f32[1024,1024]{1,0:T(8,128)} %copy-done.42, f32[1024]{0:T(1024)S(1)} %bitcast.393), kind=kOutput, calls=%fused_computation.75 | convolution fusion | flops 2161115136 | bytes 12591104 | tf_op jit(solution)/shard_map/dot_general | solution.py:137
  491.5 22.9 %collective-permute-done.21 = bf16[2,4,128,768]{3,2,0,1:T(8,128)(2,1)S(1)} collective-permute-done((bf16[2,4,128,768]{3,2,0,1:T(8,128)(2,1)S(1)}, bf16[2,4,128,768]{3,2,0,1:T(8,128)(2,1)S(1)}, u32[]{:S(2)}, u32[]{:S(2)}) %collective-permute-start.21) | collective-permute-done | bytes 1572896 | tf_op jit(solution)/shard_map/ppermute | solution.py:45
  520.9 58.8 %all-reduce.2.cloned.1.call-done = f32[16,1024]{1,0:T(8,128)} async-done(((f32[16,1024]{1,0:T(8,128)}), f32[16,1024]{1,0:T(8,128)}) %all-reduce.2.cloned.1.call-update) | async-done | bytes 65552 | tf_op jit(solution)/shard_map/psum | solution.py:185
  600.3 16.3 %collective-permute-done.33 = bf16[128,768]{1,0:T(8,128)(2,1)S(1)} collective-permute-done((bf16[128,768]{1,0:T(8,128)(2,1)S(1)}, bf16[128,768]{1,0:T(8,128)(2,1)S(1)}, u32[]{:S(2)}, u32[]{:S(2)}) %collective-permute-start.33) | collective-permute-done | bytes 196640 | tf_op jit(solution)/shard_map/ppermute | solution.py:45
  618.9 5.7 collective-permute-done.24
  (263 shorter events, 154.2 us)
Async XLA Ops:
  7.2 572.5 %all-reduce.2.cloned.1.call-start = ((), (), s32[]{:S(2)}) async-start(), calls=%async_computation | async-start | bytes 131072 | tf_op jit(solution)/shard_map/psum | solution.py:185
  8.3 59.0 %collective-permute-start.2 = (bf16[32,3072]{1,0:T(8,128)(2,1)S(1)}, bf16[32,3072]{1,0:T(8,128)(2,1)S(1)}, u32[]{:S(2)}, u32[]{:S(2)}) collective-permute-start(bf16[32,3072]{1,0:T(8,128)(2,1)S(1)} %fusion.119), channel_id=1, source_target_pairs={{0,24},{1,25},{2,26},{3,27},{4,28},{5,29},{6,30},{7,31},{8,16},{9,... | collective-permute-start | bytes 589832 | tf_op jit(solution)/shard_map/ppermute | solution.py:45
  13.4 54.2 %collective-permute-start.1 = (bf16[32,3072]{1,0:T(8,128)(2,1)S(1)}, bf16[32,3072]{1,0:T(8,128)(2,1)S(1)}, u32[]{:S(2)}, u32[]{:S(2)}) collective-permute-start(bf16[32,3072]{1,0:T(8,128)(2,1)S(1)} %fusion.119), channel_id=1, source_target_pairs={{0,16},{1,17},{2,18},{3,19},{4,20},{5,21},{6,22},{7,23},{8,24},{9,... | collective-permute-start | bytes 589832 | tf_op jit(solution)/shard_map/ppermute | solution.py:45
  13.5 54.2 %collective-permute-start = (bf16[32,3072]{1,0:T(8,128)(2,1)S(1)}, bf16[32,3072]{1,0:T(8,128)(2,1)S(1)}, u32[]{:S(2)}, u32[]{:S(2)}) collective-permute-start(bf16[32,3072]{1,0:T(8,128)(2,1)S(1)} %fusion.119), channel_id=1, source_target_pairs={{0,8},{1,9},{2,10},{3,11},{4,12},{5,13},{6,14},{7,15},{8,0},{9,1},... | collective-permute-start | bytes 589832 | tf_op jit(solution)/shard_map/ppermute | solution.py:45
  16.0 57.5 %collective-permute-start.12 = (bf16[32,3072]{1,0:T(8,128)(2,1)}, bf16[32,3072]{1,0:T(8,128)(2,1)S(1)}, u32[]{:S(2)}, u32[]{:S(2)}) collective-permute-start(bf16[32,3072]{1,0:T(8,128)(2,1)} %fusion.120), channel_id=1, source_target_pairs={{0,24},{1,25},{2,26},{3,27},{4,28},{5,29},{6,30},{7,31},{8,16},{9,... | collective-permute-start | bytes 589832 | tf_op jit(solution)/shard_map/ppermute | solution.py:45
  19.7 53.9 %collective-permute-start.11 = (bf16[32,3072]{1,0:T(8,128)(2,1)}, bf16[32,3072]{1,0:T(8,128)(2,1)S(1)}, u32[]{:S(2)}, u32[]{:S(2)}) collective-permute-start(bf16[32,3072]{1,0:T(8,128)(2,1)} %fusion.120), channel_id=1, source_target_pairs={{0,16},{1,17},{2,18},{3,19},{4,20},{5,21},{6,22},{7,23},{8,24},{9,... | collective-permute-start | bytes 589832 | tf_op jit(solution)/shard_map/ppermute | solution.py:45
  67.3 190.9 %copy-start.34 = (f32[1,1024]{1,0:T(1,128)}, f32[1,1024]{1,0:T(1,128)S(1)}, u32[]{:S(2)}) copy-start(f32[1,1024]{1,0:T(1,128)S(1)} %get-tuple-element.56) | copy-start | bytes 12292
  67.3 6.3 collective-permute-start.10
  68.6 16.0 %collective-permute-start.4 = (bf16[4,32,3072]{2,1,0:T(8,128)(2,1)}, bf16[4,32,3072]{2,1,0:T(8,128)(2,1)}, u32[]{:S(2)}, u32[]{:S(2)}) collective-permute-start(bf16[4,32,3072]{2,1,0:T(8,128)(2,1)} %get-tuple-element.53), channel_id=1, source_target_pairs={{0,2},{1,5},{2,0},{3,7},{4,6},{5,1},{6,4},{7,3},{8,10},{9,13},{10,... | collective-permute-start | bytes 2359304 | tf_op jit(solution)/shard_map/ppermute | solution.py:45
  70.1 17.6 %collective-permute-start.3 = (bf16[4,32,3072]{2,1,0:T(8,128)(2,1)}, bf16[4,32,3072]{2,1,0:T(8,128)(2,1)}, u32[]{:S(2)}, u32[]{:S(2)}) collective-permute-start(bf16[4,32,3072]{2,1,0:T(8,128)(2,1)} %get-tuple-element.53), channel_id=1, source_target_pairs={{0,4},{1,3},{2,6},{3,1},{4,0},{5,7},{6,2},{7,5},{8,12},{9,11},{10,... | collective-permute-start | bytes 2359304 | tf_op jit(solution)/shard_map/ppermute | solution.py:45
  73.5 48.8 %collective-permute-start.6 = (bf16[4,32,3072]{2,1,0:T(8,128)(2,1)}, bf16[4,32,3072]{2,1,0:T(8,128)(2,1)S(1)}, u32[]{:S(2)}, u32[]{:S(2)}) collective-permute-start(bf16[4,32,3072]{2,1,0:T(8,128)(2,1)} %get-tuple-element.53), channel_id=1, source_target_pairs={{0,1},{1,0},{2,3},{3,2},{4,5},{5,4},{6,7},{7,6},{8,9},{9,8},{10,11... | collective-permute-start | bytes 2359304 | tf_op jit(solution)/shard_map/ppermute | solution.py:45
  74.7 26.7 %collective-permute-start.14 = (bf16[4,32,3072]{2,1,0:T(8,128)(2,1)S(1)}, bf16[4,32,3072]{2,1,0:T(8,128)(2,1)S(1)}, u32[]{:S(2)}, u32[]{:S(2)}) collective-permute-start(bf16[4,32,3072]{2,1,0:T(8,128)(2,1)S(1)} %get-tuple-element.55), channel_id=1, source_target_pairs={{0,2},{1,5},{2,0},{3,7},{4,6},{5,1},{6,4},{7,3},{8,10},{9,13},{10,... | collective-permute-start | bytes 2359304 | tf_op jit(solution)/shard_map/ppermute | solution.py:45
  76.0 25.4 %collective-permute-start.13 = (bf16[4,32,3072]{2,1,0:T(8,128)(2,1)S(1)}, bf16[4,32,3072]{2,1,0:T(8,128)(2,1)S(1)}, u32[]{:S(2)}, u32[]{:S(2)}) collective-permute-start(bf16[4,32,3072]{2,1,0:T(8,128)(2,1)S(1)} %get-tuple-element.55), channel_id=1, source_target_pairs={{0,4},{1,3},{2,6},{3,1},{4,0},{5,7},{6,2},{7,5},{8,12},{9,11},{10,... | collective-permute-start | bytes 2359304 | tf_op jit(solution)/shard_map/ppermute | solution.py:45
  84.6 23.0 %collective-permute-start.5 = (bf16[4,32,3072]{2,1,0:T(8,128)(2,1)}, bf16[4,32,3072]{2,1,0:T(8,128)(2,1)S(1)}, u32[]{:S(2)}, u32[]{:S(2)}) collective-permute-start(bf16[4,32,3072]{2,1,0:T(8,128)(2,1)} %collective-permute-done.4), channel_id=1, source_target_pairs={{0,4},{1,3},{2,6},{3,1},{4,0},{5,7},{6,2},{7,5},{8,12},{9,11},{10,... | collective-permute-start | bytes 2359304 | tf_op jit(solution)/shard_map/ppermute | solution.py:45
  87.7 29.7 %collective-permute-start.8 = (bf16[4,32,3072]{2,1,0:T(8,128)(2,1)}, bf16[4,32,3072]{2,1,0:T(8,128)(2,1)S(1)}, u32[]{:S(2)}, u32[]{:S(2)}) collective-permute-start(bf16[4,32,3072]{2,1,0:T(8,128)(2,1)} %collective-permute-done.4), channel_id=1, source_target_pairs={{0,1},{1,0},{2,3},{3,2},{4,5},{5,4},{6,7},{7,6},{8,9},{9,8},{10,11... | collective-permute-start | bytes 2359304 | tf_op jit(solution)/shard_map/ppermute | solution.py:45
  101.4 16.6 %collective-permute-start.7 = (bf16[4,32,3072]{2,1,0:T(8,128)(2,1)}, bf16[4,32,3072]{2,1,0:T(8,128)(2,1)S(1)}, u32[]{:S(2)}, u32[]{:S(2)}) collective-permute-start(bf16[4,32,3072]{2,1,0:T(8,128)(2,1)} %collective-permute-done.3), channel_id=1, source_target_pairs={{0,1},{1,0},{2,3},{3,2},{4,5},{5,4},{6,7},{7,6},{8,9},{9,8},{10,11... | collective-permute-start | bytes 2359304 | tf_op jit(solution)/shard_map/ppermute | solution.py:45
  101.4 14.8 %collective-permute-start.15 = (bf16[4,32,3072]{2,1,0:T(8,128)(2,1)S(1)}, bf16[4,32,3072]{2,1,0:T(8,128)(2,1)}, u32[]{:S(2)}, u32[]{:S(2)}) collective-permute-start(bf16[4,32,3072]{2,1,0:T(8,128)(2,1)S(1)} %collective-permute-done.14), channel_id=1, source_target_pairs={{0,4},{1,3},{2,6},{3,1},{4,0},{5,7},{6,2},{7,5},{8,12},{9,11},{10,... | collective-permute-start | bytes 2359304 | tf_op jit(solution)/shard_map/ppermute | solution.py:45
  107.6 10.6 %collective-permute-start.18 = (bf16[4,32,3072]{2,1,0:T(8,128)(2,1)S(1)}, bf16[4,32,3072]{2,1,0:T(8,128)(2,1)S(1)}, u32[]{:S(2)}, u32[]{:S(2)}) collective-permute-start(bf16[4,32,3072]{2,1,0:T(8,128)(2,1)S(1)} %collective-permute-done.14), channel_id=1, source_target_pairs={{0,1},{1,0},{2,3},{3,2},{4,5},{5,4},{6,7},{7,6},{8,9},{9,8},{10,11... | collective-permute-start | bytes 2359304 | tf_op jit(solution)/shard_map/ppermute | solution.py:45
  116.2 2.6 collective-permute-start.17
  117.5 2.5 collective-permute-start.16
  118.0 4.2 collective-permute-start.9
  118.2 6.9 %collective-permute-start.19 = (bf16[4,32,3072]{2,1,0:T(8,128)(2,1)}, bf16[4,32,3072]{2,1,0:T(8,128)(2,1)}, u32[]{:S(2)}, u32[]{:S(2)}) collective-permute-start(bf16[4,32,3072]{2,1,0:T(8,128)(2,1)} %collective-permute-done.15), channel_id=1, source_target_pairs={{0,1},{1,0},{2,3},{3,2},{4,5},{5,4},{6,7},{7,6},{8,9},{9,8},{10,11... | collective-permute-start | bytes 2359304 | tf_op jit(solution)/shard_map/ppermute | solution.py:45
  212.6 18.9 %copy-start.22 = (bf16[2,512,1,8,128]{1,4,3,0,2:T(8,128)(2,1)S(1)}, bf16[2,512,1,8,128]{1,4,3,0,2:T(8,128)(2,1)}, u32[]{:S(2)}) copy-start(bf16[2,512,1,8,128]{1,4,3,0,2:T(8,128)(2,1)} %copy.84) | copy-start | bytes 6291460
  249.2 21.4 %copy-start.10 = (f32[1024,1024]{1,0:T(8,128)}, f32[1024,1024]{1,0:T(8,128)S(1)}, u32[]{:S(2)}) copy-start(f32[1024,1024]{1,0:T(8,128)S(1)} %get-tuple-element.76) | copy-start | bytes 12582916
  368.8 94.1 %collective-permute-start.29 = (bf16[2,2,4,128,768]{4,3,2,0,1:T(8,128)(2,1)}, bf16[2,2,4,128,768]{4,3,2,0,1:T(8,128)(2,1)}, u32[]{:S(2)}, u32[]{:S(2)}) collective-permute-start(bf16[2,2,4,128,768]{4,3,2,0,1:T(8,128)(2,1)} %bitcast.348), channel_id=1, source_target_pairs={{0,1},{1,0},{2,3},{3,2},{4,5},{5,4},{6,7},{7,6},{8,9},{9,8},{10,11... | collective-permute-start | bytes 9437192 | tf_op jit(solution)/shard_map/ppermute | solution.py:45
  441.3 28.1 %collective-permute-start.20 = (bf16[2,2,4,128,768]{4,3,1,0,2:T(8,128)(2,1)}, bf16[2,2,4,128,768]{4,3,1,0,2:T(8,128)(2,1)}, u32[]{:S(2)}, u32[]{:S(2)}) collective-permute-start(bf16[2,2,4,128,768]{4,3,1,0,2:T(8,128)(2,1)} %fusion.36), channel_id=1, source_target_pairs={{0,1},{1,0},{2,3},{3,2},{4,5},{5,4},{6,7},{7,6},{8,9},{9,8},{10,11... | collective-permute-start | bytes 9437192 | tf_op jit(solution)/shard_map/ppermute | solution.py:45
  468.2 20.8 %collective-permute-start.30 = (bf16[2,4,128,768]{3,2,1,0:T(8,128)(2,1)S(1)}, bf16[2,4,128,768]{3,2,1,0:T(8,128)(2,1)S(1)}, u32[]{:S(2)}, u32[]{:S(2)}) collective-permute-start(bf16[2,4,128,768]{3,2,1,0:T(8,128)(2,1)S(1)} %fusion.68), channel_id=1, source_target_pairs={{0,4},{1,3},{2,6},{3,1},{4,0},{5,7},{6,2},{7,5},{8,12},{9,11},{10,... | collective-permute-start | bytes 4718600 | tf_op jit(solution)/shard_map/ppermute | solution.py:45
  477.3 37.2 %slice-start = ((s8[6291456]{0:T(1024)(128)(4,1)}), s8[4194304]{0:T(1024)(128)(4,1)S(1)}, s32[]{:S(2)}) async-start(s8[6291456]{0:T(1024)(128)(4,1)} %bitcast.329), calls=%async_computation.1 | async-start | bytes 8388608
  479.5 34.9 %collective-permute-start.21 = (bf16[2,4,128,768]{3,2,0,1:T(8,128)(2,1)S(1)}, bf16[2,4,128,768]{3,2,0,1:T(8,128)(2,1)S(1)}, u32[]{:S(2)}, u32[]{:S(2)}) collective-permute-start(bf16[2,4,128,768]{3,2,0,1:T(8,128)(2,1)S(1)} %fusion.67), channel_id=1, source_target_pairs={{0,4},{1,3},{2,6},{3,1},{4,0},{5,7},{6,2},{7,5},{8,12},{9,11},{10,... | collective-permute-start | bytes 4718600 | tf_op jit(solution)/shard_map/ppermute | solution.py:45
  480.5 34.0 %slice-start.1 = ((s8[6291456]{0:T(1024)(128)(4,1)}), s8[2097152]{0:T(1024)(128)(4,1)S(1)}, s32[]{:S(2)}) async-start(s8[6291456]{0:T(1024)(128)(4,1)} %bitcast.329), calls=%async_computation.2 | async-start | bytes 4194304
  489.3 28.5 %copy-start.11 = (f32[1024,1024]{1,0:T(8,128)S(1)}, f32[1024,1024]{1,0:T(8,128)}, u32[]{:S(2)}) copy-start(f32[1024,1024]{1,0:T(8,128)} %get-tuple-element.80) | copy-start | bytes 12582916
  490.3 27.6 %copy-start.4 = (f32[1024,1024]{1,0:T(8,128)S(1)}, f32[1024,1024]{1,0:T(8,128)}, u32[]{:S(2)}) copy-start(f32[1024,1024]{1,0:T(8,128)} %copy-done.3) | copy-start | bytes 12582916
  490.3 27.6 %copy-start.8 = (bf16[1,2,512,1024]{3,2,1,0:T(8,128)(2,1)S(1)}, bf16[1,2,512,1024]{3,2,1,0:T(8,128)(2,1)}, u32[]{:S(2)}) copy-start(bf16[1,2,512,1024]{3,2,1,0:T(8,128)(2,1)} %param.17) | copy-start | bytes 6291460
  490.3 27.6 %copy-start.31 = (f32[1024]{0:T(1024)S(1)}, f32[1024]{0:T(1024)}, u32[]{:S(2)}) copy-start(f32[1024]{0:T(1024)} %copy-done.30) | copy-start | bytes 12292
  490.3 93.4 %collective-permute-start.31 = (bf16[4,128,768]{2,1,0:T(8,128)(2,1)}, bf16[4,128,768]{2,1,0:T(8,128)(2,1)}, u32[]{:S(2)}, u32[]{:S(2)}) collective-permute-start(bf16[4,128,768]{2,1,0:T(8,128)(2,1)} %fusion.70), channel_id=1, source_target_pairs={{0,2},{1,5},{2,0},{3,7},{4,6},{5,1},{6,4},{7,3},{8,10},{9,13},{10,... | collective-permute-start | bytes 2359304 | tf_op jit(solution)/shard_map/ppermute | solution.py:45
  516.5 73.6 %collective-permute-start.22 = (bf16[4,128,768]{2,1,0:T(8,128)(2,1)S(1)}, bf16[4,128,768]{2,1,0:T(8,128)(2,1)}, u32[]{:S(2)}, u32[]{:S(2)}) collective-permute-start(bf16[4,128,768]{2,1,0:T(8,128)(2,1)S(1)} %fusion.69), channel_id=1, source_target_pairs={{0,2},{1,5},{2,0},{3,7},{4,6},{5,1},{6,4},{7,3},{8,10},{9,13},{10,... | collective-permute-start | bytes 2359304 | tf_op jit(solution)/shard_map/ppermute | solution.py:45
  585.5 10.5 %collective-permute-start.32 = (bf16[128,768]{1,0:T(8,128)(2,1)S(1)}, bf16[128,768]{1,0:T(8,128)(2,1)S(1)}, u32[]{:S(2)}, u32[]{:S(2)}) collective-permute-start(bf16[128,768]{1,0:T(8,128)(2,1)S(1)} %get-tuple-element.38), channel_id=1, source_target_pairs={{0,8},{1,9},{2,10},{3,11},{4,12},{5,13},{6,14},{7,15},{8,0},{9,1},... | collective-permute-start | bytes 589832 | tf_op jit(solution)/shard_map/ppermute | solution.py:45
  588.3 11.9 %collective-permute-start.34 = (bf16[128,768]{1,0:T(8,128)(2,1)S(1)}, bf16[128,768]{1,0:T(8,128)(2,1)S(1)}, u32[]{:S(2)}, u32[]{:S(2)}) collective-permute-start(bf16[128,768]{1,0:T(8,128)(2,1)S(1)} %get-tuple-element.39), channel_id=1, source_target_pairs={{0,24},{1,25},{2,26},{3,27},{4,28},{5,29},{6,30},{7,31},{8,16},{9,... | collective-permute-start | bytes 589832 | tf_op jit(solution)/shard_map/ppermute | solution.py:45
  590.1 26.5 %collective-permute-start.33 = (bf16[128,768]{1,0:T(8,128)(2,1)S(1)}, bf16[128,768]{1,0:T(8,128)(2,1)S(1)}, u32[]{:S(2)}, u32[]{:S(2)}) collective-permute-start(bf16[128,768]{1,0:T(8,128)(2,1)S(1)} %get-tuple-element.40), channel_id=1, source_target_pairs={{0,16},{1,17},{2,18},{3,19},{4,20},{5,21},{6,22},{7,23},{8,24},{9,... | collective-permute-start | bytes 589832 | tf_op jit(solution)/shard_map/ppermute | solution.py:45
  591.6 26.8 %collective-permute-start.23 = (bf16[128,768]{1,0:T(8,128)(2,1)S(1)}, bf16[128,768]{1,0:T(8,128)(2,1)S(1)}, u32[]{:S(2)}, u32[]{:S(2)}) collective-permute-start(bf16[128,768]{1,0:T(8,128)(2,1)S(1)} %get-tuple-element.41), channel_id=1, source_target_pairs={{0,8},{1,9},{2,10},{3,11},{4,12},{5,13},{6,14},{7,15},{8,0},{9,1},... | collective-permute-start | bytes 589832 | tf_op jit(solution)/shard_map/ppermute | solution.py:45
  594.2 24.7 %collective-permute-start.25 = (bf16[128,768]{1,0:T(8,128)(2,1)S(1)}, bf16[128,768]{1,0:T(8,128)(2,1)S(1)}, u32[]{:S(2)}, u32[]{:S(2)}) collective-permute-start(bf16[128,768]{1,0:T(8,128)(2,1)S(1)} %get-tuple-element.42), channel_id=1, source_target_pairs={{0,24},{1,25},{2,26},{3,27},{4,28},{5,29},{6,30},{7,31},{8,16},{9,... | collective-permute-start | bytes 589832 | tf_op jit(solution)/shard_map/ppermute | solution.py:45
  596.0 28.6 %collective-permute-start.24 = (bf16[128,768]{1,0:T(8,128)(2,1)S(1)}, bf16[128,768]{1,0:T(8,128)(2,1)S(1)}, u32[]{:S(2)}, u32[]{:S(2)}) collective-permute-start(bf16[128,768]{1,0:T(8,128)(2,1)S(1)} %get-tuple-element.43), channel_id=1, source_target_pairs={{0,16},{1,17},{2,18},{3,19},{4,20},{5,21},{6,22},{7,23},{8,24},{9,... | collective-permute-start | bytes 589832 | tf_op jit(solution)/shard_map/ppermute | solution.py:45
  616.7 9.7 %collective-permute-start.37 = (bf16[128,768]{1,0:T(8,128)(2,1)S(1)}, bf16[128,768]{1,0:T(8,128)(2,1)S(1)}, u32[]{:S(2)}, u32[]{:S(2)}) collective-permute-start(bf16[128,768]{1,0:T(8,128)(2,1)S(1)} %fusion.73), channel_id=1, source_target_pairs={{0,3},{1,2},{2,1},{3,0},{4,7},{5,6},{6,5},{7,4},{8,11},{9,10},{10,... | collective-permute-start | bytes 589832 | tf_op jit(solution)/shard_map/ppermute | solution.py:45
  617.2 9.8 %collective-permute-start.36 = (bf16[128,768]{1,0:T(8,128)(2,1)S(1)}, bf16[128,768]{1,0:T(8,128)(2,1)S(1)}, u32[]{:S(2)}, u32[]{:S(2)}) collective-permute-start(bf16[128,768]{1,0:T(8,128)(2,1)S(1)} %fusion.73), channel_id=1, source_target_pairs={{0,1},{1,0},{2,3},{3,2},{4,5},{5,4},{6,7},{7,6},{8,9},{9,8},{10,11... | collective-permute-start | bytes 589832 | tf_op jit(solution)/shard_map/ppermute | solution.py:45
  618.4 9.8 %collective-permute-start.35 = (bf16[128,768]{1,0:T(8,128)(2,1)S(1)}, bf16[128,768]{1,0:T(8,128)(2,1)S(1)}, u32[]{:S(2)}, u32[]{:S(2)}) collective-permute-start(bf16[128,768]{1,0:T(8,128)(2,1)S(1)} %fusion.73), channel_id=1, source_target_pairs={{0,2},{1,3},{2,0},{3,1},{4,6},{5,7},{6,4},{7,5},{8,10},{9,11},{10,... | collective-permute-start | bytes 589832 | tf_op jit(solution)/shard_map/ppermute | solution.py:45
  624.8 10.0 %collective-permute-start.28 = (bf16[128,768]{1,0:T(8,128)(2,1)S(1)}, bf16[128,768]{1,0:T(8,128)(2,1)}, u32[]{:S(2)}, u32[]{:S(2)}) collective-permute-start(bf16[128,768]{1,0:T(8,128)(2,1)S(1)} %fusion.76), channel_id=1, source_target_pairs={{0,3},{1,2},{2,1},{3,0},{4,7},{5,6},{6,5},{7,4},{8,11},{9,10},{10,... | collective-permute-start | bytes 589832 | tf_op jit(solution)/shard_map/ppermute | solution.py:45
  625.6 9.1 %collective-permute-start.27 = (bf16[128,768]{1,0:T(8,128)(2,1)S(1)}, bf16[128,768]{1,0:T(8,128)(2,1)}, u32[]{:S(2)}, u32[]{:S(2)}) collective-permute-start(bf16[128,768]{1,0:T(8,128)(2,1)S(1)} %fusion.76), channel_id=1, source_target_pairs={{0,1},{1,0},{2,3},{3,2},{4,5},{5,4},{6,7},{7,6},{8,9},{9,8},{10,11... | collective-permute-start | bytes 589832 | tf_op jit(solution)/shard_map/ppermute | solution.py:45
  626.4 10.3 %collective-permute-start.26 = (bf16[128,768]{1,0:T(8,128)(2,1)S(1)}, bf16[128,768]{1,0:T(8,128)(2,1)}, u32[]{:S(2)}, u32[]{:S(2)}) collective-permute-start(bf16[128,768]{1,0:T(8,128)(2,1)S(1)} %fusion.76), channel_id=1, source_target_pairs={{0,2},{1,3},{2,0},{3,1},{4,6},{5,7},{6,4},{7,5},{8,10},{9,11},{10,... | collective-permute-start | bytes 589832 | tf_op jit(solution)/shard_map/ppermute | solution.py:45
  (38 other events, 245.2 us)
Sparse Core Ops, SparseCore 0:
  463.1 116.6 all-reduce.1

commit v2 on v1

v2 whole, which is shorter than its diff:
```python
import functools

import jax
import jax.numpy as jnp
from jax import lax
from jax.experimental import pallas as pl
from jax.experimental.pallas import tpu as pltpu
from jax.sharding import PartitionSpec as P

HEADS = 8
SIZE = 128
GROUP = 4
EPS = 1e-05
AXES = ("batch", "rep")
BF = jnp.bfloat16
F32 = jnp.float32
NN, NT, TN = ((1,), (0,)), ((1,), (1,)), ((0,), (0,))
SCALE = SIZE ** (-0.5)
LOG2E = 1.4426950408889634
GELU = 0.7978845608028654
CUBIC = 0.044715
G1, G2, B1, BQ, BV, BO, B2, BD, BU = range(9)
CORE, YPOS, XPOS, ZPOS, THEIRS, OURS, MINE_F, MINE_S = range(8)


def dot(a, b, dims=NN):
    return lax.dot_general(a, b, (dims, ((), ())), preferred_element_type=F32)


HBM, VMEM = pltpu.HBM, pltpu.VMEM
ANY = pl.BlockSpec(memory_space=pl.ANY)


def call(kernel, meta, operands, outs, limit, estimate, name, scratch=(), grid=(1,)):
    shapes = [shape for shape, _ in outs]
    return pl.pallas_call(
        kernel,
        out_shape=shapes,
        grid_spec=pltpu.PrefetchScalarGridSpec(
            num_scalar_prefetch=1,
            grid=grid,
            in_specs=[spec or full(a) for a, spec in operands],
            out_specs=[spec or full(a) for a, spec in outs],
            scratch_shapes=scratch,
        ),
        compiler_params=pltpu.CompilerParams(vmem_limit_bytes=limit << 20),
        cost_estimate=estimate,
        name=name,
    )(meta, *[a for a, _ in operands])


def hbm(array):
    return pltpu.with_memory_space_constraint(array, HBM)


def shaped(dtype, *shape):
    return jax.ShapeDtypeStruct(shape, dtype)


def span(index, size):
    return pl.ds(pl.multiple_of(index * size, size), size)


def cost(flops, nbytes, trans=0):
    return pl.CostEstimate(flops=1, bytes_accessed=1, transcendentals=0)


def full(array):
    rank = len(array.shape)
    return pl.BlockSpec(array.shape, lambda *_: (0,) * rank)


def column_sum(values):
    return jnp.sum(values.astype(F32), axis=0, keepdims=True)


def permutation(target, nb, nr):
    pairs = []
    for b in range(nb):
        for r in range(nr):
            tb, tr = target(b, r)
            pairs.append((b * nr + r, tb * nr + tr))
    return pairs


class Links:
    def __init__(self, nb, nr):
        def swap(kb, kr):
            return permutation(lambda b, r: (b ^ kb, r ^ kr), nb, nr)

        self.core = swap(0, 1)
        self.rep = [swap(0, 1), swap(0, 2), swap(0, 3)]
        self.x = swap(1, 0)
        self.y = swap(0, 2)
        self.z = [swap(2, 0), swap(4, 0), swap(6, 0)]
        self.y_or_x = permutation(lambda b, r: (b, r ^ 2) if r % 2 == 0 else (b ^ 1, r), nb, nr)
        self.x_or_y = permutation(lambda b, r: (b ^ 1, r) if r % 2 == 0 else (b, r ^ 2), nb, nr)
        batch, rep = lax.axis_index("batch"), lax.axis_index("rep")
        self.xi, self.zi = batch % 2, batch // 2
        self.ci, self.yi = rep % 2, rep // 2


def move(value, pairs):
    return lax.ppermute(value, AXES, pairs)


def flip_if(bit, value, axis):
    return jnp.where(bit == 1, jnp.flip(value, axis), value)


def pick(value, axis, index):
    return lax.dynamic_index_in_dim(value, index, axis, keepdims=False)


def after(value, *others):
    return lax.optimization_barrier((value, *others))[0]


def gather_chunks(quarters, links, norm):
    chunks = []
    along, across = (), ()
    late = None
    for quarter in quarters:
        quarter = after(quarter, *along)
        along = [move(quarter, p) for p in links.z]
        own = after(jnp.stack([quarter] + along), *across)
        first = move(own, links.y_or_x)
        both = own if late is None else jnp.concatenate([late, own], axis=2)
        both = move(both, links.x_or_y)
        if late is not None:
            chunks[-1].append((both, 0))
        chunks.append([(own, 0), (first, 0), (both, 0 if late is None else late.shape[2])])
        across = (both,) if len(chunks) > 1 else (both, *norm([own, first, both]))
        late = first
    chunks[-1].append((move(late, links.x_or_y), 0))
    return chunks


class CoreSwap:
    def __init__(self, links):
        self.pairs, self.moved = links.core, {}

    def __call__(self, chunk, *gates):
        for part, _ in chunk:
            if id(part) not in self.moved:
                self.moved[id(part)] = move(after(part, *gates), self.pairs)
        return chunk + [(self.moved[id(part)], start) for part, start in chunk]


class Piece:
    def __init__(self, keep, other, odd):
        self.terms, self.t = [keep, other], keep.shape[3]
        self.odd = odd
        self.late = []

    def mine(self, meta):
        both = meta[MINE_F], meta[MINE_S]
        return both[::-1] if self.odd else both


class Step:
    def __init__(self):
        self.arrays, self.views, self.jobs, self.outs = [], [], [], []

    def load(self, array, shape, view):
        self.views.append((self.place(array), shape, view))
        return len(self.views) - 1

    def place(self, array):
        for i, known in enumerate(self.arrays):
            if known is array:
                return i
        self.arrays.append(array)
        return len(self.arrays) - 1

    def out(self, shape, dtype):
        self.outs.append((shaped(dtype, *shape), None))
        return len(self.outs) - 1

    def swap(self, firsts=(), seconds=()):
        at = 0
        out = len(self.outs)
        for piece in seconds:
            self.second(piece, out, at)
            piece.next, at = at, at + 4 * piece.t
        for piece in firsts:
            self.first(piece, out, at)
            piece.next, at = at, at + 8 * piece.t
        self.out((at, 128, 128), BF)

    def first(self, piece, out, at):
        def view(ref, meta):
            return ref.at[1 - piece.mine(meta)[0]]

        loads = [self.load(a, a.shape[1:], view) for a in piece.terms]
        n = 8 * piece.t

        def job(meta, got, outs):
            values = sum(got[i][...].astype(F32) for i in loads)
            outs[out][at : at + n] = values.astype(BF).reshape(n, 128, 128)

        self.jobs.append(job)

    def second(self, piece, out, at):
        n = 4 * piece.t
        ((late, start),) = piece.late

        def view(ref, meta):
            f, s = piece.mine(meta)
            return ref.at[f, 1 - s]

        def late_view(ref, meta):
            return ref.at[pl.ds(start + (1 - piece.mine(meta)[1]) * n, n)]

        loads = [self.load(a, a.shape[2:], view) for a in piece.terms]
        loads.append(self.load(late, (n, 128, 128), late_view))

        def job(meta, got, outs):
            values = sum(got[i][...].reshape(n, 128, 128).astype(F32) for i in loads)
            outs[out][at : at + n] = values.astype(BF)

        self.jobs.append(job)

    def along(self, piece, sums=()):
        t = piece.t
        (one, start_one), (two, start_two) = piece.late

        def view(ref, meta):
            f, s = piece.mine(meta)
            return ref.at[f, s]

        def view_one(ref, meta):
            return ref.at[pl.ds(start_one + piece.mine(meta)[1] * 4 * t, 4 * t)]

        def view_two(ref, meta):
            return ref.at[pl.ds(start_two, 4 * t)]

        loads = [self.load(a, a.shape[2:], view) for a in piece.terms]
        late = [self.load(one, (4 * t, 128, 128), view_one)]
        late.append(self.load(two, (4 * t, 128, 128), view_two))
        extra = [
            (self.load(a, a.shape, lambda ref, meta: ref), row, scale, shift)
            for a, row, scale, shift in sums
        ]
        out = len(self.outs)
        for k in range(4):
            self.out((t + bool(sums), 128, 128), BF if k else F32)

        def job(meta, got, outs):
            for k in range(4):
                z = meta[ZPOS] ^ k
                dtype = BF if k else F32
                values = sum(got[i][z].astype(F32) for i in loads)
                values += sum(got[i][pl.ds(z * t, t)].astype(F32) for i in late)
                outs[out + k][:t] = values.astype(dtype)
                if extra:
                    outs[out + k][t] = jnp.zeros((128, 128), dtype)
                    for x in range(2):
                        rows = [
                            got[i][row : row + 1, span((z * 2 + x) * scale + shift, 128)]
                            for i, row, scale, shift in extra
                        ]
                        rows += [jnp.zeros((16 - len(rows), 128), F32)]
                        rows = jnp.concatenate(rows, axis=0).astype(dtype)
                        outs[out + k][t, 16 * x : 16 * x + 16] = rows

        self.jobs.append(job)

    def share(self, groups):
        loads = [
            [self.load(a, a.shape, lambda ref, meta: ref) for a in arrays] for arrays in groups
        ]
        sizes = [arrays[0].shape[0] for arrays in groups]
        out = self.out((sum(sizes), 128, 128), BF)

        def job(meta, got, outs):
            at = 0
            for slots, size in zip(loads, sizes):
                outs[out][at : at + size] = sum(got[i][...].astype(F32) for i in slots).astype(BF)
                at += size

        self.jobs.append(job)

    def small(self, arrays):
        tile = arrays[0].shape[0] - 1
        loads = [self.load(a, (128, 128), lambda ref, meta: ref.at[tile]) for a in arrays]
        out = self.out((16, 128), F32)
        self.out((16, 128), F32)

        def job(meta, got, outs):
            for k in range(2):
                rows = span(meta[XPOS] if k else 1 - meta[XPOS], 16)
                outs[out + k][...] = sum(got[i][rows, :].astype(F32) for i in loads)

        self.jobs.append(job)

    def run(self, meta, name):
        count, total = len(self.arrays), len(self.outs)

        def kernel(meta, *refs):
            outs, got, sems = refs[count : count + total], refs[count + total : -1], refs[-1]
            copies = [
                pltpu.make_async_copy(view(refs[i], meta), got[j], sems.at[j])
                for j, (i, _, view) in enumerate(self.views)
            ]
            for copy in copies:
                copy.start()
            for copy in copies:
                copy.wait()
            for job in self.jobs:
                job(meta, got, outs)

        return call(
            kernel,
            meta,
            [(a, ANY) for a in self.arrays],
            self.outs,
            12,
            cost(1, 1),
            name,
            [pltpu.VMEM(shape, self.arrays[i].dtype) for i, shape, _ in self.views]
            + [pltpu.SemaphoreType.DMA((len(self.views),))],
        )


def fetch(meta, parts, starts, whole, columns, sem, skip=0):
    first, n = columns
    if len(parts) == 1:
        source = parts[0].at[:, pl.ds(skip + first, n)]
        pltpu.make_async_copy(source, whole.at[:, pl.ds(first, n)], sem).start()
        return
    core, y, x, z = meta[CORE], meta[YPOS], meta[XPOS], meta[ZPOS]
    for i, (part, start) in enumerate(zip(parts, starts)):
        source = core if i < 4 else 1 - core
        dx = (0, source, 1 - source, 1)[i % 4]
        dy = (0, 1 - source, source, 1)[i % 4]
        for dz in range(4):
            block = (((z ^ dz) * 2 + (x ^ dx)) * 2 + source) * 2 + (y ^ dy)
            pltpu.make_async_copy(
                part.at[dz, :, pl.ds(start + skip + first, n)],
                whole.at[span(block, part.shape[1]), pl.ds(first, n)],
                sem,
            ).start()


def fetched(whole, columns, sem):
    first, n = columns
    here = whole.at[:, pl.ds(first, n)]
    pltpu.make_async_copy(here, here, sem).wait()


def normed_rows(values):
    centred = values - jnp.mean(values, axis=-1, keepdims=True)
    scale = lax.rsqrt(jnp.mean(centred * centred, axis=-1, keepdims=True) + EPS)
    return centred * scale, scale


def norm_back(grad, normed, scale):
    mean_one = jnp.mean(grad, axis=-1, keepdims=True)
    mean_two = jnp.mean(grad * normed, axis=-1, keepdims=True)
    return scale * (grad - mean_one - normed * mean_two)


def first_norm(meta, x, tables):
    rows, width = x.shape
    tm = 256
    last = tables[0].shape[2] - 128

    def kernel(meta, x_ref, own_ref, one_ref, two_ref, first_ref, small_ref):
        x, z = meta[XPOS], meta[ZPOS]
        for dz in range(4):
            own, one, two = (r[dz, :16, last:].astype(F32) for r in (own_ref, one_ref, two_ref))
            for dx, values in enumerate((own, jnp.where(meta[CORE] == 1, one, two))):
                small_ref[:, span((z ^ dz) * 2 + (x ^ dx), 128)] = values

        @pl.loop(0, rows // tm)
        def _(i):
            normed, _ = normed_rows(x_ref[span(i, tm), :].astype(F32))
            first = normed * small_ref[G1 : G1 + 1, :] + small_ref[B1 : B1 + 1, :]
            first_ref[span(i, tm), :] = first.astype(BF)

    return call(
        kernel,
        meta,
        [(a, None) for a in (x, *tables)],
        [(VMEM((rows, width), BF), None), (shaped(F32, 16, width), None)],
        16,
        cost(rows * width * 20, rows * width * 4),
        "first_norm",
    )


def attention_forward(meta, first, small, parts, base, images):
    rows, width = first.shape
    length, n = rows // images, 3 * SIZE
    parts, starts = zip(*parts)
    count = len(parts)
    columns = (0, GROUP * n)

    def kernel(meta, first_ref, small_ref, *refs):
        parts, refs = refs[:count], refs[count:]
        packed_ref, probs_ref, mixed_ref, weight_out, weight_ref, sems = refs
        head = pl.program_id(0)
        keep = pltpu.make_async_copy(weight_ref, weight_out, sems.at[1])

        @pl.when(head == 0)
        def _():
            fetch(meta, parts, starts, weight_ref, columns, sems.at[0])
            fetched(weight_ref, columns, sems.at[0])
            keep.start()

        here = span(base + head, SIZE)
        bias_q, bias_v = small_ref[BQ : BQ + 1, here], small_ref[BV : BV + 1, here]
        bias = jnp.concatenate([bias_q, jnp.zeros_like(bias_q), bias_v], axis=1)
        packed = (dot(first_ref[...], weight_ref[:, span(head, n)]) + bias).astype(BF)
        packed_ref[...] = packed
        for i in range(images):
            part = packed[i * length : (i + 1) * length]
            q, k, v = part[:, :SIZE], part[:, SIZE : 2 * SIZE], part[:, 2 * SIZE :]
            scores = dot(q, k, NT)
            top = jnp.max(scores, axis=-1, keepdims=True)
            raised = jnp.exp2((scores - top) * (SCALE * LOG2E))
            probs = raised * (1.0 / jnp.sum(raised, axis=-1, keepdims=True))
            probs = probs.astype(BF)
            probs_ref[0, i] = probs
            mixed_ref[i * length : (i + 1) * length, span(head, SIZE)] = dot(probs, v).astype(BF)

        @pl.when(head == GROUP - 1)
        def _():
            keep.wait()

    return call(
        kernel,
        meta,
        [(first, None), (small, None)] + [(p, ANY) for p in parts],
        [
            (HBM((rows, GROUP * n), BF), pl.BlockSpec((rows, n), lambda h, m: (0, h))),
            (
                HBM((GROUP, images, length, length), BF),
                pl.BlockSpec((1, images, length, length), lambda h, m: (h, 0, 0, 0)),
            ),
            (VMEM((rows, GROUP * SIZE), BF), None),
            (HBM((width, GROUP * n), BF), ANY),
        ],
        20,
        cost(
            2 * rows * width * GROUP * n * 2 + 8 * rows * length * SIZE * GROUP,
            2 * (rows * width + width * n * GROUP * 2 + rows * n * GROUP + GROUP * rows * length),
            GROUP * rows * length,
        ),
        "attention_forward",
        [pltpu.VMEM((width, GROUP * n), BF), pltpu.SemaphoreType.DMA((2,))],
        (GROUP,),
    )


def store_piece(owner, odd, piece_ref, at, values, y):
    rows = values.shape[0] // 8
    for z in range(4):
        for x in range(2):
            plain = owner == (1 if odd else 0)
            first = jnp.where(plain, x, y)
            second = jnp.where(plain, y, x)
            start = (z * 2 + x) * rows
            for j in range(values.shape[1] // 128):
                part = values[start : start + rows, j * 128 : (j + 1) * 128]
                piece_ref[first, second, z, at + j] = part.astype(BF)


def blocks(rows):
    size = min(256, rows)

    def over(body):
        pl.loop(0, rows // size)(lambda i: body(span(i, size)))

    return over


def feed_forward_first(meta, x, small, mixed, parts):
    rows, width = x.shape
    parts, starts = zip(*parts)
    count = len(parts)

    def kernel(meta, x_ref, small_ref, *refs):
        mixed_refs, parts = refs[: len(mixed)], refs[len(mixed) : len(mixed) + count]
        middle_ref, second_ref, active_ref, slope_ref, whole, sems = refs[len(mixed) + count :]
        for j in range(2):
            fetch(meta, parts, starts, whole, (j * width, width), sems.at[j])

        def row(r):
            return small_ref[r : r + 1, :]

        fetched(whole, (0, width), sems.at[0])
        fetched(whole, (width, width), sems.at[1])

        @blocks(rows)
        def _(here):
            values = jnp.concatenate([r[here, :] for r in mixed_refs], axis=1)
            middle = x_ref[here, :].astype(F32) + dot(values, whole[:, :width]) + row(BO)
            middle_ref[here, :] = middle
            normed, _ = normed_rows(middle)
            second = (normed * row(G2) + row(B2)).astype(BF)
            second_ref[here, :] = second
            v = dot(second, whole[:, width:]) + row(BU)
            square = v * v
            tanh = jnp.tanh(GELU * v * (1.0 + CUBIC * square))
            half = 0.5 * (1.0 + tanh)
            active_ref[here, :] = (v * half).astype(BF)
            slope = (0.5 * v) * (1.0 - tanh * tanh) * (GELU * (1.0 + (3 * CUBIC) * square))
            slope_ref[here, :] = (half + slope).astype(BF)

    return call(
        kernel,
        meta,
        [(x, None), (small, None)] + [(a, None) for a in mixed] + [(p, ANY) for p in parts],
        [
            (VMEM((rows, width), F32), None),
            (VMEM((rows, width), BF), None),
            (VMEM((rows, width), BF), None),
            (VMEM((rows, width), BF), None),
        ],
        24,
        cost(4 * rows * width * width, 2 * 9 * rows * width, rows * width),
        "feed_forward_first",
        [pltpu.VMEM((width, 2 * width), BF), pltpu.SemaphoreType.DMA((2,))],
    )


def store_grads(meta, pieces, m, left, right_ref, odd):
    q = right_ref.shape[1] // 4

    @pl.loop(0, 4)
    def _(j):
        core, y = j // 2, j % 2
        values = dot(left, right_ref[:, span(j, q)], TN).astype(BF)
        for piece_ref, half in zip(pieces, (THEIRS, OURS)):

            @pl.when(core == meta[half])
            def _(piece_ref=piece_ref):
                store_piece(core, odd, piece_ref, 2 * m, values, y)


def feed_forward_second(meta, cot, small, middle, second, active, slope, parts):
    rows, width = cot.shape
    parts, starts = zip(*parts)
    count = len(parts)

    def kernel(meta, cot_ref, small_ref, middle_ref, second_ref, active_ref, slope_ref, *refs):
        parts, refs = refs[:count], refs[count:]
        out_ref, hidden_ref, *pieces, sums_ref, whole, out, sems = refs
        fetch(meta, parts, starts, whole, (0, width), sems.at[0])
        store_grads(meta, pieces, 0, active_ref[...], cot_ref, False)
        fetched(whole, (0, width), sems.at[0])

        @blocks(rows)
        def _(here):
            grad = dot(cot_ref[here, :], whole[...], NT)
            hidden_ref[here, :] = (slope_ref[here, :].astype(F32) * grad).astype(BF)

        @blocks(rows)
        def _(here):
            values = middle_ref[here, :] + dot(active_ref[here, :], whole[...])
            out[here, :] = (values + small_ref[BD : BD + 1, :]).astype(BF)

        write = pltpu.make_async_copy(out, out_ref, sems.at[1])
        write.start()
        store_grads(meta, pieces, 1, second_ref[...], hidden_ref, False)
        sums_ref[...] = jnp.zeros_like(sums_ref)
        sums_ref[0:1, :] = column_sum(hidden_ref[...])
        sums_ref[1:2, :] = column_sum(cot_ref[...])
        write.wait()

    piece = VMEM((2, 2, 4, 4, width // 8, 128), BF)
    return call(
        kernel,
        meta,
        [(a, None) for a in (cot, small, middle, second, active, slope)]
        + [(p, ANY) for p in parts],
        [
            (HBM((rows, width), BF), ANY),
            (VMEM((rows, width), BF), None),
            (piece, None),
            (piece, None),
            (shaped(F32, 8, width), None),
        ],
        24,
        cost(8 * rows * width * width, 2 * 12 * rows * width),
        "feed_forward_second",
        [
            pltpu.VMEM((width, width), BF),
            pltpu.VMEM((rows, width), BF),
            pltpu.SemaphoreType.DMA((2,)),
        ],
    )


def feed_forward_third(meta, cot, small, middle, mixed, hidden, parts):
    rows, width = cot.shape
    parts, starts = zip(*parts)
    count = len(parts)

    def kernel(meta, cot_ref, small_ref, middle_ref, hidden_ref, *refs):
        mixed_refs, parts = refs[: len(mixed)], refs[len(mixed) : len(mixed) + count]
        attn_ref, *pieces, sums_ref, whole, sem = refs[len(mixed) + count :]
        fetch(meta, parts, starts, whole, (0, width), sem, width)
        fetched(whole, (0, width), sem)
        sums_ref[...] = jnp.zeros_like(sums_ref)

        @blocks(rows)
        def _(here):
            grad_second = dot(hidden_ref[here, :], whole[...], NT)
            normed, scale = normed_rows(middle_ref[here, :])
            back = norm_back(grad_second * small_ref[G2 : G2 + 1, :], normed, scale)
            grad_attn = (cot_ref[here, :].astype(F32) + back).astype(BF)
            attn_ref[here, :] = grad_attn
            sums_ref[0:1, :] += column_sum(grad_second * normed)
            sums_ref[1:2, :] += column_sum(grad_second)
            sums_ref[2:3, :] += column_sum(grad_attn)

        values = jnp.concatenate([r[...] for r in mixed_refs], axis=1)
        store_grads(meta, pieces, 0, values, attn_ref, True)

    piece = VMEM((2, 2, 4, 2, width // 8, 128), BF)
    return call(
        kernel,
        meta,
        [(a, None) for a in (cot, small, middle, hidden, *mixed)] + [(p, ANY) for p in parts],
        [(VMEM((rows, width), BF), None), (piece, None), (piece, None), (shaped(F32, 8, width), None)],
        20,
        cost(4 * rows * width * width, 2 * 12 * rows * width),
        "feed_forward_third",
        [pltpu.VMEM((width, width), BF), pltpu.SemaphoreType.DMA],
    )


def mixed_grad(meta, grad_attn, parts):
    rows, width = grad_attn.shape
    parts, starts = zip(*parts)
    count = len(parts)

    def kernel(meta, attn_ref, *refs):
        parts, (grad_ref, attn_out, whole, sems) = refs[:count], refs[count:]
        write = pltpu.make_async_copy(attn_ref, attn_out, sems.at[1])
        write.start()
        fetch(meta, parts, starts, whole, (0, width), sems.at[0])
        fetched(whole, (0, width), sems.at[0])

        @blocks(rows)
        def _(here):
            grad_ref[here, :] = dot(attn_ref[here, :], whole[...], NT).astype(BF)

        write.wait()

    return call(
        kernel,
        meta,
        [(grad_attn, None)] + [(p, ANY) for p in parts],
        [(VMEM((rows, width), BF), None), (HBM((rows, width), BF), ANY)],
        16,
        cost(2 * rows * width * width, 2 * 4 * rows * width),
        "mixed_grad",
        [pltpu.VMEM((width, width), BF), pltpu.SemaphoreType.DMA((2,))],
    )


def attention_backward(meta, first, packed, probs, grad_mixed, mixed, base, half, images, odd):
    rows, width = first.shape
    length, n = rows // images, 3 * SIZE
    pair = GROUP // 2

    def kernel(
        meta, first_ref, packed_ref, probs_ref, grad_ref, mixed_ref, grad_packed_ref, piece_ref
    ):
        j = pl.program_id(0)
        head = meta[half] * pair + j

        @pl.loop(0, images)
        def _(i):
            here = span(i, length)
            packed = packed_ref[here, :]
            q, k, v = packed[:, :SIZE], packed[:, SIZE : 2 * SIZE], packed[:, 2 * SIZE :]
            grad = grad_ref[here, span(base + head, SIZE)]
            mixed = mixed_ref[here, span(head, SIZE)]
            inner = jnp.sum(grad.astype(F32) * mixed.astype(F32), axis=-1, keepdims=True)
            probs = probs_ref[0, i]
            grad_v = dot(probs, grad, TN)
            grad_scores = (probs.astype(F32) * (dot(grad, v, NT) - inner)).astype(BF)
            grad_q = dot(grad_scores, k) * SCALE
            grad_k = dot(grad_scores, q, TN) * SCALE
            grad_packed_ref[here, :] = jnp.concatenate(
                [grad_q.astype(BF), grad_k.astype(BF), grad_v.astype(BF)], axis=1
            )

        values = dot(first_ref[...], grad_packed_ref[...], TN)
        store_piece(meta[half], odd, piece_ref, 0, values, j)

    return call(
        kernel,
        meta,
        [
            (first, None),
            (hbm(packed), pl.BlockSpec((rows, n), lambda j, m: (0, m[half] * pair + j))),
            (
                hbm(probs),
                pl.BlockSpec(
                    (1, images, length, length), lambda j, m: (m[half] * pair + j, 0, 0, 0)
                ),
            ),
            (grad_mixed, None),
            (mixed, None),
        ],
        [
            (HBM((rows, pair * n), BF), pl.BlockSpec((rows, n), lambda j, m: (0, j))),
            (VMEM((2, 2, 4, 3, width // 8, SIZE), BF), None),
        ],
        20,
        cost(
            pair * (2 * rows * width * n * 1.5 + 10 * rows * length * SIZE * 1.5),
            2 * (rows * width + pair * (rows * length + 3 * rows * n)),
        ),
        "attention_backward",
        grid=(pair,),
    )


def input_grad(meta, x, grad_attn, small, pieces, weights):
    rows, width = x.shape
    tm = min(256, rows)
    groups = len(weights)
    n = pieces[0].shape[1]

    def kernel(meta, x_ref, grad_ref, small_ref, *refs):
        pieces, weights = refs[: 2 * groups], refs[2 * groups : 3 * groups]
        out_ref, sums_ref, packed_sums_ref = refs[3 * groups :]

        @pl.when(pl.program_id(0) == 0)
        def _():
            sums_ref[...] = jnp.zeros_like(sums_ref)
            packed_sums_ref[...] = jnp.zeros_like(packed_sums_ref)

        grad = None
        for g in range(groups):
            for j, which in enumerate((THEIRS, OURS)):
                piece = pieces[2 * g + j][...]
                term = dot(piece, weights[g][:, span(meta[which], n)], NT)
                grad = term if grad is None else grad + term
                packed_sums_ref[0:1, span(2 * g + meta[which], n)] += column_sum(piece)
        normed, scale = normed_rows(x_ref[...].astype(F32))
        back = norm_back(grad * small_ref[G1 : G1 + 1, :], normed, scale)
        out_ref[...] = (grad_ref[...].astype(F32) + back).astype(BF)
        sums_ref[0:1, :] += column_sum(grad * normed)
        sums_ref[1:2, :] += column_sum(grad)

    block = pl.BlockSpec((tm, width), lambda i, m: (i, 0))
    return call(
        kernel,
        meta,
        [(hbm(x), block), (hbm(grad_attn), block), (small, None)]
        + [(hbm(p), pl.BlockSpec((tm, n), lambda i, m: (i, 0))) for p in pieces]
        + [(w, None) for w in weights],
        [
            (HBM((rows, width), BF), block),
            (shaped(F32, 8, width), None),
            (shaped(F32, 8, 3 * width), None),
        ],
        24,
        cost(6 * rows * width * width * 1.3, 2 * 9 * rows * width),
        "input_grad",
        grid=(rows // tm,),
    )


def quarter_of(meta, i):
    return (meta[CORE] ^ (i % 2)) * 2 + (meta[YPOS] ^ (i // 2))


def finish(meta, groups, places, widths, name):
    quarters = [q for group in groups for q in group]
    rows = quarters[0].shape[1]

    def kernel(meta, *refs):
        outs = refs[len(quarters) :]
        for g, place in enumerate(places):
            for i in range(4):
                part = refs[4 * g + i]
                for j in range(min(part.shape[0], len(widths) * widths[0] // 128 // 4 // len(groups))):
                    which, column = place(quarter_of(meta, i), j)
                    outs[which][:, span(column, 128)] = part[j].astype(F32)

    outs = [(shaped(F32, rows, n), None) for n in widths]
    return call(kernel, meta, [(a, None) for a in quarters], outs, 8, cost(1, 1), name)


def by_head(weight, base):
    rows = weight.shape[0]
    view = weight.reshape(rows, 3, HEADS, SIZE)[:, :, base : base + GROUP]
    return view.transpose(0, 2, 1, 3).reshape(rows, GROUP * 3 * SIZE)


def per_device(latents, w_qkv, w_out, w_up, w_down, gains, biases, ff_bias, cotangent, *, nb, nr):
    reps, images, length, width = latents.shape
    x = latents.reshape(-1, width)
    cot = cotangent.reshape(-1, width)
    count = reps * images
    bases = range(0, HEADS, GROUP)
    native = nb != 8 or nr != 4
    small = jnp.concatenate([gains, biases, ff_bias[None]], axis=0)
    small = jnp.pad(small, ((0, 16 - small.shape[0]), (0, 0)))
    if native:
        links = None
        zero = jnp.zeros((), jnp.int32)
        meta = jnp.stack([zero, zero, zero, zero, zero + 1, zero, zero, zero])

        def whole(w):
            return [(lax.all_gather(w, "batch", axis=0, tiled=True), 0)]

        table = lax.all_gather(small, "batch", axis=1, tiled=True)
        table = table.reshape(16, 4, 2, width // 8).transpose(2, 1, 0, 3)
        first, small = first_norm(meta, x, [table[0], table[1], table[1]])
        chunks = [whole(by_head(w_qkv, base)) for base in bases]
        chunks += [whole(jnp.concatenate([w_out, w_up], axis=1)), whole(w_down)]
    else:
        links = Links(nb, nr)
        mine_f = jnp.where(links.ci == 0, links.xi, links.yi)
        mine_s = jnp.where(links.ci == 0, links.yi, links.xi)
        meta = [links.ci, links.yi, links.xi, links.zi, 1 - links.ci, links.ci, mine_f, mine_s]
        meta = jnp.stack(meta).astype(jnp.int32)

        def quarter(w):
            rows = w.shape[0] // 4
            return lax.dynamic_slice_in_dim(w, (links.ci * 2 + links.yi) * rows, rows, 0)

        w_qkv = quarter(w_qkv)
        chunks = [by_head(w_qkv, base) for base in bases]
        extra = jnp.pad(small, ((0, w_qkv.shape[0] - 16), (0, 0)))
        chunks[0] = jnp.concatenate([chunks[0], extra], axis=1)
        chunks += [jnp.concatenate([quarter(w_out), quarter(w_up)], axis=1), quarter(w_down)]
        kept = []

        def norm(tables):
            kept.extend(first_norm(meta, x, tables))
            return kept

        chunks = gather_chunks(chunks, links, norm)
        first, small = kept
        other = CoreSwap(links)

    packed, probs, mixed, weights = [], [], [], []
    for base, parts in zip(bases, chunks):
        parts = parts if native else other(parts, *mixed)
        a, b, c, d = attention_forward(meta, first, small, parts, base, count)
        packed.append(a)
        probs.append(b)
        mixed.append(c)
        weights.append(d)
    outer, inner = chunks[len(bases) :]
    outer = outer if native else other(outer, mixed[0])
    middle, second, active, slope = feed_forward_first(meta, x, small, mixed, outer)
    inner = inner if native else other(inner, mixed[1])
    out, hidden, send, keep, sums_two = feed_forward_second(
        meta, cot, small, middle, second, active, slope, inner
    )
    grad_attn, send_out, keep_out, sums_three = feed_forward_third(
        meta, cot, small, middle, mixed, hidden, outer
    )

    def backward(meta, g, half):
        return attention_backward(
            meta, first, packed[g], probs[g], grad_mixed, mixed[g], bases[g], half, count, g == 1
        )

    def collect(sums_one, sums_packed):
        sums_packed = sums_packed[0].reshape(HEADS, 3, SIZE)
        sums_q, sums_v = sums_packed[:, 0].reshape(width), sums_packed[:, 2].reshape(width)
        out, two, three = sums_three[2], sums_two, sums_three
        rows = [sums_one[0], three[0], sums_one[1], sums_q, sums_v, out, three[1], two[1], two[0]]
        return jnp.stack(rows)

    def sums_of(sums_one, sums_packed):
        two, three, one, packed = sums_two, sums_three, sums_one, sums_packed
        plain = [(one, 0), (three, 0), (one, 1), None, None, (three, 2), (three, 1), (two, 1), (two, 0)]
        sums = [entry and (*entry, 1, 0) for entry in plain]
        sums[3], sums[4] = (packed, 0, 3, 0), (packed, 0, 3, 2)
        return sums

    def result(grad_x, grads, smalls):
        return (
            out.reshape(latents.shape),
            grad_x.reshape(latents.shape),
            *grads,
            smalls[:2],
            smalls[2:8],
            smalls[8],
        )

    if native:
        grad_mixed, grad_attn = mixed_grad(meta, grad_attn, outer)
        halves = [[backward(meta, g, half) for half in (THEIRS, OURS)] for g in range(len(bases))]
        pieces = [half[0] for pair in halves for half in pair]
        grad_x, sums_one, sums_packed = input_grad(meta, x, grad_attn, small, pieces, weights)
        smalls = lax.psum_scatter(
            collect(sums_one, sums_packed), "batch", scatter_dimension=1, tiled=True
        )
        smalls = lax.psum(smalls, "rep")

        def reduced(send, keep, odd):
            keep, send = (jnp.swapaxes(keep, 0, 1), send) if odd else (keep, jnp.swapaxes(send, 0, 1))
            both = jnp.stack([keep, send])
            t = both.shape[4]
            both = both.transpose(3, 1, 5, 0, 2, 4, 6).reshape(width, t * 4 * 128)
            both = lax.psum_scatter(both, "batch", scatter_dimension=0, tiled=True)
            both = lax.psum(both.astype(BF), "rep").astype(F32)
            return both.reshape(-1, 4, t, 128)

        rest = [reduced(send_out, keep_out, True), reduced(send, keep, False)]
        rows = rest[0].shape[0]
        rest = [rest[0], rest[1][:, :, 2:], rest[1][:, :, :2]]
        rest = [g.reshape(rows, width) for g in rest]
        heads = [reduced(pair[0][1], pair[1][1], g == 1) for g, pair in enumerate(halves)]
        heads = jnp.concatenate(heads, axis=1).transpose(0, 2, 1, 3).reshape(rows, 3 * width)
        return result(grad_x, [heads, *rest], smalls)

    def to_core(value):
        return move(value, links.core)

    def along(arrays):
        return [arrays[0]] + [move(a, p) for a, p in zip(arrays[1:], links.z)]

    def share(value):
        return [value] + [move(value, p) for p in links.rep]

    both = Piece(keep, to_core(send), False)
    step = Step()
    step.swap(firsts=[both])
    (sent,) = step.run(after(meta, keep_out), "step_0")
    both.late.append((move(sent, links.x_or_y), 0))
    grad_mixed, grad_attn = mixed_grad(after(meta, sent), grad_attn, outer)
    packed_1, send_1 = backward(after(meta, sent), 0, THEIRS)

    outs = Piece(keep_out, to_core(send_out), True)
    step = Step()
    step.swap(firsts=[outs], seconds=[both])
    (sent,) = step.run(after(meta, send_1), "step_1")
    moved = move(sent, links.y_or_x)
    for piece in (outs, both):
        piece.late.append((moved, piece.next))
    packed_2, keep_1 = backward(after(meta, sent), 0, OURS)
    packed_3, send_2 = backward(after(meta, sent, keep_1), 1, THEIRS)

    one = Piece(keep_1, to_core(send_1), False)
    step = Step()
    step.swap(firsts=[one], seconds=[outs])
    step.along(both)
    sent, *z_both = step.run(after(meta, send_2), "step_2")
    moved = move(sent, links.x_or_y)
    for piece in (one, outs):
        piece.late.append((moved, piece.next))
    z_both = along(z_both)
    packed_4, keep_2 = backward(after(meta, sent), 1, OURS)

    two = Piece(keep_2, to_core(send_2), True)
    step = Step()
    step.swap(firsts=[two], seconds=[one])
    step.along(outs)
    sent, *z_outs = step.run(after(meta, keep_2, *z_both[1:]), "step_3")
    moved = move(sent, links.y_or_x)
    for piece in (two, one):
        piece.late.append((moved, piece.next))
    z_outs = along(z_outs)
    pieces = [packed_1, packed_2, packed_3, packed_4]
    grad_x, sums_one, sums_packed = input_grad(
        after(meta, sent), x, grad_attn, small, pieces, weights
    )

    step = Step()
    step.swap(seconds=[two])
    step.along(one, sums_of(sums_one, sums_packed))
    step.share([z_both, z_outs])
    sent, *z_one, r_rest = step.run(after(meta, grad_x), "step_4")
    two.late.append((move(sent, links.x_or_y), 0))
    z_one, r_rest = along(z_one), share(r_rest)

    step = Step()
    step.along(two)
    step.share([z_one])
    *z_two, r_one = step.run(meta, "step_5")
    z_two, r_one = along(z_two), share(r_one)

    step = Step()
    step.share([z_two])
    step.small(r_one)
    r_two, other, smalls = step.run(meta, "step_6")
    smalls = smalls + move(other, links.x)
    rest = finish(
        after(meta, r_two),
        [r_rest],
        [lambda q, j: (2 - j // 2, q * 2 + j % 2)],
        [width] * 3,
        "finish_rest",
    )
    (heads,) = finish(
        meta,
        [r_one, share(r_two)],
        [lambda q, j: (0, j * HEADS + q), lambda q, j: (0, j * HEADS + GROUP + q)],
        [3 * width],
        "finish_heads",
    )
    return result(grad_x, [heads, *rest], smalls)


def solution(mesh):
    nb, nr = mesh.shape["batch"], mesh.shape["rep"]

    def body(*args):
        return per_device(*args, nb=nb, nr=nr)

    rows = P("batch", None)
    cols = P(None, "batch")
    data = P("rep", "batch", None, None)
    return jax.shard_map(
        body,
        mesh=mesh,
        in_specs=(data, rows, rows, rows, rows, cols, cols, P("batch"), data),
        out_specs=(data, data, rows, rows, rows, rows, cols, cols, P("batch")),
        check_vma=False,
    )
```

time: 659 us -> 264 us (0.40); the launches traced: 650 us -> 264 us
  other arithmetic: 143 us -> 1.13 us
  local copies, waits for them, and re-layouts: 144 us -> 4.99 us
  Pallas kernels: 0 us -> 134 us
  matrix products: 119 us -> 0 us
  waiting for transfers between devices: 143 us -> 61.2 us
  blocking collectives: 45.8 us -> 0 us
  starting transfers between devices: 40.6 us -> 61.6 us
  between operations: 15.4 us -> 1.12 us
    pallas_call x0 -> x21, Pallas kernels: none -> 134 us  [call(): pl.pallas_call(kernel, out_shape=shapes, grid_spec=pltpu.PrefetchScalarGr...]
    dot_general x18 -> x0, matrix products: 119 us -> none  [the longest x12 71.4 us: dot(): return lax.dot_general(a, b, (dims, ((), ())), preferred_element_type=F32)]
    psum x1 -> x0, waiting for transfers between devices: 58.8 us -> none  [per_device(): smalls = lax.psum(smalls, AXES)]
    select_n x14 -> x0, other arithmetic: 53 us -> none  [the longest x12 49 us: flip_if(): return jnp.where(bit == 1, jnp.flip(value, axis), value)]
    unnamed x105 -> x14, local copies, waits for them, and re-layouts: 49.5 us -> 1.16 us
    all_gather x1 -> x0, blocking collectives: 45.8 us -> none  [per_device(): small = lax.all_gather(small, 'batch', axis=1, tiled=True)]
    convert_element_type x12 -> x0, local copies, waits for them, and re-layouts: 32.9 us -> none  [the longest x2 19.5 us: per_device(): jnp.stack([g_q, g_k, g_v], axis=2).astype(BF).reshape(-1, 3 * width)]
    ppermute x38 -> x65, waiting for transfers between devices: 83.7 us -> 61.2 us  [move(): return lax.ppermute(value, AXES, pairs)]
  transfers between devices with their start and end apart: 39 -> 65, of which waited for: 13 -> 20; matrix products, arithmetic and copies ran while one was open for 23% -> 1% of each run, Pallas kernels for 0% -> 39%
where the time goes in v2:
time: 264 us
  Pallas kernels  134 us (51%)
  starting transfers between devices  61.6 us (23%)
  waiting for transfers between devices  61.2 us (23%)
  local copies, waits for them, and re-layouts  4.99 us (2%)
    pallas_call x21, Pallas kernels, call(): pl.pallas_call(kernel, out_shape=shapes, grid_spec=pltpu.PrefetchScalarGr...  134 us
    ppermute x65, starting transfers between devices, move(): return lax.ppermute(value, AXES, pairs)  61.6 us
    ppermute x65, waiting for transfers between devices, move(): return lax.ppermute(value, AXES, pairs)  61.2 us
  transfers between devices with their start and end apart: 65, of which 20 were waited for; matrix products, arithmetic and copies ran while one was open for 1% of the time, Pallas kernels for 39%

profile of v2, /device:TPU:0, one launch (start us, length us, event | category | flops | bytes accessed | tf_op | source)
XLA Modules:
  0.0 264.1 jit_solution(5920091135097718375)
XLA Ops:
  2.8 5.1 %collective-permute-start.2 = (bf16[32,1664]{1,0:T(8,128)(2,1)S(1)}, bf16[32,1664]{1,0:T(8,128)(2,1)S(1)}, u32[]{:S(2)}, u32[]{:S(2)}) collective-permute-start(bf16[32,1664]{1,0:T(8,128)(2,1)S(1)} %fusion.1), channel_id=1, source_target_pairs={{0,24},{1,25},{2,26},{3,27},{4,28},{5,29},{6,30},{7,31},{8,16},{9,... | collective-permute-start | bytes 319496 | tf_op jit(solution)/shard_map/ppermute | solution.py:104
  8.5 3.3 %collective-permute-done.2 = bf16[32,1664]{1,0:T(8,128)(2,1)S(1)} collective-permute-done((bf16[32,1664]{1,0:T(8,128)(2,1)S(1)}, bf16[32,1664]{1,0:T(8,128)(2,1)S(1)}, u32[]{:S(2)}, u32[]{:S(2)}) %collective-permute-start.2) | collective-permute-done | bytes 106528 | tf_op jit(solution)/shard_map/ppermute | solution.py:104
  11.8 5.1 %collective-permute-done.1 = bf16[32,1664]{1,0:T(8,128)(2,1)S(1)} collective-permute-done((bf16[32,1664]{1,0:T(8,128)(2,1)S(1)}, bf16[32,1664]{1,0:T(8,128)(2,1)S(1)}, u32[]{:S(2)}, u32[]{:S(2)}) %collective-permute-start.1) | collective-permute-done | bytes 106528 | tf_op jit(solution)/shard_map/ppermute | solution.py:104
  16.9 1.6 collective-permute-start.4
  20.2 2.5 collective-permute-start.7
  22.7 1.9 collective-permute-start.5
  24.7 2.8 %collective-permute-done.7 = bf16[32,1536]{1,0:T(8,128)(2,1)S(1)} collective-permute-done((bf16[32,1536]{1,0:T(8,128)(2,1)S(1)}, bf16[32,1536]{1,0:T(8,128)(2,1)S(1)}, u32[]{:S(2)}, u32[]{:S(2)}) %collective-permute-start.7) | collective-permute-done | bytes 98336 | tf_op jit(solution)/shard_map/ppermute | solution.py:104
  27.5 3.1 %collective-permute-done.6 = bf16[32,1536]{1,0:T(8,128)(2,1)S(1)} collective-permute-done((bf16[32,1536]{1,0:T(8,128)(2,1)S(1)}, bf16[32,1536]{1,0:T(8,128)(2,1)S(1)}, u32[]{:S(2)}, u32[]{:S(2)}) %collective-permute-start.6) | collective-permute-done | bytes 98336 | tf_op jit(solution)/shard_map/ppermute | solution.py:104
  30.7 3.1 %first_norm.1 = (bf16[1024,1024]{1,0:T(8,128)(2,1)S(1)}, f32[16,1024]{1,0:T(8,128)S(1)}) custom-call(s32[8]{0:T(128)S(1)} %stack.92.meta, bf16[1024,1024]{1,0:T(8,128)(2,1)S(1)} %bitcast.39, bf16[4,32,1664]{2,1,0:T(8,128)(2,1)S(1)} %pad_maximum_fusion.4.own_ref.refs_0_, bf16[4,32,1664]{2,1,0:T(8,128)(2,1)S(1)} %collective-permute-done.3.one_ref.refs_1_, ...), custom_call_target="tpu_custom_call" | custom-call | flops 1 | bytes 1 | tf_op jit(solution)/shard_map/first_norm/pallas_call | solution.py:36
  35.9 2.0 collective-permute-start.16
  37.9 2.5 collective-permute-start.14
  40.4 3.8 %collective-permute-done.16 = bf16[32,2048]{1,0:T(8,128)(2,1)S(1)} collective-permute-done((bf16[32,2048]{1,0:T(8,128)(2,1)S(1)}, bf16[32,2048]{1,0:T(8,128)(2,1)S(1)}, u32[]{:S(2)}, u32[]{:S(2)}) %collective-permute-start.16) | collective-permute-done | bytes 131104 | tf_op jit(solution)/shard_map/ppermute | solution.py:104
  44.2 4.3 %collective-permute-done.15 = bf16[32,2048]{1,0:T(8,128)(2,1)S(1)} collective-permute-done((bf16[32,2048]{1,0:T(8,128)(2,1)S(1)}, bf16[32,2048]{1,0:T(8,128)(2,1)S(1)}, u32[]{:S(2)}, u32[]{:S(2)}) %collective-permute-start.15) | collective-permute-done | bytes 131104 | tf_op jit(solution)/shard_map/ppermute | solution.py:104
  52.5 1.9 collective-permute-start.24
  54.4 2.5 collective-permute-start.22
  56.9 2.2 collective-permute-done.24
  61.0 6.1 %collective-permute-done.17.refs_3_.refs_4_.refs_2_ = bf16[4,32,3584]{2,1,0:T(8,128)(2,1)S(1)} collective-permute-done((bf16[4,32,3584]{2,1,0:T(8,128)(2,1)S(1)}, bf16[4,32,3584]{2,1,0:T(8,128)(2,1)S(1)}, u32[]{:S(2)}, u32[]{:S(2)}) %collective-permute-start.17) | collective-permute-done | bytes 917536 | tf_op jit(solution)/shard_map/ppermute | solution.py:104
  67.2 1.5 collective-permute-start.25
  68.9 12.9 %attention_forward.2 = (bf16[1024,1536]{1,0:T(8,128)(2,1)}, bf16[4,2,512,512]{3,2,1,0:T(8,128)(2,1)}, bf16[1024,512]{1,0:T(8,128)(2,1)S(1)}, bf16[1024,1536]{1,0:T(8,128)(2,1)}) custom-call(s32[8]{0:T(128)S(1)} %stack.92.meta, bf16[1024,1024]{1,0:T(8,128)(2,1)S(1)} %get-tuple-element.99.first_ref, f32[16,1024]{1,0:T(8,128)S(1)} %get-tuple-element.98.small_ref, ...), custom_call_target="tpu_custom_call" | custom-call | flops 1 | bytes 1 | tf_op jit(solution)/shard_map/attention_forward/pallas_call | solution.py:36
  84.1 4.3 %collective-permute-done.29.refs_1_ = bf16[4,32,1024]{2,1,0:T(8,128)(2,1)S(1)} collective-permute-done((bf16[4,32,1024]{2,1,0:T(8,128)(2,1)S(1)}, bf16[4,32,1024]{2,1,0:T(8,128)(2,1)S(1)}, u32[]{:S(2)}, u32[]{:S(2)}) %collective-permute-start.29) | collective-permute-done | bytes 262176 | tf_op jit(solution)/shard_map/ppermute | solution.py:104
  90.2 14.7 %attention_forward.3 = (bf16[1024,1536]{1,0:T(8,128)(2,1)}, bf16[4,2,512,512]{3,2,1,0:T(8,128)(2,1)}, bf16[1024,512]{1,0:T(8,128)(2,1)S(1)}, bf16[1024,1536]{1,0:T(8,128)(2,1)}) custom-call(s32[8]{0:T(128)S(1)} %stack.92.meta, bf16[1024,1024]{1,0:T(8,128)(2,1)S(1)} %get-tuple-element.99.first_ref, f32[16,1024]{1,0:T(8,128)S(1)} %get-tuple-element.98.small_ref, ...), custom_call_target="tpu_custom_call" | custom-call | flops 1 | bytes 1 | tf_op jit(solution)/shard_map/attention_forward/pallas_call | solution.py:36
  105.8 11.2 %feed_forward_first.1 = (f32[1024,1024]{1,0:T(8,128)S(1)}, bf16[1024,1024]{1,0:T(8,128)(2,1)S(1)}, bf16[1024,1024]{1,0:T(8,128)(2,1)S(1)}, bf16[1024,1024]{1,0:T(8,128)(2,1)S(1)}) custom-call(s32[8]{0:T(128)S(1)} %stack.92.meta, bf16[1024,1024]{1,0:T(8,128)(2,1)S(1)} %bitcast.40, f32[16,1024]{1,0:T(8,128)S(1)} %get-tuple-element.98.small_ref, ...), custom_call_target="tpu_custom_call" | custom-call | flops 1 | bytes 1 | tf_op jit(solution)/shard_map/feed_forward_first/pallas_call | solution.py:36
  117.0 17.2 %feed_forward_second.1 = (bf16[1024,1024]{1,0:T(8,128)(2,1)}, bf16[1024,1024]{1,0:T(8,128)(2,1)S(1)}, bf16[2,2,4,4,128,128]{5,4,3,2,1,0:T(8,128)(2,1)S(1)}, bf16...) custom-call(s32[8]{0:T(128)S(1)} %stack.92.meta, bf16[1024,1024]{1,0:T(8,128)(2,1)S(1)} %bitcast.41, ...), custom_call_target="tpu_custom_call" | custom-call | flops 1 | bytes 1 | tf_op jit(solution)/shard_map/feed_forward_second/pallas_call | solution.py:36
  134.6 10.4 %feed_forward_third.1 = (bf16[1024,1024]{1,0:T(8,128)(2,1)S(1)}, bf16[2,2,4,2,128,128]{5,4,3,2,1,0:T(8,128)(2,1)S(1)}, bf16[2,2,4,2,128,128]{5,4,3,2,1,0:T(8,128)(2,1)S(1)}, f32[8,1024]{1,0:T(8,128)S(1)}) custom-call(s32[8]{0:T(128)S(1)} %stack.92.meta, bf16[1024,1024]{1,0:T(8,128)(2,1)S(1)} %bitcast.42, f32[16,1024]{1,0:T(8,128)S(1)} %get-tuple-element.98.small_ref, ...), custom_call_target="tpu_custom_call" | custom-call | flops 1 | bytes 1 | tf_op jit(solution)/shard_map/feed_forward_third/pallas_call | solution.py:36
  146.9 4.5 %mixed_grad.1 = (bf16[1024,1024]{1,0:T(8,128)(2,1)S(1)}, bf16[1024,1024]{1,0:T(8,128)(2,1)}) custom-call(s32[8]{0:T(128)S(1)} %stack.92.meta, bf16[1024,1024]{1,0:T(8,128)(2,1)S(1)} %get-tuple-element.130.attn_ref, bf16[4,32,2048]{2,1,0:T(8,128)(2,1)S(1)} %pad_maximum_fusion.3.refs_2_.refs_0_, ...), custom_call_target="tpu_custom_call" | custom-call | flops 1 | bytes 1 | tf_op jit(solution)/shard_map/mixed_grad/pallas_call | solution.py:36
  151.4 7.7 %attention_backward.4 = (bf16[1024,768]{1,0:T(8,128)(2,1)}, bf16[2,2,4,3,128,128]{5,4,3,2,1,0:T(8,128)(2,1)S(1)}) custom-call(s32[8]{0:T(128)S(1)} %stack.92.meta, bf16[1024,1024]{1,0:T(8,128)(2,1)S(1)} %get-tuple-element.99.first_ref, bf16[1024,1536]{1,0:T(8,128)(2,1)} %get-tuple-element.128.packed_ref, ...), custom_call_target="tpu_custom_call" | custom-call | flops 1 | bytes 1 | tf_op jit(solution)/shard_map/attention_backward/pallas_call | solution.py:36
  159.1 2.0 collective-permute-done.35.refs_2_.refs_7_
  162.8 7.7 %attention_backward.5 = (bf16[1024,768]{1,0:T(8,128)(2,1)}, bf16[2,2,4,3,128,128]{5,4,3,2,1,0:T(8,128)(2,1)S(1)}) custom-call(s32[8]{0:T(128)S(1)} %stack.92.meta, bf16[1024,1024]{1,0:T(8,128)(2,1)S(1)} %get-tuple-element.99.first_ref, bf16[1024,1536]{1,0:T(8,128)(2,1)} %get-tuple-element.128.packed_ref, ...), custom_call_target="tpu_custom_call" | custom-call | flops 1 | bytes 1 | tf_op jit(solution)/shard_map/attention_backward/pallas_call | solution.py:36
  170.5 7.9 %attention_backward.6 = (bf16[1024,768]{1,0:T(8,128)(2,1)}, bf16[2,2,4,3,128,128]{5,4,3,2,1,0:T(8,128)(2,1)S(1)}) custom-call(s32[8]{0:T(128)S(1)} %stack.92.meta, bf16[1024,1024]{1,0:T(8,128)(2,1)S(1)} %get-tuple-element.99.first_ref, bf16[1024,1536]{1,0:T(8,128)(2,1)} %get-tuple-element.138.packed_ref, ...), custom_call_target="tpu_custom_call" | custom-call | flops 1 | bytes 1 | tf_op jit(solution)/shard_map/attention_backward/pallas_call | solution.py:36
  180.0 1.6 collective-permute-start.42
  181.6 2.6 collective-permute-start.40
  184.2 1.8 collective-permute-start.41
  185.9 7.7 %attention_backward.7 = (bf16[1024,768]{1,0:T(8,128)(2,1)}, bf16[2,2,4,3,128,128]{5,4,3,2,1,0:T(8,128)(2,1)S(1)}) custom-call(s32[8]{0:T(128)S(1)} %stack.92.meta, bf16[1024,1024]{1,0:T(8,128)(2,1)S(1)} %get-tuple-element.99.first_ref, bf16[1024,1536]{1,0:T(8,128)(2,1)} %get-tuple-element.138.packed_ref, ...), custom_call_target="tpu_custom_call" | custom-call | flops 1 | bytes 1 | tf_op jit(solution)/shard_map/attention_backward/pallas_call | solution.py:36
  194.9 1.8 step_3.1
  200.8 1.8 collective-permute-start.47
  202.6 12.3 %input_grad.1 = (bf16[1024,1024]{1,0:T(8,128)(2,1)}, f32[8,1024]{1,0:T(8,128)S(1)}, f32[8,3072]{1,0:T(8,128)S(1)}) custom-call(s32[8]{0:T(128)S(1)} %stack.92.meta, bf16[1024,1024]{1,0:T(8,128)(2,1)} %bitcast.38, bf16[1024,1024]{1,0:T(8,128)(2,1)} %get-tuple-element.151.grad_ref, f32[16,1024]{1,0:T(8,128)S(1)} %get-tuple-element.98.small_ref, ...), custom_call_target="tpu_custom_call" | custom-call | flops 1 | bytes 1 | tf_op jit(solution)/shard_map/input_grad/pallas_call | solution.py:36
  215.0 4.1 %step_4.1 = (bf16[12,128,128]{2,1,0:T(8,128)(2,1)S(1)}, f32[4,128,128]{2,1,0:T(8,128)S(1)}, bf16[4,128,128]{2,1,0:T(8,128)(2,1)S(1)}, bf16[4,128,128]{2,1,0:T(8,...) custom-call(s32[8]{0:T(128)S(1)} %stack.92.meta, ...), custom_call_target="tpu_custom_call" | custom-call | flops 1 | bytes 1 | tf_op jit(solution)/shard_map/step_4/pallas_call | solution.py:36
  221.1 1.5 collective-permute-start.50
  222.7 1.8 collective-permute-start.51
  224.4 3.0 %collective-permute-done.49.refs_5_ = bf16[4,128,128]{2,1,0:T(8,128)(2,1)S(1)} collective-permute-done((bf16[4,128,128]{2,1,0:T(8,128)(2,1)S(1)}, bf16[4,128,128]{2,1,0:T(8,128)(2,1)S(1)}, u32[]{:S(2)}, u32[]{:S(2)}) %collective-permute-start.49) | collective-permute-done | bytes 131104 | tf_op jit(solution)/shard_map/ppermute | solution.py:104
  227.4 4.6 %collective-permute-done.50.refs_6_ = bf16[4,128,128]{2,1,0:T(8,128)(2,1)S(1)} collective-permute-done((bf16[4,128,128]{2,1,0:T(8,128)(2,1)S(1)}, bf16[4,128,128]{2,1,0:T(8,128)(2,1)S(1)}, u32[]{:S(2)}, u32[]{:S(2)}) %collective-permute-start.50) | collective-permute-done | bytes 131104 | tf_op jit(solution)/shard_map/ppermute | solution.py:104
  232.0 2.1 step_5.1
  234.2 2.0 collective-permute-start.55
  236.9 1.8 collective-permute-start.57
  240.8 4.9 %collective-permute-done.56.refs_2_ = bf16[3,128,128]{2,1,0:T(8,128)(2,1)S(1)} collective-permute-done((bf16[3,128,128]{2,1,0:T(8,128)(2,1)S(1)}, bf16[3,128,128]{2,1,0:T(8,128)(2,1)S(1)}, u32[]{:S(2)}, u32[]{:S(2)}) %collective-permute-start.56) | collective-permute-done | bytes 98336 | tf_op jit(solution)/shard_map/ppermute | solution.py:104
  246.3 6.9 %collective-permute-done.53.refs_6_.refs_2_ = bf16[4,128,128]{2,1,0:T(8,128)(2,1)S(1)} collective-permute-done((bf16[4,128,128]{2,1,0:T(8,128)(2,1)S(1)}, bf16[4,128,128]{2,1,0:T(8,128)(2,1)S(1)}, u32[]{:S(2)}, u32[]{:S(2)}) %collective-permute-start.53) | collective-permute-done | bytes 131104 | tf_op jit(solution)/shard_map/ppermute | solution.py:104
  257.8 1.8 finish_rest.1
  262.2 1.9 finish_heads.1
  (139 shorter events, 41.2 us)
Async XLA Ops:
  2.8 9.0 %collective-permute-start.2 = (bf16[32,1664]{1,0:T(8,128)(2,1)S(1)}, bf16[32,1664]{1,0:T(8,128)(2,1)S(1)}, u32[]{:S(2)}, u32[]{:S(2)}) collective-permute-start(bf16[32,1664]{1,0:T(8,128)(2,1)S(1)} %fusion.1), channel_id=1, source_target_pairs={{0,24},{1,25},{2,26},{3,27},{4,28},{5,29},{6,30},{7,31},{8,16},{9,... | collective-permute-start | bytes 319496 | tf_op jit(solution)/shard_map/ppermute | solution.py:104
  7.9 9.0 %collective-permute-start.1 = (bf16[32,1664]{1,0:T(8,128)(2,1)S(1)}, bf16[32,1664]{1,0:T(8,128)(2,1)S(1)}, u32[]{:S(2)}, u32[]{:S(2)}) collective-permute-start(bf16[32,1664]{1,0:T(8,128)(2,1)S(1)} %fusion.1), channel_id=1, source_target_pairs={{0,16},{1,17},{2,18},{3,19},{4,20},{5,21},{6,22},{7,23},{8,24},{9,... | collective-permute-start | bytes 319496 | tf_op jit(solution)/shard_map/ppermute | solution.py:104
  7.9 9.0 %collective-permute-start = (bf16[32,1664]{1,0:T(8,128)(2,1)S(1)}, bf16[32,1664]{1,0:T(8,128)(2,1)S(1)}, u32[]{:S(2)}, u32[]{:S(2)}) collective-permute-start(bf16[32,1664]{1,0:T(8,128)(2,1)S(1)} %fusion.1), channel_id=1, source_target_pairs={{0,8},{1,9},{2,10},{3,11},{4,12},{5,13},{6,14},{7,15},{8,0},{9,1},... | collective-permute-start | bytes 319496 | tf_op jit(solution)/shard_map/ppermute | solution.py:104
  16.9 13.7 %collective-permute-start.4 = (bf16[4,32,1664]{2,1,0:T(8,128)(2,1)S(1)}, bf16[4,32,1664]{2,1,0:T(8,128)(2,1)}, u32[]{:S(2)}, u32[]{:S(2)}) collective-permute-start(bf16[4,32,1664]{2,1,0:T(8,128)(2,1)S(1)} %pad_maximum_fusion.4.own_ref.refs_0_), channel_id=1, source_target_pairs={{0,4},{1,3},{2,6},{3,1},{4,0},{5,7},{6,2},{7,5},{8,12},{9,11},{10,... | collective-permute-start | bytes 1277960 | tf_op jit(solution)/shard_map/ppermute | solution.py:104
  18.5 12.1 %collective-permute-start.3 = (bf16[4,32,1664]{2,1,0:T(8,128)(2,1)S(1)}, bf16[4,32,1664]{2,1,0:T(8,128)(2,1)S(1)}, u32[]{:S(2)}, u32[]{:S(2)}) collective-permute-start(bf16[4,32,1664]{2,1,0:T(8,128)(2,1)S(1)} %pad_maximum_fusion.4.own_ref.refs_0_), channel_id=1, source_target_pairs={{0,2},{1,5},{2,0},{3,7},{4,6},{5,1},{6,4},{7,3},{8,10},{9,13},{10,... | collective-permute-start | bytes 1277960 | tf_op jit(solution)/shard_map/ppermute | solution.py:104
  22.7 7.9 %collective-permute-start.6 = (bf16[32,1536]{1,0:T(8,128)(2,1)S(1)}, bf16[32,1536]{1,0:T(8,128)(2,1)S(1)}, u32[]{:S(2)}, u32[]{:S(2)}) collective-permute-start(bf16[32,1536]{1,0:T(8,128)(2,1)S(1)} %reshape.44), channel_id=1, source_target_pairs={{0,16},{1,17},{2,18},{3,19},{4,20},{5,21},{6,22},{7,23},{8,24},{9,... | collective-permute-start | bytes 294920 | tf_op jit(solution)/shard_map/ppermute | solution.py:104
  33.8 15.9 %collective-permute-start.8 = (bf16[4,32,3200]{2,1,0:T(8,128)(2,1)S(1)}, bf16[4,32,3200]{2,1,0:T(8,128)(2,1)S(1)}, u32[]{:S(2)}, u32[]{:S(2)}) collective-permute-start(bf16[4,32,3200]{2,1,0:T(8,128)(2,1)S(1)} %pad_maximum_fusion.1), channel_id=1, source_target_pairs={{0,4},{1,3},{2,6},{3,1},{4,0},{5,7},{6,2},{7,5},{8,12},{9,11},{10,... | collective-permute-start | bytes 2457608 | tf_op jit(solution)/shard_map/ppermute | solution.py:104
  35.3 14.4 %collective-permute-start.13 = (bf16[4,32,1536]{2,1,0:T(8,128)(2,1)S(1)}, bf16[4,32,1536]{2,1,0:T(8,128)(2,1)S(1)}, u32[]{:S(2)}, u32[]{:S(2)}) collective-permute-start(bf16[4,32,1536]{2,1,0:T(8,128)(2,1)S(1)} %pad_maximum_fusion.5.refs_0_), channel_id=1, source_target_pairs={{0,2},{1,5},{2,0},{3,7},{4,6},{5,1},{6,4},{7,3},{8,10},{9,13},{10,... | collective-permute-start | bytes 1179656 | tf_op jit(solution)/shard_map/ppermute | solution.py:104
  35.9 8.3 %collective-permute-start.16 = (bf16[32,2048]{1,0:T(8,128)(2,1)S(1)}, bf16[32,2048]{1,0:T(8,128)(2,1)S(1)}, u32[]{:S(2)}, u32[]{:S(2)}) collective-permute-start(bf16[32,2048]{1,0:T(8,128)(2,1)S(1)} %pad_maximum_fusion.7), channel_id=1, source_target_pairs={{0,24},{1,25},{2,26},{3,27},{4,28},{5,29},{6,30},{7,31},{8,16},{9,... | collective-permute-start | bytes 393224 | tf_op jit(solution)/shard_map/ppermute | solution.py:104
  37.9 10.6 %collective-permute-start.15 = (bf16[32,2048]{1,0:T(8,128)(2,1)S(1)}, bf16[32,2048]{1,0:T(8,128)(2,1)S(1)}, u32[]{:S(2)}, u32[]{:S(2)}) collective-permute-start(bf16[32,2048]{1,0:T(8,128)(2,1)S(1)} %pad_maximum_fusion.7), channel_id=1, source_target_pairs={{0,16},{1,17},{2,18},{3,19},{4,20},{5,21},{6,22},{7,23},{8,24},{9,... | collective-permute-start | bytes 393224 | tf_op jit(solution)/shard_map/ppermute | solution.py:104
  37.9 10.6 %collective-permute-start.14 = (bf16[32,2048]{1,0:T(8,128)(2,1)S(1)}, bf16[32,2048]{1,0:T(8,128)(2,1)S(1)}, u32[]{:S(2)}, u32[]{:S(2)}) collective-permute-start(bf16[32,2048]{1,0:T(8,128)(2,1)S(1)} %pad_maximum_fusion.7), channel_id=1, source_target_pairs={{0,8},{1,9},{2,10},{3,11},{4,12},{5,13},{6,14},{7,15},{8,0},{9,1},... | collective-permute-start | bytes 393224 | tf_op jit(solution)/shard_map/ppermute | solution.py:104
  49.8 17.3 %collective-permute-start.17 = (bf16[4,32,3584]{2,1,0:T(8,128)(2,1)S(1)}, bf16[4,32,3584]{2,1,0:T(8,128)(2,1)S(1)}, u32[]{:S(2)}, u32[]{:S(2)}) collective-permute-start(bf16[4,32,3584]{2,1,0:T(8,128)(2,1)S(1)} %pad_maximum_fusion), channel_id=1, source_target_pairs={{0,4},{1,3},{2,6},{3,1},{4,0},{5,7},{6,2},{7,5},{8,12},{9,11},{10,... | collective-permute-start | bytes 2752520 | tf_op jit(solution)/shard_map/ppermute | solution.py:104
  50.4 16.7 %collective-permute-start.21 = (bf16[4,32,2048]{2,1,0:T(8,128)(2,1)S(1)}, bf16[4,32,2048]{2,1,0:T(8,128)(2,1)S(1)}, u32[]{:S(2)}, u32[]{:S(2)}) collective-permute-start(bf16[4,32,2048]{2,1,0:T(8,128)(2,1)S(1)} %pad_maximum_fusion.3.refs_2_.refs_0_), channel_id=1, source_target_pairs={{0,2},{1,5},{2,0},{3,7},{4,6},{5,1},{6,4},{7,3},{8,10},{9,13},{10,... | collective-permute-start | bytes 1572872 | tf_op jit(solution)/shard_map/ppermute | solution.py:104
  59.1 9.7 %collective-permute-start.9 = (bf16[4,32,1664]{2,1,0:T(8,128)(2,1)S(1)}, bf16[4,32,1664]{2,1,0:T(8,128)(2,1)S(1)}, u32[]{:S(2)}, u32[]{:S(2)}) collective-permute-start(bf16[4,32,1664]{2,1,0:T(8,128)(2,1)S(1)} %pad_maximum_fusion.4.own_ref.refs_0_), channel_id=1, source_target_pairs={{0,1},{1,0},{2,3},{3,2},{4,5},{5,4},{6,7},{7,6},{8,9},{9,8},{10,11... | collective-permute-start | bytes 1277960 | tf_op jit(solution)/shard_map/ppermute | solution.py:104
  60.4 8.5 %collective-permute-start.12 = (bf16[4,32,3200]{2,1,0:T(8,128)(2,1)S(1)}, bf16[4,32,3200]{2,1,0:T(8,128)(2,1)S(1)}, u32[]{:S(2)}, u32[]{:S(2)}) collective-permute-start(bf16[4,32,3200]{2,1,0:T(8,128)(2,1)S(1)} %collective-permute-done.8.refs_3_.refs_2_), channel_id=1, source_target_pairs={{0,1},{1,0},{2,3},{3,2},{4,5},{5,4},{6,7},{7,6},{8,9},{9,8},{10,11... | collective-permute-start | bytes 2457608 | tf_op jit(solution)/shard_map/ppermute | solution.py:104
  60.4 8.3 %collective-permute-start.11 = (bf16[4,32,1664]{2,1,0:T(8,128)(2,1)}, bf16[4,32,1664]{2,1,0:T(8,128)(2,1)S(1)}, u32[]{:S(2)}, u32[]{:S(2)}) collective-permute-start(bf16[4,32,1664]{2,1,0:T(8,128)(2,1)} %collective-permute-done.4.two_ref.refs_2_), channel_id=1, source_target_pairs={{0,1},{1,0},{2,3},{3,2},{4,5},{5,4},{6,7},{7,6},{8,9},{9,8},{10,11... | collective-permute-start | bytes 1277960 | tf_op jit(solution)/shard_map/ppermute | solution.py:104
  67.2 16.9 %collective-permute-start.25 = (bf16[4,32,3072]{2,1,0:T(8,128)(2,1)S(1)}, bf16[4,32,3072]{2,1,0:T(8,128)(2,1)S(1)}, u32[]{:S(2)}, u32[]{:S(2)}) collective-permute-start(bf16[4,32,3072]{2,1,0:T(8,128)(2,1)S(1)} %pad_maximum_fusion.2), channel_id=1, source_target_pairs={{0,4},{1,3},{2,6},{3,1},{4,0},{5,7},{6,2},{7,5},{8,12},{9,11},{10,... | collective-permute-start | bytes 2359304 | tf_op jit(solution)/shard_map/ppermute | solution.py:104
  81.8 8.3 %collective-permute-start.20 = (bf16[4,32,3584]{2,1,0:T(8,128)(2,1)S(1)}, bf16[4,32,3584]{2,1,0:T(8,128)(2,1)S(1)}, u32[]{:S(2)}, u32[]{:S(2)}) collective-permute-start(bf16[4,32,3584]{2,1,0:T(8,128)(2,1)S(1)} %collective-permute-done.17.refs_3_.refs_4_.refs_2_), channel_id=1, source_target_pairs={{0,1},{1,0},{2,3},{3,2},{4,5},{5,4},{6,7},{7,6},{8,9},{9,8},{10,11... | collective-permute-start | bytes 2752520 | tf_op jit(solution)/shard_map/ppermute | solution.py:104
  84.1 21.7 %collective-permute-start.28 = (bf16[4,32,3072]{2,1,0:T(8,128)(2,1)S(1)}, bf16[4,32,3072]{2,1,0:T(8,128)(2,1)S(1)}, u32[]{:S(2)}, u32[]{:S(2)}) collective-permute-start(bf16[4,32,3072]{2,1,0:T(8,128)(2,1)S(1)} %collective-permute-done.25.refs_5_.refs_2_.refs_3_), channel_id=1, source_target_pairs={{0,1},{1,0},{2,3},{3,2},{4,5},{5,4},{6,7},{7,6},{8,9},{9,8},{10,11... | collective-permute-start | bytes 2359304 | tf_op jit(solution)/shard_map/ppermute | solution.py:104
  88.4 17.1 %collective-permute-start.26 = (bf16[4,32,2048]{2,1,0:T(8,128)(2,1)S(1)}, bf16[4,32,2048]{2,1,0:T(8,128)(2,1)S(1)}, u32[]{:S(2)}, u32[]{:S(2)}) collective-permute-start(bf16[4,32,2048]{2,1,0:T(8,128)(2,1)S(1)} %pad_maximum_fusion.3.refs_2_.refs_0_), channel_id=1, source_target_pairs={{0,1},{1,0},{2,3},{3,2},{4,5},{5,4},{6,7},{7,6},{8,9},{9,8},{10,11... | collective-permute-start | bytes 1572872 | tf_op jit(solution)/shard_map/ppermute | solution.py:104
  88.4 16.5 %collective-permute-start.30 = (bf16[4,32,1024]{2,1,0:T(8,128)(2,1)S(1)}, bf16[4,32,1024]{2,1,0:T(8,128)(2,1)S(1)}, u32[]{:S(2)}, u32[]{:S(2)}) collective-permute-start(bf16[4,32,1024]{2,1,0:T(8,128)(2,1)S(1)} %collective-permute-done.29.refs_1_), channel_id=1, source_target_pairs={{0,4},{1,3},{2,6},{3,1},{4,0},{5,7},{6,2},{7,5},{8,12},{9,11},{10,... | collective-permute-start | bytes 786440 | tf_op jit(solution)/shard_map/ppermute | solution.py:104
  89.9 15.9 %collective-permute-start.27 = (bf16[4,32,2048]{2,1,0:T(8,128)(2,1)S(1)}, bf16[4,32,2048]{2,1,0:T(8,128)(2,1)S(1)}, u32[]{:S(2)}, u32[]{:S(2)}) collective-permute-start(bf16[4,32,2048]{2,1,0:T(8,128)(2,1)S(1)} %collective-permute-done.21.refs_3_.refs_1_), channel_id=1, source_target_pairs={{0,1},{1,0},{2,3},{3,2},{4,5},{5,4},{6,7},{7,6},{8,9},{9,8},{10,11... | collective-permute-start | bytes 1572872 | tf_op jit(solution)/shard_map/ppermute | solution.py:104
  104.9 12.1 %collective-permute-start.31 = (bf16[4,32,1024]{2,1,0:T(8,128)(2,1)S(1)}, bf16[4,32,1024]{2,1,0:T(8,128)(2,1)S(1)}, u32[]{:S(2)}, u32[]{:S(2)}) collective-permute-start(bf16[4,32,1024]{2,1,0:T(8,128)(2,1)S(1)} %pad_maximum_fusion.6.refs_0_), channel_id=1, source_target_pairs={{0,1},{1,0},{2,3},{3,2},{4,5},{5,4},{6,7},{7,6},{8,9},{9,8},{10,11... | collective-permute-start | bytes 786440 | tf_op jit(solution)/shard_map/ppermute | solution.py:104
  105.2 11.8 %collective-permute-start.32 = (bf16[4,32,1024]{2,1,0:T(8,128)(2,1)S(1)}, bf16[4,32,1024]{2,1,0:T(8,128)(2,1)S(1)}, u32[]{:S(2)}, u32[]{:S(2)}) collective-permute-start(bf16[4,32,1024]{2,1,0:T(8,128)(2,1)S(1)} %collective-permute-done.29.refs_1_), channel_id=1, source_target_pairs={{0,1},{1,0},{2,3},{3,2},{4,5},{5,4},{6,7},{7,6},{8,9},{9,8},{10,11... | collective-permute-start | bytes 786440 | tf_op jit(solution)/shard_map/ppermute | solution.py:104
  105.5 11.5 %collective-permute-start.33 = (bf16[4,32,1024]{2,1,0:T(8,128)(2,1)S(1)}, bf16[4,32,1024]{2,1,0:T(8,128)(2,1)S(1)}, u32[]{:S(2)}, u32[]{:S(2)}) collective-permute-start(bf16[4,32,1024]{2,1,0:T(8,128)(2,1)S(1)} %collective-permute-done.30.refs_3_), channel_id=1, source_target_pairs={{0,1},{1,0},{2,3},{3,2},{4,5},{5,4},{6,7},{7,6},{8,9},{9,8},{10,11... | collective-permute-start | bytes 786440 | tf_op jit(solution)/shard_map/ppermute | solution.py:104
  134.2 11.1 %collective-permute-start.34 = (bf16[2,2,4,4,128,128]{5,4,3,2,1,0:T(8,128)(2,1)S(1)}, bf16[2,2,4,4,128,128]{5,4,3,2,1,0:T(8,128)(2,1)S(1)}, u32[]{:S(2)}, u32[]{:S(2)}) collective-permute-start(bf16[2,2,4,4,128,128]{5,4,3,2,1,0:T(8,128)(2,1)S(1)} %get-tuple-element.126), channel_id=1, source_target_pairs={{0,1},{1,0},{2,3},{3,2},{4,5},{5,4},{6,7},{7,6},{8,9},{9,8},{10,11... | collective-permute-start | bytes 6291464 | tf_op jit(solution)/shard_map/ppermute | solution.py:104
  145.0 14.1 %collective-permute-start.36 = (bf16[2,2,4,2,128,128]{5,4,3,2,1,0:T(8,128)(2,1)S(1)}, bf16[2,2,4,2,128,128]{5,4,3,2,1,0:T(8,128)(2,1)S(1)}, u32[]{:S(2)}, u32[]{:S(2)}) collective-permute-start(bf16[2,2,4,2,128,128]{5,4,3,2,1,0:T(8,128)(2,1)S(1)} %get-tuple-element.134), channel_id=1, source_target_pairs={{0,1},{1,0},{2,3},{3,2},{4,5},{5,4},{6,7},{7,6},{8,9},{9,8},{10,11... | collective-permute-start | bytes 3145736 | tf_op jit(solution)/shard_map/ppermute | solution.py:104
  146.3 14.9 %collective-permute-start.35 = (bf16[32,128,128]{2,1,0:T(8,128)(2,1)S(1)}, bf16[32,128,128]{2,1,0:T(8,128)(2,1)S(1)}, u32[]{:S(2)}, u32[]{:S(2)}) collective-permute-start(bf16[32,128,128]{2,1,0:T(8,128)(2,1)S(1)} %step_0.1), channel_id=1, source_target_pairs={{0,4},{1,3},{2,6},{3,1},{4,0},{5,7},{6,2},{7,5},{8,12},{9,11},{10,... | collective-permute-start | bytes 3145736 | tf_op jit(solution)/shard_map/ppermute | solution.py:104
  159.0 19.5 %collective-permute-start.38 = (bf16[2,2,4,3,128,128]{5,4,3,2,1,0:T(8,128)(2,1)S(1)}, bf16[2,2,4,3,128,128]{5,4,3,2,1,0:T(8,128)(2,1)S(1)}, u32[]{:S(2)}, u32[]{:S(2)}) collective-permute-start(bf16[2,2,4,3,128,128]{5,4,3,2,1,0:T(8,128)(2,1)S(1)} %get-tuple-element.132), channel_id=1, source_target_pairs={{0,1},{1,0},{2,3},{3,2},{4,5},{5,4},{6,7},{7,6},{8,9},{9,8},{10,11... | collective-permute-start | bytes 4718600 | tf_op jit(solution)/shard_map/ppermute | solution.py:104
  162.2 16.3 %collective-permute-start.37 = (bf16[32,128,128]{2,1,0:T(8,128)(2,1)S(1)}, bf16[32,128,128]{2,1,0:T(8,128)(2,1)S(1)}, u32[]{:S(2)}, u32[]{:S(2)}) collective-permute-start(bf16[32,128,128]{2,1,0:T(8,128)(2,1)S(1)} %step_1.1), channel_id=1, source_target_pairs={{0,2},{1,5},{2,0},{3,7},{4,6},{5,1},{6,4},{7,3},{8,10},{9,13},{10,... | collective-permute-start | bytes 3145736 | tf_op jit(solution)/shard_map/ppermute | solution.py:104
  178.4 16.1 %collective-permute-start.43 = (bf16[2,2,4,3,128,128]{5,4,3,2,1,0:T(8,128)(2,1)S(1)}, bf16[2,2,4,3,128,128]{5,4,3,2,1,0:T(8,128)(2,1)S(1)}, u32[]{:S(2)}, u32[]{:S(2)}) collective-permute-start(bf16[2,2,4,3,128,128]{5,4,3,2,1,0:T(8,128)(2,1)S(1)} %get-tuple-element.140), channel_id=1, source_target_pairs={{0,1},{1,0},{2,3},{3,2},{4,5},{5,4},{6,7},{7,6},{8,9},{9,8},{10,11... | collective-permute-start | bytes 4718600 | tf_op jit(solution)/shard_map/ppermute | solution.py:104
  180.0 14.9 %collective-permute-start.42 = (bf16[32,128,128]{2,1,0:T(8,128)(2,1)S(1)}, bf16[32,128,128]{2,1,0:T(8,128)(2,1)S(1)}, u32[]{:S(2)}, u32[]{:S(2)}) collective-permute-start(bf16[32,128,128]{2,1,0:T(8,128)(2,1)S(1)} %get-tuple-element.142), channel_id=1, source_target_pairs={{0,4},{1,3},{2,6},{3,1},{4,0},{5,7},{6,2},{7,5},{8,12},{9,11},{10,... | collective-permute-start | bytes 3145736 | tf_op jit(solution)/shard_map/ppermute | solution.py:104
  181.6 12.1 %collective-permute-start.39 = (bf16[4,128,128]{2,1,0:T(8,128)(2,1)S(1)}, bf16[4,128,128]{2,1,0:T(8,128)(2,1)S(1)}, u32[]{:S(2)}, u32[]{:S(2)}) collective-permute-start(bf16[4,128,128]{2,1,0:T(8,128)(2,1)S(1)} %get-tuple-element.145), channel_id=1, source_target_pairs={{0,8},{1,9},{2,10},{3,11},{4,12},{5,13},{6,14},{7,15},{8,0},{9,1},... | collective-permute-start | bytes 393224 | tf_op jit(solution)/shard_map/ppermute | solution.py:104
  181.6 12.9 %collective-permute-start.40 = (bf16[4,128,128]{2,1,0:T(8,128)(2,1)S(1)}, bf16[4,128,128]{2,1,0:T(8,128)(2,1)S(1)}, u32[]{:S(2)}, u32[]{:S(2)}) collective-permute-start(bf16[4,128,128]{2,1,0:T(8,128)(2,1)S(1)} %get-tuple-element.146), channel_id=1, source_target_pairs={{0,16},{1,17},{2,18},{3,19},{4,20},{5,21},{6,22},{7,23},{8,24},{9,... | collective-permute-start | bytes 393224 | tf_op jit(solution)/shard_map/ppermute | solution.py:104
  184.2 10.3 %collective-permute-start.41 = (bf16[4,128,128]{2,1,0:T(8,128)(2,1)S(1)}, bf16[4,128,128]{2,1,0:T(8,128)(2,1)S(1)}, u32[]{:S(2)}, u32[]{:S(2)}) collective-permute-start(bf16[4,128,128]{2,1,0:T(8,128)(2,1)S(1)} %get-tuple-element.147), channel_id=1, source_target_pairs={{0,24},{1,25},{2,26},{3,27},{4,28},{5,29},{6,30},{7,31},{8,16},{9,... | collective-permute-start | bytes 393224 | tf_op jit(solution)/shard_map/ppermute | solution.py:104
  196.7 18.3 %collective-permute-start.44 = (bf16[36,128,128]{2,1,0:T(8,128)(2,1)S(1)}, bf16[36,128,128]{2,1,0:T(8,128)(2,1)S(1)}, u32[]{:S(2)}, u32[]{:S(2)}) collective-permute-start(bf16[36,128,128]{2,1,0:T(8,128)(2,1)S(1)} %get-tuple-element.149), channel_id=1, source_target_pairs={{0,2},{1,5},{2,0},{3,7},{4,6},{5,1},{6,4},{7,3},{8,10},{9,13},{10,... | collective-permute-start | bytes 3538952 | tf_op jit(solution)/shard_map/ppermute | solution.py:104
  198.2 16.7 %collective-permute-start.45 = (bf16[2,128,128]{2,1,0:T(8,128)(2,1)S(1)}, bf16[2,128,128]{2,1,0:T(8,128)(2,1)S(1)}, u32[]{:S(2)}, u32[]{:S(2)}) collective-permute-start(bf16[2,128,128]{2,1,0:T(8,128)(2,1)S(1)} %get-tuple-element.166), channel_id=1, source_target_pairs={{0,8},{1,9},{2,10},{3,11},{4,12},{5,13},{6,14},{7,15},{8,0},{9,1},... | collective-permute-start | bytes 196616 | tf_op jit(solution)/shard_map/ppermute | solution.py:104
  199.6 15.4 %collective-permute-start.46 = (bf16[2,128,128]{2,1,0:T(8,128)(2,1)S(1)}, bf16[2,128,128]{2,1,0:T(8,128)(2,1)S(1)}, u32[]{:S(2)}, u32[]{:S(2)}) collective-permute-start(bf16[2,128,128]{2,1,0:T(8,128)(2,1)S(1)} %get-tuple-element.167), channel_id=1, source_target_pairs={{0,16},{1,17},{2,18},{3,19},{4,20},{5,21},{6,22},{7,23},{8,24},{9,... | collective-permute-start | bytes 196616 | tf_op jit(solution)/shard_map/ppermute | solution.py:104
  200.8 14.1 %collective-permute-start.47 = (bf16[2,128,128]{2,1,0:T(8,128)(2,1)S(1)}, bf16[2,128,128]{2,1,0:T(8,128)(2,1)S(1)}, u32[]{:S(2)}, u32[]{:S(2)}) collective-permute-start(bf16[2,128,128]{2,1,0:T(8,128)(2,1)S(1)} %get-tuple-element.168), channel_id=1, source_target_pairs={{0,24},{1,25},{2,26},{3,27},{4,28},{5,29},{6,30},{7,31},{8,16},{9,... | collective-permute-start | bytes 196616 | tf_op jit(solution)/shard_map/ppermute | solution.py:104
  219.1 12.9 %collective-permute-start.48 = (bf16[12,128,128]{2,1,0:T(8,128)(2,1)S(1)}, bf16[12,128,128]{2,1,0:T(8,128)(2,1)S(1)}, u32[]{:S(2)}, u32[]{:S(2)}) collective-permute-start(bf16[12,128,128]{2,1,0:T(8,128)(2,1)S(1)} %get-tuple-element.169), channel_id=1, source_target_pairs={{0,4},{1,3},{2,6},{3,1},{4,0},{5,7},{6,2},{7,5},{8,12},{9,11},{10,... | collective-permute-start | bytes 1179656 | tf_op jit(solution)/shard_map/ppermute | solution.py:104
  221.1 10.9 %collective-permute-start.50 = (bf16[4,128,128]{2,1,0:T(8,128)(2,1)S(1)}, bf16[4,128,128]{2,1,0:T(8,128)(2,1)S(1)}, u32[]{:S(2)}, u32[]{:S(2)}) collective-permute-start(bf16[4,128,128]{2,1,0:T(8,128)(2,1)S(1)} %get-tuple-element.172), channel_id=1, source_target_pairs={{0,16},{1,17},{2,18},{3,19},{4,20},{5,21},{6,22},{7,23},{8,24},{9,... | collective-permute-start | bytes 393224 | tf_op jit(solution)/shard_map/ppermute | solution.py:104
  222.7 9.4 %collective-permute-start.51 = (bf16[4,128,128]{2,1,0:T(8,128)(2,1)S(1)}, bf16[4,128,128]{2,1,0:T(8,128)(2,1)S(1)}, u32[]{:S(2)}, u32[]{:S(2)}) collective-permute-start(bf16[4,128,128]{2,1,0:T(8,128)(2,1)S(1)} %get-tuple-element.173), channel_id=1, source_target_pairs={{0,24},{1,25},{2,26},{3,27},{4,28},{5,29},{6,30},{7,31},{8,16},{9,... | collective-permute-start | bytes 393224 | tf_op jit(solution)/shard_map/ppermute | solution.py:104
  236.2 9.5 %collective-permute-start.56 = (bf16[3,128,128]{2,1,0:T(8,128)(2,1)S(1)}, bf16[3,128,128]{2,1,0:T(8,128)(2,1)S(1)}, u32[]{:S(2)}, u32[]{:S(2)}) collective-permute-start(bf16[3,128,128]{2,1,0:T(8,128)(2,1)S(1)} %get-tuple-element.177), channel_id=1, source_target_pairs={{0,16},{1,17},{2,18},{3,19},{4,20},{5,21},{6,22},{7,23},{8,24},{9,... | collective-permute-start | bytes 294920 | tf_op jit(solution)/shard_map/ppermute | solution.py:104
  236.8 9.2 %collective-permute-start.54 = (bf16[4,128,128]{2,1,0:T(8,128)(2,1)S(1)}, bf16[4,128,128]{2,1,0:T(8,128)(2,1)S(1)}, u32[]{:S(2)}, u32[]{:S(2)}) collective-permute-start(bf16[4,128,128]{2,1,0:T(8,128)(2,1)S(1)} %get-tuple-element.174.refs_4_.refs_0_), channel_id=1, source_target_pairs={{0,3},{1,2},{2,1},{3,0},{4,7},{5,6},{6,5},{7,4},{8,11},{9,10},{10,... | collective-permute-start | bytes 393224 | tf_op jit(solution)/shard_map/ppermute | solution.py:104
  236.9 8.8 %collective-permute-start.57 = (bf16[3,128,128]{2,1,0:T(8,128)(2,1)S(1)}, bf16[3,128,128]{2,1,0:T(8,128)(2,1)S(1)}, u32[]{:S(2)}, u32[]{:S(2)}) collective-permute-start(bf16[3,128,128]{2,1,0:T(8,128)(2,1)S(1)} %get-tuple-element.178), channel_id=1, source_target_pairs={{0,24},{1,25},{2,26},{3,27},{4,28},{5,29},{6,30},{7,31},{8,16},{9,... | collective-permute-start | bytes 294920 | tf_op jit(solution)/shard_map/ppermute | solution.py:104
  238.7 17.3 %collective-permute-start.63 = (bf16[6,128,128]{2,1,0:T(8,128)(2,1)S(1)}, bf16[6,128,128]{2,1,0:T(8,128)(2,1)S(1)}, u32[]{:S(2)}, u32[]{:S(2)}) collective-permute-start(bf16[6,128,128]{2,1,0:T(8,128)(2,1)S(1)} %get-tuple-element.181.refs_0_), channel_id=1, source_target_pairs={{0,3},{1,2},{2,1},{3,0},{4,7},{5,6},{6,5},{7,4},{8,11},{9,10},{10,... | collective-permute-start | bytes 589832 | tf_op jit(solution)/shard_map/ppermute | solution.py:104
  240.1 16.8 %collective-permute-start.62 = (bf16[6,128,128]{2,1,0:T(8,128)(2,1)S(1)}, bf16[6,128,128]{2,1,0:T(8,128)(2,1)S(1)}, u32[]{:S(2)}, u32[]{:S(2)}) collective-permute-start(bf16[6,128,128]{2,1,0:T(8,128)(2,1)S(1)} %get-tuple-element.181.refs_0_), channel_id=1, source_target_pairs={{0,2},{1,3},{2,0},{3,1},{4,6},{5,7},{6,4},{7,5},{8,10},{9,11},{10,... | collective-permute-start | bytes 589832 | tf_op jit(solution)/shard_map/ppermute | solution.py:104
  245.7 12.1 %collective-permute-start.61 = (bf16[6,128,128]{2,1,0:T(8,128)(2,1)S(1)}, bf16[6,128,128]{2,1,0:T(8,128)(2,1)S(1)}, u32[]{:S(2)}, u32[]{:S(2)}) collective-permute-start(bf16[6,128,128]{2,1,0:T(8,128)(2,1)S(1)} %get-tuple-element.181.refs_0_), channel_id=1, source_target_pairs={{0,1},{1,0},{2,3},{3,2},{4,5},{5,4},{6,7},{7,6},{8,9},{9,8},{10,11... | collective-permute-start | bytes 589832 | tf_op jit(solution)/shard_map/ppermute | solution.py:104
  (23 other events, 172.7 us)

commit v3 on v2

--- a/solution.py
+++ b/solution.py
@@ -116,23 +116,23 @@
     return lax.optimization_barrier((value, *others))[0]
 
 
-def gather_chunks(quarters, links, norm):
+def gather_chunks(quarters, links, visit):
     chunks = []
     along, across = (), ()
     late = None
-    for quarter in quarters:
+    for i, quarter in enumerate(quarters):
         quarter = after(quarter, *along)
         along = [move(quarter, p) for p in links.z]
-        own = after(jnp.stack([quarter] + along), *across)
+        own = jnp.stack([after(quarter, *across)] + along)
         first = move(own, links.y_or_x)
         both = own if late is None else jnp.concatenate([late, own], axis=2)
         both = move(both, links.x_or_y)
         if late is not None:
             chunks[-1].append((both, 0))
         chunks.append([(own, 0), (first, 0), (both, 0 if late is None else late.shape[2])])
-        across = (both,) if len(chunks) > 1 else (both, *norm([own, first, both]))
         late = first
-    chunks[-1].append((move(late, links.x_or_y), 0))
+        across = (both, *visit(i, chunks))
+    chunks[-1].append((move(after(late, *across[1:]), links.x_or_y), 0))
     return chunks
 
 
@@ -145,6 +145,10 @@
             if id(part) not in self.moved:
                 self.moved[id(part)] = move(after(part, *gates), self.pairs)
         return chunk + [(self.moved[id(part)], start) for part, start in chunk]
+
+    def early(self, chunk, count, *gates):
+        moved = self(chunk[:count], *gates)
+        return [part for part, _ in moved[count:]]
 
 
 class Piece:
@@ -199,7 +203,7 @@
             values = sum(got[i][...].astype(F32) for i in loads)
             outs[out][at : at + n] = values.astype(BF).reshape(n, 128, 128)
 
-        self.jobs.append(job)
+        self.jobs.append((job, len(self.views)))
 
     def second(self, piece, out, at):
         n = 4 * piece.t
@@ -219,7 +223,7 @@
             values = sum(got[i][...].reshape(n, 128, 128).astype(F32) for i in loads)
             outs[out][at : at + n] = values.astype(BF)
 
-        self.jobs.append(job)
+        self.jobs.append((job, len(self.views)))
 
     def along(self, piece, sums=()):
         t = piece.t
@@ -264,7 +268,7 @@
                         rows = jnp.concatenate(rows, axis=0).astype(dtype)
                         outs[out + k][t, 16 * x : 16 * x + 16] = rows
 
-        self.jobs.append(job)
+        self.jobs.append((job, len(self.views)))
 
     def share(self, groups):
         loads = [
@@ -279,7 +283,7 @@
                 outs[out][at : at + size] = sum(got[i][...].astype(F32) for i in slots).astype(BF)
                 at += size
 
-        self.jobs.append(job)
+        self.jobs.append((job, len(self.views)))
 
     def small(self, arrays):
         tile = arrays[0].shape[0] - 1
@@ -292,7 +296,7 @@
                 rows = span(meta[XPOS] if k else 1 - meta[XPOS], 16)
                 outs[out + k][...] = sum(got[i][rows, :].astype(F32) for i in loads)
 
-        self.jobs.append(job)
+        self.jobs.append((job, len(self.views)))
 
     def run(self, meta, name):
         count, total = len(self.arrays), len(self.outs)
@@ -305,9 +309,11 @@
             ]
             for copy in copies:
                 copy.start()
-            for copy in copies:
-                copy.wait()
-            for job in self.jobs:
+            ready = 0
+            for job, last in self.jobs:
+                for copy in copies[ready:last]:
+                    copy.wait()
+                ready = last
                 job(meta, got, outs)
 
         return call(
@@ -471,7 +477,7 @@
     size = min(256, rows)
 
     def over(body):
-        pl.loop(0, rows // size)(lambda i: body(span(i, size)))
+        pl.loop(0, rows // size)(lambda i: body(span(i, size), i))
 
     return over
 
@@ -491,22 +497,26 @@
             return small_ref[r : r + 1, :]
 
         fetched(whole, (0, width), sems.at[0])
-        fetched(whole, (width, width), sems.at[1])
 
         @blocks(rows)
-        def _(here):
+        def _(here, i):
             values = jnp.concatenate([r[here, :] for r in mixed_refs], axis=1)
             middle = x_ref[here, :].astype(F32) + dot(values, whole[:, :width]) + row(BO)
             middle_ref[here, :] = middle
             normed, _ = normed_rows(middle)
             second = (normed * row(G2) + row(B2)).astype(BF)
             second_ref[here, :] = second
+
+            @pl.when(i == 0)
+            def _():
+                fetched(whole, (width, width), sems.at[1])
+
             v = dot(second, whole[:, width:]) + row(BU)
             square = v * v
-            tanh = jnp.tanh(GELU * v * (1.0 + CUBIC * square))
-            half = 0.5 * (1.0 + tanh)
-            active_ref[here, :] = (v * half).astype(BF)
-            slope = (0.5 * v) * (1.0 - tanh * tanh) * (GELU * (1.0 + (3 * CUBIC) * square))
+            half = 0.5 * jnp.tanh(v * (GELU + (GELU * CUBIC) * square)) + 0.5
+            active = v * half
+            active_ref[here, :] = active.astype(BF)
+            slope = (1.0 - half) * active * (2 * GELU + (6 * GELU * CUBIC) * square)
             slope_ref[here, :] = (half + slope).astype(BF)
 
     return call(
@@ -526,13 +536,13 @@
     )
 
 
-def store_grads(meta, pieces, m, left, right_ref, odd):
+def store_grads(meta, pieces, m, left_ref, right_ref, odd):
     q = right_ref.shape[1] // 4
 
     @pl.loop(0, 4)
     def _(j):
         core, y = j // 2, j % 2
-        values = dot(left, right_ref[:, span(j, q)], TN).astype(BF)
+        values = dot(left_ref[...], right_ref[:, span(j, q)]).astype(BF)
         for piece_ref, half in zip(pieces, (THEIRS, OURS)):
 
             @pl.when(core == meta[half])
@@ -547,24 +557,26 @@
 
     def kernel(meta, cot_ref, small_ref, middle_ref, second_ref, active_ref, slope_ref, *refs):
         parts, refs = refs[:count], refs[count:]
-        out_ref, hidden_ref, *pieces, sums_ref, whole, out, sems = refs
+        out_ref, hidden_ref, *pieces, sums_ref, whole, out, flipped, sems = refs
         fetch(meta, parts, starts, whole, (0, width), sems.at[0])
-        store_grads(meta, pieces, 0, active_ref[...], cot_ref, False)
+        flipped[...] = active_ref[...].T
+        store_grads(meta, pieces, 0, flipped, cot_ref, False)
         fetched(whole, (0, width), sems.at[0])
 
         @blocks(rows)
-        def _(here):
+        def _(here, _):
             grad = dot(cot_ref[here, :], whole[...], NT)
             hidden_ref[here, :] = (slope_ref[here, :].astype(F32) * grad).astype(BF)
 
         @blocks(rows)
-        def _(here):
+        def _(here, _):
             values = middle_ref[here, :] + dot(active_ref[here, :], whole[...])
             out[here, :] = (values + small_ref[BD : BD + 1, :]).astype(BF)
 
         write = pltpu.make_async_copy(out, out_ref, sems.at[1])
         write.start()
-        store_grads(meta, pieces, 1, second_ref[...], hidden_ref, False)
+        flipped[...] = second_ref[...].T
+        store_grads(meta, pieces, 1, flipped, hidden_ref, False)
         sums_ref[...] = jnp.zeros_like(sums_ref)
         sums_ref[0:1, :] = column_sum(hidden_ref[...])
         sums_ref[1:2, :] = column_sum(cot_ref[...])
@@ -589,6 +601,7 @@
         [
             pltpu.VMEM((width, width), BF),
             pltpu.VMEM((rows, width), BF),
+            pltpu.VMEM((width, rows), BF),
             pltpu.SemaphoreType.DMA((2,)),
         ],
     )
@@ -601,13 +614,13 @@
 
     def kernel(meta, cot_ref, small_ref, middle_ref, hidden_ref, *refs):
         mixed_refs, parts = refs[: len(mixed)], refs[len(mixed) : len(mixed) + count]
-        attn_ref, *pieces, sums_ref, whole, sem = refs[len(mixed) + count :]
+        attn_ref, *pieces, sums_ref, whole, flipped, sem = refs[len(mixed) + count :]
         fetch(meta, parts, starts, whole, (0, width), sem, width)
         fetched(whole, (0, width), sem)
         sums_ref[...] = jnp.zeros_like(sums_ref)
 
         @blocks(rows)
-        def _(here):
+        def _(here, _):
             grad_second = dot(hidden_ref[here, :], whole[...], NT)
             normed, scale = normed_rows(middle_ref[here, :])
             back = norm_back(grad_second * small_ref[G2 : G2 + 1, :], normed, scale)
@@ -617,8 +630,10 @@
             sums_ref[1:2, :] += column_sum(grad_second)
             sums_ref[2:3, :] += column_sum(grad_attn)
 
-        values = jnp.concatenate([r[...] for r in mixed_refs], axis=1)
-        store_grads(meta, pieces, 0, values, attn_ref, True)
+        for i, ref in enumerate(mixed_refs):
+            n = ref.shape[1]
+            flipped[i * n : (i + 1) * n, :] = ref[...].T
+        store_grads(meta, pieces, 0, flipped, attn_ref, True)
 
     piece = VMEM((2, 2, 4, 2, width // 8, 128), BF)
     return call(
@@ -629,7 +644,11 @@
         20,
         cost(4 * rows * width * width, 2 * 12 * rows * width),
         "feed_forward_third",
-        [pltpu.VMEM((width, width), BF), pltpu.SemaphoreType.DMA],
+        [
+            pltpu.VMEM((width, width), BF),
+            pltpu.VMEM((width, rows), BF),
+            pltpu.SemaphoreType.DMA,
+        ],
     )
 
 
@@ -646,7 +665,7 @@
         fetched(whole, (0, width), sems.at[0])
 
         @blocks(rows)
-        def _(here):
+        def _(here, _):
             grad_ref[here, :] = dot(attn_ref[here, :], whole[...], NT).astype(BF)
 
         write.wait()
@@ -835,26 +854,38 @@
         extra = jnp.pad(small, ((0, w_qkv.shape[0] - 16), (0, 0)))
         chunks[0] = jnp.concatenate([chunks[0], extra], axis=1)
         chunks += [jnp.concatenate([quarter(w_out), quarter(w_up)], axis=1), quarter(w_down)]
-        kept = []
-
-        def norm(tables):
-            kept.extend(first_norm(meta, x, tables))
-            return kept
-
-        chunks = gather_chunks(chunks, links, norm)
-        first, small = kept
         other = CoreSwap(links)
 
-    packed, probs, mixed, weights = [], [], [], []
-    for base, parts in zip(bases, chunks):
+        def visit(i, chunks):
+            if i == 0:
+                return ()
+            if i == 1:
+                kept.extend(first_norm(meta, x, [part for part, _ in chunks[0][:3]]))
+                return kept + other.early(chunks[0], 3)
+            return other.early(chunks[i - 1], 2) + forward(i - 2, chunks[i - 2])
+
+    packed, probs, mixed, weights, kept = [], [], [], [], []
+
+    def forward(i, parts):
         parts = parts if native else other(parts, *mixed)
-        a, b, c, d = attention_forward(meta, first, small, parts, base, count)
+        a, b, c, d = attention_forward(meta, kept[0], kept[1], parts, bases[i], count)
         packed.append(a)
         probs.append(b)
         mixed.append(c)
         weights.append(d)
+        return [c]
+
+    if native:
+        kept.extend((first, small))
+        for i in range(len(bases)):
+            forward(i, chunks[i])
+    else:
+        chunks = gather_chunks(chunks, links, visit)
+        for i in range(len(mixed), len(bases)):
+            forward(i, chunks[i])
+        first, small = kept
     outer, inner = chunks[len(bases) :]
-    outer = outer if native else other(outer, mixed[0])
+    outer = outer if native else other(outer, mixed[1])
     middle, second, active, slope = feed_forward_first(meta, x, small, mixed, outer)
     inner = inner if native else other(inner, mixed[1])
     out, hidden, send, keep, sums_two = feed_forward_second(

time: 264 us -> 257 us (0.973)
  waiting for transfers between devices: 61.2 us -> 47.2 us
  other arithmetic: 1.13 us -> 4.99 us
  local copies, waits for them, and re-layouts: 4.99 us -> 8.84 us
    ppermute x65, waiting for transfers between devices: 61.2 us -> 47.2 us  [move(): return lax.ppermute(value, AXES, pairs)]
  transfers between devices with their start and end apart: 65 -> 65, of which waited for: 20 -> 16; matrix products, arithmetic and copies ran while one was open for 1% -> 3% of each run, Pallas kernels for 39% -> 41%
where the time goes in v3:
time: 257 us
  Pallas kernels  133 us (52%)
  starting transfers between devices  61.8 us (24%)
  waiting for transfers between devices  47.2 us (18%)
  local copies, waits for them, and re-layouts  8.84 us (3%)
  other arithmetic  4.99 us (2%)
    pallas_call x21, Pallas kernels, call(): pl.pallas_call(kernel, out_shape=shapes, grid_spec=pltpu.PrefetchScalarGr...  133 us
    ppermute x65, starting transfers between devices, move(): return lax.ppermute(value, AXES, pairs)  61.8 us
    ppermute x65, waiting for transfers between devices, move(): return lax.ppermute(value, AXES, pairs)  47.2 us
  transfers between devices with their start and end apart: 65, of which 16 were waited for; matrix products, arithmetic and copies ran while one was open for 3% of the time, Pallas kernels for 41%

profile of v3, /device:TPU:0, one launch (start us, length us, event | category | flops | bytes accessed | tf_op | source)
XLA Modules:
  0.0 256.7 jit_solution(14181312802442924860)
XLA Ops:
  2.8 5.1 %collective-permute-start.2 = (bf16[32,1664]{1,0:T(8,128)(2,1)S(1)}, bf16[32,1664]{1,0:T(8,128)(2,1)S(1)}, u32[]{:S(2)}, u32[]{:S(2)}) collective-permute-start(bf16[32,1664]{1,0:T(8,128)(2,1)S(1)} %fusion.1), channel_id=1, source_target_pairs={{0,24},{1,25},{2,26},{3,27},{4,28},{5,29},{6,30},{7,31},{8,16},{9,... | collective-permute-start | bytes 319496 | tf_op jit(solution)/shard_map/ppermute | solution.py:104
  8.5 3.3 %collective-permute-done.2 = bf16[32,1664]{1,0:T(8,128)(2,1)S(1)} collective-permute-done((bf16[32,1664]{1,0:T(8,128)(2,1)S(1)}, bf16[32,1664]{1,0:T(8,128)(2,1)S(1)}, u32[]{:S(2)}, u32[]{:S(2)}) %collective-permute-start.2) | collective-permute-done | bytes 106528 | tf_op jit(solution)/shard_map/ppermute | solution.py:104
  11.8 5.1 %collective-permute-done.1 = bf16[32,1664]{1,0:T(8,128)(2,1)S(1)} collective-permute-done((bf16[32,1664]{1,0:T(8,128)(2,1)S(1)}, bf16[32,1664]{1,0:T(8,128)(2,1)S(1)}, u32[]{:S(2)}, u32[]{:S(2)}) %collective-permute-start.1) | collective-permute-done | bytes 106528 | tf_op jit(solution)/shard_map/ppermute | solution.py:104
  17.0 1.6 collective-permute-start.4
  18.5 1.5 collective-permute-start.3
  21.7 2.5 collective-permute-start.7
  24.3 1.9 collective-permute-start.5
  26.2 2.9 %collective-permute-done.4.two_ref.refs_2_ = bf16[4,32,1664]{2,1,0:T(8,128)(2,1)S(1)} collective-permute-done((bf16[4,32,1664]{2,1,0:T(8,128)(2,1)S(1)}, bf16[4,32,1664]{2,1,0:T(8,128)(2,1)S(1)}, u32[]{:S(2)}, u32[]{:S(2)}) %collective-permute-start.4) | collective-permute-done | bytes 426016 | tf_op jit(solution)/shard_map/ppermute | solution.py:104
  29.1 3.0 %collective-permute-done.6 = bf16[32,1536]{1,0:T(8,128)(2,1)S(1)} collective-permute-done((bf16[32,1536]{1,0:T(8,128)(2,1)S(1)}, bf16[32,1536]{1,0:T(8,128)(2,1)S(1)}, u32[]{:S(2)}, u32[]{:S(2)}) %collective-permute-start.6) | collective-permute-done | bytes 98336 | tf_op jit(solution)/shard_map/ppermute | solution.py:104
  37.1 1.9 collective-permute-start.16
  40.6 2.5 collective-permute-start.14
  43.1 2.1 first_norm.1
  45.3 4.7 %collective-permute-done.8.refs_3_.refs_2_ = bf16[4,32,3200]{2,1,0:T(8,128)(2,1)} collective-permute-done((bf16[4,32,3200]{2,1,0:T(8,128)(2,1)}, bf16[4,32,3200]{2,1,0:T(8,128)(2,1)}, u32[]{:S(2)}, u32[]{:S(2)}) %collective-permute-start.8) | collective-permute-done | bytes 819232 | tf_op jit(solution)/shard_map/ppermute | solution.py:104
  57.3 1.9 collective-permute-start.24
  59.3 2.5 collective-permute-start.22
  61.8 13.2 %attention_forward.2 = (bf16[1024,1536]{1,0:T(8,128)(2,1)}, bf16[4,2,512,512]{3,2,1,0:T(8,128)(2,1)}, bf16[1024,512]{1,0:T(8,128)(2,1)S(1)}, bf16[1024,1536]{1,0:T(8,128)(2,1)}) custom-call(s32[8]{0:T(128)S(1)} %stack.92.meta, bf16[1024,1024]{1,0:T(8,128)(2,1)S(1)} %get-tuple-element.96.first_ref, f32[16,1024]{1,0:T(8,128)S(1)} %get-tuple-element.95.small_ref, ...), custom_call_target="tpu_custom_call" | custom-call | flops 1 | bytes 1 | tf_op jit(solution)/shard_map/attention_forward/pallas_call | solution.py:36
  78.0 13.3 %attention_forward.3 = (bf16[1024,1536]{1,0:T(8,128)(2,1)}, bf16[4,2,512,512]{3,2,1,0:T(8,128)(2,1)}, bf16[1024,512]{1,0:T(8,128)(2,1)S(1)}, bf16[1024,1536]{1,0:T(8,128)(2,1)}) custom-call(s32[8]{0:T(128)S(1)} %stack.92.meta, bf16[1024,1024]{1,0:T(8,128)(2,1)S(1)} %get-tuple-element.96.first_ref, f32[16,1024]{1,0:T(8,128)S(1)} %get-tuple-element.95.small_ref, ...), custom_call_target="tpu_custom_call" | custom-call | flops 1 | bytes 1 | tf_op jit(solution)/shard_map/attention_forward/pallas_call | solution.py:36
  92.8 5.1 %collective-permute-done.30.refs_3_ = bf16[4,32,1024]{2,1,0:T(8,128)(2,1)S(1)} collective-permute-done((bf16[4,32,1024]{2,1,0:T(8,128)(2,1)S(1)}, bf16[4,32,1024]{2,1,0:T(8,128)(2,1)S(1)}, u32[]{:S(2)}, u32[]{:S(2)}) %collective-permute-start.30) | collective-permute-done | bytes 262176 | tf_op jit(solution)/shard_map/ppermute | solution.py:104
  97.9 11.2 %feed_forward_first.1 = (f32[1024,1024]{1,0:T(8,128)S(1)}, bf16[1024,1024]{1,0:T(8,128)(2,1)S(1)}, bf16[1024,1024]{1,0:T(8,128)(2,1)S(1)}, bf16[1024,1024]{1,0:T(8,128)(2,1)S(1)}) custom-call(s32[8]{0:T(128)S(1)} %stack.92.meta, bf16[1024,1024]{1,0:T(8,128)(2,1)S(1)} %bitcast.40, f32[16,1024]{1,0:T(8,128)S(1)} %get-tuple-element.95.small_ref, ...), custom_call_target="tpu_custom_call" | custom-call | flops 1 | bytes 1 | tf_op jit(solution)/shard_map/feed_forward_first/pallas_call | solution.py:36
  109.1 17.6 %feed_forward_second.1 = (bf16[1024,1024]{1,0:T(8,128)(2,1)}, bf16[1024,1024]{1,0:T(8,128)(2,1)S(1)}, bf16[2,2,4,4,128,128]{5,4,3,2,1,0:T(8,128)(2,1)S(1)}, bf16...) custom-call(s32[8]{0:T(128)S(1)} %stack.92.meta, bf16[1024,1024]{1,0:T(8,128)(2,1)S(1)} %bitcast.41, ...), custom_call_target="tpu_custom_call" | custom-call | flops 1 | bytes 1 | tf_op jit(solution)/shard_map/feed_forward_second/pallas_call | solution.py:36
  127.3 10.7 %feed_forward_third.1 = (bf16[1024,1024]{1,0:T(8,128)(2,1)S(1)}, bf16[2,2,4,2,128,128]{5,4,3,2,1,0:T(8,128)(2,1)S(1)}, bf16[2,2,4,2,128,128]{5,4,3,2,1,0:T(8,128)(2,1)S(1)}, f32[8,1024]{1,0:T(8,128)S(1)}) custom-call(s32[8]{0:T(128)S(1)} %stack.92.meta, bf16[1024,1024]{1,0:T(8,128)(2,1)S(1)} %bitcast.42, f32[16,1024]{1,0:T(8,128)S(1)} %get-tuple-element.95.small_ref, ...), custom_call_target="tpu_custom_call" | custom-call | flops 1 | bytes 1 | tf_op jit(solution)/shard_map/feed_forward_third/pallas_call | solution.py:36
  139.9 4.5 %mixed_grad.1 = (bf16[1024,1024]{1,0:T(8,128)(2,1)S(1)}, bf16[1024,1024]{1,0:T(8,128)(2,1)}) custom-call(s32[8]{0:T(128)S(1)} %stack.92.meta, bf16[1024,1024]{1,0:T(8,128)(2,1)S(1)} %get-tuple-element.124.attn_ref, bf16[4,32,2048]{2,1,0:T(8,128)(2,1)S(1)} %pad_maximum_fusion.refs_2_.refs_0_, ...), custom_call_target="tpu_custom_call" | custom-call | flops 1 | bytes 1 | tf_op jit(solution)/shard_map/mixed_grad/pallas_call | solution.py:36
  144.4 7.7 %attention_backward.4 = (bf16[1024,768]{1,0:T(8,128)(2,1)}, bf16[2,2,4,3,128,128]{5,4,3,2,1,0:T(8,128)(2,1)S(1)}) custom-call(s32[8]{0:T(128)S(1)} %stack.92.meta, bf16[1024,1024]{1,0:T(8,128)(2,1)S(1)} %get-tuple-element.96.first_ref, bf16[1024,1536]{1,0:T(8,128)(2,1)} %get-tuple-element.122.packed_ref, ...), custom_call_target="tpu_custom_call" | custom-call | flops 1 | bytes 1 | tf_op jit(solution)/shard_map/attention_backward/pallas_call | solution.py:36
  152.3 1.6 collective-permute-done.35.refs_2_.refs_7_
  155.8 7.7 %attention_backward.5 = (bf16[1024,768]{1,0:T(8,128)(2,1)}, bf16[2,2,4,3,128,128]{5,4,3,2,1,0:T(8,128)(2,1)S(1)}) custom-call(s32[8]{0:T(128)S(1)} %stack.92.meta, bf16[1024,1024]{1,0:T(8,128)(2,1)S(1)} %get-tuple-element.96.first_ref, bf16[1024,1536]{1,0:T(8,128)(2,1)} %get-tuple-element.122.packed_ref, ...), custom_call_target="tpu_custom_call" | custom-call | flops 1 | bytes 1 | tf_op jit(solution)/shard_map/attention_backward/pallas_call | solution.py:36
  163.5 7.9 %attention_backward.6 = (bf16[1024,768]{1,0:T(8,128)(2,1)}, bf16[2,2,4,3,128,128]{5,4,3,2,1,0:T(8,128)(2,1)S(1)}) custom-call(s32[8]{0:T(128)S(1)} %stack.92.meta, bf16[1024,1024]{1,0:T(8,128)(2,1)S(1)} %get-tuple-element.96.first_ref, bf16[1024,1536]{1,0:T(8,128)(2,1)} %get-tuple-element.132.packed_ref, ...), custom_call_target="tpu_custom_call" | custom-call | flops 1 | bytes 1 | tf_op jit(solution)/shard_map/attention_backward/pallas_call | solution.py:36
  171.5 1.5 step_2.1
  174.2 2.5 collective-permute-start.40
  176.7 1.9 collective-permute-start.41
  178.6 7.7 %attention_backward.7 = (bf16[1024,768]{1,0:T(8,128)(2,1)}, bf16[2,2,4,3,128,128]{5,4,3,2,1,0:T(8,128)(2,1)S(1)}) custom-call(s32[8]{0:T(128)S(1)} %stack.92.meta, bf16[1024,1024]{1,0:T(8,128)(2,1)S(1)} %get-tuple-element.96.first_ref, bf16[1024,1536]{1,0:T(8,128)(2,1)} %get-tuple-element.132.packed_ref, ...), custom_call_target="tpu_custom_call" | custom-call | flops 1 | bytes 1 | tf_op jit(solution)/shard_map/attention_backward/pallas_call | solution.py:36
  187.9 1.8 step_3.1
  191.0 1.5 collective-permute-start.45
  193.5 1.9 collective-permute-start.47
  195.4 12.4 %input_grad.1 = (bf16[1024,1024]{1,0:T(8,128)(2,1)}, f32[8,1024]{1,0:T(8,128)S(1)}, f32[8,3072]{1,0:T(8,128)S(1)}) custom-call(s32[8]{0:T(128)S(1)} %stack.92.meta, bf16[1024,1024]{1,0:T(8,128)(2,1)} %bitcast.38, bf16[1024,1024]{1,0:T(8,128)(2,1)} %get-tuple-element.145.grad_ref, f32[16,1024]{1,0:T(8,128)S(1)} %get-tuple-element.95.small_ref, ...), custom_call_target="tpu_custom_call" | custom-call | flops 1 | bytes 1 | tf_op jit(solution)/shard_map/input_grad/pallas_call | solution.py:36
  207.8 4.2 %step_4.1 = (bf16[12,128,128]{2,1,0:T(8,128)(2,1)S(1)}, f32[4,128,128]{2,1,0:T(8,128)S(1)}, bf16[4,128,128]{2,1,0:T(8,128)(2,1)S(1)}, bf16[4,128,128]{2,1,0:T(8,...) custom-call(s32[8]{0:T(128)S(1)} %stack.92.meta, ...), custom_call_target="tpu_custom_call" | custom-call | flops 1 | bytes 1 | tf_op jit(solution)/shard_map/step_4/pallas_call | solution.py:36
  213.8 1.5 collective-permute-start.50
  215.3 1.9 collective-permute-start.51
  217.2 2.8 %collective-permute-done.49.refs_5_ = bf16[4,128,128]{2,1,0:T(8,128)(2,1)S(1)} collective-permute-done((bf16[4,128,128]{2,1,0:T(8,128)(2,1)S(1)}, bf16[4,128,128]{2,1,0:T(8,128)(2,1)S(1)}, u32[]{:S(2)}, u32[]{:S(2)}) %collective-permute-start.49) | collective-permute-done | bytes 131104 | tf_op jit(solution)/shard_map/ppermute | solution.py:104
  220.0 4.4 %collective-permute-done.50.refs_6_ = bf16[4,128,128]{2,1,0:T(8,128)(2,1)S(1)} collective-permute-done((bf16[4,128,128]{2,1,0:T(8,128)(2,1)S(1)}, bf16[4,128,128]{2,1,0:T(8,128)(2,1)S(1)}, u32[]{:S(2)}, u32[]{:S(2)}) %collective-permute-start.50) | collective-permute-done | bytes 131104 | tf_op jit(solution)/shard_map/ppermute | solution.py:104
  224.4 2.2 step_5.1
  226.6 2.0 collective-permute-start.55
  229.1 1.9 collective-permute-start.57
  233.8 4.1 %collective-permute-done.56.refs_2_ = bf16[3,128,128]{2,1,0:T(8,128)(2,1)S(1)} collective-permute-done((bf16[3,128,128]{2,1,0:T(8,128)(2,1)S(1)}, bf16[3,128,128]{2,1,0:T(8,128)(2,1)S(1)}, u32[]{:S(2)}, u32[]{:S(2)}) %collective-permute-start.56) | collective-permute-done | bytes 98336 | tf_op jit(solution)/shard_map/ppermute | solution.py:104
  237.9 1.5 collective-permute-start.53
  239.7 6.3 %collective-permute-done.53.refs_6_.refs_2_ = bf16[4,128,128]{2,1,0:T(8,128)(2,1)S(1)} collective-permute-done((bf16[4,128,128]{2,1,0:T(8,128)(2,1)S(1)}, bf16[4,128,128]{2,1,0:T(8,128)(2,1)S(1)}, u32[]{:S(2)}, u32[]{:S(2)}) %collective-permute-start.53) | collective-permute-done | bytes 131104 | tf_op jit(solution)/shard_map/ppermute | solution.py:104
  246.0 1.5 step_6.1
  250.7 1.8 finish_rest.1
  254.8 1.9 finish_heads.1
  (151 shorter events, 43.5 us)
Async XLA Ops:
  2.8 9.0 %collective-permute-start.2 = (bf16[32,1664]{1,0:T(8,128)(2,1)S(1)}, bf16[32,1664]{1,0:T(8,128)(2,1)S(1)}, u32[]{:S(2)}, u32[]{:S(2)}) collective-permute-start(bf16[32,1664]{1,0:T(8,128)(2,1)S(1)} %fusion.1), channel_id=1, source_target_pairs={{0,24},{1,25},{2,26},{3,27},{4,28},{5,29},{6,30},{7,31},{8,16},{9,... | collective-permute-start | bytes 319496 | tf_op jit(solution)/shard_map/ppermute | solution.py:104
  7.9 9.0 %collective-permute-start.1 = (bf16[32,1664]{1,0:T(8,128)(2,1)S(1)}, bf16[32,1664]{1,0:T(8,128)(2,1)S(1)}, u32[]{:S(2)}, u32[]{:S(2)}) collective-permute-start(bf16[32,1664]{1,0:T(8,128)(2,1)S(1)} %fusion.1), channel_id=1, source_target_pairs={{0,16},{1,17},{2,18},{3,19},{4,20},{5,21},{6,22},{7,23},{8,24},{9,... | collective-permute-start | bytes 319496 | tf_op jit(solution)/shard_map/ppermute | solution.py:104
  7.9 9.0 %collective-permute-start = (bf16[32,1664]{1,0:T(8,128)(2,1)S(1)}, bf16[32,1664]{1,0:T(8,128)(2,1)S(1)}, u32[]{:S(2)}, u32[]{:S(2)}) collective-permute-start(bf16[32,1664]{1,0:T(8,128)(2,1)S(1)} %fusion.1), channel_id=1, source_target_pairs={{0,8},{1,9},{2,10},{3,11},{4,12},{5,13},{6,14},{7,15},{8,0},{9,1},... | collective-permute-start | bytes 319496 | tf_op jit(solution)/shard_map/ppermute | solution.py:104
  17.0 12.2 %collective-permute-start.4 = (bf16[4,32,1664]{2,1,0:T(8,128)(2,1)S(1)}, bf16[4,32,1664]{2,1,0:T(8,128)(2,1)S(1)}, u32[]{:S(2)}, u32[]{:S(2)}) collective-permute-start(bf16[4,32,1664]{2,1,0:T(8,128)(2,1)S(1)} %pad_maximum_fusion.1.own_ref.refs_0_), channel_id=1, source_target_pairs={{0,4},{1,3},{2,6},{3,1},{4,0},{5,7},{6,2},{7,5},{8,12},{9,11},{10,... | collective-permute-start | bytes 1277960 | tf_op jit(solution)/shard_map/ppermute | solution.py:104
  18.5 13.6 %collective-permute-start.3 = (bf16[4,32,1664]{2,1,0:T(8,128)(2,1)S(1)}, bf16[4,32,1664]{2,1,0:T(8,128)(2,1)S(1)}, u32[]{:S(2)}, u32[]{:S(2)}) collective-permute-start(bf16[4,32,1664]{2,1,0:T(8,128)(2,1)S(1)} %pad_maximum_fusion.1.own_ref.refs_0_), channel_id=1, source_target_pairs={{0,2},{1,5},{2,0},{3,7},{4,6},{5,1},{6,4},{7,3},{8,10},{9,13},{10,... | collective-permute-start | bytes 1277960 | tf_op jit(solution)/shard_map/ppermute | solution.py:104
  24.3 7.9 %collective-permute-start.6 = (bf16[32,1536]{1,0:T(8,128)(2,1)S(1)}, bf16[32,1536]{1,0:T(8,128)(2,1)S(1)}, u32[]{:S(2)}, u32[]{:S(2)}) collective-permute-start(bf16[32,1536]{1,0:T(8,128)(2,1)S(1)} %reshape.44), channel_id=1, source_target_pairs={{0,16},{1,17},{2,18},{3,19},{4,20},{5,21},{6,22},{7,23},{8,24},{9,... | collective-permute-start | bytes 294920 | tf_op jit(solution)/shard_map/ppermute | solution.py:104
  24.3 7.9 %collective-permute-start.5 = (bf16[32,1536]{1,0:T(8,128)(2,1)S(1)}, bf16[32,1536]{1,0:T(8,128)(2,1)S(1)}, u32[]{:S(2)}, u32[]{:S(2)}) collective-permute-start(bf16[32,1536]{1,0:T(8,128)(2,1)S(1)} %reshape.44), channel_id=1, source_target_pairs={{0,8},{1,9},{2,10},{3,11},{4,12},{5,13},{6,14},{7,15},{8,0},{9,1},... | collective-permute-start | bytes 294920 | tf_op jit(solution)/shard_map/ppermute | solution.py:104
  33.1 16.9 %collective-permute-start.8 = (bf16[4,32,3200]{2,1,0:T(8,128)(2,1)}, bf16[4,32,3200]{2,1,0:T(8,128)(2,1)}, u32[]{:S(2)}, u32[]{:S(2)}) collective-permute-start(bf16[4,32,3200]{2,1,0:T(8,128)(2,1)} %maximum_maximum_fusion.1), channel_id=1, source_target_pairs={{0,4},{1,3},{2,6},{3,1},{4,0},{5,7},{6,2},{7,5},{8,12},{9,11},{10,... | collective-permute-start | bytes 2457608 | tf_op jit(solution)/shard_map/ppermute | solution.py:104
  35.0 16.1 %collective-permute-start.13 = (bf16[4,32,1536]{2,1,0:T(8,128)(2,1)}, bf16[4,32,1536]{2,1,0:T(8,128)(2,1)}, u32[]{:S(2)}, u32[]{:S(2)}) collective-permute-start(bf16[4,32,1536]{2,1,0:T(8,128)(2,1)} %pad_maximum_fusion.2.refs_0_), channel_id=1, source_target_pairs={{0,2},{1,5},{2,0},{3,7},{4,6},{5,1},{6,4},{7,3},{8,10},{9,13},{10,... | collective-permute-start | bytes 1179656 | tf_op jit(solution)/shard_map/ppermute | solution.py:104
  37.1 12.8 %collective-permute-start.16 = (bf16[32,2048]{1,0:T(8,128)(2,1)S(1)}, bf16[32,2048]{1,0:T(8,128)(2,1)}, u32[]{:S(2)}, u32[]{:S(2)}) collective-permute-start(bf16[32,2048]{1,0:T(8,128)(2,1)S(1)} %pad_maximum_fusion.4), channel_id=1, source_target_pairs={{0,24},{1,25},{2,26},{3,27},{4,28},{5,29},{6,30},{7,31},{8,16},{9,... | collective-permute-start | bytes 393224 | tf_op jit(solution)/shard_map/ppermute | solution.py:104
  39.8 11.2 %collective-permute-start.15 = (bf16[32,2048]{1,0:T(8,128)(2,1)S(1)}, bf16[32,2048]{1,0:T(8,128)(2,1)}, u32[]{:S(2)}, u32[]{:S(2)}) collective-permute-start(bf16[32,2048]{1,0:T(8,128)(2,1)S(1)} %pad_maximum_fusion.4), channel_id=1, source_target_pairs={{0,16},{1,17},{2,18},{3,19},{4,20},{5,21},{6,22},{7,23},{8,24},{9,... | collective-permute-start | bytes 393224 | tf_op jit(solution)/shard_map/ppermute | solution.py:104
  40.6 10.4 %collective-permute-start.14 = (bf16[32,2048]{1,0:T(8,128)(2,1)S(1)}, bf16[32,2048]{1,0:T(8,128)(2,1)}, u32[]{:S(2)}, u32[]{:S(2)}) collective-permute-start(bf16[32,2048]{1,0:T(8,128)(2,1)S(1)} %pad_maximum_fusion.4), channel_id=1, source_target_pairs={{0,8},{1,9},{2,10},{3,11},{4,12},{5,13},{6,14},{7,15},{8,0},{9,1},... | collective-permute-start | bytes 393224 | tf_op jit(solution)/shard_map/ppermute | solution.py:104
  52.3 22.6 %collective-permute-start.17 = (bf16[4,32,3584]{2,1,0:T(8,128)(2,1)S(1)}, bf16[4,32,3584]{2,1,0:T(8,128)(2,1)S(1)}, u32[]{:S(2)}, u32[]{:S(2)}) collective-permute-start(bf16[4,32,3584]{2,1,0:T(8,128)(2,1)S(1)} %maximum_maximum_fusion), channel_id=1, source_target_pairs={{0,4},{1,3},{2,6},{3,1},{4,0},{5,7},{6,2},{7,5},{8,12},{9,11},{10,... | collective-permute-start | bytes 2752520 | tf_op jit(solution)/shard_map/ppermute | solution.py:104
  54.2 20.8 %collective-permute-start.21 = (bf16[4,32,2048]{2,1,0:T(8,128)(2,1)S(1)}, bf16[4,32,2048]{2,1,0:T(8,128)(2,1)S(1)}, u32[]{:S(2)}, u32[]{:S(2)}) collective-permute-start(bf16[4,32,2048]{2,1,0:T(8,128)(2,1)S(1)} %pad_maximum_fusion.refs_2_.refs_0_), channel_id=1, source_target_pairs={{0,2},{1,5},{2,0},{3,7},{4,6},{5,1},{6,4},{7,3},{8,10},{9,13},{10,... | collective-permute-start | bytes 1572872 | tf_op jit(solution)/shard_map/ppermute | solution.py:104
  57.3 17.7 %collective-permute-start.24 = (bf16[32,1024]{1,0:T(8,128)(2,1)S(1)}, bf16[32,1024]{1,0:T(8,128)(2,1)S(1)}, u32[]{:S(2)}, u32[]{:S(2)}) collective-permute-start(bf16[32,1024]{1,0:T(8,128)(2,1)S(1)} %constant_dynamic-slice_fusion), channel_id=1, source_target_pairs={{0,24},{1,25},{2,26},{3,27},{4,28},{5,29},{6,30},{7,31},{8,16},{9,... | collective-permute-start | bytes 196616 | tf_op jit(solution)/shard_map/ppermute | solution.py:104
  59.3 15.8 %collective-permute-start.23 = (bf16[32,1024]{1,0:T(8,128)(2,1)S(1)}, bf16[32,1024]{1,0:T(8,128)(2,1)S(1)}, u32[]{:S(2)}, u32[]{:S(2)}) collective-permute-start(bf16[32,1024]{1,0:T(8,128)(2,1)S(1)} %constant_dynamic-slice_fusion), channel_id=1, source_target_pairs={{0,16},{1,17},{2,18},{3,19},{4,20},{5,21},{6,22},{7,23},{8,24},{9,... | collective-permute-start | bytes 196616 | tf_op jit(solution)/shard_map/ppermute | solution.py:104
  59.3 15.8 %collective-permute-start.22 = (bf16[32,1024]{1,0:T(8,128)(2,1)S(1)}, bf16[32,1024]{1,0:T(8,128)(2,1)S(1)}, u32[]{:S(2)}, u32[]{:S(2)}) collective-permute-start(bf16[32,1024]{1,0:T(8,128)(2,1)S(1)} %constant_dynamic-slice_fusion), channel_id=1, source_target_pairs={{0,8},{1,9},{2,10},{3,11},{4,12},{5,13},{6,14},{7,15},{8,0},{9,1},... | collective-permute-start | bytes 196616 | tf_op jit(solution)/shard_map/ppermute | solution.py:104
  75.1 16.2 %collective-permute-start.25 = (bf16[4,32,3072]{2,1,0:T(8,128)(2,1)S(1)}, bf16[4,32,3072]{2,1,0:T(8,128)(2,1)S(1)}, u32[]{:S(2)}, u32[]{:S(2)}) collective-permute-start(bf16[4,32,3072]{2,1,0:T(8,128)(2,1)S(1)} %maximum_maximum_fusion.2), channel_id=1, source_target_pairs={{0,4},{1,3},{2,6},{3,1},{4,0},{5,7},{6,2},{7,5},{8,12},{9,11},{10,... | collective-permute-start | bytes 2359304 | tf_op jit(solution)/shard_map/ppermute | solution.py:104
  76.1 15.4 %collective-permute-start.26 = (bf16[4,32,2048]{2,1,0:T(8,128)(2,1)S(1)}, bf16[4,32,2048]{2,1,0:T(8,128)(2,1)S(1)}, u32[]{:S(2)}, u32[]{:S(2)}) collective-permute-start(bf16[4,32,2048]{2,1,0:T(8,128)(2,1)S(1)} %pad_maximum_fusion.refs_2_.refs_0_), channel_id=1, source_target_pairs={{0,1},{1,0},{2,3},{3,2},{4,5},{5,4},{6,7},{7,6},{8,9},{9,8},{10,11... | collective-permute-start | bytes 1572872 | tf_op jit(solution)/shard_map/ppermute | solution.py:104
  76.3 15.1 %collective-permute-start.27 = (bf16[4,32,2048]{2,1,0:T(8,128)(2,1)S(1)}, bf16[4,32,2048]{2,1,0:T(8,128)(2,1)S(1)}, u32[]{:S(2)}, u32[]{:S(2)}) collective-permute-start(bf16[4,32,2048]{2,1,0:T(8,128)(2,1)S(1)} %collective-permute-done.21.refs_3_.refs_1_), channel_id=1, source_target_pairs={{0,1},{1,0},{2,3},{3,2},{4,5},{5,4},{6,7},{7,6},{8,9},{9,8},{10,11... | collective-permute-start | bytes 1572872 | tf_op jit(solution)/shard_map/ppermute | solution.py:104
  76.6 14.8 %collective-permute-start.29 = (bf16[4,32,1024]{2,1,0:T(8,128)(2,1)S(1)}, bf16[4,32,1024]{2,1,0:T(8,128)(2,1)S(1)}, u32[]{:S(2)}, u32[]{:S(2)}) collective-permute-start(bf16[4,32,1024]{2,1,0:T(8,128)(2,1)S(1)} %pad_maximum_fusion.3.refs_0_), channel_id=1, source_target_pairs={{0,2},{1,5},{2,0},{3,7},{4,6},{5,1},{6,4},{7,3},{8,10},{9,13},{10,... | collective-permute-start | bytes 786440 | tf_op jit(solution)/shard_map/ppermute | solution.py:104
  92.3 16.8 %collective-permute-start.31 = (bf16[4,32,1024]{2,1,0:T(8,128)(2,1)S(1)}, bf16[4,32,1024]{2,1,0:T(8,128)(2,1)S(1)}, u32[]{:S(2)}, u32[]{:S(2)}) collective-permute-start(bf16[4,32,1024]{2,1,0:T(8,128)(2,1)S(1)} %pad_maximum_fusion.3.refs_0_), channel_id=1, source_target_pairs={{0,1},{1,0},{2,3},{3,2},{4,5},{5,4},{6,7},{7,6},{8,9},{9,8},{10,11... | collective-permute-start | bytes 786440 | tf_op jit(solution)/shard_map/ppermute | solution.py:104
  92.5 16.6 %collective-permute-start.32 = (bf16[4,32,1024]{2,1,0:T(8,128)(2,1)S(1)}, bf16[4,32,1024]{2,1,0:T(8,128)(2,1)S(1)}, u32[]{:S(2)}, u32[]{:S(2)}) collective-permute-start(bf16[4,32,1024]{2,1,0:T(8,128)(2,1)S(1)} %collective-permute-done.29.refs_1_), channel_id=1, source_target_pairs={{0,1},{1,0},{2,3},{3,2},{4,5},{5,4},{6,7},{7,6},{8,9},{9,8},{10,11... | collective-permute-start | bytes 786440 | tf_op jit(solution)/shard_map/ppermute | solution.py:104
  97.9 11.2 %collective-permute-start.33 = (bf16[4,32,1024]{2,1,0:T(8,128)(2,1)S(1)}, bf16[4,32,1024]{2,1,0:T(8,128)(2,1)S(1)}, u32[]{:S(2)}, u32[]{:S(2)}) collective-permute-start(bf16[4,32,1024]{2,1,0:T(8,128)(2,1)S(1)} %collective-permute-done.30.refs_3_), channel_id=1, source_target_pairs={{0,1},{1,0},{2,3},{3,2},{4,5},{5,4},{6,7},{7,6},{8,9},{9,8},{10,11... | collective-permute-start | bytes 786440 | tf_op jit(solution)/shard_map/ppermute | solution.py:104
  126.7 11.4 %collective-permute-start.34 = (bf16[2,2,4,4,128,128]{5,4,3,2,1,0:T(8,128)(2,1)S(1)}, bf16[2,2,4,4,128,128]{5,4,3,2,1,0:T(8,128)(2,1)S(1)}, u32[]{:S(2)}, u32[]{:S(2)}) collective-permute-start(bf16[2,2,4,4,128,128]{5,4,3,2,1,0:T(8,128)(2,1)S(1)} %get-tuple-element.120), channel_id=1, source_target_pairs={{0,1},{1,0},{2,3},{3,2},{4,5},{5,4},{6,7},{7,6},{8,9},{9,8},{10,11... | collective-permute-start | bytes 6291464 | tf_op jit(solution)/shard_map/ppermute | solution.py:104
  138.0 14.3 %collective-permute-start.36 = (bf16[2,2,4,2,128,128]{5,4,3,2,1,0:T(8,128)(2,1)S(1)}, bf16[2,2,4,2,128,128]{5,4,3,2,1,0:T(8,128)(2,1)S(1)}, u32[]{:S(2)}, u32[]{:S(2)}) collective-permute-start(bf16[2,2,4,2,128,128]{5,4,3,2,1,0:T(8,128)(2,1)S(1)} %get-tuple-element.128), channel_id=1, source_target_pairs={{0,1},{1,0},{2,3},{3,2},{4,5},{5,4},{6,7},{7,6},{8,9},{9,8},{10,11... | collective-permute-start | bytes 3145736 | tf_op jit(solution)/shard_map/ppermute | solution.py:104
  139.1 14.9 %collective-permute-start.35 = (bf16[32,128,128]{2,1,0:T(8,128)(2,1)S(1)}, bf16[32,128,128]{2,1,0:T(8,128)(2,1)S(1)}, u32[]{:S(2)}, u32[]{:S(2)}) collective-permute-start(bf16[32,128,128]{2,1,0:T(8,128)(2,1)S(1)} %step_0.1), channel_id=1, source_target_pairs={{0,4},{1,3},{2,6},{3,1},{4,0},{5,7},{6,2},{7,5},{8,12},{9,11},{10,... | collective-permute-start | bytes 3145736 | tf_op jit(solution)/shard_map/ppermute | solution.py:104
  152.1 19.4 %collective-permute-start.38 = (bf16[2,2,4,3,128,128]{5,4,3,2,1,0:T(8,128)(2,1)S(1)}, bf16[2,2,4,3,128,128]{5,4,3,2,1,0:T(8,128)(2,1)S(1)}, u32[]{:S(2)}, u32[]{:S(2)}) collective-permute-start(bf16[2,2,4,3,128,128]{5,4,3,2,1,0:T(8,128)(2,1)S(1)} %get-tuple-element.126), channel_id=1, source_target_pairs={{0,1},{1,0},{2,3},{3,2},{4,5},{5,4},{6,7},{7,6},{8,9},{9,8},{10,11... | collective-permute-start | bytes 4718600 | tf_op jit(solution)/shard_map/ppermute | solution.py:104
  155.0 16.5 %collective-permute-start.37 = (bf16[32,128,128]{2,1,0:T(8,128)(2,1)S(1)}, bf16[32,128,128]{2,1,0:T(8,128)(2,1)S(1)}, u32[]{:S(2)}, u32[]{:S(2)}) collective-permute-start(bf16[32,128,128]{2,1,0:T(8,128)(2,1)S(1)} %step_1.1), channel_id=1, source_target_pairs={{0,2},{1,5},{2,0},{3,7},{4,6},{5,1},{6,4},{7,3},{8,10},{9,13},{10,... | collective-permute-start | bytes 3145736 | tf_op jit(solution)/shard_map/ppermute | solution.py:104
  171.4 15.7 %collective-permute-start.43 = (bf16[2,2,4,3,128,128]{5,4,3,2,1,0:T(8,128)(2,1)S(1)}, bf16[2,2,4,3,128,128]{5,4,3,2,1,0:T(8,128)(2,1)S(1)}, u32[]{:S(2)}, u32[]{:S(2)}) collective-permute-start(bf16[2,2,4,3,128,128]{5,4,3,2,1,0:T(8,128)(2,1)S(1)} %get-tuple-element.134), channel_id=1, source_target_pairs={{0,1},{1,0},{2,3},{3,2},{4,5},{5,4},{6,7},{7,6},{8,9},{9,8},{10,11... | collective-permute-start | bytes 4718600 | tf_op jit(solution)/shard_map/ppermute | solution.py:104
  173.0 14.9 %collective-permute-start.42 = (bf16[32,128,128]{2,1,0:T(8,128)(2,1)S(1)}, bf16[32,128,128]{2,1,0:T(8,128)(2,1)S(1)}, u32[]{:S(2)}, u32[]{:S(2)}) collective-permute-start(bf16[32,128,128]{2,1,0:T(8,128)(2,1)S(1)} %get-tuple-element.136), channel_id=1, source_target_pairs={{0,4},{1,3},{2,6},{3,1},{4,0},{5,7},{6,2},{7,5},{8,12},{9,11},{10,... | collective-permute-start | bytes 3145736 | tf_op jit(solution)/shard_map/ppermute | solution.py:104
  174.2 12.1 %collective-permute-start.39 = (bf16[4,128,128]{2,1,0:T(8,128)(2,1)S(1)}, bf16[4,128,128]{2,1,0:T(8,128)(2,1)S(1)}, u32[]{:S(2)}, u32[]{:S(2)}) collective-permute-start(bf16[4,128,128]{2,1,0:T(8,128)(2,1)S(1)} %get-tuple-element.139), channel_id=1, source_target_pairs={{0,8},{1,9},{2,10},{3,11},{4,12},{5,13},{6,14},{7,15},{8,0},{9,1},... | collective-permute-start | bytes 393224 | tf_op jit(solution)/shard_map/ppermute | solution.py:104
  174.2 12.9 %collective-permute-start.40 = (bf16[4,128,128]{2,1,0:T(8,128)(2,1)S(1)}, bf16[4,128,128]{2,1,0:T(8,128)(2,1)S(1)}, u32[]{:S(2)}, u32[]{:S(2)}) collective-permute-start(bf16[4,128,128]{2,1,0:T(8,128)(2,1)S(1)} %get-tuple-element.140), channel_id=1, source_target_pairs={{0,16},{1,17},{2,18},{3,19},{4,20},{5,21},{6,22},{7,23},{8,24},{9,... | collective-permute-start | bytes 393224 | tf_op jit(solution)/shard_map/ppermute | solution.py:104
  176.7 10.4 %collective-permute-start.41 = (bf16[4,128,128]{2,1,0:T(8,128)(2,1)S(1)}, bf16[4,128,128]{2,1,0:T(8,128)(2,1)S(1)}, u32[]{:S(2)}, u32[]{:S(2)}) collective-permute-start(bf16[4,128,128]{2,1,0:T(8,128)(2,1)S(1)} %get-tuple-element.141), channel_id=1, source_target_pairs={{0,24},{1,25},{2,26},{3,27},{4,28},{5,29},{6,30},{7,31},{8,16},{9,... | collective-permute-start | bytes 393224 | tf_op jit(solution)/shard_map/ppermute | solution.py:104
  189.7 18.1 %collective-permute-start.44 = (bf16[36,128,128]{2,1,0:T(8,128)(2,1)S(1)}, bf16[36,128,128]{2,1,0:T(8,128)(2,1)S(1)}, u32[]{:S(2)}, u32[]{:S(2)}) collective-permute-start(bf16[36,128,128]{2,1,0:T(8,128)(2,1)S(1)} %get-tuple-element.143), channel_id=1, source_target_pairs={{0,2},{1,5},{2,0},{3,7},{4,6},{5,1},{6,4},{7,3},{8,10},{9,13},{10,... | collective-permute-start | bytes 3538952 | tf_op jit(solution)/shard_map/ppermute | solution.py:104
  191.0 16.8 %collective-permute-start.45 = (bf16[2,128,128]{2,1,0:T(8,128)(2,1)S(1)}, bf16[2,128,128]{2,1,0:T(8,128)(2,1)S(1)}, u32[]{:S(2)}, u32[]{:S(2)}) collective-permute-start(bf16[2,128,128]{2,1,0:T(8,128)(2,1)S(1)} %get-tuple-element.160), channel_id=1, source_target_pairs={{0,8},{1,9},{2,10},{3,11},{4,12},{5,13},{6,14},{7,15},{8,0},{9,1},... | collective-permute-start | bytes 196616 | tf_op jit(solution)/shard_map/ppermute | solution.py:104
  192.6 15.3 %collective-permute-start.46 = (bf16[2,128,128]{2,1,0:T(8,128)(2,1)S(1)}, bf16[2,128,128]{2,1,0:T(8,128)(2,1)S(1)}, u32[]{:S(2)}, u32[]{:S(2)}) collective-permute-start(bf16[2,128,128]{2,1,0:T(8,128)(2,1)S(1)} %get-tuple-element.161), channel_id=1, source_target_pairs={{0,16},{1,17},{2,18},{3,19},{4,20},{5,21},{6,22},{7,23},{8,24},{9,... | collective-permute-start | bytes 196616 | tf_op jit(solution)/shard_map/ppermute | solution.py:104
  193.5 14.3 %collective-permute-start.47 = (bf16[2,128,128]{2,1,0:T(8,128)(2,1)S(1)}, bf16[2,128,128]{2,1,0:T(8,128)(2,1)S(1)}, u32[]{:S(2)}, u32[]{:S(2)}) collective-permute-start(bf16[2,128,128]{2,1,0:T(8,128)(2,1)S(1)} %get-tuple-element.162), channel_id=1, source_target_pairs={{0,24},{1,25},{2,26},{3,27},{4,28},{5,29},{6,30},{7,31},{8,16},{9,... | collective-permute-start | bytes 196616 | tf_op jit(solution)/shard_map/ppermute | solution.py:104
  212.0 12.4 %collective-permute-start.48 = (bf16[12,128,128]{2,1,0:T(8,128)(2,1)S(1)}, bf16[12,128,128]{2,1,0:T(8,128)(2,1)S(1)}, u32[]{:S(2)}, u32[]{:S(2)}) collective-permute-start(bf16[12,128,128]{2,1,0:T(8,128)(2,1)S(1)} %get-tuple-element.163), channel_id=1, source_target_pairs={{0,4},{1,3},{2,6},{3,1},{4,0},{5,7},{6,2},{7,5},{8,12},{9,11},{10,... | collective-permute-start | bytes 1179656 | tf_op jit(solution)/shard_map/ppermute | solution.py:104
  213.8 10.6 %collective-permute-start.50 = (bf16[4,128,128]{2,1,0:T(8,128)(2,1)S(1)}, bf16[4,128,128]{2,1,0:T(8,128)(2,1)S(1)}, u32[]{:S(2)}, u32[]{:S(2)}) collective-permute-start(bf16[4,128,128]{2,1,0:T(8,128)(2,1)S(1)} %get-tuple-element.166), channel_id=1, source_target_pairs={{0,16},{1,17},{2,18},{3,19},{4,20},{5,21},{6,22},{7,23},{8,24},{9,... | collective-permute-start | bytes 393224 | tf_op jit(solution)/shard_map/ppermute | solution.py:104
  215.3 9.1 %collective-permute-start.51 = (bf16[4,128,128]{2,1,0:T(8,128)(2,1)S(1)}, bf16[4,128,128]{2,1,0:T(8,128)(2,1)S(1)}, u32[]{:S(2)}, u32[]{:S(2)}) collective-permute-start(bf16[4,128,128]{2,1,0:T(8,128)(2,1)S(1)} %get-tuple-element.167), channel_id=1, source_target_pairs={{0,24},{1,25},{2,26},{3,27},{4,28},{5,29},{6,30},{7,31},{8,16},{9,... | collective-permute-start | bytes 393224 | tf_op jit(solution)/shard_map/ppermute | solution.py:104
  228.6 9.3 %collective-permute-start.56 = (bf16[3,128,128]{2,1,0:T(8,128)(2,1)S(1)}, bf16[3,128,128]{2,1,0:T(8,128)(2,1)S(1)}, u32[]{:S(2)}, u32[]{:S(2)}) collective-permute-start(bf16[3,128,128]{2,1,0:T(8,128)(2,1)S(1)} %get-tuple-element.171), channel_id=1, source_target_pairs={{0,16},{1,17},{2,18},{3,19},{4,20},{5,21},{6,22},{7,23},{8,24},{9,... | collective-permute-start | bytes 294920 | tf_op jit(solution)/shard_map/ppermute | solution.py:104
  229.1 10.3 %collective-permute-start.54 = (bf16[4,128,128]{2,1,0:T(8,128)(2,1)S(1)}, bf16[4,128,128]{2,1,0:T(8,128)(2,1)S(1)}, u32[]{:S(2)}, u32[]{:S(2)}) collective-permute-start(bf16[4,128,128]{2,1,0:T(8,128)(2,1)S(1)} %get-tuple-element.168.refs_4_.refs_0_), channel_id=1, source_target_pairs={{0,3},{1,2},{2,1},{3,0},{4,7},{5,6},{6,5},{7,4},{8,11},{9,10},{10,... | collective-permute-start | bytes 393224 | tf_op jit(solution)/shard_map/ppermute | solution.py:104
  229.1 8.8 %collective-permute-start.57 = (bf16[3,128,128]{2,1,0:T(8,128)(2,1)S(1)}, bf16[3,128,128]{2,1,0:T(8,128)(2,1)S(1)}, u32[]{:S(2)}, u32[]{:S(2)}) collective-permute-start(bf16[3,128,128]{2,1,0:T(8,128)(2,1)S(1)} %get-tuple-element.172), channel_id=1, source_target_pairs={{0,24},{1,25},{2,26},{3,27},{4,28},{5,29},{6,30},{7,31},{8,16},{9,... | collective-permute-start | bytes 294920 | tf_op jit(solution)/shard_map/ppermute | solution.py:104
  231.0 17.7 %collective-permute-start.63 = (bf16[6,128,128]{2,1,0:T(8,128)(2,1)S(1)}, bf16[6,128,128]{2,1,0:T(8,128)(2,1)S(1)}, u32[]{:S(2)}, u32[]{:S(2)}) collective-permute-start(bf16[6,128,128]{2,1,0:T(8,128)(2,1)S(1)} %get-tuple-element.175.refs_0_), channel_id=1, source_target_pairs={{0,3},{1,2},{2,1},{3,0},{4,7},{5,6},{6,5},{7,4},{8,11},{9,10},{10,... | collective-permute-start | bytes 589832 | tf_op jit(solution)/shard_map/ppermute | solution.py:104
  232.5 17.1 %collective-permute-start.62 = (bf16[6,128,128]{2,1,0:T(8,128)(2,1)S(1)}, bf16[6,128,128]{2,1,0:T(8,128)(2,1)S(1)}, u32[]{:S(2)}, u32[]{:S(2)}) collective-permute-start(bf16[6,128,128]{2,1,0:T(8,128)(2,1)S(1)} %get-tuple-element.175.refs_0_), channel_id=1, source_target_pairs={{0,2},{1,3},{2,0},{3,1},{4,6},{5,7},{6,4},{7,5},{8,10},{9,11},{10,... | collective-permute-start | bytes 589832 | tf_op jit(solution)/shard_map/ppermute | solution.py:104
  237.9 12.8 %collective-permute-start.61 = (bf16[6,128,128]{2,1,0:T(8,128)(2,1)S(1)}, bf16[6,128,128]{2,1,0:T(8,128)(2,1)S(1)}, u32[]{:S(2)}, u32[]{:S(2)}) collective-permute-start(bf16[6,128,128]{2,1,0:T(8,128)(2,1)S(1)} %get-tuple-element.175.refs_0_), channel_id=1, source_target_pairs={{0,1},{1,0},{2,3},{3,2},{4,5},{5,4},{6,7},{7,6},{8,9},{9,8},{10,11... | collective-permute-start | bytes 589832 | tf_op jit(solution)/shard_map/ppermute | solution.py:104
  237.9 8.1 %collective-permute-start.53 = (bf16[4,128,128]{2,1,0:T(8,128)(2,1)S(1)}, bf16[4,128,128]{2,1,0:T(8,128)(2,1)S(1)}, u32[]{:S(2)}, u32[]{:S(2)}) collective-permute-start(bf16[4,128,128]{2,1,0:T(8,128)(2,1)S(1)} %get-tuple-element.168.refs_4_.refs_0_), channel_id=1, source_target_pairs={{0,2},{1,3},{2,0},{3,1},{4,6},{5,7},{6,4},{7,5},{8,10},{9,11},{10,... | collective-permute-start | bytes 393224 | tf_op jit(solution)/shard_map/ppermute | solution.py:104
  (29 other events, 212.8 us)

commit v4 on v3

--- a/solution.py
+++ b/solution.py
@@ -123,7 +123,8 @@
     for i, quarter in enumerate(quarters):
         quarter = after(quarter, *along)
         along = [move(quarter, p) for p in links.z]
-        own = jnp.stack([after(quarter, *across)] + along)
+        ahead = quarters[1:] if i == 0 else ()
+        own = jnp.stack([after(quarter, *across, *ahead)] + along)
         first = move(own, links.y_or_x)
         both = own if late is None else jnp.concatenate([late, own], axis=2)
         both = move(both, links.x_or_y)
@@ -372,10 +373,19 @@
     tm = 256
     last = tables[0].shape[2] - 128
 
-    def kernel(meta, x_ref, own_ref, one_ref, two_ref, first_ref, small_ref):
+    def kernel(meta, x_ref, *refs):
+        parts, (first_ref, small_ref, table, sems) = refs[:3], refs[3:]
+        copies = [
+            pltpu.make_async_copy(ref.at[:, pl.ds(0, 16), pl.ds(last, 128)], table.at[i], sems.at[i])
+            for i, ref in enumerate(parts)
+        ]
+        for copy in copies:
+            copy.start()
+        for copy in copies:
+            copy.wait()
         x, z = meta[XPOS], meta[ZPOS]
         for dz in range(4):
-            own, one, two = (r[dz, :16, last:].astype(F32) for r in (own_ref, one_ref, two_ref))
+            own, one, two = (table[i, dz].astype(F32) for i in range(3))
             for dx, values in enumerate((own, jnp.where(meta[CORE] == 1, one, two))):
                 small_ref[:, span((z ^ dz) * 2 + (x ^ dx), 128)] = values
 
@@ -388,11 +398,12 @@
     return call(
         kernel,
         meta,
-        [(a, None) for a in (x, *tables)],
+        [(x, None)] + [(a, ANY) for a in tables],
         [(VMEM((rows, width), BF), None), (shaped(F32, 16, width), None)],
         16,
         cost(rows * width * 20, rows * width * 4),
         "first_norm",
+        [pltpu.VMEM((3, 4, 16, 128), BF), pltpu.SemaphoreType.DMA((3,))],
     )
 
 
@@ -1004,23 +1015,30 @@
     )
 
     step = Step()
+    step.along(one, sums_of(sums_one, sums_packed))
+    z_one = step.run(after(meta, grad_x, *z_outs[1:]), "step_4")
+    step = Step()
     step.swap(seconds=[two])
-    step.along(one, sums_of(sums_one, sums_packed))
+    (sent,) = step.run(after(meta, z_one[0]), "step_5")
+    two.late.append((move(sent, links.x_or_y), 0))
+    step = Step()
     step.share([z_both, z_outs])
-    sent, *z_one, r_rest = step.run(after(meta, grad_x), "step_4")
-    two.late.append((move(sent, links.x_or_y), 0))
-    z_one, r_rest = along(z_one), share(r_rest)
+    (r_rest,) = step.run(after(meta, sent), "step_6")
+    z_one = along(z_one)
+    r_rest = share(after(r_rest, z_one[1]))
 
     step = Step()
     step.along(two)
+    z_two = step.run(after(meta, z_one[1]), "step_7")
+    step = Step()
     step.share([z_one])
-    *z_two, r_one = step.run(meta, "step_5")
+    (r_one,) = step.run(after(meta, z_two[0], *r_rest[1:]), "step_8")
     z_two, r_one = along(z_two), share(r_one)
 
     step = Step()
     step.share([z_two])
     step.small(r_one)
-    r_two, other, smalls = step.run(meta, "step_6")
+    r_two, other, smalls = step.run(meta, "step_9")
     smalls = smalls + move(other, links.x)
     rest = finish(
         after(meta, r_two),

time: 257 us -> 255 us (level)
  waiting for transfers between devices: 47.2 us -> 42.1 us
    ppermute x65, waiting for transfers between devices: 47.2 us -> 42.1 us  [move(): return lax.ppermute(value, AXES, pairs)]
    pallas_call x21 -> x24, Pallas kernels: 133 us -> 134 us  [call(): pl.pallas_call(kernel, out_shape=shapes, grid_spec=pltpu.PrefetchScalarGr...]
  transfers between devices with their start and end apart: 65 -> 65, of which waited for: 16 -> 16; matrix products, arithmetic and copies ran while one was open for 3% -> 3% of each run, Pallas kernels for 41% -> 42%
where the time goes in v4:
time: 255 us
  Pallas kernels  134 us (53%)
  starting transfers between devices  62.6 us (25%)
  waiting for transfers between devices  42.1 us (17%)
  local copies, waits for them, and re-layouts  8.75 us (3%)
  other arithmetic  5.89 us (2%)
    pallas_call x24, Pallas kernels, call(): pl.pallas_call(kernel, out_shape=shapes, grid_spec=pltpu.PrefetchScalarGr...  134 us
    ppermute x65, starting transfers between devices, move(): return lax.ppermute(value, AXES, pairs)  62.6 us
    ppermute x65, waiting for transfers between devices, move(): return lax.ppermute(value, AXES, pairs)  42.1 us
  transfers between devices with their start and end apart: 65, of which 16 were waited for; matrix products, arithmetic and copies ran while one was open for 3% of the time, Pallas kernels for 42%

profile of v4, /device:TPU:0, one launch (start us, length us, event | category | flops | bytes accessed | tf_op | source)
XLA Modules:
  0.0 254.8 jit_solution(11793425154250416907)
XLA Ops:
  2.8 5.1 %collective-permute-start.2 = (bf16[32,1664]{1,0:T(8,128)(2,1)S(1)}, bf16[32,1664]{1,0:T(8,128)(2,1)S(1)}, u32[]{:S(2)}, u32[]{:S(2)}) collective-permute-start(bf16[32,1664]{1,0:T(8,128)(2,1)S(1)} %fusion.1), channel_id=1, source_target_pairs={{0,24},{1,25},{2,26},{3,27},{4,28},{5,29},{6,30},{7,31},{8,16},{9,... | collective-permute-start | bytes 319496 | tf_op jit(solution)/shard_map/ppermute | solution.py:104
  10.3 1.6 constant_dynamic-slice_fusion
  11.9 5.0 %collective-permute-done.1 = bf16[32,1664]{1,0:T(8,128)(2,1)S(1)} collective-permute-done((bf16[32,1664]{1,0:T(8,128)(2,1)S(1)}, bf16[32,1664]{1,0:T(8,128)(2,1)S(1)}, u32[]{:S(2)}, u32[]{:S(2)}) %collective-permute-start.1) | collective-permute-done | bytes 106528 | tf_op jit(solution)/shard_map/ppermute | solution.py:104
  16.9 1.6 collective-permute-start.4
  18.5 1.5 collective-permute-start.3
  20.0 2.5 collective-permute-start.7
  22.5 1.9 collective-permute-start.5
  24.4 4.7 %collective-permute-done.4.refs_2_ = bf16[4,32,1664]{2,1,0:T(8,128)(2,1)S(1)} collective-permute-done((bf16[4,32,1664]{2,1,0:T(8,128)(2,1)S(1)}, bf16[4,32,1664]{2,1,0:T(8,128)(2,1)S(1)}, u32[]{:S(2)}, u32[]{:S(2)}) %collective-permute-start.4) | collective-permute-done | bytes 426016 | tf_op jit(solution)/shard_map/ppermute | solution.py:104
  29.1 1.5 collective-permute-done.6
  30.6 1.8 maximum_maximum_fusion.1
  35.6 1.9 collective-permute-start.16
  39.0 2.5 collective-permute-start.14
  41.6 2.1 first_norm.1
  43.7 5.6 %collective-permute-done.8.refs_3_.refs_2_ = bf16[4,32,3200]{2,1,0:T(8,128)(2,1)} collective-permute-done((bf16[4,32,3200]{2,1,0:T(8,128)(2,1)}, bf16[4,32,3200]{2,1,0:T(8,128)(2,1)}, u32[]{:S(2)}, u32[]{:S(2)}) %collective-permute-start.8) | collective-permute-done | bytes 819232 | tf_op jit(solution)/shard_map/ppermute | solution.py:104
  55.9 1.8 collective-permute-start.24
  57.7 2.6 %collective-permute-start.22 = (bf16[32,1024]{1,0:T(8,128)(2,1)S(1)}, bf16[32,1024]{1,0:T(8,128)(2,1)S(1)}, u32[]{:S(2)}, u32[]{:S(2)}) collective-permute-start(bf16[32,1024]{1,0:T(8,128)(2,1)S(1)} %copy-done.13), channel_id=1, source_target_pairs={{0,8},{1,9},{2,10},{3,11},{4,12},{5,13},{6,14},{7,15},{8,0},{9,1},... | collective-permute-start | bytes 196616 | tf_op jit(solution)/shard_map/ppermute | solution.py:104
  60.3 13.2 %attention_forward.2 = (bf16[1024,1536]{1,0:T(8,128)(2,1)}, bf16[4,2,512,512]{3,2,1,0:T(8,128)(2,1)}, bf16[1024,512]{1,0:T(8,128)(2,1)S(1)}, bf16[1024,1536]{1,0:T(8,128)(2,1)}) custom-call(s32[8]{0:T(128)S(1)} %stack.92.meta, bf16[1024,1024]{1,0:T(8,128)(2,1)S(1)} %get-tuple-element.100.first_ref, f32[16,1024]{1,0:T(8,128)S(1)} %get-tuple-element.99.small_ref, ...), custom_call_target="tpu_custom_call" | custom-call | flops 1 | bytes 1 | tf_op jit(solution)/shard_map/attention_forward/pallas_call | solution.py:36
  76.6 13.4 %attention_forward.3 = (bf16[1024,1536]{1,0:T(8,128)(2,1)}, bf16[4,2,512,512]{3,2,1,0:T(8,128)(2,1)}, bf16[1024,512]{1,0:T(8,128)(2,1)S(1)}, bf16[1024,1536]{1,0:T(8,128)(2,1)}) custom-call(s32[8]{0:T(128)S(1)} %stack.92.meta, bf16[1024,1024]{1,0:T(8,128)(2,1)S(1)} %get-tuple-element.100.first_ref, f32[16,1024]{1,0:T(8,128)S(1)} %get-tuple-element.99.small_ref, ...), custom_call_target="tpu_custom_call" | custom-call | flops 1 | bytes 1 | tf_op jit(solution)/shard_map/attention_forward/pallas_call | solution.py:36
  91.5 5.1 %collective-permute-done.30.refs_3_ = bf16[4,32,1024]{2,1,0:T(8,128)(2,1)S(1)} collective-permute-done((bf16[4,32,1024]{2,1,0:T(8,128)(2,1)S(1)}, bf16[4,32,1024]{2,1,0:T(8,128)(2,1)S(1)}, u32[]{:S(2)}, u32[]{:S(2)}) %collective-permute-start.30) | collective-permute-done | bytes 262176 | tf_op jit(solution)/shard_map/ppermute | solution.py:104
  96.6 11.2 %feed_forward_first.1 = (f32[1024,1024]{1,0:T(8,128)S(1)}, bf16[1024,1024]{1,0:T(8,128)(2,1)S(1)}, bf16[1024,1024]{1,0:T(8,128)(2,1)S(1)}, bf16[1024,1024]{1,0:T(8,128)(2,1)S(1)}) custom-call(s32[8]{0:T(128)S(1)} %stack.92.meta, bf16[1024,1024]{1,0:T(8,128)(2,1)S(1)} %bitcast.40, f32[16,1024]{1,0:T(8,128)S(1)} %get-tuple-element.99.small_ref, ...), custom_call_target="tpu_custom_call" | custom-call | flops 1 | bytes 1 | tf_op jit(solution)/shard_map/feed_forward_first/pallas_call | solution.py:36
  107.8 17.6 %feed_forward_second.1 = (bf16[1024,1024]{1,0:T(8,128)(2,1)}, bf16[1024,1024]{1,0:T(8,128)(2,1)S(1)}, bf16[2,2,4,4,128,128]{5,4,3,2,1,0:T(8,128)(2,1)S(1)}, bf16...) custom-call(s32[8]{0:T(128)S(1)} %stack.92.meta, bf16[1024,1024]{1,0:T(8,128)(2,1)S(1)} %bitcast.41, ...), custom_call_target="tpu_custom_call" | custom-call | flops 1 | bytes 1 | tf_op jit(solution)/shard_map/feed_forward_second/pallas_call | solution.py:36
  126.0 10.7 %feed_forward_third.1 = (bf16[1024,1024]{1,0:T(8,128)(2,1)S(1)}, bf16[2,2,4,2,128,128]{5,4,3,2,1,0:T(8,128)(2,1)S(1)}, bf16[2,2,4,2,128,128]{5,4,3,2,1,0:T(8,128)(2,1)S(1)}, f32[8,1024]{1,0:T(8,128)S(1)}) custom-call(s32[8]{0:T(128)S(1)} %stack.92.meta, bf16[1024,1024]{1,0:T(8,128)(2,1)S(1)} %bitcast.42, f32[16,1024]{1,0:T(8,128)S(1)} %get-tuple-element.99.small_ref, ...), custom_call_target="tpu_custom_call" | custom-call | flops 1 | bytes 1 | tf_op jit(solution)/shard_map/feed_forward_third/pallas_call | solution.py:36
  138.5 4.5 %mixed_grad.1 = (bf16[1024,1024]{1,0:T(8,128)(2,1)S(1)}, bf16[1024,1024]{1,0:T(8,128)(2,1)}) custom-call(s32[8]{0:T(128)S(1)} %stack.92.meta, bf16[1024,1024]{1,0:T(8,128)(2,1)S(1)} %get-tuple-element.128.attn_ref, bf16[4,32,2048]{2,1,0:T(8,128)(2,1)S(1)} %pad_maximum_fusion.refs_2_.refs_0_, ...), custom_call_target="tpu_custom_call" | custom-call | flops 1 | bytes 1 | tf_op jit(solution)/shard_map/mixed_grad/pallas_call | solution.py:36
  143.0 7.7 %attention_backward.4 = (bf16[1024,768]{1,0:T(8,128)(2,1)}, bf16[2,2,4,3,128,128]{5,4,3,2,1,0:T(8,128)(2,1)S(1)}) custom-call(s32[8]{0:T(128)S(1)} %stack.92.meta, bf16[1024,1024]{1,0:T(8,128)(2,1)S(1)} %get-tuple-element.100.first_ref, bf16[1024,1536]{1,0:T(8,128)(2,1)} %get-tuple-element.126.packed_ref, ...), custom_call_target="tpu_custom_call" | custom-call | flops 1 | bytes 1 | tf_op jit(solution)/shard_map/attention_backward/pallas_call | solution.py:36
  150.9 1.7 collective-permute-done.35.refs_2_.refs_7_
  154.4 7.7 %attention_backward.5 = (bf16[1024,768]{1,0:T(8,128)(2,1)}, bf16[2,2,4,3,128,128]{5,4,3,2,1,0:T(8,128)(2,1)S(1)}) custom-call(s32[8]{0:T(128)S(1)} %stack.92.meta, bf16[1024,1024]{1,0:T(8,128)(2,1)S(1)} %get-tuple-element.100.first_ref, bf16[1024,1536]{1,0:T(8,128)(2,1)} %get-tuple-element.126.packed_ref, ...), custom_call_target="tpu_custom_call" | custom-call | flops 1 | bytes 1 | tf_op jit(solution)/shard_map/attention_backward/pallas_call | solution.py:36
  162.1 7.9 %attention_backward.6 = (bf16[1024,768]{1,0:T(8,128)(2,1)}, bf16[2,2,4,3,128,128]{5,4,3,2,1,0:T(8,128)(2,1)S(1)}) custom-call(s32[8]{0:T(128)S(1)} %stack.92.meta, bf16[1024,1024]{1,0:T(8,128)(2,1)S(1)} %get-tuple-element.100.first_ref, bf16[1024,1536]{1,0:T(8,128)(2,1)} %get-tuple-element.136.packed_ref, ...), custom_call_target="tpu_custom_call" | custom-call | flops 1 | bytes 1 | tf_op jit(solution)/shard_map/attention_backward/pallas_call | solution.py:36
  170.0 1.5 step_2.1
  172.9 2.3 collective-permute-start.40
  175.2 2.1 collective-permute-start.41
  177.2 7.7 %attention_backward.7 = (bf16[1024,768]{1,0:T(8,128)(2,1)}, bf16[2,2,4,3,128,128]{5,4,3,2,1,0:T(8,128)(2,1)S(1)}) custom-call(s32[8]{0:T(128)S(1)} %stack.92.meta, bf16[1024,1024]{1,0:T(8,128)(2,1)S(1)} %get-tuple-element.100.first_ref, bf16[1024,1536]{1,0:T(8,128)(2,1)} %get-tuple-element.136.packed_ref, ...), custom_call_target="tpu_custom_call" | custom-call | flops 1 | bytes 1 | tf_op jit(solution)/shard_map/attention_backward/pallas_call | solution.py:36
  186.4 1.8 step_3.1
  188.2 1.4 collective-permute-start.47
  192.0 2.1 collective-permute-start.46
  194.1 12.4 %input_grad.1 = (bf16[1024,1024]{1,0:T(8,128)(2,1)}, f32[8,1024]{1,0:T(8,128)S(1)}, f32[8,3072]{1,0:T(8,128)S(1)}) custom-call(s32[8]{0:T(128)S(1)} %stack.92.meta, bf16[1024,1024]{1,0:T(8,128)(2,1)} %bitcast.38, bf16[1024,1024]{1,0:T(8,128)(2,1)} %get-tuple-element.149.grad_ref, f32[16,1024]{1,0:T(8,128)S(1)} %get-tuple-element.99.small_ref, ...), custom_call_target="tpu_custom_call" | custom-call | flops 1 | bytes 1 | tf_op jit(solution)/shard_map/input_grad/pallas_call | solution.py:36
  206.5 2.2 step_4.1
  211.8 1.7 step_6.1.refs_0_
  213.4 2.4 collective-permute-done.48.refs_1_
  218.9 2.1 collective-permute-start.54
  221.0 1.5 step_7.1
  223.9 2.7 %collective-permute-done.51.refs_2_ = bf16[6,128,128]{2,1,0:T(8,128)(2,1)S(1)} collective-permute-done((bf16[6,128,128]{2,1,0:T(8,128)(2,1)S(1)}, bf16[6,128,128]{2,1,0:T(8,128)(2,1)S(1)}, u32[]{:S(2)}, u32[]{:S(2)}) %collective-permute-start.51) | collective-permute-done | bytes 196640 | tf_op jit(solution)/shard_map/ppermute | solution.py:104
  226.6 3.5 %collective-permute-done.53.refs_2_ = bf16[4,128,128]{2,1,0:T(8,128)(2,1)S(1)} collective-permute-done((bf16[4,128,128]{2,1,0:T(8,128)(2,1)S(1)}, bf16[4,128,128]{2,1,0:T(8,128)(2,1)S(1)}, u32[]{:S(2)}, u32[]{:S(2)}) %collective-permute-start.53) | collective-permute-done | bytes 131104 | tf_op jit(solution)/shard_map/ppermute | solution.py:104
  233.2 3.2 %collective-permute-start.59 = (bf16[3,128,128]{2,1,0:T(8,128)(2,1)S(1)}, bf16[3,128,128]{2,1,0:T(8,128)(2,1)S(1)}, u32[]{:S(2)}, u32[]{:S(2)}) collective-permute-start(bf16[3,128,128]{2,1,0:T(8,128)(2,1)S(1)} %get-tuple-element.178), channel_id=1, source_target_pairs={{0,16},{1,17},{2,18},{3,19},{4,20},{5,21},{6,22},{7,23},{8,24},{9,... | collective-permute-start | bytes 294920 | tf_op jit(solution)/shard_map/ppermute | solution.py:104
  236.3 2.1 collective-permute-start.60
  238.4 5.7 %collective-permute-done.59.refs_2_ = bf16[3,128,128]{2,1,0:T(8,128)(2,1)S(1)} collective-permute-done((bf16[3,128,128]{2,1,0:T(8,128)(2,1)S(1)}, bf16[3,128,128]{2,1,0:T(8,128)(2,1)S(1)}, u32[]{:S(2)}, u32[]{:S(2)}) %collective-permute-start.59) | collective-permute-done | bytes 98336 | tf_op jit(solution)/shard_map/ppermute | solution.py:104
  244.2 1.5 step_9.1
  248.8 1.8 finish_rest.1
  252.9 1.9 finish_heads.1
  (158 shorter events, 46.0 us)
Async XLA Ops:
  2.8 9.1 %collective-permute-start.2 = (bf16[32,1664]{1,0:T(8,128)(2,1)S(1)}, bf16[32,1664]{1,0:T(8,128)(2,1)S(1)}, u32[]{:S(2)}, u32[]{:S(2)}) collective-permute-start(bf16[32,1664]{1,0:T(8,128)(2,1)S(1)} %fusion.1), channel_id=1, source_target_pairs={{0,24},{1,25},{2,26},{3,27},{4,28},{5,29},{6,30},{7,31},{8,16},{9,... | collective-permute-start | bytes 319496 | tf_op jit(solution)/shard_map/ppermute | solution.py:104
  7.9 9.0 %collective-permute-start.1 = (bf16[32,1664]{1,0:T(8,128)(2,1)S(1)}, bf16[32,1664]{1,0:T(8,128)(2,1)S(1)}, u32[]{:S(2)}, u32[]{:S(2)}) collective-permute-start(bf16[32,1664]{1,0:T(8,128)(2,1)S(1)} %fusion.1), channel_id=1, source_target_pairs={{0,16},{1,17},{2,18},{3,19},{4,20},{5,21},{6,22},{7,23},{8,24},{9,... | collective-permute-start | bytes 319496 | tf_op jit(solution)/shard_map/ppermute | solution.py:104
  7.9 9.0 %collective-permute-start = (bf16[32,1664]{1,0:T(8,128)(2,1)S(1)}, bf16[32,1664]{1,0:T(8,128)(2,1)S(1)}, u32[]{:S(2)}, u32[]{:S(2)}) collective-permute-start(bf16[32,1664]{1,0:T(8,128)(2,1)S(1)} %fusion.1), channel_id=1, source_target_pairs={{0,8},{1,9},{2,10},{3,11},{4,12},{5,13},{6,14},{7,15},{8,0},{9,1},... | collective-permute-start | bytes 319496 | tf_op jit(solution)/shard_map/ppermute | solution.py:104
  16.9 12.2 %collective-permute-start.4 = (bf16[4,32,1664]{2,1,0:T(8,128)(2,1)S(1)}, bf16[4,32,1664]{2,1,0:T(8,128)(2,1)S(1)}, u32[]{:S(2)}, u32[]{:S(2)}) collective-permute-start(bf16[4,32,1664]{2,1,0:T(8,128)(2,1)S(1)} %pad_maximum_fusion.1.refs_0_), channel_id=1, source_target_pairs={{0,4},{1,3},{2,6},{3,1},{4,0},{5,7},{6,2},{7,5},{8,12},{9,11},{10,... | collective-permute-start | bytes 1277960 | tf_op jit(solution)/shard_map/ppermute | solution.py:104
  18.5 12.1 %collective-permute-start.3 = (bf16[4,32,1664]{2,1,0:T(8,128)(2,1)S(1)}, bf16[4,32,1664]{2,1,0:T(8,128)(2,1)S(1)}, u32[]{:S(2)}, u32[]{:S(2)}) collective-permute-start(bf16[4,32,1664]{2,1,0:T(8,128)(2,1)S(1)} %pad_maximum_fusion.1.refs_0_), channel_id=1, source_target_pairs={{0,2},{1,5},{2,0},{3,7},{4,6},{5,1},{6,4},{7,3},{8,10},{9,13},{10,... | collective-permute-start | bytes 1277960 | tf_op jit(solution)/shard_map/ppermute | solution.py:104
  20.0 9.1 %collective-permute-start.7 = (bf16[32,1536]{1,0:T(8,128)(2,1)}, bf16[32,1536]{1,0:T(8,128)(2,1)S(1)}, u32[]{:S(2)}, u32[]{:S(2)}) collective-permute-start(bf16[32,1536]{1,0:T(8,128)(2,1)} %reshape.44), channel_id=1, source_target_pairs={{0,24},{1,25},{2,26},{3,27},{4,28},{5,29},{6,30},{7,31},{8,16},{9,... | collective-permute-start | bytes 294920 | tf_op jit(solution)/shard_map/ppermute | solution.py:104
  22.5 8.1 %collective-permute-start.6 = (bf16[32,1536]{1,0:T(8,128)(2,1)}, bf16[32,1536]{1,0:T(8,128)(2,1)S(1)}, u32[]{:S(2)}, u32[]{:S(2)}) collective-permute-start(bf16[32,1536]{1,0:T(8,128)(2,1)} %reshape.44), channel_id=1, source_target_pairs={{0,16},{1,17},{2,18},{3,19},{4,20},{5,21},{6,22},{7,23},{8,24},{9,... | collective-permute-start | bytes 294920 | tf_op jit(solution)/shard_map/ppermute | solution.py:104
  32.4 16.9 %collective-permute-start.8 = (bf16[4,32,3200]{2,1,0:T(8,128)(2,1)}, bf16[4,32,3200]{2,1,0:T(8,128)(2,1)}, u32[]{:S(2)}, u32[]{:S(2)}) collective-permute-start(bf16[4,32,3200]{2,1,0:T(8,128)(2,1)} %maximum_maximum_fusion.1), channel_id=1, source_target_pairs={{0,4},{1,3},{2,6},{3,1},{4,0},{5,7},{6,2},{7,5},{8,12},{9,11},{10,... | collective-permute-start | bytes 2457608 | tf_op jit(solution)/shard_map/ppermute | solution.py:104
  34.3 15.3 %collective-permute-start.13 = (bf16[4,32,1536]{2,1,0:T(8,128)(2,1)}, bf16[4,32,1536]{2,1,0:T(8,128)(2,1)}, u32[]{:S(2)}, u32[]{:S(2)}) collective-permute-start(bf16[4,32,1536]{2,1,0:T(8,128)(2,1)} %pad_maximum_fusion.2.refs_0_), channel_id=1, source_target_pairs={{0,2},{1,5},{2,0},{3,7},{4,6},{5,1},{6,4},{7,3},{8,10},{9,13},{10,... | collective-permute-start | bytes 1179656 | tf_op jit(solution)/shard_map/ppermute | solution.py:104
  35.6 13.8 %collective-permute-start.16 = (bf16[32,2048]{1,0:T(8,128)(2,1)S(1)}, bf16[32,2048]{1,0:T(8,128)(2,1)}, u32[]{:S(2)}, u32[]{:S(2)}) collective-permute-start(bf16[32,2048]{1,0:T(8,128)(2,1)S(1)} %pad_maximum_fusion.4), channel_id=1, source_target_pairs={{0,24},{1,25},{2,26},{3,27},{4,28},{5,29},{6,30},{7,31},{8,16},{9,... | collective-permute-start | bytes 393224 | tf_op jit(solution)/shard_map/ppermute | solution.py:104
  38.2 11.4 %collective-permute-start.15 = (bf16[32,2048]{1,0:T(8,128)(2,1)S(1)}, bf16[32,2048]{1,0:T(8,128)(2,1)}, u32[]{:S(2)}, u32[]{:S(2)}) collective-permute-start(bf16[32,2048]{1,0:T(8,128)(2,1)S(1)} %pad_maximum_fusion.4), channel_id=1, source_target_pairs={{0,16},{1,17},{2,18},{3,19},{4,20},{5,21},{6,22},{7,23},{8,24},{9,... | collective-permute-start | bytes 393224 | tf_op jit(solution)/shard_map/ppermute | solution.py:104
  39.0 10.6 %collective-permute-start.14 = (bf16[32,2048]{1,0:T(8,128)(2,1)S(1)}, bf16[32,2048]{1,0:T(8,128)(2,1)}, u32[]{:S(2)}, u32[]{:S(2)}) collective-permute-start(bf16[32,2048]{1,0:T(8,128)(2,1)S(1)} %pad_maximum_fusion.4), channel_id=1, source_target_pairs={{0,8},{1,9},{2,10},{3,11},{4,12},{5,13},{6,14},{7,15},{8,0},{9,1},... | collective-permute-start | bytes 393224 | tf_op jit(solution)/shard_map/ppermute | solution.py:104
  50.9 22.6 %collective-permute-start.17 = (bf16[4,32,3584]{2,1,0:T(8,128)(2,1)S(1)}, bf16[4,32,3584]{2,1,0:T(8,128)(2,1)S(1)}, u32[]{:S(2)}, u32[]{:S(2)}) collective-permute-start(bf16[4,32,3584]{2,1,0:T(8,128)(2,1)S(1)} %maximum_maximum_fusion), channel_id=1, source_target_pairs={{0,4},{1,3},{2,6},{3,1},{4,0},{5,7},{6,2},{7,5},{8,12},{9,11},{10,... | collective-permute-start | bytes 2752520 | tf_op jit(solution)/shard_map/ppermute | solution.py:104
  52.8 20.8 %collective-permute-start.21 = (bf16[4,32,2048]{2,1,0:T(8,128)(2,1)S(1)}, bf16[4,32,2048]{2,1,0:T(8,128)(2,1)S(1)}, u32[]{:S(2)}, u32[]{:S(2)}) collective-permute-start(bf16[4,32,2048]{2,1,0:T(8,128)(2,1)S(1)} %pad_maximum_fusion.refs_2_.refs_0_), channel_id=1, source_target_pairs={{0,2},{1,5},{2,0},{3,7},{4,6},{5,1},{6,4},{7,3},{8,10},{9,13},{10,... | collective-permute-start | bytes 1572872 | tf_op jit(solution)/shard_map/ppermute | solution.py:104
  55.9 17.7 %collective-permute-start.24 = (bf16[32,1024]{1,0:T(8,128)(2,1)S(1)}, bf16[32,1024]{1,0:T(8,128)(2,1)S(1)}, u32[]{:S(2)}, u32[]{:S(2)}) collective-permute-start(bf16[32,1024]{1,0:T(8,128)(2,1)S(1)} %copy-done.13), channel_id=1, source_target_pairs={{0,24},{1,25},{2,26},{3,27},{4,28},{5,29},{6,30},{7,31},{8,16},{9,... | collective-permute-start | bytes 196616 | tf_op jit(solution)/shard_map/ppermute | solution.py:104
  57.7 15.9 %collective-permute-start.23 = (bf16[32,1024]{1,0:T(8,128)(2,1)S(1)}, bf16[32,1024]{1,0:T(8,128)(2,1)S(1)}, u32[]{:S(2)}, u32[]{:S(2)}) collective-permute-start(bf16[32,1024]{1,0:T(8,128)(2,1)S(1)} %copy-done.13), channel_id=1, source_target_pairs={{0,16},{1,17},{2,18},{3,19},{4,20},{5,21},{6,22},{7,23},{8,24},{9,... | collective-permute-start | bytes 196616 | tf_op jit(solution)/shard_map/ppermute | solution.py:104
  57.7 15.9 %collective-permute-start.22 = (bf16[32,1024]{1,0:T(8,128)(2,1)S(1)}, bf16[32,1024]{1,0:T(8,128)(2,1)S(1)}, u32[]{:S(2)}, u32[]{:S(2)}) collective-permute-start(bf16[32,1024]{1,0:T(8,128)(2,1)S(1)} %copy-done.13), channel_id=1, source_target_pairs={{0,8},{1,9},{2,10},{3,11},{4,12},{5,13},{6,14},{7,15},{8,0},{9,1},... | collective-permute-start | bytes 196616 | tf_op jit(solution)/shard_map/ppermute | solution.py:104
  73.7 16.3 %collective-permute-start.25 = (bf16[4,32,3072]{2,1,0:T(8,128)(2,1)S(1)}, bf16[4,32,3072]{2,1,0:T(8,128)(2,1)S(1)}, u32[]{:S(2)}, u32[]{:S(2)}) collective-permute-start(bf16[4,32,3072]{2,1,0:T(8,128)(2,1)S(1)} %maximum_maximum_fusion.2), channel_id=1, source_target_pairs={{0,4},{1,3},{2,6},{3,1},{4,0},{5,7},{6,2},{7,5},{8,12},{9,11},{10,... | collective-permute-start | bytes 2359304 | tf_op jit(solution)/shard_map/ppermute | solution.py:104
  74.6 15.5 %collective-permute-start.26 = (bf16[4,32,2048]{2,1,0:T(8,128)(2,1)S(1)}, bf16[4,32,2048]{2,1,0:T(8,128)(2,1)S(1)}, u32[]{:S(2)}, u32[]{:S(2)}) collective-permute-start(bf16[4,32,2048]{2,1,0:T(8,128)(2,1)S(1)} %pad_maximum_fusion.refs_2_.refs_0_), channel_id=1, source_target_pairs={{0,1},{1,0},{2,3},{3,2},{4,5},{5,4},{6,7},{7,6},{8,9},{9,8},{10,11... | collective-permute-start | bytes 1572872 | tf_op jit(solution)/shard_map/ppermute | solution.py:104
  74.9 15.2 %collective-permute-start.27 = (bf16[4,32,2048]{2,1,0:T(8,128)(2,1)S(1)}, bf16[4,32,2048]{2,1,0:T(8,128)(2,1)S(1)}, u32[]{:S(2)}, u32[]{:S(2)}) collective-permute-start(bf16[4,32,2048]{2,1,0:T(8,128)(2,1)S(1)} %collective-permute-done.21.refs_3_.refs_1_), channel_id=1, source_target_pairs={{0,1},{1,0},{2,3},{3,2},{4,5},{5,4},{6,7},{7,6},{8,9},{9,8},{10,11... | collective-permute-start | bytes 1572872 | tf_op jit(solution)/shard_map/ppermute | solution.py:104
  75.1 15.0 %collective-permute-start.29 = (bf16[4,32,1024]{2,1,0:T(8,128)(2,1)S(1)}, bf16[4,32,1024]{2,1,0:T(8,128)(2,1)S(1)}, u32[]{:S(2)}, u32[]{:S(2)}) collective-permute-start(bf16[4,32,1024]{2,1,0:T(8,128)(2,1)S(1)} %pad_maximum_fusion.3.refs_0_), channel_id=1, source_target_pairs={{0,2},{1,5},{2,0},{3,7},{4,6},{5,1},{6,4},{7,3},{8,10},{9,13},{10,... | collective-permute-start | bytes 786440 | tf_op jit(solution)/shard_map/ppermute | solution.py:104
  91.0 16.8 %collective-permute-start.31 = (bf16[4,32,1024]{2,1,0:T(8,128)(2,1)S(1)}, bf16[4,32,1024]{2,1,0:T(8,128)(2,1)S(1)}, u32[]{:S(2)}, u32[]{:S(2)}) collective-permute-start(bf16[4,32,1024]{2,1,0:T(8,128)(2,1)S(1)} %pad_maximum_fusion.3.refs_0_), channel_id=1, source_target_pairs={{0,1},{1,0},{2,3},{3,2},{4,5},{5,4},{6,7},{7,6},{8,9},{9,8},{10,11... | collective-permute-start | bytes 786440 | tf_op jit(solution)/shard_map/ppermute | solution.py:104
  91.0 16.7 %collective-permute-start.32 = (bf16[4,32,1024]{2,1,0:T(8,128)(2,1)S(1)}, bf16[4,32,1024]{2,1,0:T(8,128)(2,1)S(1)}, u32[]{:S(2)}, u32[]{:S(2)}) collective-permute-start(bf16[4,32,1024]{2,1,0:T(8,128)(2,1)S(1)} %collective-permute-done.29.refs_1_), channel_id=1, source_target_pairs={{0,1},{1,0},{2,3},{3,2},{4,5},{5,4},{6,7},{7,6},{8,9},{9,8},{10,11... | collective-permute-start | bytes 786440 | tf_op jit(solution)/shard_map/ppermute | solution.py:104
  96.6 11.2 %collective-permute-start.33 = (bf16[4,32,1024]{2,1,0:T(8,128)(2,1)S(1)}, bf16[4,32,1024]{2,1,0:T(8,128)(2,1)S(1)}, u32[]{:S(2)}, u32[]{:S(2)}) collective-permute-start(bf16[4,32,1024]{2,1,0:T(8,128)(2,1)S(1)} %collective-permute-done.30.refs_3_), channel_id=1, source_target_pairs={{0,1},{1,0},{2,3},{3,2},{4,5},{5,4},{6,7},{7,6},{8,9},{9,8},{10,11... | collective-permute-start | bytes 786440 | tf_op jit(solution)/shard_map/ppermute | solution.py:104
  125.4 11.4 %collective-permute-start.34 = (bf16[2,2,4,4,128,128]{5,4,3,2,1,0:T(8,128)(2,1)S(1)}, bf16[2,2,4,4,128,128]{5,4,3,2,1,0:T(8,128)(2,1)S(1)}, u32[]{:S(2)}, u32[]{:S(2)}) collective-permute-start(bf16[2,2,4,4,128,128]{5,4,3,2,1,0:T(8,128)(2,1)S(1)} %get-tuple-element.124), channel_id=1, source_target_pairs={{0,1},{1,0},{2,3},{3,2},{4,5},{5,4},{6,7},{7,6},{8,9},{9,8},{10,11... | collective-permute-start | bytes 6291464 | tf_op jit(solution)/shard_map/ppermute | solution.py:104
  136.7 14.2 %collective-permute-start.36 = (bf16[2,2,4,2,128,128]{5,4,3,2,1,0:T(8,128)(2,1)S(1)}, bf16[2,2,4,2,128,128]{5,4,3,2,1,0:T(8,128)(2,1)S(1)}, u32[]{:S(2)}, u32[]{:S(2)}) collective-permute-start(bf16[2,2,4,2,128,128]{5,4,3,2,1,0:T(8,128)(2,1)S(1)} %get-tuple-element.132), channel_id=1, source_target_pairs={{0,1},{1,0},{2,3},{3,2},{4,5},{5,4},{6,7},{7,6},{8,9},{9,8},{10,11... | collective-permute-start | bytes 3145736 | tf_op jit(solution)/shard_map/ppermute | solution.py:104
  137.7 14.9 %collective-permute-start.35 = (bf16[32,128,128]{2,1,0:T(8,128)(2,1)S(1)}, bf16[32,128,128]{2,1,0:T(8,128)(2,1)S(1)}, u32[]{:S(2)}, u32[]{:S(2)}) collective-permute-start(bf16[32,128,128]{2,1,0:T(8,128)(2,1)S(1)} %step_0.1), channel_id=1, source_target_pairs={{0,4},{1,3},{2,6},{3,1},{4,0},{5,7},{6,2},{7,5},{8,12},{9,11},{10,... | collective-permute-start | bytes 3145736 | tf_op jit(solution)/shard_map/ppermute | solution.py:104
  150.7 19.3 %collective-permute-start.38 = (bf16[2,2,4,3,128,128]{5,4,3,2,1,0:T(8,128)(2,1)S(1)}, bf16[2,2,4,3,128,128]{5,4,3,2,1,0:T(8,128)(2,1)S(1)}, u32[]{:S(2)}, u32[]{:S(2)}) collective-permute-start(bf16[2,2,4,3,128,128]{5,4,3,2,1,0:T(8,128)(2,1)S(1)} %get-tuple-element.130), channel_id=1, source_target_pairs={{0,1},{1,0},{2,3},{3,2},{4,5},{5,4},{6,7},{7,6},{8,9},{9,8},{10,11... | collective-permute-start | bytes 4718600 | tf_op jit(solution)/shard_map/ppermute | solution.py:104
  153.7 16.4 %collective-permute-start.37 = (bf16[32,128,128]{2,1,0:T(8,128)(2,1)S(1)}, bf16[32,128,128]{2,1,0:T(8,128)(2,1)S(1)}, u32[]{:S(2)}, u32[]{:S(2)}) collective-permute-start(bf16[32,128,128]{2,1,0:T(8,128)(2,1)S(1)} %step_1.1), channel_id=1, source_target_pairs={{0,2},{1,5},{2,0},{3,7},{4,6},{5,1},{6,4},{7,3},{8,10},{9,13},{10,... | collective-permute-start | bytes 3145736 | tf_op jit(solution)/shard_map/ppermute | solution.py:104
  169.9 15.8 %collective-permute-start.43 = (bf16[2,2,4,3,128,128]{5,4,3,2,1,0:T(8,128)(2,1)S(1)}, bf16[2,2,4,3,128,128]{5,4,3,2,1,0:T(8,128)(2,1)S(1)}, u32[]{:S(2)}, u32[]{:S(2)}) collective-permute-start(bf16[2,2,4,3,128,128]{5,4,3,2,1,0:T(8,128)(2,1)S(1)} %get-tuple-element.138), channel_id=1, source_target_pairs={{0,1},{1,0},{2,3},{3,2},{4,5},{5,4},{6,7},{7,6},{8,9},{9,8},{10,11... | collective-permute-start | bytes 4718600 | tf_op jit(solution)/shard_map/ppermute | solution.py:104
  171.5 14.9 %collective-permute-start.42 = (bf16[32,128,128]{2,1,0:T(8,128)(2,1)S(1)}, bf16[32,128,128]{2,1,0:T(8,128)(2,1)S(1)}, u32[]{:S(2)}, u32[]{:S(2)}) collective-permute-start(bf16[32,128,128]{2,1,0:T(8,128)(2,1)S(1)} %get-tuple-element.140), channel_id=1, source_target_pairs={{0,4},{1,3},{2,6},{3,1},{4,0},{5,7},{6,2},{7,5},{8,12},{9,11},{10,... | collective-permute-start | bytes 3145736 | tf_op jit(solution)/shard_map/ppermute | solution.py:104
  172.8 12.1 %collective-permute-start.39 = (bf16[4,128,128]{2,1,0:T(8,128)(2,1)S(1)}, bf16[4,128,128]{2,1,0:T(8,128)(2,1)S(1)}, u32[]{:S(2)}, u32[]{:S(2)}) collective-permute-start(bf16[4,128,128]{2,1,0:T(8,128)(2,1)S(1)} %get-tuple-element.143), channel_id=1, source_target_pairs={{0,8},{1,9},{2,10},{3,11},{4,12},{5,13},{6,14},{7,15},{8,0},{9,1},... | collective-permute-start | bytes 393224 | tf_op jit(solution)/shard_map/ppermute | solution.py:104
  172.9 12.9 %collective-permute-start.40 = (bf16[4,128,128]{2,1,0:T(8,128)(2,1)S(1)}, bf16[4,128,128]{2,1,0:T(8,128)(2,1)S(1)}, u32[]{:S(2)}, u32[]{:S(2)}) collective-permute-start(bf16[4,128,128]{2,1,0:T(8,128)(2,1)S(1)} %get-tuple-element.144), channel_id=1, source_target_pairs={{0,16},{1,17},{2,18},{3,19},{4,20},{5,21},{6,22},{7,23},{8,24},{9,... | collective-permute-start | bytes 393224 | tf_op jit(solution)/shard_map/ppermute | solution.py:104
  175.2 10.6 %collective-permute-start.41 = (bf16[4,128,128]{2,1,0:T(8,128)(2,1)S(1)}, bf16[4,128,128]{2,1,0:T(8,128)(2,1)S(1)}, u32[]{:S(2)}, u32[]{:S(2)}) collective-permute-start(bf16[4,128,128]{2,1,0:T(8,128)(2,1)S(1)} %get-tuple-element.145), channel_id=1, source_target_pairs={{0,24},{1,25},{2,26},{3,27},{4,28},{5,29},{6,30},{7,31},{8,16},{9,... | collective-permute-start | bytes 393224 | tf_op jit(solution)/shard_map/ppermute | solution.py:104
  188.2 18.2 %collective-permute-start.47 = (bf16[36,128,128]{2,1,0:T(8,128)(2,1)S(1)}, bf16[36,128,128]{2,1,0:T(8,128)(2,1)S(1)}, u32[]{:S(2)}, u32[]{:S(2)}) collective-permute-start(bf16[36,128,128]{2,1,0:T(8,128)(2,1)S(1)} %get-tuple-element.147), channel_id=1, source_target_pairs={{0,2},{1,5},{2,0},{3,7},{4,6},{5,1},{6,4},{7,3},{8,10},{9,13},{10,... | collective-permute-start | bytes 3538952 | tf_op jit(solution)/shard_map/ppermute | solution.py:104
  189.7 16.8 %collective-permute-start.44 = (bf16[2,128,128]{2,1,0:T(8,128)(2,1)S(1)}, bf16[2,128,128]{2,1,0:T(8,128)(2,1)S(1)}, u32[]{:S(2)}, u32[]{:S(2)}) collective-permute-start(bf16[2,128,128]{2,1,0:T(8,128)(2,1)S(1)} %get-tuple-element.157), channel_id=1, source_target_pairs={{0,8},{1,9},{2,10},{3,11},{4,12},{5,13},{6,14},{7,15},{8,0},{9,1},... | collective-permute-start | bytes 196616 | tf_op jit(solution)/shard_map/ppermute | solution.py:104
  191.1 15.4 %collective-permute-start.45 = (bf16[2,128,128]{2,1,0:T(8,128)(2,1)S(1)}, bf16[2,128,128]{2,1,0:T(8,128)(2,1)S(1)}, u32[]{:S(2)}, u32[]{:S(2)}) collective-permute-start(bf16[2,128,128]{2,1,0:T(8,128)(2,1)S(1)} %get-tuple-element.158), channel_id=1, source_target_pairs={{0,16},{1,17},{2,18},{3,19},{4,20},{5,21},{6,22},{7,23},{8,24},{9,... | collective-permute-start | bytes 196616 | tf_op jit(solution)/shard_map/ppermute | solution.py:104
  192.0 14.5 %collective-permute-start.46 = (bf16[2,128,128]{2,1,0:T(8,128)(2,1)S(1)}, bf16[2,128,128]{2,1,0:T(8,128)(2,1)S(1)}, u32[]{:S(2)}, u32[]{:S(2)}) collective-permute-start(bf16[2,128,128]{2,1,0:T(8,128)(2,1)S(1)} %get-tuple-element.159), channel_id=1, source_target_pairs={{0,24},{1,25},{2,26},{3,27},{4,28},{5,29},{6,30},{7,31},{8,16},{9,... | collective-permute-start | bytes 196616 | tf_op jit(solution)/shard_map/ppermute | solution.py:104
  210.0 8.9 %collective-permute-start.49 = (bf16[12,128,128]{2,1,0:T(8,128)(2,1)S(1)}, bf16[12,128,128]{2,1,0:T(8,128)(2,1)S(1)}, u32[]{:S(2)}, u32[]{:S(2)}) collective-permute-start(bf16[12,128,128]{2,1,0:T(8,128)(2,1)S(1)} %step_5.1), channel_id=1, source_target_pairs={{0,4},{1,3},{2,6},{3,1},{4,0},{5,7},{6,2},{7,5},{8,12},{9,11},{10,... | collective-permute-start | bytes 1179656 | tf_op jit(solution)/shard_map/ppermute | solution.py:104
  215.8 10.8 %collective-permute-start.51 = (bf16[6,128,128]{2,1,0:T(8,128)(2,1)S(1)}, bf16[6,128,128]{2,1,0:T(8,128)(2,1)S(1)}, u32[]{:S(2)}, u32[]{:S(2)}) collective-permute-start(bf16[6,128,128]{2,1,0:T(8,128)(2,1)S(1)} %step_6.1.refs_0_), channel_id=1, source_target_pairs={{0,2},{1,3},{2,0},{3,1},{4,6},{5,7},{6,4},{7,5},{8,10},{9,11},{10,... | collective-permute-start | bytes 589832 | tf_op jit(solution)/shard_map/ppermute | solution.py:104
  216.9 9.7 %collective-permute-start.50 = (bf16[6,128,128]{2,1,0:T(8,128)(2,1)S(1)}, bf16[6,128,128]{2,1,0:T(8,128)(2,1)S(1)}, u32[]{:S(2)}, u32[]{:S(2)}) collective-permute-start(bf16[6,128,128]{2,1,0:T(8,128)(2,1)S(1)} %step_6.1.refs_0_), channel_id=1, source_target_pairs={{0,1},{1,0},{2,3},{3,2},{4,5},{5,4},{6,7},{7,6},{8,9},{9,8},{10,11... | collective-permute-start | bytes 589832 | tf_op jit(solution)/shard_map/ppermute | solution.py:104
  217.6 12.4 %collective-permute-start.53 = (bf16[4,128,128]{2,1,0:T(8,128)(2,1)S(1)}, bf16[4,128,128]{2,1,0:T(8,128)(2,1)S(1)}, u32[]{:S(2)}, u32[]{:S(2)}) collective-permute-start(bf16[4,128,128]{2,1,0:T(8,128)(2,1)S(1)} %get-tuple-element.175), channel_id=1, source_target_pairs={{0,16},{1,17},{2,18},{3,19},{4,20},{5,21},{6,22},{7,23},{8,24},{9,... | collective-permute-start | bytes 393224 | tf_op jit(solution)/shard_map/ppermute | solution.py:104
  218.9 11.2 %collective-permute-start.54 = (bf16[4,128,128]{2,1,0:T(8,128)(2,1)S(1)}, bf16[4,128,128]{2,1,0:T(8,128)(2,1)S(1)}, u32[]{:S(2)}, u32[]{:S(2)}) collective-permute-start(bf16[4,128,128]{2,1,0:T(8,128)(2,1)S(1)} %get-tuple-element.176), channel_id=1, source_target_pairs={{0,24},{1,25},{2,26},{3,27},{4,28},{5,29},{6,30},{7,31},{8,16},{9,... | collective-permute-start | bytes 393224 | tf_op jit(solution)/shard_map/ppermute | solution.py:104
  222.9 13.5 %collective-permute-start.58 = (bf16[3,128,128]{2,1,0:T(8,128)(2,1)S(1)}, bf16[3,128,128]{2,1,0:T(8,128)(2,1)S(1)}, u32[]{:S(2)}, u32[]{:S(2)}) collective-permute-start(bf16[3,128,128]{2,1,0:T(8,128)(2,1)S(1)} %get-tuple-element.177), channel_id=1, source_target_pairs={{0,8},{1,9},{2,10},{3,11},{4,12},{5,13},{6,14},{7,15},{8,0},{9,1},... | collective-permute-start | bytes 294920 | tf_op jit(solution)/shard_map/ppermute | solution.py:104
  231.3 12.9 %collective-permute-start.57 = (bf16[4,128,128]{2,1,0:T(8,128)(2,1)S(1)}, bf16[4,128,128]{2,1,0:T(8,128)(2,1)S(1)}, u32[]{:S(2)}, u32[]{:S(2)}) collective-permute-start(bf16[4,128,128]{2,1,0:T(8,128)(2,1)S(1)} %step_8.1.refs_4_.refs_0_), channel_id=1, source_target_pairs={{0,3},{1,2},{2,1},{3,0},{4,7},{5,6},{6,5},{7,4},{8,11},{9,10},{10,... | collective-permute-start | bytes 393224 | tf_op jit(solution)/shard_map/ppermute | solution.py:104
  231.3 12.8 %collective-permute-start.56 = (bf16[4,128,128]{2,1,0:T(8,128)(2,1)S(1)}, bf16[4,128,128]{2,1,0:T(8,128)(2,1)S(1)}, u32[]{:S(2)}, u32[]{:S(2)}) collective-permute-start(bf16[4,128,128]{2,1,0:T(8,128)(2,1)S(1)} %step_8.1.refs_4_.refs_0_), channel_id=1, source_target_pairs={{0,2},{1,3},{2,0},{3,1},{4,6},{5,7},{6,4},{7,5},{8,10},{9,11},{10,... | collective-permute-start | bytes 393224 | tf_op jit(solution)/shard_map/ppermute | solution.py:104
  232.3 11.9 %collective-permute-start.55 = (bf16[4,128,128]{2,1,0:T(8,128)(2,1)S(1)}, bf16[4,128,128]{2,1,0:T(8,128)(2,1)S(1)}, u32[]{:S(2)}, u32[]{:S(2)}) collective-permute-start(bf16[4,128,128]{2,1,0:T(8,128)(2,1)S(1)} %step_8.1.refs_4_.refs_0_), channel_id=1, source_target_pairs={{0,1},{1,0},{2,3},{3,2},{4,5},{5,4},{6,7},{7,6},{8,9},{9,8},{10,11... | collective-permute-start | bytes 393224 | tf_op jit(solution)/shard_map/ppermute | solution.py:104
  233.2 11.0 %collective-permute-start.59 = (bf16[3,128,128]{2,1,0:T(8,128)(2,1)S(1)}, bf16[3,128,128]{2,1,0:T(8,128)(2,1)S(1)}, u32[]{:S(2)}, u32[]{:S(2)}) collective-permute-start(bf16[3,128,128]{2,1,0:T(8,128)(2,1)S(1)} %get-tuple-element.178), channel_id=1, source_target_pairs={{0,16},{1,17},{2,18},{3,19},{4,20},{5,21},{6,22},{7,23},{8,24},{9,... | collective-permute-start | bytes 294920 | tf_op jit(solution)/shard_map/ppermute | solution.py:104
  (31 other events, 252.5 us)

commit v5 on v4

--- a/solution.py
+++ b/solution.py
@@ -547,18 +547,28 @@
     )
 
 
-def store_grads(meta, pieces, m, left_ref, right_ref, odd):
-    q = right_ref.shape[1] // 4
-
-    @pl.loop(0, 4)
-    def _(j):
-        core, y = j // 2, j % 2
-        values = dot(left_ref[...], right_ref[:, span(j, q)]).astype(BF)
-        for piece_ref, half in zip(pieces, (THEIRS, OURS)):
-
-            @pl.when(core == meta[half])
-            def _(piece_ref=piece_ref):
-                store_piece(core, odd, piece_ref, 2 * m, values, y)
+def store_grads(meta, both, m, left_ref, right_ref, odd):
+    half = right_ref.shape[1] // 2
+
+    @pl.loop(0, 2)
+    def _(core):
+        values = dot(left_ref[...], right_ref[:, span(core, half)]).astype(BF)
+        for y in range(2):
+            part = values[:, y * half // 2 : (y + 1) * half // 2]
+            store_piece(core, odd, both.at[core], 2 * m, part, y)
+
+
+def send_grads(meta, both, m, pieces, sems):
+    tiles = pl.ds(2 * m, 2)
+    copies = [
+        pltpu.make_async_copy(
+            both.at[meta[half], :, :, :, tiles], piece.at[:, :, :, tiles], sems.at[2 * m + i]
+        )
+        for i, (half, piece) in enumerate(zip((THEIRS, OURS), pieces))
+    ]
+    for copy in copies:
+        copy.start()
+    return copies
 
 
 def feed_forward_second(meta, cot, small, middle, second, active, slope, parts):
@@ -568,32 +578,39 @@
 
     def kernel(meta, cot_ref, small_ref, middle_ref, second_ref, active_ref, slope_ref, *refs):
         parts, refs = refs[:count], refs[count:]
-        out_ref, hidden_ref, *pieces, sums_ref, whole, out, flipped, sems = refs
-        fetch(meta, parts, starts, whole, (0, width), sems.at[0])
+        out_ref, hidden_ref, *pieces, sums_ref, whole, out, flipped, halves, sems = refs
+        fetch(meta, parts, starts, whole, (0, width), sems.at[4])
         flipped[...] = active_ref[...].T
-        store_grads(meta, pieces, 0, flipped, cot_ref, False)
-        fetched(whole, (0, width), sems.at[0])
-
-        @blocks(rows)
+        store_grads(meta, halves, 0, flipped, cot_ref, False)
+        copies = send_grads(meta, halves, 0, pieces, sems)
+        fetched(whole, (0, width), sems.at[4])
+
+        @blocks(width)
         def _(here, _):
-            grad = dot(cot_ref[here, :], whole[...], NT)
-            hidden_ref[here, :] = (slope_ref[here, :].astype(F32) * grad).astype(BF)
-
-        @blocks(rows)
+            grad = dot(cot_ref[...], whole[here, :], NT)
+            hidden_ref[:, here] = (slope_ref[:, here].astype(F32) * grad).astype(BF)
+
+        flipped[...] = second_ref[...].T
+        store_grads(meta, halves, 1, flipped, hidden_ref, False)
+        copies += send_grads(meta, halves, 1, pieces, sems)
+
+        def write(here):
+            return pltpu.make_async_copy(out.at[:, here], out_ref.at[:, here], sems.at[5])
+
+        @blocks(width)
         def _(here, _):
-            values = middle_ref[here, :] + dot(active_ref[here, :], whole[...])
-            out[here, :] = (values + small_ref[BD : BD + 1, :]).astype(BF)
-
-        write = pltpu.make_async_copy(out, out_ref, sems.at[1])
-        write.start()
-        flipped[...] = second_ref[...].T
-        store_grads(meta, pieces, 1, flipped, hidden_ref, False)
+            values = middle_ref[:, here] + dot(active_ref[...], whole[:, here])
+            out[:, here] = (values + small_ref[BD : BD + 1, here]).astype(BF)
+            write(here).start()
+
         sums_ref[...] = jnp.zeros_like(sums_ref)
         sums_ref[0:1, :] = column_sum(hidden_ref[...])
         sums_ref[1:2, :] = column_sum(cot_ref[...])
-        write.wait()
-
-    piece = VMEM((2, 2, 4, 4, width // 8, 128), BF)
+        for copy in (write(pl.ds(0, width)), *copies):
+            copy.wait()
+
+    shape = (2, 2, 4, 4, width // 8, 128)
+    piece = VMEM(shape, BF)
     return call(
         kernel,
         meta,
@@ -602,8 +619,8 @@
         [
             (HBM((rows, width), BF), ANY),
             (VMEM((rows, width), BF), None),
-            (piece, None),
-            (piece, None),
+            (piece, ANY),
+            (piece, ANY),
             (shaped(F32, 8, width), None),
         ],
         24,
@@ -613,7 +630,8 @@
             pltpu.VMEM((width, width), BF),
             pltpu.VMEM((rows, width), BF),
             pltpu.VMEM((width, rows), BF),
-            pltpu.SemaphoreType.DMA((2,)),
+            pltpu.VMEM((2, *shape), BF),
+            pltpu.SemaphoreType.DMA((6,)),
         ],
     )
 
@@ -625,7 +643,7 @@
 
     def kernel(meta, cot_ref, small_ref, middle_ref, hidden_ref, *refs):
         mixed_refs, parts = refs[: len(mixed)], refs[len(mixed) : len(mixed) + count]
-        attn_ref, *pieces, sums_ref, whole, flipped, sem = refs[len(mixed) + count :]
+        attn_ref, *pieces, sums_ref, whole, flipped, halves, sem, sems = refs[len(mixed) + count :]
         fetch(meta, parts, starts, whole, (0, width), sem, width)
         fetched(whole, (0, width), sem)
         sums_ref[...] = jnp.zeros_like(sums_ref)
@@ -644,21 +662,26 @@
         for i, ref in enumerate(mixed_refs):
             n = ref.shape[1]
             flipped[i * n : (i + 1) * n, :] = ref[...].T
-        store_grads(meta, pieces, 0, flipped, attn_ref, True)
-
-    piece = VMEM((2, 2, 4, 2, width // 8, 128), BF)
+        store_grads(meta, halves, 0, flipped, attn_ref, True)
+        for copy in send_grads(meta, halves, 0, pieces, sems):
+            copy.wait()
+
+    shape = (2, 2, 4, 2, width // 8, 128)
+    piece = VMEM(shape, BF)
     return call(
         kernel,
         meta,
         [(a, None) for a in (cot, small, middle, hidden, *mixed)] + [(p, ANY) for p in parts],
-        [(VMEM((rows, width), BF), None), (piece, None), (piece, None), (shaped(F32, 8, width), None)],
+        [(VMEM((rows, width), BF), None), (piece, ANY), (piece, ANY), (shaped(F32, 8, width), None)],
         20,
         cost(4 * rows * width * width, 2 * 12 * rows * width),
         "feed_forward_third",
         [
             pltpu.VMEM((width, width), BF),
             pltpu.VMEM((width, rows), BF),
+            pltpu.VMEM((2, *shape), BF),
             pltpu.SemaphoreType.DMA,
+            pltpu.SemaphoreType.DMA((2,)),
         ],
     )
 
@@ -969,7 +992,8 @@
         return [arrays[0]] + [move(a, p) for a, p in zip(arrays[1:], links.z)]
 
     def share(value):
-        return [value] + [move(value, p) for p in links.rep]
+        by_y = move(value, links.y)
+        return [value, move(value, links.core), by_y, move(by_y, links.core)]
 
     both = Piece(keep, to_core(send), False)
     step = Step()
@@ -1032,8 +1056,9 @@
     z_two = step.run(after(meta, z_one[1]), "step_7")
     step = Step()
     step.share([z_one])
-    (r_one,) = step.run(after(meta, z_two[0], *r_rest[1:]), "step_8")
-    z_two, r_one = along(z_two), share(r_one)
+    (r_one,) = step.run(after(meta, z_two[0]), "step_8")
+    z_two = along(z_two)
+    r_one = share(after(r_one, z_two[1]))
 
     step = Step()
     step.share([z_two])

time: 255 us -> 247 us (0.969)
  starting transfers between devices: 62.6 us -> 58.1 us
    ppermute x65, starting transfers between devices: 62.6 us -> 58.1 us  [move(): return lax.ppermute(value, AXES, pairs)]
  transfers between devices with their start and end apart: 65 -> 65, of which waited for: 16 -> 16; matrix products, arithmetic and copies ran while one was open for 3% -> 3% of each run, Pallas kernels for 42% -> 44%
where the time goes in v5:
time: 247 us
  Pallas kernels  133 us (54%)
  starting transfers between devices  58.1 us (24%)
  waiting for transfers between devices  40 us (16%)
  local copies, waits for them, and re-layouts  8.75 us (4%)
  other arithmetic  5.89 us (2%)
    pallas_call x24, Pallas kernels, call(): pl.pallas_call(kernel, out_shape=shapes, grid_spec=pltpu.PrefetchScalarGr...  133 us
    ppermute x65, starting transfers between devices, move(): return lax.ppermute(value, AXES, pairs)  58.1 us
    ppermute x65, waiting for transfers between devices, move(): return lax.ppermute(value, AXES, pairs)  40 us
  transfers between devices with their start and end apart: 65, of which 16 were waited for; matrix products, arithmetic and copies ran while one was open for 3% of the time, Pallas kernels for 44%

profile of v5, /device:TPU:0, one launch (start us, length us, event | category | flops | bytes accessed | tf_op | source)
XLA Modules:
  0.0 247.1 jit_solution(6592814858075970816)
XLA Ops:
  2.8 5.1 %collective-permute-start.2 = (bf16[32,1664]{1,0:T(8,128)(2,1)S(1)}, bf16[32,1664]{1,0:T(8,128)(2,1)S(1)}, u32[]{:S(2)}, u32[]{:S(2)}) collective-permute-start(bf16[32,1664]{1,0:T(8,128)(2,1)S(1)} %fusion.1), channel_id=1, source_target_pairs={{0,24},{1,25},{2,26},{3,27},{4,28},{5,29},{6,30},{7,31},{8,16},{9,... | collective-permute-start | bytes 319496 | tf_op jit(solution)/shard_map/ppermute | solution.py:104
  10.3 1.6 constant_dynamic-slice_fusion
  11.9 5.0 %collective-permute-done.1 = bf16[32,1664]{1,0:T(8,128)(2,1)S(1)} collective-permute-done((bf16[32,1664]{1,0:T(8,128)(2,1)S(1)}, bf16[32,1664]{1,0:T(8,128)(2,1)S(1)}, u32[]{:S(2)}, u32[]{:S(2)}) %collective-permute-start.1) | collective-permute-done | bytes 106528 | tf_op jit(solution)/shard_map/ppermute | solution.py:104
  16.9 1.6 collective-permute-start.4
  18.5 1.5 collective-permute-start.3
  20.0 2.5 %collective-permute-start.7 = (bf16[32,1536]{1,0:T(8,128)(2,1)}, bf16[32,1536]{1,0:T(8,128)(2,1)S(1)}, u32[]{:S(2)}, u32[]{:S(2)}) collective-permute-start(bf16[32,1536]{1,0:T(8,128)(2,1)} %reshape.44), channel_id=1, source_target_pairs={{0,24},{1,25},{2,26},{3,27},{4,28},{5,29},{6,30},{7,31},{8,16},{9,... | collective-permute-start | bytes 294920 | tf_op jit(solution)/shard_map/ppermute | solution.py:104
  22.5 1.9 collective-permute-start.5
  24.4 4.7 %collective-permute-done.4.refs_2_ = bf16[4,32,1664]{2,1,0:T(8,128)(2,1)S(1)} collective-permute-done((bf16[4,32,1664]{2,1,0:T(8,128)(2,1)S(1)}, bf16[4,32,1664]{2,1,0:T(8,128)(2,1)S(1)}, u32[]{:S(2)}, u32[]{:S(2)}) %collective-permute-start.4) | collective-permute-done | bytes 426016 | tf_op jit(solution)/shard_map/ppermute | solution.py:104
  29.1 1.5 collective-permute-done.6
  30.6 1.8 maximum_maximum_fusion.1
  35.6 1.9 collective-permute-start.16
  39.0 2.5 collective-permute-start.14
  41.6 2.1 first_norm.1
  43.7 5.6 %collective-permute-done.8.refs_3_.refs_2_ = bf16[4,32,3200]{2,1,0:T(8,128)(2,1)} collective-permute-done((bf16[4,32,3200]{2,1,0:T(8,128)(2,1)}, bf16[4,32,3200]{2,1,0:T(8,128)(2,1)}, u32[]{:S(2)}, u32[]{:S(2)}) %collective-permute-start.8) | collective-permute-done | bytes 819232 | tf_op jit(solution)/shard_map/ppermute | solution.py:104
  54.5 1.4 collective-permute-done.18.refs_4_
  55.9 1.8 collective-permute-start.24
  57.7 2.6 %collective-permute-start.22 = (bf16[32,1024]{1,0:T(8,128)(2,1)S(1)}, bf16[32,1024]{1,0:T(8,128)(2,1)S(1)}, u32[]{:S(2)}, u32[]{:S(2)}) collective-permute-start(bf16[32,1024]{1,0:T(8,128)(2,1)S(1)} %copy-done.13), channel_id=1, source_target_pairs={{0,8},{1,9},{2,10},{3,11},{4,12},{5,13},{6,14},{7,15},{8,0},{9,1},... | collective-permute-start | bytes 196616 | tf_op jit(solution)/shard_map/ppermute | solution.py:104
  60.3 13.2 %attention_forward.2 = (bf16[1024,1536]{1,0:T(8,128)(2,1)}, bf16[4,2,512,512]{3,2,1,0:T(8,128)(2,1)}, bf16[1024,512]{1,0:T(8,128)(2,1)S(1)}, bf16[1024,1536]{1,0:T(8,128)(2,1)}) custom-call(s32[8]{0:T(128)S(1)} %stack.92.meta, bf16[1024,1024]{1,0:T(8,128)(2,1)S(1)} %get-tuple-element.101.first_ref, f32[16,1024]{1,0:T(8,128)S(1)} %get-tuple-element.100.small_ref, ...), custom_call_target="tpu_custom_call" | custom-call | flops 1 | bytes 1 | tf_op jit(solution)/shard_map/attention_forward/pallas_call | solution.py:36
  75.1 1.4 collective-permute-start.29
  76.6 13.4 %attention_forward.3 = (bf16[1024,1536]{1,0:T(8,128)(2,1)}, bf16[4,2,512,512]{3,2,1,0:T(8,128)(2,1)}, bf16[1024,512]{1,0:T(8,128)(2,1)S(1)}, bf16[1024,1536]{1,0:T(8,128)(2,1)}) custom-call(s32[8]{0:T(128)S(1)} %stack.92.meta, bf16[1024,1024]{1,0:T(8,128)(2,1)S(1)} %get-tuple-element.101.first_ref, f32[16,1024]{1,0:T(8,128)S(1)} %get-tuple-element.100.small_ref, ...), custom_call_target="tpu_custom_call" | custom-call | flops 1 | bytes 1 | tf_op jit(solution)/shard_map/attention_forward/pallas_call | solution.py:36
  91.5 5.1 %collective-permute-done.30.refs_3_ = bf16[4,32,1024]{2,1,0:T(8,128)(2,1)S(1)} collective-permute-done((bf16[4,32,1024]{2,1,0:T(8,128)(2,1)S(1)}, bf16[4,32,1024]{2,1,0:T(8,128)(2,1)S(1)}, u32[]{:S(2)}, u32[]{:S(2)}) %collective-permute-start.30) | collective-permute-done | bytes 262176 | tf_op jit(solution)/shard_map/ppermute | solution.py:104
  96.6 11.2 %feed_forward_first.1 = (f32[1024,1024]{1,0:T(8,128)S(1)}, bf16[1024,1024]{1,0:T(8,128)(2,1)S(1)}, bf16[1024,1024]{1,0:T(8,128)(2,1)S(1)}, bf16[1024,1024]{1,0:T(8,128)(2,1)S(1)}) custom-call(s32[8]{0:T(128)S(1)} %stack.92.meta, bf16[1024,1024]{1,0:T(8,128)(2,1)S(1)} %bitcast.40, f32[16,1024]{1,0:T(8,128)S(1)} %get-tuple-element.100.small_ref, ...), custom_call_target="tpu_custom_call" | custom-call | flops 1 | bytes 1 | tf_op jit(solution)/shard_map/feed_forward_first/pallas_call | solution.py:36
  107.8 16.8 %feed_forward_second.1 = (bf16[1024,1024]{1,0:T(8,128)(2,1)}, bf16[1024,1024]{1,0:T(8,128)(2,1)S(1)}, bf16[2,2,4,4,128,128]{5,4,3,2,1,0:T(8,128)(2,1)S(1)}, bf16...) custom-call(s32[8]{0:T(128)S(1)} %stack.92.meta, bf16[1024,1024]{1,0:T(8,128)(2,1)S(1)} %bitcast.41, ...), custom_call_target="tpu_custom_call" | custom-call | flops 1 | bytes 1 | tf_op jit(solution)/shard_map/feed_forward_second/pallas_call | solution.py:36
  125.2 10.3 %feed_forward_third.1 = (bf16[1024,1024]{1,0:T(8,128)(2,1)S(1)}, bf16[2,2,4,2,128,128]{5,4,3,2,1,0:T(8,128)(2,1)S(1)}, bf16[2,2,4,2,128,128]{5,4,3,2,1,0:T(8,128)(2,1)S(1)}, f32[8,1024]{1,0:T(8,128)S(1)}) custom-call(s32[8]{0:T(128)S(1)} %stack.92.meta, bf16[1024,1024]{1,0:T(8,128)(2,1)S(1)} %bitcast.42, f32[16,1024]{1,0:T(8,128)S(1)} %get-tuple-element.100.small_ref, ...), custom_call_target="tpu_custom_call" | custom-call | flops 1 | bytes 1 | tf_op jit(solution)/shard_map/feed_forward_third/pallas_call | solution.py:36
  137.4 4.5 %mixed_grad.1 = (bf16[1024,1024]{1,0:T(8,128)(2,1)S(1)}, bf16[1024,1024]{1,0:T(8,128)(2,1)}) custom-call(s32[8]{0:T(128)S(1)} %stack.92.meta, bf16[1024,1024]{1,0:T(8,128)(2,1)S(1)} %get-tuple-element.129.attn_ref, bf16[4,32,2048]{2,1,0:T(8,128)(2,1)S(1)} %pad_maximum_fusion.refs_2_.refs_0_, ...), custom_call_target="tpu_custom_call" | custom-call | flops 1 | bytes 1 | tf_op jit(solution)/shard_map/mixed_grad/pallas_call | solution.py:36
  141.9 7.7 %attention_backward.4 = (bf16[1024,768]{1,0:T(8,128)(2,1)}, bf16[2,2,4,3,128,128]{5,4,3,2,1,0:T(8,128)(2,1)S(1)}) custom-call(s32[8]{0:T(128)S(1)} %stack.92.meta, bf16[1024,1024]{1,0:T(8,128)(2,1)S(1)} %get-tuple-element.101.first_ref, bf16[1024,1536]{1,0:T(8,128)(2,1)} %get-tuple-element.127.packed_ref, ...), custom_call_target="tpu_custom_call" | custom-call | flops 1 | bytes 1 | tf_op jit(solution)/shard_map/attention_backward/pallas_call | solution.py:36
  149.7 1.7 collective-permute-done.35.refs_2_.refs_7_
  153.2 7.7 %attention_backward.5 = (bf16[1024,768]{1,0:T(8,128)(2,1)}, bf16[2,2,4,3,128,128]{5,4,3,2,1,0:T(8,128)(2,1)S(1)}) custom-call(s32[8]{0:T(128)S(1)} %stack.92.meta, bf16[1024,1024]{1,0:T(8,128)(2,1)S(1)} %get-tuple-element.101.first_ref, bf16[1024,1536]{1,0:T(8,128)(2,1)} %get-tuple-element.127.packed_ref, ...), custom_call_target="tpu_custom_call" | custom-call | flops 1 | bytes 1 | tf_op jit(solution)/shard_map/attention_backward/pallas_call | solution.py:36
  160.9 7.9 %attention_backward.6 = (bf16[1024,768]{1,0:T(8,128)(2,1)}, bf16[2,2,4,3,128,128]{5,4,3,2,1,0:T(8,128)(2,1)S(1)}) custom-call(s32[8]{0:T(128)S(1)} %stack.92.meta, bf16[1024,1024]{1,0:T(8,128)(2,1)S(1)} %get-tuple-element.101.first_ref, bf16[1024,1536]{1,0:T(8,128)(2,1)} %get-tuple-element.137.packed_ref, ...), custom_call_target="tpu_custom_call" | custom-call | flops 1 | bytes 1 | tf_op jit(solution)/shard_map/attention_backward/pallas_call | solution.py:36
  168.9 1.5 step_2.1
  171.7 2.3 collective-permute-start.40
  174.0 2.1 collective-permute-start.41
  176.1 7.7 %attention_backward.7 = (bf16[1024,768]{1,0:T(8,128)(2,1)}, bf16[2,2,4,3,128,128]{5,4,3,2,1,0:T(8,128)(2,1)S(1)}) custom-call(s32[8]{0:T(128)S(1)} %stack.92.meta, bf16[1024,1024]{1,0:T(8,128)(2,1)S(1)} %get-tuple-element.101.first_ref, bf16[1024,1536]{1,0:T(8,128)(2,1)} %get-tuple-element.137.packed_ref, ...), custom_call_target="tpu_custom_call" | custom-call | flops 1 | bytes 1 | tf_op jit(solution)/shard_map/attention_backward/pallas_call | solution.py:36
  185.2 1.8 step_3.1
  190.8 2.1 collective-permute-start.46
  192.9 12.3 %input_grad.1 = (bf16[1024,1024]{1,0:T(8,128)(2,1)}, f32[8,1024]{1,0:T(8,128)S(1)}, f32[8,3072]{1,0:T(8,128)S(1)}) custom-call(s32[8]{0:T(128)S(1)} %stack.92.meta, bf16[1024,1024]{1,0:T(8,128)(2,1)} %bitcast.38, bf16[1024,1024]{1,0:T(8,128)(2,1)} %get-tuple-element.150.grad_ref, f32[16,1024]{1,0:T(8,128)S(1)} %get-tuple-element.100.small_ref, ...), custom_call_target="tpu_custom_call" | custom-call | flops 1 | bytes 1 | tf_op jit(solution)/shard_map/input_grad/pallas_call | solution.py:36
  205.3 2.2 step_4.1
  211.9 2.1 collective-permute-start.51
  214.0 2.8 %collective-permute-done.48.refs_1_ = bf16[4,128,128]{2,1,0:T(8,128)(2,1)S(1)} collective-permute-done((bf16[4,128,128]{2,1,0:T(8,128)(2,1)S(1)}, bf16[4,128,128]{2,1,0:T(8,128)(2,1)S(1)}, u32[]{:S(2)}, u32[]{:S(2)}) %collective-permute-start.48) | collective-permute-done | bytes 131104 | tf_op jit(solution)/shard_map/ppermute | solution.py:104
  216.8 1.5 step_7.1
  218.8 1.7 step_6.1.refs_0_
  224.2 1.7 collective-permute-start.56
  226.0 2.9 %collective-permute-done.54.refs_6_.refs_2_ = bf16[4,128,128]{2,1,0:T(8,128)(2,1)S(1)} collective-permute-done((bf16[4,128,128]{2,1,0:T(8,128)(2,1)S(1)}, bf16[4,128,128]{2,1,0:T(8,128)(2,1)S(1)}, u32[]{:S(2)}, u32[]{:S(2)}) %collective-permute-start.54) | collective-permute-done | bytes 131104 | tf_op jit(solution)/shard_map/ppermute | solution.py:104
  230.8 1.8 collective-permute-start.57
  232.6 4.7 %collective-permute-done.57.refs_3_ = bf16[3,128,128]{2,1,0:T(8,128)(2,1)S(1)} collective-permute-done((bf16[3,128,128]{2,1,0:T(8,128)(2,1)S(1)}, bf16[3,128,128]{2,1,0:T(8,128)(2,1)S(1)}, u32[]{:S(2)}, u32[]{:S(2)}) %collective-permute-start.57) | collective-permute-done | bytes 98336 | tf_op jit(solution)/shard_map/ppermute | solution.py:104
  237.3 1.5 step_9.1
  240.3 1.8 finish_rest.1
  245.2 1.9 finish_heads.1
  (158 shorter events, 43.7 us)
Async XLA Ops:
  2.8 9.1 %collective-permute-start.2 = (bf16[32,1664]{1,0:T(8,128)(2,1)S(1)}, bf16[32,1664]{1,0:T(8,128)(2,1)S(1)}, u32[]{:S(2)}, u32[]{:S(2)}) collective-permute-start(bf16[32,1664]{1,0:T(8,128)(2,1)S(1)} %fusion.1), channel_id=1, source_target_pairs={{0,24},{1,25},{2,26},{3,27},{4,28},{5,29},{6,30},{7,31},{8,16},{9,... | collective-permute-start | bytes 319496 | tf_op jit(solution)/shard_map/ppermute | solution.py:104
  7.9 9.0 %collective-permute-start.1 = (bf16[32,1664]{1,0:T(8,128)(2,1)S(1)}, bf16[32,1664]{1,0:T(8,128)(2,1)S(1)}, u32[]{:S(2)}, u32[]{:S(2)}) collective-permute-start(bf16[32,1664]{1,0:T(8,128)(2,1)S(1)} %fusion.1), channel_id=1, source_target_pairs={{0,16},{1,17},{2,18},{3,19},{4,20},{5,21},{6,22},{7,23},{8,24},{9,... | collective-permute-start | bytes 319496 | tf_op jit(solution)/shard_map/ppermute | solution.py:104
  7.9 9.0 %collective-permute-start = (bf16[32,1664]{1,0:T(8,128)(2,1)S(1)}, bf16[32,1664]{1,0:T(8,128)(2,1)S(1)}, u32[]{:S(2)}, u32[]{:S(2)}) collective-permute-start(bf16[32,1664]{1,0:T(8,128)(2,1)S(1)} %fusion.1), channel_id=1, source_target_pairs={{0,8},{1,9},{2,10},{3,11},{4,12},{5,13},{6,14},{7,15},{8,0},{9,1},... | collective-permute-start | bytes 319496 | tf_op jit(solution)/shard_map/ppermute | solution.py:104
  16.9 12.2 %collective-permute-start.4 = (bf16[4,32,1664]{2,1,0:T(8,128)(2,1)S(1)}, bf16[4,32,1664]{2,1,0:T(8,128)(2,1)S(1)}, u32[]{:S(2)}, u32[]{:S(2)}) collective-permute-start(bf16[4,32,1664]{2,1,0:T(8,128)(2,1)S(1)} %pad_maximum_fusion.1.refs_0_), channel_id=1, source_target_pairs={{0,4},{1,3},{2,6},{3,1},{4,0},{5,7},{6,2},{7,5},{8,12},{9,11},{10,... | collective-permute-start | bytes 1277960 | tf_op jit(solution)/shard_map/ppermute | solution.py:104
  18.5 12.1 %collective-permute-start.3 = (bf16[4,32,1664]{2,1,0:T(8,128)(2,1)S(1)}, bf16[4,32,1664]{2,1,0:T(8,128)(2,1)S(1)}, u32[]{:S(2)}, u32[]{:S(2)}) collective-permute-start(bf16[4,32,1664]{2,1,0:T(8,128)(2,1)S(1)} %pad_maximum_fusion.1.refs_0_), channel_id=1, source_target_pairs={{0,2},{1,5},{2,0},{3,7},{4,6},{5,1},{6,4},{7,3},{8,10},{9,13},{10,... | collective-permute-start | bytes 1277960 | tf_op jit(solution)/shard_map/ppermute | solution.py:104
  20.0 9.1 %collective-permute-start.7 = (bf16[32,1536]{1,0:T(8,128)(2,1)}, bf16[32,1536]{1,0:T(8,128)(2,1)S(1)}, u32[]{:S(2)}, u32[]{:S(2)}) collective-permute-start(bf16[32,1536]{1,0:T(8,128)(2,1)} %reshape.44), channel_id=1, source_target_pairs={{0,24},{1,25},{2,26},{3,27},{4,28},{5,29},{6,30},{7,31},{8,16},{9,... | collective-permute-start | bytes 294920 | tf_op jit(solution)/shard_map/ppermute | solution.py:104
  22.5 8.1 %collective-permute-start.6 = (bf16[32,1536]{1,0:T(8,128)(2,1)}, bf16[32,1536]{1,0:T(8,128)(2,1)S(1)}, u32[]{:S(2)}, u32[]{:S(2)}) collective-permute-start(bf16[32,1536]{1,0:T(8,128)(2,1)} %reshape.44), channel_id=1, source_target_pairs={{0,16},{1,17},{2,18},{3,19},{4,20},{5,21},{6,22},{7,23},{8,24},{9,... | collective-permute-start | bytes 294920 | tf_op jit(solution)/shard_map/ppermute | solution.py:104
  22.5 8.1 %collective-permute-start.5 = (bf16[32,1536]{1,0:T(8,128)(2,1)}, bf16[32,1536]{1,0:T(8,128)(2,1)S(1)}, u32[]{:S(2)}, u32[]{:S(2)}) collective-permute-start(bf16[32,1536]{1,0:T(8,128)(2,1)} %reshape.44), channel_id=1, source_target_pairs={{0,8},{1,9},{2,10},{3,11},{4,12},{5,13},{6,14},{7,15},{8,0},{9,1},... | collective-permute-start | bytes 294920 | tf_op jit(solution)/shard_map/ppermute | solution.py:104
  32.4 16.9 %collective-permute-start.8 = (bf16[4,32,3200]{2,1,0:T(8,128)(2,1)}, bf16[4,32,3200]{2,1,0:T(8,128)(2,1)}, u32[]{:S(2)}, u32[]{:S(2)}) collective-permute-start(bf16[4,32,3200]{2,1,0:T(8,128)(2,1)} %maximum_maximum_fusion.1), channel_id=1, source_target_pairs={{0,4},{1,3},{2,6},{3,1},{4,0},{5,7},{6,2},{7,5},{8,12},{9,11},{10,... | collective-permute-start | bytes 2457608 | tf_op jit(solution)/shard_map/ppermute | solution.py:104
  34.3 15.3 %collective-permute-start.13 = (bf16[4,32,1536]{2,1,0:T(8,128)(2,1)}, bf16[4,32,1536]{2,1,0:T(8,128)(2,1)}, u32[]{:S(2)}, u32[]{:S(2)}) collective-permute-start(bf16[4,32,1536]{2,1,0:T(8,128)(2,1)} %pad_maximum_fusion.2.refs_0_), channel_id=1, source_target_pairs={{0,2},{1,5},{2,0},{3,7},{4,6},{5,1},{6,4},{7,3},{8,10},{9,13},{10,... | collective-permute-start | bytes 1179656 | tf_op jit(solution)/shard_map/ppermute | solution.py:104
  35.6 13.8 %collective-permute-start.16 = (bf16[32,2048]{1,0:T(8,128)(2,1)S(1)}, bf16[32,2048]{1,0:T(8,128)(2,1)}, u32[]{:S(2)}, u32[]{:S(2)}) collective-permute-start(bf16[32,2048]{1,0:T(8,128)(2,1)S(1)} %pad_maximum_fusion.4), channel_id=1, source_target_pairs={{0,24},{1,25},{2,26},{3,27},{4,28},{5,29},{6,30},{7,31},{8,16},{9,... | collective-permute-start | bytes 393224 | tf_op jit(solution)/shard_map/ppermute | solution.py:104
  38.2 11.4 %collective-permute-start.15 = (bf16[32,2048]{1,0:T(8,128)(2,1)S(1)}, bf16[32,2048]{1,0:T(8,128)(2,1)}, u32[]{:S(2)}, u32[]{:S(2)}) collective-permute-start(bf16[32,2048]{1,0:T(8,128)(2,1)S(1)} %pad_maximum_fusion.4), channel_id=1, source_target_pairs={{0,16},{1,17},{2,18},{3,19},{4,20},{5,21},{6,22},{7,23},{8,24},{9,... | collective-permute-start | bytes 393224 | tf_op jit(solution)/shard_map/ppermute | solution.py:104
  39.0 10.6 %collective-permute-start.14 = (bf16[32,2048]{1,0:T(8,128)(2,1)S(1)}, bf16[32,2048]{1,0:T(8,128)(2,1)}, u32[]{:S(2)}, u32[]{:S(2)}) collective-permute-start(bf16[32,2048]{1,0:T(8,128)(2,1)S(1)} %pad_maximum_fusion.4), channel_id=1, source_target_pairs={{0,8},{1,9},{2,10},{3,11},{4,12},{5,13},{6,14},{7,15},{8,0},{9,1},... | collective-permute-start | bytes 393224 | tf_op jit(solution)/shard_map/ppermute | solution.py:104
  50.9 22.6 %collective-permute-start.17 = (bf16[4,32,3584]{2,1,0:T(8,128)(2,1)S(1)}, bf16[4,32,3584]{2,1,0:T(8,128)(2,1)S(1)}, u32[]{:S(2)}, u32[]{:S(2)}) collective-permute-start(bf16[4,32,3584]{2,1,0:T(8,128)(2,1)S(1)} %maximum_maximum_fusion), channel_id=1, source_target_pairs={{0,4},{1,3},{2,6},{3,1},{4,0},{5,7},{6,2},{7,5},{8,12},{9,11},{10,... | collective-permute-start | bytes 2752520 | tf_op jit(solution)/shard_map/ppermute | solution.py:104
  52.8 20.8 %collective-permute-start.21 = (bf16[4,32,2048]{2,1,0:T(8,128)(2,1)S(1)}, bf16[4,32,2048]{2,1,0:T(8,128)(2,1)S(1)}, u32[]{:S(2)}, u32[]{:S(2)}) collective-permute-start(bf16[4,32,2048]{2,1,0:T(8,128)(2,1)S(1)} %pad_maximum_fusion.refs_2_.refs_0_), channel_id=1, source_target_pairs={{0,2},{1,5},{2,0},{3,7},{4,6},{5,1},{6,4},{7,3},{8,10},{9,13},{10,... | collective-permute-start | bytes 1572872 | tf_op jit(solution)/shard_map/ppermute | solution.py:104
  55.9 17.7 %collective-permute-start.24 = (bf16[32,1024]{1,0:T(8,128)(2,1)S(1)}, bf16[32,1024]{1,0:T(8,128)(2,1)S(1)}, u32[]{:S(2)}, u32[]{:S(2)}) collective-permute-start(bf16[32,1024]{1,0:T(8,128)(2,1)S(1)} %copy-done.13), channel_id=1, source_target_pairs={{0,24},{1,25},{2,26},{3,27},{4,28},{5,29},{6,30},{7,31},{8,16},{9,... | collective-permute-start | bytes 196616 | tf_op jit(solution)/shard_map/ppermute | solution.py:104
  57.7 15.9 %collective-permute-start.23 = (bf16[32,1024]{1,0:T(8,128)(2,1)S(1)}, bf16[32,1024]{1,0:T(8,128)(2,1)S(1)}, u32[]{:S(2)}, u32[]{:S(2)}) collective-permute-start(bf16[32,1024]{1,0:T(8,128)(2,1)S(1)} %copy-done.13), channel_id=1, source_target_pairs={{0,16},{1,17},{2,18},{3,19},{4,20},{5,21},{6,22},{7,23},{8,24},{9,... | collective-permute-start | bytes 196616 | tf_op jit(solution)/shard_map/ppermute | solution.py:104
  57.7 15.9 %collective-permute-start.22 = (bf16[32,1024]{1,0:T(8,128)(2,1)S(1)}, bf16[32,1024]{1,0:T(8,128)(2,1)S(1)}, u32[]{:S(2)}, u32[]{:S(2)}) collective-permute-start(bf16[32,1024]{1,0:T(8,128)(2,1)S(1)} %copy-done.13), channel_id=1, source_target_pairs={{0,8},{1,9},{2,10},{3,11},{4,12},{5,13},{6,14},{7,15},{8,0},{9,1},... | collective-permute-start | bytes 196616 | tf_op jit(solution)/shard_map/ppermute | solution.py:104
  73.7 16.3 %collective-permute-start.25 = (bf16[4,32,3072]{2,1,0:T(8,128)(2,1)S(1)}, bf16[4,32,3072]{2,1,0:T(8,128)(2,1)S(1)}, u32[]{:S(2)}, u32[]{:S(2)}) collective-permute-start(bf16[4,32,3072]{2,1,0:T(8,128)(2,1)S(1)} %maximum_maximum_fusion.2), channel_id=1, source_target_pairs={{0,4},{1,3},{2,6},{3,1},{4,0},{5,7},{6,2},{7,5},{8,12},{9,11},{10,... | collective-permute-start | bytes 2359304 | tf_op jit(solution)/shard_map/ppermute | solution.py:104
  74.6 15.5 %collective-permute-start.26 = (bf16[4,32,2048]{2,1,0:T(8,128)(2,1)S(1)}, bf16[4,32,2048]{2,1,0:T(8,128)(2,1)S(1)}, u32[]{:S(2)}, u32[]{:S(2)}) collective-permute-start(bf16[4,32,2048]{2,1,0:T(8,128)(2,1)S(1)} %pad_maximum_fusion.refs_2_.refs_0_), channel_id=1, source_target_pairs={{0,1},{1,0},{2,3},{3,2},{4,5},{5,4},{6,7},{7,6},{8,9},{9,8},{10,11... | collective-permute-start | bytes 1572872 | tf_op jit(solution)/shard_map/ppermute | solution.py:104
  74.9 15.2 %collective-permute-start.27 = (bf16[4,32,2048]{2,1,0:T(8,128)(2,1)S(1)}, bf16[4,32,2048]{2,1,0:T(8,128)(2,1)S(1)}, u32[]{:S(2)}, u32[]{:S(2)}) collective-permute-start(bf16[4,32,2048]{2,1,0:T(8,128)(2,1)S(1)} %collective-permute-done.21.refs_3_.refs_1_), channel_id=1, source_target_pairs={{0,1},{1,0},{2,3},{3,2},{4,5},{5,4},{6,7},{7,6},{8,9},{9,8},{10,11... | collective-permute-start | bytes 1572872 | tf_op jit(solution)/shard_map/ppermute | solution.py:104
  75.1 15.0 %collective-permute-start.29 = (bf16[4,32,1024]{2,1,0:T(8,128)(2,1)S(1)}, bf16[4,32,1024]{2,1,0:T(8,128)(2,1)S(1)}, u32[]{:S(2)}, u32[]{:S(2)}) collective-permute-start(bf16[4,32,1024]{2,1,0:T(8,128)(2,1)S(1)} %pad_maximum_fusion.3.refs_0_), channel_id=1, source_target_pairs={{0,2},{1,5},{2,0},{3,7},{4,6},{5,1},{6,4},{7,3},{8,10},{9,13},{10,... | collective-permute-start | bytes 786440 | tf_op jit(solution)/shard_map/ppermute | solution.py:104
  91.0 16.8 %collective-permute-start.31 = (bf16[4,32,1024]{2,1,0:T(8,128)(2,1)S(1)}, bf16[4,32,1024]{2,1,0:T(8,128)(2,1)S(1)}, u32[]{:S(2)}, u32[]{:S(2)}) collective-permute-start(bf16[4,32,1024]{2,1,0:T(8,128)(2,1)S(1)} %pad_maximum_fusion.3.refs_0_), channel_id=1, source_target_pairs={{0,1},{1,0},{2,3},{3,2},{4,5},{5,4},{6,7},{7,6},{8,9},{9,8},{10,11... | collective-permute-start | bytes 786440 | tf_op jit(solution)/shard_map/ppermute | solution.py:104
  91.0 16.7 %collective-permute-start.32 = (bf16[4,32,1024]{2,1,0:T(8,128)(2,1)S(1)}, bf16[4,32,1024]{2,1,0:T(8,128)(2,1)S(1)}, u32[]{:S(2)}, u32[]{:S(2)}) collective-permute-start(bf16[4,32,1024]{2,1,0:T(8,128)(2,1)S(1)} %collective-permute-done.29.refs_1_), channel_id=1, source_target_pairs={{0,1},{1,0},{2,3},{3,2},{4,5},{5,4},{6,7},{7,6},{8,9},{9,8},{10,11... | collective-permute-start | bytes 786440 | tf_op jit(solution)/shard_map/ppermute | solution.py:104
  96.6 11.2 %collective-permute-start.33 = (bf16[4,32,1024]{2,1,0:T(8,128)(2,1)S(1)}, bf16[4,32,1024]{2,1,0:T(8,128)(2,1)S(1)}, u32[]{:S(2)}, u32[]{:S(2)}) collective-permute-start(bf16[4,32,1024]{2,1,0:T(8,128)(2,1)S(1)} %collective-permute-done.30.refs_3_), channel_id=1, source_target_pairs={{0,1},{1,0},{2,3},{3,2},{4,5},{5,4},{6,7},{7,6},{8,9},{9,8},{10,11... | collective-permute-start | bytes 786440 | tf_op jit(solution)/shard_map/ppermute | solution.py:104
  124.6 11.0 %collective-permute-start.34 = (bf16[2,2,4,4,128,128]{5,4,3,2,1,0:T(8,128)(2,1)S(1)}, bf16[2,2,4,4,128,128]{5,4,3,2,1,0:T(8,128)(2,1)S(1)}, u32[]{:S(2)}, u32[]{:S(2)}) collective-permute-start(bf16[2,2,4,4,128,128]{5,4,3,2,1,0:T(8,128)(2,1)S(1)} %get-tuple-element.125), channel_id=1, source_target_pairs={{0,1},{1,0},{2,3},{3,2},{4,5},{5,4},{6,7},{7,6},{8,9},{9,8},{10,11... | collective-permute-start | bytes 6291464 | tf_op jit(solution)/shard_map/ppermute | solution.py:104
  135.5 14.2 %collective-permute-start.36 = (bf16[2,2,4,2,128,128]{5,4,3,2,1,0:T(8,128)(2,1)S(1)}, bf16[2,2,4,2,128,128]{5,4,3,2,1,0:T(8,128)(2,1)S(1)}, u32[]{:S(2)}, u32[]{:S(2)}) collective-permute-start(bf16[2,2,4,2,128,128]{5,4,3,2,1,0:T(8,128)(2,1)S(1)} %get-tuple-element.133), channel_id=1, source_target_pairs={{0,1},{1,0},{2,3},{3,2},{4,5},{5,4},{6,7},{7,6},{8,9},{9,8},{10,11... | collective-permute-start | bytes 3145736 | tf_op jit(solution)/shard_map/ppermute | solution.py:104
  136.5 14.9 %collective-permute-start.35 = (bf16[32,128,128]{2,1,0:T(8,128)(2,1)S(1)}, bf16[32,128,128]{2,1,0:T(8,128)(2,1)S(1)}, u32[]{:S(2)}, u32[]{:S(2)}) collective-permute-start(bf16[32,128,128]{2,1,0:T(8,128)(2,1)S(1)} %step_0.1), channel_id=1, source_target_pairs={{0,4},{1,3},{2,6},{3,1},{4,0},{5,7},{6,2},{7,5},{8,12},{9,11},{10,... | collective-permute-start | bytes 3145736 | tf_op jit(solution)/shard_map/ppermute | solution.py:104
  149.5 19.3 %collective-permute-start.38 = (bf16[2,2,4,3,128,128]{5,4,3,2,1,0:T(8,128)(2,1)S(1)}, bf16[2,2,4,3,128,128]{5,4,3,2,1,0:T(8,128)(2,1)S(1)}, u32[]{:S(2)}, u32[]{:S(2)}) collective-permute-start(bf16[2,2,4,3,128,128]{5,4,3,2,1,0:T(8,128)(2,1)S(1)} %get-tuple-element.131), channel_id=1, source_target_pairs={{0,1},{1,0},{2,3},{3,2},{4,5},{5,4},{6,7},{7,6},{8,9},{9,8},{10,11... | collective-permute-start | bytes 4718600 | tf_op jit(solution)/shard_map/ppermute | solution.py:104
  152.5 16.4 %collective-permute-start.37 = (bf16[32,128,128]{2,1,0:T(8,128)(2,1)S(1)}, bf16[32,128,128]{2,1,0:T(8,128)(2,1)S(1)}, u32[]{:S(2)}, u32[]{:S(2)}) collective-permute-start(bf16[32,128,128]{2,1,0:T(8,128)(2,1)S(1)} %step_1.1), channel_id=1, source_target_pairs={{0,2},{1,5},{2,0},{3,7},{4,6},{5,1},{6,4},{7,3},{8,10},{9,13},{10,... | collective-permute-start | bytes 3145736 | tf_op jit(solution)/shard_map/ppermute | solution.py:104
  168.8 15.8 %collective-permute-start.43 = (bf16[2,2,4,3,128,128]{5,4,3,2,1,0:T(8,128)(2,1)S(1)}, bf16[2,2,4,3,128,128]{5,4,3,2,1,0:T(8,128)(2,1)S(1)}, u32[]{:S(2)}, u32[]{:S(2)}) collective-permute-start(bf16[2,2,4,3,128,128]{5,4,3,2,1,0:T(8,128)(2,1)S(1)} %get-tuple-element.139), channel_id=1, source_target_pairs={{0,1},{1,0},{2,3},{3,2},{4,5},{5,4},{6,7},{7,6},{8,9},{9,8},{10,11... | collective-permute-start | bytes 4718600 | tf_op jit(solution)/shard_map/ppermute | solution.py:104
  170.4 14.9 %collective-permute-start.42 = (bf16[32,128,128]{2,1,0:T(8,128)(2,1)S(1)}, bf16[32,128,128]{2,1,0:T(8,128)(2,1)S(1)}, u32[]{:S(2)}, u32[]{:S(2)}) collective-permute-start(bf16[32,128,128]{2,1,0:T(8,128)(2,1)S(1)} %get-tuple-element.141), channel_id=1, source_target_pairs={{0,4},{1,3},{2,6},{3,1},{4,0},{5,7},{6,2},{7,5},{8,12},{9,11},{10,... | collective-permute-start | bytes 3145736 | tf_op jit(solution)/shard_map/ppermute | solution.py:104
  171.7 12.1 %collective-permute-start.39 = (bf16[4,128,128]{2,1,0:T(8,128)(2,1)S(1)}, bf16[4,128,128]{2,1,0:T(8,128)(2,1)S(1)}, u32[]{:S(2)}, u32[]{:S(2)}) collective-permute-start(bf16[4,128,128]{2,1,0:T(8,128)(2,1)S(1)} %get-tuple-element.144), channel_id=1, source_target_pairs={{0,8},{1,9},{2,10},{3,11},{4,12},{5,13},{6,14},{7,15},{8,0},{9,1},... | collective-permute-start | bytes 393224 | tf_op jit(solution)/shard_map/ppermute | solution.py:104
  171.7 12.9 %collective-permute-start.40 = (bf16[4,128,128]{2,1,0:T(8,128)(2,1)S(1)}, bf16[4,128,128]{2,1,0:T(8,128)(2,1)S(1)}, u32[]{:S(2)}, u32[]{:S(2)}) collective-permute-start(bf16[4,128,128]{2,1,0:T(8,128)(2,1)S(1)} %get-tuple-element.145), channel_id=1, source_target_pairs={{0,16},{1,17},{2,18},{3,19},{4,20},{5,21},{6,22},{7,23},{8,24},{9,... | collective-permute-start | bytes 393224 | tf_op jit(solution)/shard_map/ppermute | solution.py:104
  174.0 10.6 %collective-permute-start.41 = (bf16[4,128,128]{2,1,0:T(8,128)(2,1)S(1)}, bf16[4,128,128]{2,1,0:T(8,128)(2,1)S(1)}, u32[]{:S(2)}, u32[]{:S(2)}) collective-permute-start(bf16[4,128,128]{2,1,0:T(8,128)(2,1)S(1)} %get-tuple-element.146), channel_id=1, source_target_pairs={{0,24},{1,25},{2,26},{3,27},{4,28},{5,29},{6,30},{7,31},{8,16},{9,... | collective-permute-start | bytes 393224 | tf_op jit(solution)/shard_map/ppermute | solution.py:104
  187.1 18.2 %collective-permute-start.47 = (bf16[36,128,128]{2,1,0:T(8,128)(2,1)S(1)}, bf16[36,128,128]{2,1,0:T(8,128)(2,1)S(1)}, u32[]{:S(2)}, u32[]{:S(2)}) collective-permute-start(bf16[36,128,128]{2,1,0:T(8,128)(2,1)S(1)} %get-tuple-element.148), channel_id=1, source_target_pairs={{0,2},{1,5},{2,0},{3,7},{4,6},{5,1},{6,4},{7,3},{8,10},{9,13},{10,... | collective-permute-start | bytes 3538952 | tf_op jit(solution)/shard_map/ppermute | solution.py:104
  188.5 16.7 %collective-permute-start.44 = (bf16[2,128,128]{2,1,0:T(8,128)(2,1)S(1)}, bf16[2,128,128]{2,1,0:T(8,128)(2,1)S(1)}, u32[]{:S(2)}, u32[]{:S(2)}) collective-permute-start(bf16[2,128,128]{2,1,0:T(8,128)(2,1)S(1)} %get-tuple-element.158), channel_id=1, source_target_pairs={{0,8},{1,9},{2,10},{3,11},{4,12},{5,13},{6,14},{7,15},{8,0},{9,1},... | collective-permute-start | bytes 196616 | tf_op jit(solution)/shard_map/ppermute | solution.py:104
  189.9 15.3 %collective-permute-start.45 = (bf16[2,128,128]{2,1,0:T(8,128)(2,1)S(1)}, bf16[2,128,128]{2,1,0:T(8,128)(2,1)S(1)}, u32[]{:S(2)}, u32[]{:S(2)}) collective-permute-start(bf16[2,128,128]{2,1,0:T(8,128)(2,1)S(1)} %get-tuple-element.159), channel_id=1, source_target_pairs={{0,16},{1,17},{2,18},{3,19},{4,20},{5,21},{6,22},{7,23},{8,24},{9,... | collective-permute-start | bytes 196616 | tf_op jit(solution)/shard_map/ppermute | solution.py:104
  190.8 14.4 %collective-permute-start.46 = (bf16[2,128,128]{2,1,0:T(8,128)(2,1)S(1)}, bf16[2,128,128]{2,1,0:T(8,128)(2,1)S(1)}, u32[]{:S(2)}, u32[]{:S(2)}) collective-permute-start(bf16[2,128,128]{2,1,0:T(8,128)(2,1)S(1)} %get-tuple-element.160), channel_id=1, source_target_pairs={{0,24},{1,25},{2,26},{3,27},{4,28},{5,29},{6,30},{7,31},{8,16},{9,... | collective-permute-start | bytes 196616 | tf_op jit(solution)/shard_map/ppermute | solution.py:104
  208.8 8.0 %collective-permute-start.49 = (bf16[12,128,128]{2,1,0:T(8,128)(2,1)S(1)}, bf16[12,128,128]{2,1,0:T(8,128)(2,1)S(1)}, u32[]{:S(2)}, u32[]{:S(2)}) collective-permute-start(bf16[12,128,128]{2,1,0:T(8,128)(2,1)S(1)} %step_5.1), channel_id=1, source_target_pairs={{0,4},{1,3},{2,6},{3,1},{4,0},{5,7},{6,2},{7,5},{8,12},{9,11},{10,... | collective-permute-start | bytes 1179656 | tf_op jit(solution)/shard_map/ppermute | solution.py:104
  209.6 7.2 %collective-permute-start.48 = (bf16[4,128,128]{2,1,0:T(8,128)(2,1)S(1)}, bf16[4,128,128]{2,1,0:T(8,128)(2,1)S(1)}, u32[]{:S(2)}, u32[]{:S(2)}) collective-permute-start(bf16[4,128,128]{2,1,0:T(8,128)(2,1)S(1)} %get-tuple-element.166), channel_id=1, source_target_pairs={{0,8},{1,9},{2,10},{3,11},{4,12},{5,13},{6,14},{7,15},{8,0},{9,1},... | collective-permute-start | bytes 393224 | tf_op jit(solution)/shard_map/ppermute | solution.py:104
  210.6 11.2 %collective-permute-start.50 = (bf16[4,128,128]{2,1,0:T(8,128)(2,1)S(1)}, bf16[4,128,128]{2,1,0:T(8,128)(2,1)S(1)}, u32[]{:S(2)}, u32[]{:S(2)}) collective-permute-start(bf16[4,128,128]{2,1,0:T(8,128)(2,1)S(1)} %get-tuple-element.172), channel_id=1, source_target_pairs={{0,16},{1,17},{2,18},{3,19},{4,20},{5,21},{6,22},{7,23},{8,24},{9,... | collective-permute-start | bytes 393224 | tf_op jit(solution)/shard_map/ppermute | solution.py:104
  211.9 9.9 %collective-permute-start.51 = (bf16[4,128,128]{2,1,0:T(8,128)(2,1)S(1)}, bf16[4,128,128]{2,1,0:T(8,128)(2,1)S(1)}, u32[]{:S(2)}, u32[]{:S(2)}) collective-permute-start(bf16[4,128,128]{2,1,0:T(8,128)(2,1)S(1)} %get-tuple-element.173), channel_id=1, source_target_pairs={{0,24},{1,25},{2,26},{3,27},{4,28},{5,29},{6,30},{7,31},{8,16},{9,... | collective-permute-start | bytes 393224 | tf_op jit(solution)/shard_map/ppermute | solution.py:104
  220.4 8.9 %collective-permute-start.62 = (bf16[6,128,128]{2,1,0:T(8,128)(2,1)S(1)}, bf16[6,128,128]{2,1,0:T(8,128)(2,1)S(1)}, u32[]{:S(2)}, u32[]{:S(2)}) collective-permute-start(bf16[6,128,128]{2,1,0:T(8,128)(2,1)S(1)} %step_6.1.refs_0_), channel_id=1, source_target_pairs={{0,2},{1,3},{2,0},{3,1},{4,6},{5,7},{6,4},{7,5},{8,10},{9,11},{10,... | collective-permute-start | bytes 589832 | tf_op jit(solution)/shard_map/ppermute | solution.py:104
  226.0 11.3 %collective-permute-start.53 = (bf16[4,128,128]{2,1,0:T(8,128)(2,1)S(1)}, bf16[4,128,128]{2,1,0:T(8,128)(2,1)S(1)}, u32[]{:S(2)}, u32[]{:S(2)}) collective-permute-start(bf16[4,128,128]{2,1,0:T(8,128)(2,1)S(1)} %step_8.1.refs_4_.refs_0_), channel_id=1, source_target_pairs={{0,1},{1,0},{2,3},{3,2},{4,5},{5,4},{6,7},{7,6},{8,9},{9,8},{10,11... | collective-permute-start | bytes 393224 | tf_op jit(solution)/shard_map/ppermute | solution.py:104
  228.8 8.5 %collective-permute-start.55 = (bf16[4,128,128]{2,1,0:T(8,128)(2,1)S(1)}, bf16[4,128,128]{2,1,0:T(8,128)(2,1)S(1)}, u32[]{:S(2)}, u32[]{:S(2)}) collective-permute-start(bf16[4,128,128]{2,1,0:T(8,128)(2,1)S(1)} %collective-permute-done.54.refs_6_.refs_2_), channel_id=1, source_target_pairs={{0,1},{1,0},{2,3},{3,2},{4,5},{5,4},{6,7},{7,6},{8,9},{9,8},{10,11... | collective-permute-start | bytes 393224 | tf_op jit(solution)/shard_map/ppermute | solution.py:104
  228.8 11.4 %collective-permute-start.61 = (bf16[6,128,128]{2,1,0:T(8,128)(2,1)S(1)}, bf16[6,128,128]{2,1,0:T(8,128)(2,1)S(1)}, u32[]{:S(2)}, u32[]{:S(2)}) collective-permute-start(bf16[6,128,128]{2,1,0:T(8,128)(2,1)S(1)} %step_6.1.refs_0_), channel_id=1, source_target_pairs={{0,1},{1,0},{2,3},{3,2},{4,5},{5,4},{6,7},{7,6},{8,9},{9,8},{10,11... | collective-permute-start | bytes 589832 | tf_op jit(solution)/shard_map/ppermute | solution.py:104
  229.4 10.9 %collective-permute-start.63 = (bf16[6,128,128]{2,1,0:T(8,128)(2,1)S(1)}, bf16[6,128,128]{2,1,0:T(8,128)(2,1)S(1)}, u32[]{:S(2)}, u32[]{:S(2)}) collective-permute-start(bf16[6,128,128]{2,1,0:T(8,128)(2,1)S(1)} %collective-permute-done.62.refs_2_), channel_id=1, source_target_pairs={{0,1},{1,0},{2,3},{3,2},{4,5},{5,4},{6,7},{7,6},{8,9},{9,8},{10,11... | collective-permute-start | bytes 589832 | tf_op jit(solution)/shard_map/ppermute | solution.py:104
  (31 other events, 240.7 us)

commit v6 on v5

--- a/solution.py
+++ b/solution.py
@@ -896,7 +896,8 @@
             if i == 1:
                 kept.extend(first_norm(meta, x, [part for part, _ in chunks[0][:3]]))
                 return kept + other.early(chunks[0], 3)
-            return other.early(chunks[i - 1], 2) + forward(i - 2, chunks[i - 2])
+            gates = other.early(chunks[i - 1], 2) + forward(i - 2, chunks[i - 2])
+            return gates + other.early(chunks[i], 2, *mixed) if i == 3 else gates
 
     packed, probs, mixed, weights, kept = [], [], [], [], []
 
@@ -921,7 +922,7 @@
     outer, inner = chunks[len(bases) :]
     outer = outer if native else other(outer, mixed[1])
     middle, second, active, slope = feed_forward_first(meta, x, small, mixed, outer)
-    inner = inner if native else other(inner, mixed[1])
+    inner = inner if native else other(inner, active)
     out, hidden, send, keep, sums_two = feed_forward_second(
         meta, cot, small, middle, second, active, slope, inner
     )
@@ -991,9 +992,10 @@
     def along(arrays):
         return [arrays[0]] + [move(a, p) for a, p in zip(arrays[1:], links.z)]
 
-    def share(value):
+    def share(value, *gates):
         by_y = move(value, links.y)
-        return [value, move(value, links.core), by_y, move(by_y, links.core)]
+        own, theirs = (move(after(v, *gates), links.core) for v in (value, by_y))
+        return [value, own, by_y, theirs]
 
     both = Piece(keep, to_core(send), False)
     step = Step()
@@ -1058,23 +1060,27 @@
     step.share([z_one])
     (r_one,) = step.run(after(meta, z_two[0]), "step_8")
     z_two = along(z_two)
-    r_one = share(after(r_one, z_two[1]))
+    r_one = after(r_one, z_two[1])
 
     step = Step()
     step.share([z_two])
+    (r_two,) = step.run(meta, "step_9")
+    r_one = share(r_one, r_two)
+    step = Step()
     step.small(r_one)
-    r_two, other, smalls = step.run(meta, "step_9")
-    smalls = smalls + move(other, links.x)
+    other, smalls = step.run(after(meta, r_two), "step_10")
     rest = finish(
-        after(meta, r_two),
+        after(meta, other),
         [r_rest],
         [lambda q, j: (2 - j // 2, q * 2 + j % 2)],
         [width] * 3,
         "finish_rest",
     )
+    r_two = share(r_two, rest[0])
+    smalls = smalls + move(other, links.x)
     (heads,) = finish(
         meta,
-        [r_one, share(r_two)],
+        [r_one, r_two],
         [lambda q, j: (0, j * HEADS + q), lambda q, j: (0, j * HEADS + GROUP + q)],
         [3 * width],
         "finish_heads",

time: 247 us -> 243 us (0.984)
  waiting for transfers between devices: 40 us -> 34.8 us
    ppermute x65, waiting for transfers between devices: 40 us -> 34.8 us  [move(): return lax.ppermute(value, AXES, pairs)]
    pallas_call x24 -> x25, Pallas kernels: 133 us -> 134 us  [call(): pl.pallas_call(kernel, out_shape=shapes, grid_spec=pltpu.PrefetchScalarGr...]
  transfers between devices with their start and end apart: 65 -> 65, of which waited for: 16 -> 17; matrix products, arithmetic and copies ran while one was open for 3% -> 3% of each run, Pallas kernels for 44% -> 45%
where the time goes in v6:
time: 243 us
  Pallas kernels  134 us (55%)
  starting transfers between devices  58.7 us (24%)
  waiting for transfers between devices  34.8 us (14%)
  local copies, waits for them, and re-layouts  8.75 us (4%)
  other arithmetic  5.89 us (2%)
    pallas_call x25, Pallas kernels, call(): pl.pallas_call(kernel, out_shape=shapes, grid_spec=pltpu.PrefetchScalarGr...  134 us
    ppermute x65, starting transfers between devices, move(): return lax.ppermute(value, AXES, pairs)  58.7 us
    ppermute x65, waiting for transfers between devices, move(): return lax.ppermute(value, AXES, pairs)  34.8 us
  transfers between devices with their start and end apart: 65, of which 17 were waited for; matrix products, arithmetic and copies ran while one was open for 3% of the time, Pallas kernels for 45%

profile of v6, /device:TPU:0, one launch (start us, length us, event | category | flops | bytes accessed | tf_op | source)
XLA Modules:
  0.0 243.0 jit_solution(13992793663356637348)
XLA Ops:
  2.8 5.1 %collective-permute-start.2 = (bf16[32,1664]{1,0:T(8,128)(2,1)S(1)}, bf16[32,1664]{1,0:T(8,128)(2,1)S(1)}, u32[]{:S(2)}, u32[]{:S(2)}) collective-permute-start(bf16[32,1664]{1,0:T(8,128)(2,1)S(1)} %fusion.1), channel_id=1, source_target_pairs={{0,24},{1,25},{2,26},{3,27},{4,28},{5,29},{6,30},{7,31},{8,16},{9,... | collective-permute-start | bytes 319496 | tf_op jit(solution)/shard_map/ppermute | solution.py:104
  10.3 1.6 constant_dynamic-slice_fusion
  11.9 5.0 %collective-permute-done.1 = bf16[32,1664]{1,0:T(8,128)(2,1)S(1)} collective-permute-done((bf16[32,1664]{1,0:T(8,128)(2,1)S(1)}, bf16[32,1664]{1,0:T(8,128)(2,1)S(1)}, u32[]{:S(2)}, u32[]{:S(2)}) %collective-permute-start.1) | collective-permute-done | bytes 106528 | tf_op jit(solution)/shard_map/ppermute | solution.py:104
  16.9 1.6 collective-permute-start.4
  18.5 1.5 collective-permute-start.3
  20.0 2.5 %collective-permute-start.7 = (bf16[32,1536]{1,0:T(8,128)(2,1)}, bf16[32,1536]{1,0:T(8,128)(2,1)S(1)}, u32[]{:S(2)}, u32[]{:S(2)}) collective-permute-start(bf16[32,1536]{1,0:T(8,128)(2,1)} %reshape.44), channel_id=1, source_target_pairs={{0,24},{1,25},{2,26},{3,27},{4,28},{5,29},{6,30},{7,31},{8,16},{9,... | collective-permute-start | bytes 294920 | tf_op jit(solution)/shard_map/ppermute | solution.py:104
  22.5 1.9 collective-permute-start.5
  24.4 4.7 %collective-permute-done.4.refs_2_ = bf16[4,32,1664]{2,1,0:T(8,128)(2,1)S(1)} collective-permute-done((bf16[4,32,1664]{2,1,0:T(8,128)(2,1)S(1)}, bf16[4,32,1664]{2,1,0:T(8,128)(2,1)S(1)}, u32[]{:S(2)}, u32[]{:S(2)}) %collective-permute-start.4) | collective-permute-done | bytes 426016 | tf_op jit(solution)/shard_map/ppermute | solution.py:104
  29.1 1.5 collective-permute-done.6
  30.6 1.8 maximum_maximum_fusion.1
  35.6 1.9 collective-permute-start.16
  39.0 2.5 %collective-permute-start.14 = (bf16[32,2048]{1,0:T(8,128)(2,1)S(1)}, bf16[32,2048]{1,0:T(8,128)(2,1)}, u32[]{:S(2)}, u32[]{:S(2)}) collective-permute-start(bf16[32,2048]{1,0:T(8,128)(2,1)S(1)} %pad_maximum_fusion.4), channel_id=1, source_target_pairs={{0,8},{1,9},{2,10},{3,11},{4,12},{5,13},{6,14},{7,15},{8,0},{9,1},... | collective-permute-start | bytes 393224 | tf_op jit(solution)/shard_map/ppermute | solution.py:104
  41.6 2.1 first_norm.1
  43.7 5.6 %collective-permute-done.8.refs_3_.refs_2_ = bf16[4,32,3200]{2,1,0:T(8,128)(2,1)} collective-permute-done((bf16[4,32,3200]{2,1,0:T(8,128)(2,1)}, bf16[4,32,3200]{2,1,0:T(8,128)(2,1)}, u32[]{:S(2)}, u32[]{:S(2)}) %collective-permute-start.8) | collective-permute-done | bytes 819232 | tf_op jit(solution)/shard_map/ppermute | solution.py:104
  54.5 1.4 collective-permute-done.18.refs_4_
  55.9 1.8 collective-permute-start.24
  57.7 2.6 %collective-permute-start.22 = (bf16[32,1024]{1,0:T(8,128)(2,1)S(1)}, bf16[32,1024]{1,0:T(8,128)(2,1)S(1)}, u32[]{:S(2)}, u32[]{:S(2)}) collective-permute-start(bf16[32,1024]{1,0:T(8,128)(2,1)S(1)} %copy-done.13), channel_id=1, source_target_pairs={{0,8},{1,9},{2,10},{3,11},{4,12},{5,13},{6,14},{7,15},{8,0},{9,1},... | collective-permute-start | bytes 196616 | tf_op jit(solution)/shard_map/ppermute | solution.py:104
  60.3 13.2 %attention_forward.2 = (bf16[1024,1536]{1,0:T(8,128)(2,1)}, bf16[4,2,512,512]{3,2,1,0:T(8,128)(2,1)}, bf16[1024,512]{1,0:T(8,128)(2,1)S(1)}, bf16[1024,1536]{1,0:T(8,128)(2,1)}) custom-call(s32[8]{0:T(128)S(1)} %stack.92.meta, bf16[1024,1024]{1,0:T(8,128)(2,1)S(1)} %get-tuple-element.105.first_ref, f32[16,1024]{1,0:T(8,128)S(1)} %get-tuple-element.104.small_ref, ...), custom_call_target="tpu_custom_call" | custom-call | flops 1 | bytes 1 | tf_op jit(solution)/shard_map/attention_forward/pallas_call | solution.py:36
  76.1 13.4 %attention_forward.3 = (bf16[1024,1536]{1,0:T(8,128)(2,1)}, bf16[4,2,512,512]{3,2,1,0:T(8,128)(2,1)}, bf16[1024,512]{1,0:T(8,128)(2,1)S(1)}, bf16[1024,1536]{1,0:T(8,128)(2,1)}) custom-call(s32[8]{0:T(128)S(1)} %stack.92.meta, bf16[1024,1024]{1,0:T(8,128)(2,1)S(1)} %get-tuple-element.105.first_ref, f32[16,1024]{1,0:T(8,128)S(1)} %get-tuple-element.104.small_ref, ...), custom_call_target="tpu_custom_call" | custom-call | flops 1 | bytes 1 | tf_op jit(solution)/shard_map/attention_forward/pallas_call | solution.py:36
  90.7 1.8 collective-permute-done.30.refs_4_
  93.6 11.2 %feed_forward_first.1 = (f32[1024,1024]{1,0:T(8,128)S(1)}, bf16[1024,1024]{1,0:T(8,128)(2,1)S(1)}, bf16[1024,1024]{1,0:T(8,128)(2,1)S(1)}, bf16[1024,1024]{1,0:T(8,128)(2,1)S(1)}) custom-call(s32[8]{0:T(128)S(1)} %stack.92.meta, bf16[1024,1024]{1,0:T(8,128)(2,1)S(1)} %bitcast.40, f32[16,1024]{1,0:T(8,128)S(1)} %get-tuple-element.104.small_ref, ...), custom_call_target="tpu_custom_call" | custom-call | flops 1 | bytes 1 | tf_op jit(solution)/shard_map/feed_forward_first/pallas_call | solution.py:36
  106.4 16.8 %feed_forward_second.1 = (bf16[1024,1024]{1,0:T(8,128)(2,1)}, bf16[1024,1024]{1,0:T(8,128)(2,1)S(1)}, bf16[2,2,4,4,128,128]{5,4,3,2,1,0:T(8,128)(2,1)S(1)}, bf16...) custom-call(s32[8]{0:T(128)S(1)} %stack.92.meta, bf16[1024,1024]{1,0:T(8,128)(2,1)S(1)} %bitcast.41, ...), custom_call_target="tpu_custom_call" | custom-call | flops 1 | bytes 1 | tf_op jit(solution)/shard_map/feed_forward_second/pallas_call | solution.py:36
  123.5 10.3 %feed_forward_third.1 = (bf16[1024,1024]{1,0:T(8,128)(2,1)S(1)}, bf16[2,2,4,2,128,128]{5,4,3,2,1,0:T(8,128)(2,1)S(1)}, bf16[2,2,4,2,128,128]{5,4,3,2,1,0:T(8,128)(2,1)S(1)}, f32[8,1024]{1,0:T(8,128)S(1)}) custom-call(s32[8]{0:T(128)S(1)} %stack.92.meta, bf16[1024,1024]{1,0:T(8,128)(2,1)S(1)} %bitcast.42, f32[16,1024]{1,0:T(8,128)S(1)} %get-tuple-element.104.small_ref, ...), custom_call_target="tpu_custom_call" | custom-call | flops 1 | bytes 1 | tf_op jit(solution)/shard_map/feed_forward_third/pallas_call | solution.py:36
  135.1 1.3 collective-permute-start.35
  136.4 4.5 %mixed_grad.1 = (bf16[1024,1024]{1,0:T(8,128)(2,1)S(1)}, bf16[1024,1024]{1,0:T(8,128)(2,1)}) custom-call(s32[8]{0:T(128)S(1)} %stack.92.meta, bf16[1024,1024]{1,0:T(8,128)(2,1)S(1)} %get-tuple-element.133.attn_ref, bf16[4,32,2048]{2,1,0:T(8,128)(2,1)S(1)} %pad_maximum_fusion.refs_2_.refs_0_, ...), custom_call_target="tpu_custom_call" | custom-call | flops 1 | bytes 1 | tf_op jit(solution)/shard_map/mixed_grad/pallas_call | solution.py:36
  140.9 7.7 %attention_backward.4 = (bf16[1024,768]{1,0:T(8,128)(2,1)}, bf16[2,2,4,3,128,128]{5,4,3,2,1,0:T(8,128)(2,1)S(1)}) custom-call(s32[8]{0:T(128)S(1)} %stack.92.meta, bf16[1024,1024]{1,0:T(8,128)(2,1)S(1)} %get-tuple-element.105.first_ref, bf16[1024,1536]{1,0:T(8,128)(2,1)} %get-tuple-element.131.packed_ref, ...), custom_call_target="tpu_custom_call" | custom-call | flops 1 | bytes 1 | tf_op jit(solution)/shard_map/attention_backward/pallas_call | solution.py:36
  151.0 1.4 collective-permute-start.37
  152.5 7.7 %attention_backward.5 = (bf16[1024,768]{1,0:T(8,128)(2,1)}, bf16[2,2,4,3,128,128]{5,4,3,2,1,0:T(8,128)(2,1)S(1)}) custom-call(s32[8]{0:T(128)S(1)} %stack.92.meta, bf16[1024,1024]{1,0:T(8,128)(2,1)S(1)} %get-tuple-element.105.first_ref, bf16[1024,1536]{1,0:T(8,128)(2,1)} %get-tuple-element.131.packed_ref, ...), custom_call_target="tpu_custom_call" | custom-call | flops 1 | bytes 1 | tf_op jit(solution)/shard_map/attention_backward/pallas_call | solution.py:36
  160.2 7.9 %attention_backward.6 = (bf16[1024,768]{1,0:T(8,128)(2,1)}, bf16[2,2,4,3,128,128]{5,4,3,2,1,0:T(8,128)(2,1)S(1)}) custom-call(s32[8]{0:T(128)S(1)} %stack.92.meta, bf16[1024,1024]{1,0:T(8,128)(2,1)S(1)} %get-tuple-element.105.first_ref, bf16[1024,1536]{1,0:T(8,128)(2,1)} %get-tuple-element.141.packed_ref, ...), custom_call_target="tpu_custom_call" | custom-call | flops 1 | bytes 1 | tf_op jit(solution)/shard_map/attention_backward/pallas_call | solution.py:36
  168.1 1.5 step_2.1
  170.5 2.3 collective-permute-start.40
  172.8 2.1 collective-permute-start.41
  174.9 7.7 %attention_backward.7 = (bf16[1024,768]{1,0:T(8,128)(2,1)}, bf16[2,2,4,3,128,128]{5,4,3,2,1,0:T(8,128)(2,1)S(1)}) custom-call(s32[8]{0:T(128)S(1)} %stack.92.meta, bf16[1024,1024]{1,0:T(8,128)(2,1)S(1)} %get-tuple-element.105.first_ref, bf16[1024,1536]{1,0:T(8,128)(2,1)} %get-tuple-element.141.packed_ref, ...), custom_call_target="tpu_custom_call" | custom-call | flops 1 | bytes 1 | tf_op jit(solution)/shard_map/attention_backward/pallas_call | solution.py:36
  184.5 1.8 step_3.1
  187.0 2.2 collective-permute-start.44
  189.5 2.1 collective-permute-start.46
  191.6 12.3 %input_grad.1 = (bf16[1024,1024]{1,0:T(8,128)(2,1)}, f32[8,1024]{1,0:T(8,128)S(1)}, f32[8,3072]{1,0:T(8,128)S(1)}) custom-call(s32[8]{0:T(128)S(1)} %stack.92.meta, bf16[1024,1024]{1,0:T(8,128)(2,1)} %bitcast.38, bf16[1024,1024]{1,0:T(8,128)(2,1)} %get-tuple-element.154.grad_ref, f32[16,1024]{1,0:T(8,128)S(1)} %get-tuple-element.104.small_ref, ...), custom_call_target="tpu_custom_call" | custom-call | flops 1 | bytes 1 | tf_op jit(solution)/shard_map/input_grad/pallas_call | solution.py:36
  203.9 2.2 step_4.1
  209.4 1.5 collective-permute-start.50
  210.9 2.1 collective-permute-start.51
  213.0 1.7 step_6.1.refs_0_
  216.7 1.5 step_7.1
  218.4 2.0 collective-permute-done.50.refs_2_
  221.6 1.3 collective-permute-done.52.refs_1_
  224.6 2.1 collective-permute-start.54
  227.2 4.9 %collective-permute-done.53.refs_2_ = bf16[3,128,128]{2,1,0:T(8,128)(2,1)S(1)} collective-permute-done((bf16[3,128,128]{2,1,0:T(8,128)(2,1)S(1)}, bf16[3,128,128]{2,1,0:T(8,128)(2,1)S(1)}, u32[]{:S(2)}, u32[]{:S(2)}) %collective-permute-start.53) | collective-permute-done | bytes 98336 | tf_op jit(solution)/shard_map/ppermute | solution.py:104
  237.0 1.8 finish_rest.1
  241.1 1.9 finish_heads.1
  (159 shorter events, 44.8 us)
Async XLA Ops:
  2.8 9.1 %collective-permute-start.2 = (bf16[32,1664]{1,0:T(8,128)(2,1)S(1)}, bf16[32,1664]{1,0:T(8,128)(2,1)S(1)}, u32[]{:S(2)}, u32[]{:S(2)}) collective-permute-start(bf16[32,1664]{1,0:T(8,128)(2,1)S(1)} %fusion.1), channel_id=1, source_target_pairs={{0,24},{1,25},{2,26},{3,27},{4,28},{5,29},{6,30},{7,31},{8,16},{9,... | collective-permute-start | bytes 319496 | tf_op jit(solution)/shard_map/ppermute | solution.py:104
  7.9 9.0 %collective-permute-start.1 = (bf16[32,1664]{1,0:T(8,128)(2,1)S(1)}, bf16[32,1664]{1,0:T(8,128)(2,1)S(1)}, u32[]{:S(2)}, u32[]{:S(2)}) collective-permute-start(bf16[32,1664]{1,0:T(8,128)(2,1)S(1)} %fusion.1), channel_id=1, source_target_pairs={{0,16},{1,17},{2,18},{3,19},{4,20},{5,21},{6,22},{7,23},{8,24},{9,... | collective-permute-start | bytes 319496 | tf_op jit(solution)/shard_map/ppermute | solution.py:104
  7.9 9.0 %collective-permute-start = (bf16[32,1664]{1,0:T(8,128)(2,1)S(1)}, bf16[32,1664]{1,0:T(8,128)(2,1)S(1)}, u32[]{:S(2)}, u32[]{:S(2)}) collective-permute-start(bf16[32,1664]{1,0:T(8,128)(2,1)S(1)} %fusion.1), channel_id=1, source_target_pairs={{0,8},{1,9},{2,10},{3,11},{4,12},{5,13},{6,14},{7,15},{8,0},{9,1},... | collective-permute-start | bytes 319496 | tf_op jit(solution)/shard_map/ppermute | solution.py:104
  16.9 12.2 %collective-permute-start.4 = (bf16[4,32,1664]{2,1,0:T(8,128)(2,1)S(1)}, bf16[4,32,1664]{2,1,0:T(8,128)(2,1)S(1)}, u32[]{:S(2)}, u32[]{:S(2)}) collective-permute-start(bf16[4,32,1664]{2,1,0:T(8,128)(2,1)S(1)} %pad_maximum_fusion.1.refs_0_), channel_id=1, source_target_pairs={{0,4},{1,3},{2,6},{3,1},{4,0},{5,7},{6,2},{7,5},{8,12},{9,11},{10,... | collective-permute-start | bytes 1277960 | tf_op jit(solution)/shard_map/ppermute | solution.py:104
  18.5 12.1 %collective-permute-start.3 = (bf16[4,32,1664]{2,1,0:T(8,128)(2,1)S(1)}, bf16[4,32,1664]{2,1,0:T(8,128)(2,1)S(1)}, u32[]{:S(2)}, u32[]{:S(2)}) collective-permute-start(bf16[4,32,1664]{2,1,0:T(8,128)(2,1)S(1)} %pad_maximum_fusion.1.refs_0_), channel_id=1, source_target_pairs={{0,2},{1,5},{2,0},{3,7},{4,6},{5,1},{6,4},{7,3},{8,10},{9,13},{10,... | collective-permute-start | bytes 1277960 | tf_op jit(solution)/shard_map/ppermute | solution.py:104
  20.0 9.1 %collective-permute-start.7 = (bf16[32,1536]{1,0:T(8,128)(2,1)}, bf16[32,1536]{1,0:T(8,128)(2,1)S(1)}, u32[]{:S(2)}, u32[]{:S(2)}) collective-permute-start(bf16[32,1536]{1,0:T(8,128)(2,1)} %reshape.44), channel_id=1, source_target_pairs={{0,24},{1,25},{2,26},{3,27},{4,28},{5,29},{6,30},{7,31},{8,16},{9,... | collective-permute-start | bytes 294920 | tf_op jit(solution)/shard_map/ppermute | solution.py:104
  22.5 8.1 %collective-permute-start.6 = (bf16[32,1536]{1,0:T(8,128)(2,1)}, bf16[32,1536]{1,0:T(8,128)(2,1)S(1)}, u32[]{:S(2)}, u32[]{:S(2)}) collective-permute-start(bf16[32,1536]{1,0:T(8,128)(2,1)} %reshape.44), channel_id=1, source_target_pairs={{0,16},{1,17},{2,18},{3,19},{4,20},{5,21},{6,22},{7,23},{8,24},{9,... | collective-permute-start | bytes 294920 | tf_op jit(solution)/shard_map/ppermute | solution.py:104
  22.5 8.1 %collective-permute-start.5 = (bf16[32,1536]{1,0:T(8,128)(2,1)}, bf16[32,1536]{1,0:T(8,128)(2,1)S(1)}, u32[]{:S(2)}, u32[]{:S(2)}) collective-permute-start(bf16[32,1536]{1,0:T(8,128)(2,1)} %reshape.44), channel_id=1, source_target_pairs={{0,8},{1,9},{2,10},{3,11},{4,12},{5,13},{6,14},{7,15},{8,0},{9,1},... | collective-permute-start | bytes 294920 | tf_op jit(solution)/shard_map/ppermute | solution.py:104
  32.4 16.9 %collective-permute-start.8 = (bf16[4,32,3200]{2,1,0:T(8,128)(2,1)}, bf16[4,32,3200]{2,1,0:T(8,128)(2,1)}, u32[]{:S(2)}, u32[]{:S(2)}) collective-permute-start(bf16[4,32,3200]{2,1,0:T(8,128)(2,1)} %maximum_maximum_fusion.1), channel_id=1, source_target_pairs={{0,4},{1,3},{2,6},{3,1},{4,0},{5,7},{6,2},{7,5},{8,12},{9,11},{10,... | collective-permute-start | bytes 2457608 | tf_op jit(solution)/shard_map/ppermute | solution.py:104
  34.3 15.3 %collective-permute-start.13 = (bf16[4,32,1536]{2,1,0:T(8,128)(2,1)}, bf16[4,32,1536]{2,1,0:T(8,128)(2,1)}, u32[]{:S(2)}, u32[]{:S(2)}) collective-permute-start(bf16[4,32,1536]{2,1,0:T(8,128)(2,1)} %pad_maximum_fusion.2.refs_0_), channel_id=1, source_target_pairs={{0,2},{1,5},{2,0},{3,7},{4,6},{5,1},{6,4},{7,3},{8,10},{9,13},{10,... | collective-permute-start | bytes 1179656 | tf_op jit(solution)/shard_map/ppermute | solution.py:104
  35.6 13.8 %collective-permute-start.16 = (bf16[32,2048]{1,0:T(8,128)(2,1)S(1)}, bf16[32,2048]{1,0:T(8,128)(2,1)}, u32[]{:S(2)}, u32[]{:S(2)}) collective-permute-start(bf16[32,2048]{1,0:T(8,128)(2,1)S(1)} %pad_maximum_fusion.4), channel_id=1, source_target_pairs={{0,24},{1,25},{2,26},{3,27},{4,28},{5,29},{6,30},{7,31},{8,16},{9,... | collective-permute-start | bytes 393224 | tf_op jit(solution)/shard_map/ppermute | solution.py:104
  38.2 11.4 %collective-permute-start.15 = (bf16[32,2048]{1,0:T(8,128)(2,1)S(1)}, bf16[32,2048]{1,0:T(8,128)(2,1)}, u32[]{:S(2)}, u32[]{:S(2)}) collective-permute-start(bf16[32,2048]{1,0:T(8,128)(2,1)S(1)} %pad_maximum_fusion.4), channel_id=1, source_target_pairs={{0,16},{1,17},{2,18},{3,19},{4,20},{5,21},{6,22},{7,23},{8,24},{9,... | collective-permute-start | bytes 393224 | tf_op jit(solution)/shard_map/ppermute | solution.py:104
  39.0 10.6 %collective-permute-start.14 = (bf16[32,2048]{1,0:T(8,128)(2,1)S(1)}, bf16[32,2048]{1,0:T(8,128)(2,1)}, u32[]{:S(2)}, u32[]{:S(2)}) collective-permute-start(bf16[32,2048]{1,0:T(8,128)(2,1)S(1)} %pad_maximum_fusion.4), channel_id=1, source_target_pairs={{0,8},{1,9},{2,10},{3,11},{4,12},{5,13},{6,14},{7,15},{8,0},{9,1},... | collective-permute-start | bytes 393224 | tf_op jit(solution)/shard_map/ppermute | solution.py:104
  50.9 22.6 %collective-permute-start.17 = (bf16[4,32,3584]{2,1,0:T(8,128)(2,1)S(1)}, bf16[4,32,3584]{2,1,0:T(8,128)(2,1)S(1)}, u32[]{:S(2)}, u32[]{:S(2)}) collective-permute-start(bf16[4,32,3584]{2,1,0:T(8,128)(2,1)S(1)} %maximum_maximum_fusion), channel_id=1, source_target_pairs={{0,4},{1,3},{2,6},{3,1},{4,0},{5,7},{6,2},{7,5},{8,12},{9,11},{10,... | collective-permute-start | bytes 2752520 | tf_op jit(solution)/shard_map/ppermute | solution.py:104
  51.7 6.0 %collective-permute-start.12 = (bf16[4,32,3200]{2,1,0:T(8,128)(2,1)}, bf16[4,32,3200]{2,1,0:T(8,128)(2,1)S(1)}, u32[]{:S(2)}, u32[]{:S(2)}) collective-permute-start(bf16[4,32,3200]{2,1,0:T(8,128)(2,1)} %collective-permute-done.8.refs_3_.refs_2_), channel_id=1, source_target_pairs={{0,1},{1,0},{2,3},{3,2},{4,5},{5,4},{6,7},{7,6},{8,9},{9,8},{10,11... | collective-permute-start | bytes 2457608 | tf_op jit(solution)/shard_map/ppermute | solution.py:104
  52.8 20.8 %collective-permute-start.21 = (bf16[4,32,2048]{2,1,0:T(8,128)(2,1)S(1)}, bf16[4,32,2048]{2,1,0:T(8,128)(2,1)S(1)}, u32[]{:S(2)}, u32[]{:S(2)}) collective-permute-start(bf16[4,32,2048]{2,1,0:T(8,128)(2,1)S(1)} %pad_maximum_fusion.refs_2_.refs_0_), channel_id=1, source_target_pairs={{0,2},{1,5},{2,0},{3,7},{4,6},{5,1},{6,4},{7,3},{8,10},{9,13},{10,... | collective-permute-start | bytes 1572872 | tf_op jit(solution)/shard_map/ppermute | solution.py:104
  55.9 17.7 %collective-permute-start.24 = (bf16[32,1024]{1,0:T(8,128)(2,1)S(1)}, bf16[32,1024]{1,0:T(8,128)(2,1)S(1)}, u32[]{:S(2)}, u32[]{:S(2)}) collective-permute-start(bf16[32,1024]{1,0:T(8,128)(2,1)S(1)} %copy-done.13), channel_id=1, source_target_pairs={{0,24},{1,25},{2,26},{3,27},{4,28},{5,29},{6,30},{7,31},{8,16},{9,... | collective-permute-start | bytes 196616 | tf_op jit(solution)/shard_map/ppermute | solution.py:104
  57.7 15.9 %collective-permute-start.23 = (bf16[32,1024]{1,0:T(8,128)(2,1)S(1)}, bf16[32,1024]{1,0:T(8,128)(2,1)S(1)}, u32[]{:S(2)}, u32[]{:S(2)}) collective-permute-start(bf16[32,1024]{1,0:T(8,128)(2,1)S(1)} %copy-done.13), channel_id=1, source_target_pairs={{0,16},{1,17},{2,18},{3,19},{4,20},{5,21},{6,22},{7,23},{8,24},{9,... | collective-permute-start | bytes 196616 | tf_op jit(solution)/shard_map/ppermute | solution.py:104
  57.7 15.9 %collective-permute-start.22 = (bf16[32,1024]{1,0:T(8,128)(2,1)S(1)}, bf16[32,1024]{1,0:T(8,128)(2,1)S(1)}, u32[]{:S(2)}, u32[]{:S(2)}) collective-permute-start(bf16[32,1024]{1,0:T(8,128)(2,1)S(1)} %copy-done.13), channel_id=1, source_target_pairs={{0,8},{1,9},{2,10},{3,11},{4,12},{5,13},{6,14},{7,15},{8,0},{9,1},... | collective-permute-start | bytes 196616 | tf_op jit(solution)/shard_map/ppermute | solution.py:104
  73.7 15.9 %collective-permute-start.25 = (bf16[4,32,3072]{2,1,0:T(8,128)(2,1)S(1)}, bf16[4,32,3072]{2,1,0:T(8,128)(2,1)S(1)}, u32[]{:S(2)}, u32[]{:S(2)}) collective-permute-start(bf16[4,32,3072]{2,1,0:T(8,128)(2,1)S(1)} %maximum_maximum_fusion.2), channel_id=1, source_target_pairs={{0,4},{1,3},{2,6},{3,1},{4,0},{5,7},{6,2},{7,5},{8,12},{9,11},{10,... | collective-permute-start | bytes 2359304 | tf_op jit(solution)/shard_map/ppermute | solution.py:104
  74.6 16.1 %collective-permute-start.26 = (bf16[4,32,2048]{2,1,0:T(8,128)(2,1)S(1)}, bf16[4,32,2048]{2,1,0:T(8,128)(2,1)S(1)}, u32[]{:S(2)}, u32[]{:S(2)}) collective-permute-start(bf16[4,32,2048]{2,1,0:T(8,128)(2,1)S(1)} %pad_maximum_fusion.refs_2_.refs_0_), channel_id=1, source_target_pairs={{0,1},{1,0},{2,3},{3,2},{4,5},{5,4},{6,7},{7,6},{8,9},{9,8},{10,11... | collective-permute-start | bytes 1572872 | tf_op jit(solution)/shard_map/ppermute | solution.py:104
  74.9 15.2 %collective-permute-start.29 = (bf16[4,32,1024]{2,1,0:T(8,128)(2,1)S(1)}, bf16[4,32,1024]{2,1,0:T(8,128)(2,1)S(1)}, u32[]{:S(2)}, u32[]{:S(2)}) collective-permute-start(bf16[4,32,1024]{2,1,0:T(8,128)(2,1)S(1)} %pad_maximum_fusion.3.refs_0_), channel_id=1, source_target_pairs={{0,2},{1,5},{2,0},{3,7},{4,6},{5,1},{6,4},{7,3},{8,10},{9,13},{10,... | collective-permute-start | bytes 786440 | tf_op jit(solution)/shard_map/ppermute | solution.py:104
  76.1 14.5 %collective-permute-start.27 = (bf16[4,32,2048]{2,1,0:T(8,128)(2,1)S(1)}, bf16[4,32,2048]{2,1,0:T(8,128)(2,1)S(1)}, u32[]{:S(2)}, u32[]{:S(2)}) collective-permute-start(bf16[4,32,2048]{2,1,0:T(8,128)(2,1)S(1)} %collective-permute-done.21.refs_3_.refs_1_), channel_id=1, source_target_pairs={{0,1},{1,0},{2,3},{3,2},{4,5},{5,4},{6,7},{7,6},{8,9},{9,8},{10,11... | collective-permute-start | bytes 1572872 | tf_op jit(solution)/shard_map/ppermute | solution.py:104
  92.8 12.0 %collective-permute-start.32 = (bf16[4,32,1024]{2,1,0:T(8,128)(2,1)S(1)}, bf16[4,32,1024]{2,1,0:T(8,128)(2,1)S(1)}, u32[]{:S(2)}, u32[]{:S(2)}) collective-permute-start(bf16[4,32,1024]{2,1,0:T(8,128)(2,1)S(1)} %collective-permute-done.29.refs_1_), channel_id=1, source_target_pairs={{0,4},{1,3},{2,6},{3,1},{4,0},{5,7},{6,2},{7,5},{8,12},{9,11},{10,... | collective-permute-start | bytes 786440 | tf_op jit(solution)/shard_map/ppermute | solution.py:104
  123.2 10.9 %collective-permute-start.34 = (bf16[2,2,4,4,128,128]{5,4,3,2,1,0:T(8,128)(2,1)S(1)}, bf16[2,2,4,4,128,128]{5,4,3,2,1,0:T(8,128)(2,1)S(1)}, u32[]{:S(2)}, u32[]{:S(2)}) collective-permute-start(bf16[2,2,4,4,128,128]{5,4,3,2,1,0:T(8,128)(2,1)S(1)} %get-tuple-element.129), channel_id=1, source_target_pairs={{0,1},{1,0},{2,3},{3,2},{4,5},{5,4},{6,7},{7,6},{8,9},{9,8},{10,11... | collective-permute-start | bytes 6291464 | tf_op jit(solution)/shard_map/ppermute | solution.py:104
  133.8 14.8 %collective-permute-start.36 = (bf16[2,2,4,2,128,128]{5,4,3,2,1,0:T(8,128)(2,1)S(1)}, bf16[2,2,4,2,128,128]{5,4,3,2,1,0:T(8,128)(2,1)S(1)}, u32[]{:S(2)}, u32[]{:S(2)}) collective-permute-start(bf16[2,2,4,2,128,128]{5,4,3,2,1,0:T(8,128)(2,1)S(1)} %get-tuple-element.137), channel_id=1, source_target_pairs={{0,1},{1,0},{2,3},{3,2},{4,5},{5,4},{6,7},{7,6},{8,9},{9,8},{10,11... | collective-permute-start | bytes 3145736 | tf_op jit(solution)/shard_map/ppermute | solution.py:104
  135.1 14.9 %collective-permute-start.35 = (bf16[32,128,128]{2,1,0:T(8,128)(2,1)S(1)}, bf16[32,128,128]{2,1,0:T(8,128)(2,1)S(1)}, u32[]{:S(2)}, u32[]{:S(2)}) collective-permute-start(bf16[32,128,128]{2,1,0:T(8,128)(2,1)S(1)} %step_0.1), channel_id=1, source_target_pairs={{0,4},{1,3},{2,6},{3,1},{4,0},{5,7},{6,2},{7,5},{8,12},{9,11},{10,... | collective-permute-start | bytes 3145736 | tf_op jit(solution)/shard_map/ppermute | solution.py:104
  148.5 19.6 %collective-permute-start.38 = (bf16[2,2,4,3,128,128]{5,4,3,2,1,0:T(8,128)(2,1)S(1)}, bf16[2,2,4,3,128,128]{5,4,3,2,1,0:T(8,128)(2,1)S(1)}, u32[]{:S(2)}, u32[]{:S(2)}) collective-permute-start(bf16[2,2,4,3,128,128]{5,4,3,2,1,0:T(8,128)(2,1)S(1)} %get-tuple-element.135), channel_id=1, source_target_pairs={{0,1},{1,0},{2,3},{3,2},{4,5},{5,4},{6,7},{7,6},{8,9},{9,8},{10,11... | collective-permute-start | bytes 4718600 | tf_op jit(solution)/shard_map/ppermute | solution.py:104
  151.0 17.1 %collective-permute-start.37 = (bf16[32,128,128]{2,1,0:T(8,128)(2,1)S(1)}, bf16[32,128,128]{2,1,0:T(8,128)(2,1)S(1)}, u32[]{:S(2)}, u32[]{:S(2)}) collective-permute-start(bf16[32,128,128]{2,1,0:T(8,128)(2,1)S(1)} %step_1.1), channel_id=1, source_target_pairs={{0,2},{1,5},{2,0},{3,7},{4,6},{5,1},{6,4},{7,3},{8,10},{9,13},{10,... | collective-permute-start | bytes 3145736 | tf_op jit(solution)/shard_map/ppermute | solution.py:104
  168.0 15.4 %collective-permute-start.43 = (bf16[2,2,4,3,128,128]{5,4,3,2,1,0:T(8,128)(2,1)S(1)}, bf16[2,2,4,3,128,128]{5,4,3,2,1,0:T(8,128)(2,1)S(1)}, u32[]{:S(2)}, u32[]{:S(2)}) collective-permute-start(bf16[2,2,4,3,128,128]{5,4,3,2,1,0:T(8,128)(2,1)S(1)} %get-tuple-element.143), channel_id=1, source_target_pairs={{0,1},{1,0},{2,3},{3,2},{4,5},{5,4},{6,7},{7,6},{8,9},{9,8},{10,11... | collective-permute-start | bytes 4718600 | tf_op jit(solution)/shard_map/ppermute | solution.py:104
  169.6 14.9 %collective-permute-start.42 = (bf16[32,128,128]{2,1,0:T(8,128)(2,1)S(1)}, bf16[32,128,128]{2,1,0:T(8,128)(2,1)S(1)}, u32[]{:S(2)}, u32[]{:S(2)}) collective-permute-start(bf16[32,128,128]{2,1,0:T(8,128)(2,1)S(1)} %get-tuple-element.145), channel_id=1, source_target_pairs={{0,4},{1,3},{2,6},{3,1},{4,0},{5,7},{6,2},{7,5},{8,12},{9,11},{10,... | collective-permute-start | bytes 3145736 | tf_op jit(solution)/shard_map/ppermute | solution.py:104
  170.5 12.1 %collective-permute-start.39 = (bf16[4,128,128]{2,1,0:T(8,128)(2,1)S(1)}, bf16[4,128,128]{2,1,0:T(8,128)(2,1)S(1)}, u32[]{:S(2)}, u32[]{:S(2)}) collective-permute-start(bf16[4,128,128]{2,1,0:T(8,128)(2,1)S(1)} %get-tuple-element.148), channel_id=1, source_target_pairs={{0,8},{1,9},{2,10},{3,11},{4,12},{5,13},{6,14},{7,15},{8,0},{9,1},... | collective-permute-start | bytes 393224 | tf_op jit(solution)/shard_map/ppermute | solution.py:104
  170.5 12.9 %collective-permute-start.40 = (bf16[4,128,128]{2,1,0:T(8,128)(2,1)S(1)}, bf16[4,128,128]{2,1,0:T(8,128)(2,1)S(1)}, u32[]{:S(2)}, u32[]{:S(2)}) collective-permute-start(bf16[4,128,128]{2,1,0:T(8,128)(2,1)S(1)} %get-tuple-element.149), channel_id=1, source_target_pairs={{0,16},{1,17},{2,18},{3,19},{4,20},{5,21},{6,22},{7,23},{8,24},{9,... | collective-permute-start | bytes 393224 | tf_op jit(solution)/shard_map/ppermute | solution.py:104
  172.8 10.6 %collective-permute-start.41 = (bf16[4,128,128]{2,1,0:T(8,128)(2,1)S(1)}, bf16[4,128,128]{2,1,0:T(8,128)(2,1)S(1)}, u32[]{:S(2)}, u32[]{:S(2)}) collective-permute-start(bf16[4,128,128]{2,1,0:T(8,128)(2,1)S(1)} %get-tuple-element.150), channel_id=1, source_target_pairs={{0,24},{1,25},{2,26},{3,27},{4,28},{5,29},{6,30},{7,31},{8,16},{9,... | collective-permute-start | bytes 393224 | tf_op jit(solution)/shard_map/ppermute | solution.py:104
  186.3 17.6 %collective-permute-start.47 = (bf16[36,128,128]{2,1,0:T(8,128)(2,1)S(1)}, bf16[36,128,128]{2,1,0:T(8,128)(2,1)S(1)}, u32[]{:S(2)}, u32[]{:S(2)}) collective-permute-start(bf16[36,128,128]{2,1,0:T(8,128)(2,1)S(1)} %get-tuple-element.152), channel_id=1, source_target_pairs={{0,2},{1,5},{2,0},{3,7},{4,6},{5,1},{6,4},{7,3},{8,10},{9,13},{10,... | collective-permute-start | bytes 3538952 | tf_op jit(solution)/shard_map/ppermute | solution.py:104
  187.0 16.9 %collective-permute-start.44 = (bf16[2,128,128]{2,1,0:T(8,128)(2,1)S(1)}, bf16[2,128,128]{2,1,0:T(8,128)(2,1)S(1)}, u32[]{:S(2)}, u32[]{:S(2)}) collective-permute-start(bf16[2,128,128]{2,1,0:T(8,128)(2,1)S(1)} %get-tuple-element.162), channel_id=1, source_target_pairs={{0,8},{1,9},{2,10},{3,11},{4,12},{5,13},{6,14},{7,15},{8,0},{9,1},... | collective-permute-start | bytes 196616 | tf_op jit(solution)/shard_map/ppermute | solution.py:104
  189.2 14.7 %collective-permute-start.45 = (bf16[2,128,128]{2,1,0:T(8,128)(2,1)S(1)}, bf16[2,128,128]{2,1,0:T(8,128)(2,1)S(1)}, u32[]{:S(2)}, u32[]{:S(2)}) collective-permute-start(bf16[2,128,128]{2,1,0:T(8,128)(2,1)S(1)} %get-tuple-element.163), channel_id=1, source_target_pairs={{0,16},{1,17},{2,18},{3,19},{4,20},{5,21},{6,22},{7,23},{8,24},{9,... | collective-permute-start | bytes 196616 | tf_op jit(solution)/shard_map/ppermute | solution.py:104
  189.5 14.4 %collective-permute-start.46 = (bf16[2,128,128]{2,1,0:T(8,128)(2,1)S(1)}, bf16[2,128,128]{2,1,0:T(8,128)(2,1)S(1)}, u32[]{:S(2)}, u32[]{:S(2)}) collective-permute-start(bf16[2,128,128]{2,1,0:T(8,128)(2,1)S(1)} %get-tuple-element.164), channel_id=1, source_target_pairs={{0,24},{1,25},{2,26},{3,27},{4,28},{5,29},{6,30},{7,31},{8,16},{9,... | collective-permute-start | bytes 196616 | tf_op jit(solution)/shard_map/ppermute | solution.py:104
  207.4 9.2 %collective-permute-start.49 = (bf16[12,128,128]{2,1,0:T(8,128)(2,1)S(1)}, bf16[12,128,128]{2,1,0:T(8,128)(2,1)S(1)}, u32[]{:S(2)}, u32[]{:S(2)}) collective-permute-start(bf16[12,128,128]{2,1,0:T(8,128)(2,1)S(1)} %step_5.1), channel_id=1, source_target_pairs={{0,4},{1,3},{2,6},{3,1},{4,0},{5,7},{6,2},{7,5},{8,12},{9,11},{10,... | collective-permute-start | bytes 1179656 | tf_op jit(solution)/shard_map/ppermute | solution.py:104
  208.6 7.3 %collective-permute-start.48 = (bf16[4,128,128]{2,1,0:T(8,128)(2,1)S(1)}, bf16[4,128,128]{2,1,0:T(8,128)(2,1)S(1)}, u32[]{:S(2)}, u32[]{:S(2)}) collective-permute-start(bf16[4,128,128]{2,1,0:T(8,128)(2,1)S(1)} %get-tuple-element.170), channel_id=1, source_target_pairs={{0,8},{1,9},{2,10},{3,11},{4,12},{5,13},{6,14},{7,15},{8,0},{9,1},... | collective-permute-start | bytes 393224 | tf_op jit(solution)/shard_map/ppermute | solution.py:104
  209.4 11.0 %collective-permute-start.50 = (bf16[4,128,128]{2,1,0:T(8,128)(2,1)S(1)}, bf16[4,128,128]{2,1,0:T(8,128)(2,1)S(1)}, u32[]{:S(2)}, u32[]{:S(2)}) collective-permute-start(bf16[4,128,128]{2,1,0:T(8,128)(2,1)S(1)} %get-tuple-element.176), channel_id=1, source_target_pairs={{0,16},{1,17},{2,18},{3,19},{4,20},{5,21},{6,22},{7,23},{8,24},{9,... | collective-permute-start | bytes 393224 | tf_op jit(solution)/shard_map/ppermute | solution.py:104
  210.9 9.5 %collective-permute-start.51 = (bf16[4,128,128]{2,1,0:T(8,128)(2,1)S(1)}, bf16[4,128,128]{2,1,0:T(8,128)(2,1)S(1)}, u32[]{:S(2)}, u32[]{:S(2)}) collective-permute-start(bf16[4,128,128]{2,1,0:T(8,128)(2,1)S(1)} %get-tuple-element.177), channel_id=1, source_target_pairs={{0,24},{1,25},{2,26},{3,27},{4,28},{5,29},{6,30},{7,31},{8,16},{9,... | collective-permute-start | bytes 393224 | tf_op jit(solution)/shard_map/ppermute | solution.py:104
  215.9 10.8 %collective-permute-start.59 = (bf16[6,128,128]{2,1,0:T(8,128)(2,1)S(1)}, bf16[6,128,128]{2,1,0:T(8,128)(2,1)S(1)}, u32[]{:S(2)}, u32[]{:S(2)}) collective-permute-start(bf16[6,128,128]{2,1,0:T(8,128)(2,1)S(1)} %step_6.1.refs_0_), channel_id=1, source_target_pairs={{0,2},{1,3},{2,0},{3,1},{4,6},{5,7},{6,4},{7,5},{8,10},{9,11},{10,... | collective-permute-start | bytes 589832 | tf_op jit(solution)/shard_map/ppermute | solution.py:104
  222.9 10.6 %collective-permute-start.56 = (bf16[4,128,128]{2,1,0:T(8,128)(2,1)S(1)}, bf16[4,128,128]{2,1,0:T(8,128)(2,1)S(1)}, u32[]{:S(2)}, u32[]{:S(2)}) collective-permute-start(bf16[4,128,128]{2,1,0:T(8,128)(2,1)S(1)} %step_8.1.refs_0_), channel_id=1, source_target_pairs={{0,2},{1,3},{2,0},{3,1},{4,6},{5,7},{6,4},{7,5},{8,10},{9,11},{10,... | collective-permute-start | bytes 393224 | tf_op jit(solution)/shard_map/ppermute | solution.py:104
  224.1 7.9 %collective-permute-start.53 = (bf16[3,128,128]{2,1,0:T(8,128)(2,1)S(1)}, bf16[3,128,128]{2,1,0:T(8,128)(2,1)S(1)}, u32[]{:S(2)}, u32[]{:S(2)}) collective-permute-start(bf16[3,128,128]{2,1,0:T(8,128)(2,1)S(1)} %get-tuple-element.180), channel_id=1, source_target_pairs={{0,16},{1,17},{2,18},{3,19},{4,20},{5,21},{6,22},{7,23},{8,24},{9,... | collective-permute-start | bytes 294920 | tf_op jit(solution)/shard_map/ppermute | solution.py:104
  224.6 7.5 %collective-permute-start.54 = (bf16[3,128,128]{2,1,0:T(8,128)(2,1)S(1)}, bf16[3,128,128]{2,1,0:T(8,128)(2,1)S(1)}, u32[]{:S(2)}, u32[]{:S(2)}) collective-permute-start(bf16[3,128,128]{2,1,0:T(8,128)(2,1)S(1)} %get-tuple-element.181), channel_id=1, source_target_pairs={{0,24},{1,25},{2,26},{3,27},{4,28},{5,29},{6,30},{7,31},{8,16},{9,... | collective-permute-start | bytes 294920 | tf_op jit(solution)/shard_map/ppermute | solution.py:104
  226.7 10.3 %collective-permute-start.58 = (bf16[6,128,128]{2,1,0:T(8,128)(2,1)S(1)}, bf16[6,128,128]{2,1,0:T(8,128)(2,1)S(1)}, u32[]{:S(2)}, u32[]{:S(2)}) collective-permute-start(bf16[6,128,128]{2,1,0:T(8,128)(2,1)S(1)} %step_6.1.refs_0_), channel_id=1, source_target_pairs={{0,1},{1,0},{2,3},{3,2},{4,5},{5,4},{6,7},{7,6},{8,9},{9,8},{10,11... | collective-permute-start | bytes 589832 | tf_op jit(solution)/shard_map/ppermute | solution.py:104
  226.7 10.3 %collective-permute-start.60 = (bf16[6,128,128]{2,1,0:T(8,128)(2,1)S(1)}, bf16[6,128,128]{2,1,0:T(8,128)(2,1)S(1)}, u32[]{:S(2)}, u32[]{:S(2)}) collective-permute-start(bf16[6,128,128]{2,1,0:T(8,128)(2,1)S(1)} %collective-permute-done.59.refs_2_), channel_id=1, source_target_pairs={{0,1},{1,0},{2,3},{3,2},{4,5},{5,4},{6,7},{7,6},{8,9},{9,8},{10,11... | collective-permute-start | bytes 589832 | tf_op jit(solution)/shard_map/ppermute | solution.py:104
  (31 other events, 213.2 us)

commit v7 on v6

--- a/solution.py
+++ b/solution.py
@@ -1060,7 +1060,6 @@
     step.share([z_one])
     (r_one,) = step.run(after(meta, z_two[0]), "step_8")
     z_two = along(z_two)
-    r_one = after(r_one, z_two[1])
 
     step = Step()
     step.share([z_two])

time: 243 us -> 243 us (level)
  transfers between devices with their start and end apart: 65 -> 65, of which waited for: 17 -> 16; matrix products, arithmetic and copies ran while one was open for 3% -> 3% of each run, Pallas kernels for 45% -> 45%
where the time goes in v7:
time: 243 us; the launch traced here: 242 us
  Pallas kernels  134 us (55%)
  starting transfers between devices  60.5 us (25%)
  waiting for transfers between devices  32.4 us (13%)
  local copies, waits for them, and re-layouts  8.75 us (4%)
  other arithmetic  5.89 us (2%)
    pallas_call x25, Pallas kernels, call(): pl.pallas_call(kernel, out_shape=shapes, grid_spec=pltpu.PrefetchScalarGr...  134 us
    ppermute x65, starting transfers between devices, move(): return lax.ppermute(value, AXES, pairs)  60.5 us
    ppermute x65, waiting for transfers between devices, move(): return lax.ppermute(value, AXES, pairs)  32.4 us
  transfers between devices with their start and end apart: 65, of which 16 were waited for; matrix products, arithmetic and copies ran while one was open for 3% of the time, Pallas kernels for 45%

profile of v7, /device:TPU:0, one launch (start us, length us, event | category | flops | bytes accessed | tf_op | source)
XLA Modules:
  0.0 242.4 jit_solution(464857877331854379)
XLA Ops:
  2.8 5.1 %collective-permute-start.2 = (bf16[32,1664]{1,0:T(8,128)(2,1)S(1)}, bf16[32,1664]{1,0:T(8,128)(2,1)S(1)}, u32[]{:S(2)}, u32[]{:S(2)}) collective-permute-start(bf16[32,1664]{1,0:T(8,128)(2,1)S(1)} %fusion.1), channel_id=1, source_target_pairs={{0,24},{1,25},{2,26},{3,27},{4,28},{5,29},{6,30},{7,31},{8,16},{9,... | collective-permute-start | bytes 319496 | tf_op jit(solution)/shard_map/ppermute | solution.py:104
  10.3 1.6 constant_dynamic-slice_fusion
  11.9 5.0 %collective-permute-done.1 = bf16[32,1664]{1,0:T(8,128)(2,1)S(1)} collective-permute-done((bf16[32,1664]{1,0:T(8,128)(2,1)S(1)}, bf16[32,1664]{1,0:T(8,128)(2,1)S(1)}, u32[]{:S(2)}, u32[]{:S(2)}) %collective-permute-start.1) | collective-permute-done | bytes 106528 | tf_op jit(solution)/shard_map/ppermute | solution.py:104
  16.9 1.6 collective-permute-start.4
  18.5 1.5 collective-permute-start.3
  20.0 2.5 %collective-permute-start.7 = (bf16[32,1536]{1,0:T(8,128)(2,1)}, bf16[32,1536]{1,0:T(8,128)(2,1)S(1)}, u32[]{:S(2)}, u32[]{:S(2)}) collective-permute-start(bf16[32,1536]{1,0:T(8,128)(2,1)} %reshape.44), channel_id=1, source_target_pairs={{0,24},{1,25},{2,26},{3,27},{4,28},{5,29},{6,30},{7,31},{8,16},{9,... | collective-permute-start | bytes 294920 | tf_op jit(solution)/shard_map/ppermute | solution.py:104
  22.5 1.9 collective-permute-start.5
  24.4 4.7 %collective-permute-done.4.refs_2_ = bf16[4,32,1664]{2,1,0:T(8,128)(2,1)S(1)} collective-permute-done((bf16[4,32,1664]{2,1,0:T(8,128)(2,1)S(1)}, bf16[4,32,1664]{2,1,0:T(8,128)(2,1)S(1)}, u32[]{:S(2)}, u32[]{:S(2)}) %collective-permute-start.4) | collective-permute-done | bytes 426016 | tf_op jit(solution)/shard_map/ppermute | solution.py:104
  29.1 1.5 collective-permute-done.6
  30.6 1.8 maximum_maximum_fusion.1
  35.6 1.9 collective-permute-start.16
  39.0 2.5 %collective-permute-start.14 = (bf16[32,2048]{1,0:T(8,128)(2,1)S(1)}, bf16[32,2048]{1,0:T(8,128)(2,1)}, u32[]{:S(2)}, u32[]{:S(2)}) collective-permute-start(bf16[32,2048]{1,0:T(8,128)(2,1)S(1)} %pad_maximum_fusion.4), channel_id=1, source_target_pairs={{0,8},{1,9},{2,10},{3,11},{4,12},{5,13},{6,14},{7,15},{8,0},{9,1},... | collective-permute-start | bytes 393224 | tf_op jit(solution)/shard_map/ppermute | solution.py:104
  41.6 2.1 first_norm.1
  43.7 5.6 %collective-permute-done.8.refs_3_.refs_2_ = bf16[4,32,3200]{2,1,0:T(8,128)(2,1)} collective-permute-done((bf16[4,32,3200]{2,1,0:T(8,128)(2,1)}, bf16[4,32,3200]{2,1,0:T(8,128)(2,1)}, u32[]{:S(2)}, u32[]{:S(2)}) %collective-permute-start.8) | collective-permute-done | bytes 819232 | tf_op jit(solution)/shard_map/ppermute | solution.py:104
  54.5 1.4 collective-permute-done.18.refs_4_
  55.9 1.8 collective-permute-start.24
  57.7 2.6 %collective-permute-start.22 = (bf16[32,1024]{1,0:T(8,128)(2,1)S(1)}, bf16[32,1024]{1,0:T(8,128)(2,1)S(1)}, u32[]{:S(2)}, u32[]{:S(2)}) collective-permute-start(bf16[32,1024]{1,0:T(8,128)(2,1)S(1)} %copy-done.13), channel_id=1, source_target_pairs={{0,8},{1,9},{2,10},{3,11},{4,12},{5,13},{6,14},{7,15},{8,0},{9,1},... | collective-permute-start | bytes 196616 | tf_op jit(solution)/shard_map/ppermute | solution.py:104
  60.3 13.2 %attention_forward.2 = (bf16[1024,1536]{1,0:T(8,128)(2,1)}, bf16[4,2,512,512]{3,2,1,0:T(8,128)(2,1)}, bf16[1024,512]{1,0:T(8,128)(2,1)S(1)}, bf16[1024,1536]{1,0:T(8,128)(2,1)}) custom-call(s32[8]{0:T(128)S(1)} %stack.92.meta, bf16[1024,1024]{1,0:T(8,128)(2,1)S(1)} %get-tuple-element.104.first_ref, f32[16,1024]{1,0:T(8,128)S(1)} %get-tuple-element.103.small_ref, ...), custom_call_target="tpu_custom_call" | custom-call | flops 1 | bytes 1 | tf_op jit(solution)/shard_map/attention_forward/pallas_call | solution.py:36
  76.1 13.4 %attention_forward.3 = (bf16[1024,1536]{1,0:T(8,128)(2,1)}, bf16[4,2,512,512]{3,2,1,0:T(8,128)(2,1)}, bf16[1024,512]{1,0:T(8,128)(2,1)S(1)}, bf16[1024,1536]{1,0:T(8,128)(2,1)}) custom-call(s32[8]{0:T(128)S(1)} %stack.92.meta, bf16[1024,1024]{1,0:T(8,128)(2,1)S(1)} %get-tuple-element.104.first_ref, f32[16,1024]{1,0:T(8,128)S(1)} %get-tuple-element.103.small_ref, ...), custom_call_target="tpu_custom_call" | custom-call | flops 1 | bytes 1 | tf_op jit(solution)/shard_map/attention_forward/pallas_call | solution.py:36
  90.7 1.8 collective-permute-done.30.refs_4_
  93.6 11.2 %feed_forward_first.1 = (f32[1024,1024]{1,0:T(8,128)S(1)}, bf16[1024,1024]{1,0:T(8,128)(2,1)S(1)}, bf16[1024,1024]{1,0:T(8,128)(2,1)S(1)}, bf16[1024,1024]{1,0:T(8,128)(2,1)S(1)}) custom-call(s32[8]{0:T(128)S(1)} %stack.92.meta, bf16[1024,1024]{1,0:T(8,128)(2,1)S(1)} %bitcast.40, f32[16,1024]{1,0:T(8,128)S(1)} %get-tuple-element.103.small_ref, ...), custom_call_target="tpu_custom_call" | custom-call | flops 1 | bytes 1 | tf_op jit(solution)/shard_map/feed_forward_first/pallas_call | solution.py:36
  106.4 16.8 %feed_forward_second.1 = (bf16[1024,1024]{1,0:T(8,128)(2,1)}, bf16[1024,1024]{1,0:T(8,128)(2,1)S(1)}, bf16[2,2,4,4,128,128]{5,4,3,2,1,0:T(8,128)(2,1)S(1)}, bf16...) custom-call(s32[8]{0:T(128)S(1)} %stack.92.meta, bf16[1024,1024]{1,0:T(8,128)(2,1)S(1)} %bitcast.41, ...), custom_call_target="tpu_custom_call" | custom-call | flops 1 | bytes 1 | tf_op jit(solution)/shard_map/feed_forward_second/pallas_call | solution.py:36
  123.5 10.3 %feed_forward_third.1 = (bf16[1024,1024]{1,0:T(8,128)(2,1)S(1)}, bf16[2,2,4,2,128,128]{5,4,3,2,1,0:T(8,128)(2,1)S(1)}, bf16[2,2,4,2,128,128]{5,4,3,2,1,0:T(8,128)(2,1)S(1)}, f32[8,1024]{1,0:T(8,128)S(1)}) custom-call(s32[8]{0:T(128)S(1)} %stack.92.meta, bf16[1024,1024]{1,0:T(8,128)(2,1)S(1)} %bitcast.42, f32[16,1024]{1,0:T(8,128)S(1)} %get-tuple-element.103.small_ref, ...), custom_call_target="tpu_custom_call" | custom-call | flops 1 | bytes 1 | tf_op jit(solution)/shard_map/feed_forward_third/pallas_call | solution.py:36
  136.4 4.5 %mixed_grad.1 = (bf16[1024,1024]{1,0:T(8,128)(2,1)S(1)}, bf16[1024,1024]{1,0:T(8,128)(2,1)}) custom-call(s32[8]{0:T(128)S(1)} %stack.92.meta, bf16[1024,1024]{1,0:T(8,128)(2,1)S(1)} %get-tuple-element.132.attn_ref, bf16[4,32,2048]{2,1,0:T(8,128)(2,1)S(1)} %pad_maximum_fusion.refs_2_.refs_0_, ...), custom_call_target="tpu_custom_call" | custom-call | flops 1 | bytes 1 | tf_op jit(solution)/shard_map/mixed_grad/pallas_call | solution.py:36
  140.9 7.7 %attention_backward.4 = (bf16[1024,768]{1,0:T(8,128)(2,1)}, bf16[2,2,4,3,128,128]{5,4,3,2,1,0:T(8,128)(2,1)S(1)}) custom-call(s32[8]{0:T(128)S(1)} %stack.92.meta, bf16[1024,1024]{1,0:T(8,128)(2,1)S(1)} %get-tuple-element.104.first_ref, bf16[1024,1536]{1,0:T(8,128)(2,1)} %get-tuple-element.130.packed_ref, ...), custom_call_target="tpu_custom_call" | custom-call | flops 1 | bytes 1 | tf_op jit(solution)/shard_map/attention_backward/pallas_call | solution.py:36
  151.0 1.4 collective-permute-start.37
  152.5 7.7 %attention_backward.5 = (bf16[1024,768]{1,0:T(8,128)(2,1)}, bf16[2,2,4,3,128,128]{5,4,3,2,1,0:T(8,128)(2,1)S(1)}) custom-call(s32[8]{0:T(128)S(1)} %stack.92.meta, bf16[1024,1024]{1,0:T(8,128)(2,1)S(1)} %get-tuple-element.104.first_ref, bf16[1024,1536]{1,0:T(8,128)(2,1)} %get-tuple-element.130.packed_ref, ...), custom_call_target="tpu_custom_call" | custom-call | flops 1 | bytes 1 | tf_op jit(solution)/shard_map/attention_backward/pallas_call | solution.py:36
  160.2 7.9 %attention_backward.6 = (bf16[1024,768]{1,0:T(8,128)(2,1)}, bf16[2,2,4,3,128,128]{5,4,3,2,1,0:T(8,128)(2,1)S(1)}) custom-call(s32[8]{0:T(128)S(1)} %stack.92.meta, bf16[1024,1024]{1,0:T(8,128)(2,1)S(1)} %get-tuple-element.104.first_ref, bf16[1024,1536]{1,0:T(8,128)(2,1)} %get-tuple-element.140.packed_ref, ...), custom_call_target="tpu_custom_call" | custom-call | flops 1 | bytes 1 | tf_op jit(solution)/shard_map/attention_backward/pallas_call | solution.py:36
  168.1 1.5 step_2.1
  170.5 2.3 collective-permute-start.40
  172.8 2.1 collective-permute-start.41
  174.9 7.7 %attention_backward.7 = (bf16[1024,768]{1,0:T(8,128)(2,1)}, bf16[2,2,4,3,128,128]{5,4,3,2,1,0:T(8,128)(2,1)S(1)}) custom-call(s32[8]{0:T(128)S(1)} %stack.92.meta, bf16[1024,1024]{1,0:T(8,128)(2,1)S(1)} %get-tuple-element.104.first_ref, bf16[1024,1536]{1,0:T(8,128)(2,1)} %get-tuple-element.140.packed_ref, ...), custom_call_target="tpu_custom_call" | custom-call | flops 1 | bytes 1 | tf_op jit(solution)/shard_map/attention_backward/pallas_call | solution.py:36
  184.5 1.8 step_3.1
  187.0 2.2 collective-permute-start.44
  189.5 2.1 collective-permute-start.46
  191.6 12.3 %input_grad.1 = (bf16[1024,1024]{1,0:T(8,128)(2,1)}, f32[8,1024]{1,0:T(8,128)S(1)}, f32[8,3072]{1,0:T(8,128)S(1)}) custom-call(s32[8]{0:T(128)S(1)} %stack.92.meta, bf16[1024,1024]{1,0:T(8,128)(2,1)} %bitcast.38, bf16[1024,1024]{1,0:T(8,128)(2,1)} %get-tuple-element.153.grad_ref, f32[16,1024]{1,0:T(8,128)S(1)} %get-tuple-element.103.small_ref, ...), custom_call_target="tpu_custom_call" | custom-call | flops 1 | bytes 1 | tf_op jit(solution)/shard_map/input_grad/pallas_call | solution.py:36
  203.9 2.2 step_4.1
  209.4 1.5 collective-permute-start.50
  210.9 2.1 collective-permute-start.51
  213.0 1.7 step_6.1.refs_0_
  216.7 1.5 step_7.1
  218.4 2.0 collective-permute-done.50.refs_2_
  222.4 2.2 collective-permute-start.53
  224.6 2.1 collective-permute-start.54
  227.2 2.7 %collective-permute-done.53.refs_2_ = bf16[3,128,128]{2,1,0:T(8,128)(2,1)S(1)} collective-permute-done((bf16[3,128,128]{2,1,0:T(8,128)(2,1)S(1)}, bf16[3,128,128]{2,1,0:T(8,128)(2,1)S(1)}, u32[]{:S(2)}, u32[]{:S(2)}) %collective-permute-start.53) | collective-permute-done | bytes 98336 | tf_op jit(solution)/shard_map/ppermute | solution.py:104
  235.0 1.4 collective-permute-start.64
  236.5 1.8 finish_rest.1
  240.5 1.9 finish_heads.1
  (159 shorter events, 45.3 us)
Async XLA Ops:
  2.8 9.1 %collective-permute-start.2 = (bf16[32,1664]{1,0:T(8,128)(2,1)S(1)}, bf16[32,1664]{1,0:T(8,128)(2,1)S(1)}, u32[]{:S(2)}, u32[]{:S(2)}) collective-permute-start(bf16[32,1664]{1,0:T(8,128)(2,1)S(1)} %fusion.1), channel_id=1, source_target_pairs={{0,24},{1,25},{2,26},{3,27},{4,28},{5,29},{6,30},{7,31},{8,16},{9,... | collective-permute-start | bytes 319496 | tf_op jit(solution)/shard_map/ppermute | solution.py:104
  7.9 9.0 %collective-permute-start.1 = (bf16[32,1664]{1,0:T(8,128)(2,1)S(1)}, bf16[32,1664]{1,0:T(8,128)(2,1)S(1)}, u32[]{:S(2)}, u32[]{:S(2)}) collective-permute-start(bf16[32,1664]{1,0:T(8,128)(2,1)S(1)} %fusion.1), channel_id=1, source_target_pairs={{0,16},{1,17},{2,18},{3,19},{4,20},{5,21},{6,22},{7,23},{8,24},{9,... | collective-permute-start | bytes 319496 | tf_op jit(solution)/shard_map/ppermute | solution.py:104
  7.9 9.0 %collective-permute-start = (bf16[32,1664]{1,0:T(8,128)(2,1)S(1)}, bf16[32,1664]{1,0:T(8,128)(2,1)S(1)}, u32[]{:S(2)}, u32[]{:S(2)}) collective-permute-start(bf16[32,1664]{1,0:T(8,128)(2,1)S(1)} %fusion.1), channel_id=1, source_target_pairs={{0,8},{1,9},{2,10},{3,11},{4,12},{5,13},{6,14},{7,15},{8,0},{9,1},... | collective-permute-start | bytes 319496 | tf_op jit(solution)/shard_map/ppermute | solution.py:104
  16.9 12.2 %collective-permute-start.4 = (bf16[4,32,1664]{2,1,0:T(8,128)(2,1)S(1)}, bf16[4,32,1664]{2,1,0:T(8,128)(2,1)S(1)}, u32[]{:S(2)}, u32[]{:S(2)}) collective-permute-start(bf16[4,32,1664]{2,1,0:T(8,128)(2,1)S(1)} %pad_maximum_fusion.1.refs_0_), channel_id=1, source_target_pairs={{0,4},{1,3},{2,6},{3,1},{4,0},{5,7},{6,2},{7,5},{8,12},{9,11},{10,... | collective-permute-start | bytes 1277960 | tf_op jit(solution)/shard_map/ppermute | solution.py:104
  18.5 12.1 %collective-permute-start.3 = (bf16[4,32,1664]{2,1,0:T(8,128)(2,1)S(1)}, bf16[4,32,1664]{2,1,0:T(8,128)(2,1)S(1)}, u32[]{:S(2)}, u32[]{:S(2)}) collective-permute-start(bf16[4,32,1664]{2,1,0:T(8,128)(2,1)S(1)} %pad_maximum_fusion.1.refs_0_), channel_id=1, source_target_pairs={{0,2},{1,5},{2,0},{3,7},{4,6},{5,1},{6,4},{7,3},{8,10},{9,13},{10,... | collective-permute-start | bytes 1277960 | tf_op jit(solution)/shard_map/ppermute | solution.py:104
  20.0 9.1 %collective-permute-start.7 = (bf16[32,1536]{1,0:T(8,128)(2,1)}, bf16[32,1536]{1,0:T(8,128)(2,1)S(1)}, u32[]{:S(2)}, u32[]{:S(2)}) collective-permute-start(bf16[32,1536]{1,0:T(8,128)(2,1)} %reshape.44), channel_id=1, source_target_pairs={{0,24},{1,25},{2,26},{3,27},{4,28},{5,29},{6,30},{7,31},{8,16},{9,... | collective-permute-start | bytes 294920 | tf_op jit(solution)/shard_map/ppermute | solution.py:104
  22.5 8.1 %collective-permute-start.6 = (bf16[32,1536]{1,0:T(8,128)(2,1)}, bf16[32,1536]{1,0:T(8,128)(2,1)S(1)}, u32[]{:S(2)}, u32[]{:S(2)}) collective-permute-start(bf16[32,1536]{1,0:T(8,128)(2,1)} %reshape.44), channel_id=1, source_target_pairs={{0,16},{1,17},{2,18},{3,19},{4,20},{5,21},{6,22},{7,23},{8,24},{9,... | collective-permute-start | bytes 294920 | tf_op jit(solution)/shard_map/ppermute | solution.py:104
  22.5 8.1 %collective-permute-start.5 = (bf16[32,1536]{1,0:T(8,128)(2,1)}, bf16[32,1536]{1,0:T(8,128)(2,1)S(1)}, u32[]{:S(2)}, u32[]{:S(2)}) collective-permute-start(bf16[32,1536]{1,0:T(8,128)(2,1)} %reshape.44), channel_id=1, source_target_pairs={{0,8},{1,9},{2,10},{3,11},{4,12},{5,13},{6,14},{7,15},{8,0},{9,1},... | collective-permute-start | bytes 294920 | tf_op jit(solution)/shard_map/ppermute | solution.py:104
  32.4 16.9 %collective-permute-start.8 = (bf16[4,32,3200]{2,1,0:T(8,128)(2,1)}, bf16[4,32,3200]{2,1,0:T(8,128)(2,1)}, u32[]{:S(2)}, u32[]{:S(2)}) collective-permute-start(bf16[4,32,3200]{2,1,0:T(8,128)(2,1)} %maximum_maximum_fusion.1), channel_id=1, source_target_pairs={{0,4},{1,3},{2,6},{3,1},{4,0},{5,7},{6,2},{7,5},{8,12},{9,11},{10,... | collective-permute-start | bytes 2457608 | tf_op jit(solution)/shard_map/ppermute | solution.py:104
  34.3 15.3 %collective-permute-start.13 = (bf16[4,32,1536]{2,1,0:T(8,128)(2,1)}, bf16[4,32,1536]{2,1,0:T(8,128)(2,1)}, u32[]{:S(2)}, u32[]{:S(2)}) collective-permute-start(bf16[4,32,1536]{2,1,0:T(8,128)(2,1)} %pad_maximum_fusion.2.refs_0_), channel_id=1, source_target_pairs={{0,2},{1,5},{2,0},{3,7},{4,6},{5,1},{6,4},{7,3},{8,10},{9,13},{10,... | collective-permute-start | bytes 1179656 | tf_op jit(solution)/shard_map/ppermute | solution.py:104
  35.6 13.8 %collective-permute-start.16 = (bf16[32,2048]{1,0:T(8,128)(2,1)S(1)}, bf16[32,2048]{1,0:T(8,128)(2,1)}, u32[]{:S(2)}, u32[]{:S(2)}) collective-permute-start(bf16[32,2048]{1,0:T(8,128)(2,1)S(1)} %pad_maximum_fusion.4), channel_id=1, source_target_pairs={{0,24},{1,25},{2,26},{3,27},{4,28},{5,29},{6,30},{7,31},{8,16},{9,... | collective-permute-start | bytes 393224 | tf_op jit(solution)/shard_map/ppermute | solution.py:104
  38.2 11.4 %collective-permute-start.15 = (bf16[32,2048]{1,0:T(8,128)(2,1)S(1)}, bf16[32,2048]{1,0:T(8,128)(2,1)}, u32[]{:S(2)}, u32[]{:S(2)}) collective-permute-start(bf16[32,2048]{1,0:T(8,128)(2,1)S(1)} %pad_maximum_fusion.4), channel_id=1, source_target_pairs={{0,16},{1,17},{2,18},{3,19},{4,20},{5,21},{6,22},{7,23},{8,24},{9,... | collective-permute-start | bytes 393224 | tf_op jit(solution)/shard_map/ppermute | solution.py:104
  39.0 10.6 %collective-permute-start.14 = (bf16[32,2048]{1,0:T(8,128)(2,1)S(1)}, bf16[32,2048]{1,0:T(8,128)(2,1)}, u32[]{:S(2)}, u32[]{:S(2)}) collective-permute-start(bf16[32,2048]{1,0:T(8,128)(2,1)S(1)} %pad_maximum_fusion.4), channel_id=1, source_target_pairs={{0,8},{1,9},{2,10},{3,11},{4,12},{5,13},{6,14},{7,15},{8,0},{9,1},... | collective-permute-start | bytes 393224 | tf_op jit(solution)/shard_map/ppermute | solution.py:104
  50.9 22.6 %collective-permute-start.17 = (bf16[4,32,3584]{2,1,0:T(8,128)(2,1)S(1)}, bf16[4,32,3584]{2,1,0:T(8,128)(2,1)S(1)}, u32[]{:S(2)}, u32[]{:S(2)}) collective-permute-start(bf16[4,32,3584]{2,1,0:T(8,128)(2,1)S(1)} %maximum_maximum_fusion), channel_id=1, source_target_pairs={{0,4},{1,3},{2,6},{3,1},{4,0},{5,7},{6,2},{7,5},{8,12},{9,11},{10,... | collective-permute-start | bytes 2752520 | tf_op jit(solution)/shard_map/ppermute | solution.py:104
  52.8 20.8 %collective-permute-start.21 = (bf16[4,32,2048]{2,1,0:T(8,128)(2,1)S(1)}, bf16[4,32,2048]{2,1,0:T(8,128)(2,1)S(1)}, u32[]{:S(2)}, u32[]{:S(2)}) collective-permute-start(bf16[4,32,2048]{2,1,0:T(8,128)(2,1)S(1)} %pad_maximum_fusion.refs_2_.refs_0_), channel_id=1, source_target_pairs={{0,2},{1,5},{2,0},{3,7},{4,6},{5,1},{6,4},{7,3},{8,10},{9,13},{10,... | collective-permute-start | bytes 1572872 | tf_op jit(solution)/shard_map/ppermute | solution.py:104
  55.9 17.7 %collective-permute-start.24 = (bf16[32,1024]{1,0:T(8,128)(2,1)S(1)}, bf16[32,1024]{1,0:T(8,128)(2,1)S(1)}, u32[]{:S(2)}, u32[]{:S(2)}) collective-permute-start(bf16[32,1024]{1,0:T(8,128)(2,1)S(1)} %copy-done.13), channel_id=1, source_target_pairs={{0,24},{1,25},{2,26},{3,27},{4,28},{5,29},{6,30},{7,31},{8,16},{9,... | collective-permute-start | bytes 196616 | tf_op jit(solution)/shard_map/ppermute | solution.py:104
  57.7 15.9 %collective-permute-start.23 = (bf16[32,1024]{1,0:T(8,128)(2,1)S(1)}, bf16[32,1024]{1,0:T(8,128)(2,1)S(1)}, u32[]{:S(2)}, u32[]{:S(2)}) collective-permute-start(bf16[32,1024]{1,0:T(8,128)(2,1)S(1)} %copy-done.13), channel_id=1, source_target_pairs={{0,16},{1,17},{2,18},{3,19},{4,20},{5,21},{6,22},{7,23},{8,24},{9,... | collective-permute-start | bytes 196616 | tf_op jit(solution)/shard_map/ppermute | solution.py:104
  57.7 15.9 %collective-permute-start.22 = (bf16[32,1024]{1,0:T(8,128)(2,1)S(1)}, bf16[32,1024]{1,0:T(8,128)(2,1)S(1)}, u32[]{:S(2)}, u32[]{:S(2)}) collective-permute-start(bf16[32,1024]{1,0:T(8,128)(2,1)S(1)} %copy-done.13), channel_id=1, source_target_pairs={{0,8},{1,9},{2,10},{3,11},{4,12},{5,13},{6,14},{7,15},{8,0},{9,1},... | collective-permute-start | bytes 196616 | tf_op jit(solution)/shard_map/ppermute | solution.py:104
  73.7 15.9 %collective-permute-start.25 = (bf16[4,32,3072]{2,1,0:T(8,128)(2,1)S(1)}, bf16[4,32,3072]{2,1,0:T(8,128)(2,1)S(1)}, u32[]{:S(2)}, u32[]{:S(2)}) collective-permute-start(bf16[4,32,3072]{2,1,0:T(8,128)(2,1)S(1)} %maximum_maximum_fusion.2), channel_id=1, source_target_pairs={{0,4},{1,3},{2,6},{3,1},{4,0},{5,7},{6,2},{7,5},{8,12},{9,11},{10,... | collective-permute-start | bytes 2359304 | tf_op jit(solution)/shard_map/ppermute | solution.py:104
  74.6 16.1 %collective-permute-start.26 = (bf16[4,32,2048]{2,1,0:T(8,128)(2,1)S(1)}, bf16[4,32,2048]{2,1,0:T(8,128)(2,1)S(1)}, u32[]{:S(2)}, u32[]{:S(2)}) collective-permute-start(bf16[4,32,2048]{2,1,0:T(8,128)(2,1)S(1)} %pad_maximum_fusion.refs_2_.refs_0_), channel_id=1, source_target_pairs={{0,1},{1,0},{2,3},{3,2},{4,5},{5,4},{6,7},{7,6},{8,9},{9,8},{10,11... | collective-permute-start | bytes 1572872 | tf_op jit(solution)/shard_map/ppermute | solution.py:104
  74.9 15.2 %collective-permute-start.29 = (bf16[4,32,1024]{2,1,0:T(8,128)(2,1)S(1)}, bf16[4,32,1024]{2,1,0:T(8,128)(2,1)S(1)}, u32[]{:S(2)}, u32[]{:S(2)}) collective-permute-start(bf16[4,32,1024]{2,1,0:T(8,128)(2,1)S(1)} %pad_maximum_fusion.3.refs_0_), channel_id=1, source_target_pairs={{0,2},{1,5},{2,0},{3,7},{4,6},{5,1},{6,4},{7,3},{8,10},{9,13},{10,... | collective-permute-start | bytes 786440 | tf_op jit(solution)/shard_map/ppermute | solution.py:104
  76.1 14.5 %collective-permute-start.27 = (bf16[4,32,2048]{2,1,0:T(8,128)(2,1)S(1)}, bf16[4,32,2048]{2,1,0:T(8,128)(2,1)S(1)}, u32[]{:S(2)}, u32[]{:S(2)}) collective-permute-start(bf16[4,32,2048]{2,1,0:T(8,128)(2,1)S(1)} %collective-permute-done.21.refs_3_.refs_1_), channel_id=1, source_target_pairs={{0,1},{1,0},{2,3},{3,2},{4,5},{5,4},{6,7},{7,6},{8,9},{9,8},{10,11... | collective-permute-start | bytes 1572872 | tf_op jit(solution)/shard_map/ppermute | solution.py:104
  92.8 12.0 %collective-permute-start.32 = (bf16[4,32,1024]{2,1,0:T(8,128)(2,1)S(1)}, bf16[4,32,1024]{2,1,0:T(8,128)(2,1)S(1)}, u32[]{:S(2)}, u32[]{:S(2)}) collective-permute-start(bf16[4,32,1024]{2,1,0:T(8,128)(2,1)S(1)} %collective-permute-done.29.refs_1_), channel_id=1, source_target_pairs={{0,4},{1,3},{2,6},{3,1},{4,0},{5,7},{6,2},{7,5},{8,12},{9,11},{10,... | collective-permute-start | bytes 786440 | tf_op jit(solution)/shard_map/ppermute | solution.py:104
  123.2 10.9 %collective-permute-start.34 = (bf16[2,2,4,4,128,128]{5,4,3,2,1,0:T(8,128)(2,1)S(1)}, bf16[2,2,4,4,128,128]{5,4,3,2,1,0:T(8,128)(2,1)S(1)}, u32[]{:S(2)}, u32[]{:S(2)}) collective-permute-start(bf16[2,2,4,4,128,128]{5,4,3,2,1,0:T(8,128)(2,1)S(1)} %get-tuple-element.128), channel_id=1, source_target_pairs={{0,1},{1,0},{2,3},{3,2},{4,5},{5,4},{6,7},{7,6},{8,9},{9,8},{10,11... | collective-permute-start | bytes 6291464 | tf_op jit(solution)/shard_map/ppermute | solution.py:104
  133.8 14.8 %collective-permute-start.36 = (bf16[2,2,4,2,128,128]{5,4,3,2,1,0:T(8,128)(2,1)S(1)}, bf16[2,2,4,2,128,128]{5,4,3,2,1,0:T(8,128)(2,1)S(1)}, u32[]{:S(2)}, u32[]{:S(2)}) collective-permute-start(bf16[2,2,4,2,128,128]{5,4,3,2,1,0:T(8,128)(2,1)S(1)} %get-tuple-element.136), channel_id=1, source_target_pairs={{0,1},{1,0},{2,3},{3,2},{4,5},{5,4},{6,7},{7,6},{8,9},{9,8},{10,11... | collective-permute-start | bytes 3145736 | tf_op jit(solution)/shard_map/ppermute | solution.py:104
  135.1 14.9 %collective-permute-start.35 = (bf16[32,128,128]{2,1,0:T(8,128)(2,1)S(1)}, bf16[32,128,128]{2,1,0:T(8,128)(2,1)S(1)}, u32[]{:S(2)}, u32[]{:S(2)}) collective-permute-start(bf16[32,128,128]{2,1,0:T(8,128)(2,1)S(1)} %step_0.1), channel_id=1, source_target_pairs={{0,4},{1,3},{2,6},{3,1},{4,0},{5,7},{6,2},{7,5},{8,12},{9,11},{10,... | collective-permute-start | bytes 3145736 | tf_op jit(solution)/shard_map/ppermute | solution.py:104
  148.5 19.6 %collective-permute-start.38 = (bf16[2,2,4,3,128,128]{5,4,3,2,1,0:T(8,128)(2,1)S(1)}, bf16[2,2,4,3,128,128]{5,4,3,2,1,0:T(8,128)(2,1)S(1)}, u32[]{:S(2)}, u32[]{:S(2)}) collective-permute-start(bf16[2,2,4,3,128,128]{5,4,3,2,1,0:T(8,128)(2,1)S(1)} %get-tuple-element.134), channel_id=1, source_target_pairs={{0,1},{1,0},{2,3},{3,2},{4,5},{5,4},{6,7},{7,6},{8,9},{9,8},{10,11... | collective-permute-start | bytes 4718600 | tf_op jit(solution)/shard_map/ppermute | solution.py:104
  151.0 17.1 %collective-permute-start.37 = (bf16[32,128,128]{2,1,0:T(8,128)(2,1)S(1)}, bf16[32,128,128]{2,1,0:T(8,128)(2,1)S(1)}, u32[]{:S(2)}, u32[]{:S(2)}) collective-permute-start(bf16[32,128,128]{2,1,0:T(8,128)(2,1)S(1)} %step_1.1), channel_id=1, source_target_pairs={{0,2},{1,5},{2,0},{3,7},{4,6},{5,1},{6,4},{7,3},{8,10},{9,13},{10,... | collective-permute-start | bytes 3145736 | tf_op jit(solution)/shard_map/ppermute | solution.py:104
  168.0 15.4 %collective-permute-start.43 = (bf16[2,2,4,3,128,128]{5,4,3,2,1,0:T(8,128)(2,1)S(1)}, bf16[2,2,4,3,128,128]{5,4,3,2,1,0:T(8,128)(2,1)S(1)}, u32[]{:S(2)}, u32[]{:S(2)}) collective-permute-start(bf16[2,2,4,3,128,128]{5,4,3,2,1,0:T(8,128)(2,1)S(1)} %get-tuple-element.142), channel_id=1, source_target_pairs={{0,1},{1,0},{2,3},{3,2},{4,5},{5,4},{6,7},{7,6},{8,9},{9,8},{10,11... | collective-permute-start | bytes 4718600 | tf_op jit(solution)/shard_map/ppermute | solution.py:104
  169.6 14.9 %collective-permute-start.42 = (bf16[32,128,128]{2,1,0:T(8,128)(2,1)S(1)}, bf16[32,128,128]{2,1,0:T(8,128)(2,1)S(1)}, u32[]{:S(2)}, u32[]{:S(2)}) collective-permute-start(bf16[32,128,128]{2,1,0:T(8,128)(2,1)S(1)} %get-tuple-element.144), channel_id=1, source_target_pairs={{0,4},{1,3},{2,6},{3,1},{4,0},{5,7},{6,2},{7,5},{8,12},{9,11},{10,... | collective-permute-start | bytes 3145736 | tf_op jit(solution)/shard_map/ppermute | solution.py:104
  170.5 12.1 %collective-permute-start.39 = (bf16[4,128,128]{2,1,0:T(8,128)(2,1)S(1)}, bf16[4,128,128]{2,1,0:T(8,128)(2,1)S(1)}, u32[]{:S(2)}, u32[]{:S(2)}) collective-permute-start(bf16[4,128,128]{2,1,0:T(8,128)(2,1)S(1)} %get-tuple-element.147), channel_id=1, source_target_pairs={{0,8},{1,9},{2,10},{3,11},{4,12},{5,13},{6,14},{7,15},{8,0},{9,1},... | collective-permute-start | bytes 393224 | tf_op jit(solution)/shard_map/ppermute | solution.py:104
  170.5 12.9 %collective-permute-start.40 = (bf16[4,128,128]{2,1,0:T(8,128)(2,1)S(1)}, bf16[4,128,128]{2,1,0:T(8,128)(2,1)S(1)}, u32[]{:S(2)}, u32[]{:S(2)}) collective-permute-start(bf16[4,128,128]{2,1,0:T(8,128)(2,1)S(1)} %get-tuple-element.148), channel_id=1, source_target_pairs={{0,16},{1,17},{2,18},{3,19},{4,20},{5,21},{6,22},{7,23},{8,24},{9,... | collective-permute-start | bytes 393224 | tf_op jit(solution)/shard_map/ppermute | solution.py:104
  172.8 10.6 %collective-permute-start.41 = (bf16[4,128,128]{2,1,0:T(8,128)(2,1)S(1)}, bf16[4,128,128]{2,1,0:T(8,128)(2,1)S(1)}, u32[]{:S(2)}, u32[]{:S(2)}) collective-permute-start(bf16[4,128,128]{2,1,0:T(8,128)(2,1)S(1)} %get-tuple-element.149), channel_id=1, source_target_pairs={{0,24},{1,25},{2,26},{3,27},{4,28},{5,29},{6,30},{7,31},{8,16},{9,... | collective-permute-start | bytes 393224 | tf_op jit(solution)/shard_map/ppermute | solution.py:104
  186.3 17.6 %collective-permute-start.47 = (bf16[36,128,128]{2,1,0:T(8,128)(2,1)S(1)}, bf16[36,128,128]{2,1,0:T(8,128)(2,1)S(1)}, u32[]{:S(2)}, u32[]{:S(2)}) collective-permute-start(bf16[36,128,128]{2,1,0:T(8,128)(2,1)S(1)} %get-tuple-element.151), channel_id=1, source_target_pairs={{0,2},{1,5},{2,0},{3,7},{4,6},{5,1},{6,4},{7,3},{8,10},{9,13},{10,... | collective-permute-start | bytes 3538952 | tf_op jit(solution)/shard_map/ppermute | solution.py:104
  187.0 16.9 %collective-permute-start.44 = (bf16[2,128,128]{2,1,0:T(8,128)(2,1)S(1)}, bf16[2,128,128]{2,1,0:T(8,128)(2,1)S(1)}, u32[]{:S(2)}, u32[]{:S(2)}) collective-permute-start(bf16[2,128,128]{2,1,0:T(8,128)(2,1)S(1)} %get-tuple-element.161), channel_id=1, source_target_pairs={{0,8},{1,9},{2,10},{3,11},{4,12},{5,13},{6,14},{7,15},{8,0},{9,1},... | collective-permute-start | bytes 196616 | tf_op jit(solution)/shard_map/ppermute | solution.py:104
  189.2 14.7 %collective-permute-start.45 = (bf16[2,128,128]{2,1,0:T(8,128)(2,1)S(1)}, bf16[2,128,128]{2,1,0:T(8,128)(2,1)S(1)}, u32[]{:S(2)}, u32[]{:S(2)}) collective-permute-start(bf16[2,128,128]{2,1,0:T(8,128)(2,1)S(1)} %get-tuple-element.162), channel_id=1, source_target_pairs={{0,16},{1,17},{2,18},{3,19},{4,20},{5,21},{6,22},{7,23},{8,24},{9,... | collective-permute-start | bytes 196616 | tf_op jit(solution)/shard_map/ppermute | solution.py:104
  189.5 14.4 %collective-permute-start.46 = (bf16[2,128,128]{2,1,0:T(8,128)(2,1)S(1)}, bf16[2,128,128]{2,1,0:T(8,128)(2,1)S(1)}, u32[]{:S(2)}, u32[]{:S(2)}) collective-permute-start(bf16[2,128,128]{2,1,0:T(8,128)(2,1)S(1)} %get-tuple-element.163), channel_id=1, source_target_pairs={{0,24},{1,25},{2,26},{3,27},{4,28},{5,29},{6,30},{7,31},{8,16},{9,... | collective-permute-start | bytes 196616 | tf_op jit(solution)/shard_map/ppermute | solution.py:104
  207.4 9.2 %collective-permute-start.49 = (bf16[12,128,128]{2,1,0:T(8,128)(2,1)S(1)}, bf16[12,128,128]{2,1,0:T(8,128)(2,1)S(1)}, u32[]{:S(2)}, u32[]{:S(2)}) collective-permute-start(bf16[12,128,128]{2,1,0:T(8,128)(2,1)S(1)} %step_5.1), channel_id=1, source_target_pairs={{0,4},{1,3},{2,6},{3,1},{4,0},{5,7},{6,2},{7,5},{8,12},{9,11},{10,... | collective-permute-start | bytes 1179656 | tf_op jit(solution)/shard_map/ppermute | solution.py:104
  208.6 7.3 %collective-permute-start.48 = (bf16[4,128,128]{2,1,0:T(8,128)(2,1)S(1)}, bf16[4,128,128]{2,1,0:T(8,128)(2,1)S(1)}, u32[]{:S(2)}, u32[]{:S(2)}) collective-permute-start(bf16[4,128,128]{2,1,0:T(8,128)(2,1)S(1)} %get-tuple-element.169), channel_id=1, source_target_pairs={{0,8},{1,9},{2,10},{3,11},{4,12},{5,13},{6,14},{7,15},{8,0},{9,1},... | collective-permute-start | bytes 393224 | tf_op jit(solution)/shard_map/ppermute | solution.py:104
  209.4 11.0 %collective-permute-start.50 = (bf16[4,128,128]{2,1,0:T(8,128)(2,1)S(1)}, bf16[4,128,128]{2,1,0:T(8,128)(2,1)S(1)}, u32[]{:S(2)}, u32[]{:S(2)}) collective-permute-start(bf16[4,128,128]{2,1,0:T(8,128)(2,1)S(1)} %get-tuple-element.175), channel_id=1, source_target_pairs={{0,16},{1,17},{2,18},{3,19},{4,20},{5,21},{6,22},{7,23},{8,24},{9,... | collective-permute-start | bytes 393224 | tf_op jit(solution)/shard_map/ppermute | solution.py:104
  210.9 9.5 %collective-permute-start.51 = (bf16[4,128,128]{2,1,0:T(8,128)(2,1)S(1)}, bf16[4,128,128]{2,1,0:T(8,128)(2,1)S(1)}, u32[]{:S(2)}, u32[]{:S(2)}) collective-permute-start(bf16[4,128,128]{2,1,0:T(8,128)(2,1)S(1)} %get-tuple-element.176), channel_id=1, source_target_pairs={{0,24},{1,25},{2,26},{3,27},{4,28},{5,29},{6,30},{7,31},{8,16},{9,... | collective-permute-start | bytes 393224 | tf_op jit(solution)/shard_map/ppermute | solution.py:104
  215.9 10.8 %collective-permute-start.59 = (bf16[6,128,128]{2,1,0:T(8,128)(2,1)S(1)}, bf16[6,128,128]{2,1,0:T(8,128)(2,1)S(1)}, u32[]{:S(2)}, u32[]{:S(2)}) collective-permute-start(bf16[6,128,128]{2,1,0:T(8,128)(2,1)S(1)} %step_6.1.refs_0_), channel_id=1, source_target_pairs={{0,2},{1,3},{2,0},{3,1},{4,6},{5,7},{6,4},{7,5},{8,10},{9,11},{10,... | collective-permute-start | bytes 589832 | tf_op jit(solution)/shard_map/ppermute | solution.py:104
  218.2 8.5 %collective-permute-start.52 = (bf16[3,128,128]{2,1,0:T(8,128)(2,1)S(1)}, bf16[3,128,128]{2,1,0:T(8,128)(2,1)S(1)}, u32[]{:S(2)}, u32[]{:S(2)}) collective-permute-start(bf16[3,128,128]{2,1,0:T(8,128)(2,1)S(1)} %get-tuple-element.177), channel_id=1, source_target_pairs={{0,8},{1,9},{2,10},{3,11},{4,12},{5,13},{6,14},{7,15},{8,0},{9,1},... | collective-permute-start | bytes 294920 | tf_op jit(solution)/shard_map/ppermute | solution.py:104
  221.6 10.9 %collective-permute-start.56 = (bf16[4,128,128]{2,1,0:T(8,128)(2,1)S(1)}, bf16[4,128,128]{2,1,0:T(8,128)(2,1)S(1)}, u32[]{:S(2)}, u32[]{:S(2)}) collective-permute-start(bf16[4,128,128]{2,1,0:T(8,128)(2,1)S(1)} %step_8.1.refs_0_), channel_id=1, source_target_pairs={{0,2},{1,3},{2,0},{3,1},{4,6},{5,7},{6,4},{7,5},{8,10},{9,11},{10,... | collective-permute-start | bytes 393224 | tf_op jit(solution)/shard_map/ppermute | solution.py:104
  222.4 7.5 %collective-permute-start.53 = (bf16[3,128,128]{2,1,0:T(8,128)(2,1)S(1)}, bf16[3,128,128]{2,1,0:T(8,128)(2,1)S(1)}, u32[]{:S(2)}, u32[]{:S(2)}) collective-permute-start(bf16[3,128,128]{2,1,0:T(8,128)(2,1)S(1)} %get-tuple-element.178), channel_id=1, source_target_pairs={{0,16},{1,17},{2,18},{3,19},{4,20},{5,21},{6,22},{7,23},{8,24},{9,... | collective-permute-start | bytes 294920 | tf_op jit(solution)/shard_map/ppermute | solution.py:104
  224.6 6.5 %collective-permute-start.54 = (bf16[3,128,128]{2,1,0:T(8,128)(2,1)S(1)}, bf16[3,128,128]{2,1,0:T(8,128)(2,1)S(1)}, u32[]{:S(2)}, u32[]{:S(2)}) collective-permute-start(bf16[3,128,128]{2,1,0:T(8,128)(2,1)S(1)} %get-tuple-element.179), channel_id=1, source_target_pairs={{0,24},{1,25},{2,26},{3,27},{4,28},{5,29},{6,30},{7,31},{8,16},{9,... | collective-permute-start | bytes 294920 | tf_op jit(solution)/shard_map/ppermute | solution.py:104
  226.7 9.8 %collective-permute-start.58 = (bf16[6,128,128]{2,1,0:T(8,128)(2,1)S(1)}, bf16[6,128,128]{2,1,0:T(8,128)(2,1)S(1)}, u32[]{:S(2)}, u32[]{:S(2)}) collective-permute-start(bf16[6,128,128]{2,1,0:T(8,128)(2,1)S(1)} %step_6.1.refs_0_), channel_id=1, source_target_pairs={{0,1},{1,0},{2,3},{3,2},{4,5},{5,4},{6,7},{7,6},{8,9},{9,8},{10,11... | collective-permute-start | bytes 589832 | tf_op jit(solution)/shard_map/ppermute | solution.py:104
  226.7 9.8 %collective-permute-start.60 = (bf16[6,128,128]{2,1,0:T(8,128)(2,1)S(1)}, bf16[6,128,128]{2,1,0:T(8,128)(2,1)S(1)}, u32[]{:S(2)}, u32[]{:S(2)}) collective-permute-start(bf16[6,128,128]{2,1,0:T(8,128)(2,1)S(1)} %collective-permute-done.59.refs_2_), channel_id=1, source_target_pairs={{0,1},{1,0},{2,3},{3,2},{4,5},{5,4},{6,7},{7,6},{8,9},{9,8},{10,11... | collective-permute-start | bytes 589832 | tf_op jit(solution)/shard_map/ppermute | solution.py:104
  (31 other events, 215.7 us)
